TPU v7x, 256 devices: a whole 4x4x8 slice. The times are simulated.
256 devices in a mesh: lm: 8 (over x, y_hi), tx: 32 (over y_lo, z, core).
Axes of the slice: x: 4, y: 4 (y_hi: 2, y_lo: 2; y = y_hi * 2 + y_lo), z: 8, core: 2. Of those that a mesh axis runs over, the one named last changes fastest.
Arguments:
- features: bfloat16 [65536, 256], P('tx'), may hold values from -1.7265625 to 1.7265625
- landmarks: bfloat16 [8192, 256], P(('lm', 'tx')), may hold values from -1.7265625 to 1.7265625
- whitening: bfloat16 [8192, 64], P(('lm', 'tx')), may hold values from -192 to 192
- cotangent: bfloat16 [65536, 64], P('tx'), may hold values from -6 to 6
Outputs:
- feature_grad: float32 [65536, 256], P(('tx', 'lm'))
- landmark_grad: float32 [8192, 256], P(('lm', 'tx'))
All inputs are finite; a program needn't handle non-finite values.
Results may differ from a plain program's by a relative error of at most 0.013.
Values may be sent and summed in bfloat16 or wider, within the bound.
No kernel may reach another device: no remote copies, remote signals or barrier semaphores. Data moves between devices by JAX's collectives and lax.ppermute only.
A program may use at most 64 MiB of HBM per device.

v0:
```python
import jax
import jax.numpy as jnp
from jax import lax
from jax.sharding import PartitionSpec as P


def norm_backward(embed, upstream):
    scale = lax.rsqrt(jnp.mean(embed * embed, axis=1, keepdims=True) + 1e-06)
    normed = embed * scale
    grad = scale * (upstream - normed * jnp.mean(upstream * normed, axis=1, keepdims=True))
    return grad.astype(jnp.bfloat16)


def per_device(features, landmarks, whitening, cotangent):
    land_rows, white_rows = (
        lax.all_gather(landmarks, "tx", axis=0, tiled=True),
        lax.all_gather(whitening, "tx", axis=0, tiled=True),
    )
    width = features.shape[1]
    tok_rows = features.shape[0]
    gamma = 4.0 / width
    feat32 = features.astype(jnp.float32)
    land32 = land_rows.astype(jnp.float32)
    sq_feat = jnp.sum(feat32 * feat32, axis=1, keepdims=True)
    sq_land = jnp.sum(land32 * land32, axis=1)
    cross = jnp.einsum("nf,mf->nm", features, land_rows, preferred_element_type=jnp.float32)
    kernel = jnp.exp(-gamma * (sq_feat + sq_land[None, :] - 2.0 * cross))
    kernel_b = kernel.astype(jnp.bfloat16)
    partial_embed = jnp.dot(kernel_b, white_rows, preferred_element_type=jnp.float32)
    groups = lax.axis_size("lm")
    group_rows = tok_rows // groups
    position = lax.axis_index("lm")
    embed = lax.psum(partial_embed, "lm")
    dembed = norm_backward(embed, cotangent.astype(jnp.float32))
    dkernel = jnp.einsum("nr,mr->nm", dembed, white_rows, preferred_element_type=jnp.float32)
    coef = (-gamma * dkernel * kernel).astype(jnp.bfloat16)
    row_total = jnp.sum(coef, axis=1, keepdims=True, dtype=jnp.float32)
    col_total = jnp.sum(coef, axis=0, dtype=jnp.float32)
    pulled = jnp.dot(coef, land_rows, preferred_element_type=jnp.float32)
    summed = lax.psum(2.0 * (row_total * feat32 - pulled), "lm")
    feature_grad = lax.dynamic_slice_in_dim(summed, position * group_rows, group_rows, 0)
    pulled = jnp.einsum("nm,nf->mf", coef, features, preferred_element_type=jnp.float32)
    landmark_grad = lax.psum_scatter(
        2.0 * (col_total[:, None] * land32 - pulled), "tx", scatter_dimension=0, tiled=True
    )
    return (feature_grad, landmark_grad)


def solution(mesh):
    placed = (P("tx", None), P(("lm", "tx"), None), P(("lm", "tx"), None), P("tx", None))
    return jax.shard_map(
        per_device,
        mesh=mesh,
        in_specs=placed,
        out_specs=(P(("tx", "lm"), None), P(("lm", "tx"), None)),
        check_vma=False,
    )
```

profile of v0, /device:TPU:24, one launch (start us, length us, event | category | flops | bytes accessed | tf_op | source)
XLA Modules:
  0.0 423.7 jit_solution(10804046327774706561)
XLA Ops:
  7.2 0.0 copy-start.1
  7.2 0.0 copy-start.3
  7.2 0.0 all-reduce.3.cloned.1.call-start
  7.2 38.2 %all_gather.6 = bf16[1024,256]{1,0:T(8,128)(2,1)S(1)} all-gather(bf16[32,256]{1,0:T(8,128)(2,1)} %param.5), channel_id=1, replica_groups=mesh['lm'=8,'tx'=32] {'tx'}, dimensions={0}, use_global_device_ids=true | all-gather | bytes 540672 | tf_op jit(solution)/shard_map/all_gather | solution.py:16
  45.4 0.2 fusion.6
  45.6 2.5 fusion.15
  48.1 0.0 copy-done.1
  48.2 0.0 copy-start
  48.2 0.0 copy-start.2
  48.2 0.3 fusion.4
  48.5 0.0 copy-done.3
  48.5 31.4 %all_gather.7 = bf16[1024,64]{1,0:T(8,128)(2,1)S(1)} all-gather(bf16[32,64]{1,0:T(8,128)(2,1)S(1)} %copy-done.3), channel_id=1, replica_groups=mesh['lm'=8,'tx'=32] {'tx'}, dimensions={0}, use_global_device_ids=true | all-gather | bytes 135168 | tf_op jit(solution)/shard_map/all_gather | solution.py:17
  80.0 0.0 copy-done
  80.0 3.1 fusion.1
  83.1 0.0 all-reduce.3.cloned.1.call-update
  83.1 0.0 all-reduce.5.cloned.1.call-start
  83.2 85.5 %all-reduce.3.cloned.1.call-done = f32[2048,64]{0,1:T(8,128)} async-done(((f32[2048,64]{0,1:T(8,128)}), f32[2048,64]{0,1:T(8,128)}) %all-reduce.3.cloned.1.call-update) | async-done | bytes 524304 | tf_op jit(solution)/shard_map/psum | solution.py:33
  168.7 1.1 multiply_reduce_fusion
  169.8 0.0 copy-done.2
  169.8 1.1 fusion.7
  171.0 6.1 %convert_reduce_fusion = (f32[1024]{0:T(1024)S(1)}, f32[2048]{0:T(1024)S(1)}, bf16[2048,1024]{1,0:T(8,128)(2,1)S(1)}) fusion(f32[2048,1024]{1,0:T(8,128)} %copy-done, f32[1024]{0:T(1024)S(1)} %fusion.6, f32[2048]{0:T(1024)S(1)} %fusion.4, bf16[1024,64]{1,0:T(8,128)(2,1)S(1)} %all_gather.7, bf16[2048,64]{0,1:T(8,128)(2,1)S(1)} %copy-done.2, ...), kind=kOutput, calls=%fused_computation | convolution fusion | flops 290190336 | bytes 13541376 | tf_op jit(solution)/shard_map/nr,mr->nm/dot_general | solution.py:35
  177.1 0.0 copy-start.4
  177.1 1.9 copy-done.4
  179.1 2.7 fusion.3
  181.7 0.0 all-reduce.5.cloned.1.call-update
  181.8 0.0 reduce-scatter.2.cloned.1.call-start
  181.8 4.6 %fusion.5 = f32[1024,256]{1,0:T(8,128)} fusion(bf16[2048,1024]{1,0:T(8,128)(2,1)} %copy-done.4, bf16[2048,256]{1,0:T(8,128)(2,1)S(1)} %copy-done.1, bf16[1024,256]{1,0:T(8,128)(2,1)S(1)} %all_gather.6, f32[1024]{0:T(1024)S(1)} %get-tuple-element.2), kind=kOutput, calls=%fused_computation.14 | convolution fusion | flops 1074790400 | bytes 6819840 | tf_op jit(solution)/shard_map/nm,nf->mf/dot_general | solution.py:42
  186.4 0.0 reduce-scatter.2.cloned.1.call-update
  186.4 109.6 %all-reduce.5.cloned.1.call-done = f32[2048,256]{1,0:T(8,128)} async-done(((f32[2048,256]{1,0:T(8,128)}), f32[2048,256]{1,0:T(8,128)}) %all-reduce.5.cloned.1.call-update) | async-done | bytes 2097168 | tf_op jit(solution)/shard_map/psum | solution.py:40
  296.0 1.7 constant_dynamic-slice_fusion
  297.7 119.5 %reduce-scatter.2.cloned.1.call-done = f32[32,256]{1,0:T(8,128)} async-done(((f32[1024,256]{1,0:T(8,128)}), f32[32,256]{1,0:T(8,128)}) %reduce-scatter.2.cloned.1.call-update) | async-done | bytes 32784 | tf_op jit(solution)/shard_map/reduce_scatter | solution.py:43
  (2 shorter events, 0.0 us)
Async XLA Ops:
  7.2 41.0 %copy-start.1 = (bf16[2048,256]{1,0:T(8,128)(2,1)S(1)}, bf16[2048,256]{1,0:T(8,128)(2,1)}, u32[]{:S(2)}) copy-start(bf16[2048,256]{1,0:T(8,128)(2,1)} %param.4) | copy-start | bytes 3145732
  7.2 41.4 %copy-start.3 = (bf16[32,64]{1,0:T(8,128)(2,1)S(1)}, bf16[32,64]{1,0:T(8,128)(2,1)}, u32[]{:S(2)}) copy-start(bf16[32,64]{1,0:T(8,128)(2,1)} %param.6) | copy-start | bytes 12292
  7.2 161.5 %all-reduce.3.cloned.1.call-start = ((), (), s32[]{:S(2)}) async-start(), calls=%async_computation.1 | async-start | bytes 1048576 | tf_op jit(solution)/shard_map/psum | solution.py:33
  48.2 31.8 %copy-start = (f32[2048,1024]{1,0:T(8,128)}, f32[2048,1024]{1,0:T(8,128)S(1)}, u32[]{:S(2)}) copy-start(f32[2048,1024]{1,0:T(8,128)S(1)} %fusion.15) | copy-start | bytes 25165828
  48.2 121.7 %copy-start.2 = (bf16[2048,64]{0,1:T(8,128)(2,1)S(1)}, bf16[2048,64]{0,1:T(8,128)(2,1)}, u32[]{:S(2)}) copy-start(bf16[2048,64]{0,1:T(8,128)(2,1)} %param.7) | copy-start | bytes 786436
  83.1 212.9 %all-reduce.5.cloned.1.call-start = ((), (), s32[]{:S(2)}) async-start(), calls=%async_computation.2 | async-start | bytes 4194304 | tf_op jit(solution)/shard_map/psum | solution.py:40
  177.1 1.9 copy-start.4
  181.8 235.4 %reduce-scatter.2.cloned.1.call-start = ((), (), s32[]{:S(2)}) async-start(), calls=%async_computation.3 | async-start | bytes 1081344 | tf_op jit(solution)/shard_map/reduce_scatter | solution.py:43
Sparse Core Ops, SparseCore 0:
  83.2 85.4 all-reduce.2
  181.9 114.0 all-reduce.4
  299.2 117.8 reduce-scatter.1
where the time goes:
time: 425 us; the launch traced here: 424 us
  waiting for transfers between devices  315 us (74%)
  blocking collectives  69.6 us (16%)
  matrix products  19 us (4%)
  between operations  13.9 us (3%)
    reduce_scatter x1, waiting for transfers between devices, per_device(): lax.psum_scatter(2.0 * (col_total[:, None] * land32 - pulled), 'tx', scat...  119 us
    psum x1, waiting for transfers between devices, per_device(): summed = lax.psum(2.0 * (row_total * feat32 - pulled), 'lm')  110 us
    psum x1, waiting for transfers between devices, per_device(): embed = lax.psum(partial_embed, 'lm')  85.5 us
    all_gather x1, blocking collectives, per_device(): lax.all_gather(landmarks, 'tx', axis=0, tiled=True)  38.2 us
    all_gather x1, blocking collectives, per_device(): lax.all_gather(whitening, 'tx', axis=0, tiled=True)  31.4 us
  transfers between devices with their start and end apart: 3, of which 3 were waited for; matrix products, arithmetic and copies ran while one was open for 1% of the time, Pallas kernels for 0%

commit v1 on v0

v1 whole, which is shorter than its diff:
```python
import jax
import jax.numpy as jnp
from jax import lax
from jax.sharding import Mesh, PartitionSpec as P

LM = ("x", "h")
CHIPS = ("l", "z")
F32 = jnp.float32
BF16 = jnp.bfloat16


def spread(block, axes, size):
    return lax.all_to_all(jnp.broadcast_to(block[None], (size,) + block.shape), axes, 0, 0, tiled=True)


def norm_backward(embed, upstream):
    scale = lax.rsqrt(jnp.mean(embed * embed, axis=1, keepdims=True) + 1e-06)
    normed = embed * scale
    grad = scale * (upstream - normed * jnp.mean(upstream * normed, axis=1, keepdims=True))
    return grad.astype(BF16)


def per_device(features, landmarks, whitening, cotangent):
    toks, width = features.shape
    rank = whitening.shape[1]
    groups = lax.axis_size(LM)
    chips = lax.axis_size(CHIPS)
    rows = landmarks.shape[0]
    group_toks = toks // groups
    gamma = 4.0 / width
    place = lax.axis_index(LM)
    core = lax.axis_index("c")

    both = jnp.concatenate([landmarks, whitening], axis=1)
    both = spread(both, CHIPS, chips).reshape(chips * rows, width + rank)
    both = lax.all_gather(both, "c", axis=0, tiled=True)
    land_rows, white_rows = both[:, :width], both[:, width:]

    feat32 = features.astype(F32)
    land32 = land_rows.astype(F32)
    sq_feat = jnp.sum(feat32 * feat32, axis=1, keepdims=True)
    sq_land = jnp.sum(land32 * land32, axis=1)
    cross = jnp.einsum("nf,mf->nm", features, land_rows, preferred_element_type=F32)
    kernel = jnp.exp(-gamma * (sq_feat + sq_land[None, :] - 2.0 * cross))
    partial_embed = jnp.dot(kernel.astype(BF16), white_rows, preferred_element_type=F32)

    shares = partial_embed.astype(BF16).reshape(groups, group_toks, rank)
    embed = jnp.sum(lax.all_to_all(shares, LM, 0, 0, tiled=True).astype(F32), axis=0)
    own_cot = lax.dynamic_slice_in_dim(cotangent, place * group_toks, group_toks, 0)
    own_dembed = norm_backward(embed, own_cot.astype(F32))
    dembed = spread(own_dembed, LM, groups).reshape(toks, rank)

    dkernel = jnp.einsum("nr,mr->nm", dembed, white_rows, preferred_element_type=F32)
    coef = (-gamma * dkernel * kernel).astype(BF16)
    row_total = jnp.sum(coef, axis=1, keepdims=True, dtype=F32)
    col_total = jnp.sum(coef, axis=0, dtype=F32)

    pulled = jnp.einsum("nm,nf->mf", coef, features, preferred_element_type=F32)
    land_share = (2.0 * (col_total[:, None] * land32 - pulled)).reshape(2, chips, rows, width)
    mine = lax.dynamic_index_in_dim(land_share, core, 0, keepdims=False)
    theirs = lax.dynamic_index_in_dim(land_share, 1 - core, 0, keepdims=False)
    mine = mine + lax.ppermute(theirs.astype(BF16), "c", [(0, 1), (1, 0)]).astype(F32)

    pulled = jnp.dot(coef, land_rows, preferred_element_type=F32)
    feat_share = (2.0 * (row_total * feat32 - pulled)).astype(BF16).reshape(groups, group_toks, width)
    feature_grad = jnp.sum(lax.all_to_all(feat_share, LM, 0, 0, tiled=True).astype(F32), axis=0)

    landmark_grad = jnp.sum(lax.all_to_all(mine.astype(BF16), CHIPS, 0, 0, tiled=True).astype(F32), axis=0)
    return (feature_grad, landmark_grad)


def solution(mesh):
    fine = Mesh(mesh.devices.reshape(4, 2, 2, 8, 2), ("x", "h", "l", "z", "c"))
    tx = ("l", "z", "c")
    placed = (P(tx, None), P(LM + tx, None), P(LM + tx, None), P(tx, None))
    return jax.shard_map(
        per_device,
        mesh=fine,
        in_specs=placed,
        out_specs=(P(tx + LM, None), P(LM + tx, None)),
        check_vma=False,
    )
```

time: 425 us -> 108 us (0.25)
  waiting for transfers between devices: 315 us -> 41.8 us
  blocking collectives: 69.6 us -> 2.36 us
  starting transfers between devices: 0.12 us -> 34.7 us
  between operations: 13.9 us -> 0.74 us
    psum x2 -> x0, waiting for transfers between devices: 195 us -> none  [the longest x1 110 us: per_device(): summed = lax.psum(2.0 * (row_total * feat32 - pulled), 'lm')]
    reduce_scatter x1 -> x0, waiting for transfers between devices: 119 us -> none  [per_device(): lax.psum_scatter(2.0 * (col_total[:, None] * land32 - pulled), 'tx', scat...]
    all_gather x2 -> x1, blocking collectives: 69.6 us -> 2.36 us  [per_device(): both = lax.all_gather(both, 'c', axis=0, tiled=True)]
    all_to_all x0 -> x5, waiting for transfers between devices: none -> 40.3 us  [the longest x2 16.4 us: spread(): lax.all_to_all(jnp.broadcast_to(block[None], (size,) + block.shape), axes...]
    all_to_all x0 -> x5, starting transfers between devices: none -> 34.6 us  [the longest x2 15.6 us: spread(): lax.all_to_all(jnp.broadcast_to(block[None], (size,) + block.shape), axes...]
  transfers between devices with their start and end apart: 3 -> 6, of which waited for: 3 -> 6; matrix products, arithmetic and copies ran while one was open for 1% -> 7% of each run, Pallas kernels for 0% -> 0%
where the time goes in v1:
time: 108 us; the launch traced here: 106 us
  waiting for transfers between devices  41.8 us (39%)
  starting transfers between devices  34.7 us (32%)
  matrix products  16.6 us (15%)
  other arithmetic  6.47 us (6%)
  local copies, waits for them, and re-layouts  3.71 us (3%)
  blocking collectives  2.36 us (2%)
    all_to_all x2, waiting for transfers between devices, spread(): lax.all_to_all(jnp.broadcast_to(block[None], (size,) + block.shape), axes...  16.4 us
    all_to_all x2, starting transfers between devices, spread(): lax.all_to_all(jnp.broadcast_to(block[None], (size,) + block.shape), axes...  15.6 us
    all_to_all x1, waiting for transfers between devices, per_device(): lax.all_to_all(feat_share, LM, 0, 0, tiled=True).astype(F32)  12.5 us
    all_to_all x1, starting transfers between devices, per_device(): lax.all_to_all(shares, LM, 0, 0, tiled=True).astype(F32)  7.26 us
    all_to_all x1, waiting for transfers between devices, per_device(): lax.all_to_all(shares, LM, 0, 0, tiled=True).astype(F32)  6.41 us
    all_to_all x1, starting transfers between devices, per_device(): lax.all_to_all(feat_share, LM, 0, 0, tiled=True).astype(F32)  6.11 us
    dot_general x1, matrix products, per_device(): jnp.einsum('nr,mr->nm', dembed, white_rows, preferred_element_type=F32)  5.84 us
    all_to_all x1, starting transfers between devices, per_device(): lax.all_to_all(mine.astype(BF16), CHIPS, 0, 0, tiled=True).astype(F32)  5.56 us
  transfers between devices with their start and end apart: 6, of which 6 were waited for; matrix products, arithmetic and copies ran while one was open for 7% of the time, Pallas kernels for 0%

profile of v1, /device:TPU:24, one launch (start us, length us, event | category | flops | bytes accessed | tf_op | source)
XLA Modules:
  0.0 106.4 jit_solution(1779536080963916609)
XLA Ops:
  0.6 0.7 pad_maximum_fusion
  1.4 0.8 broadcast_in_dim.4
  2.1 9.9 %all-to-all-start = ((bf16[16,32,320]{2,1,0:T(8,128)(2,1)}), bf16[16,32,320]{2,1,0:T(8,128)(2,1)S(1)}, u32[]{:S(2)}, u32[]{:S(2)}) async-start(bf16[16,32,320]{2,1,0:T(8,128)(2,1)} %broadcast_in_dim.4), calls=%async_computation | async-start | bytes 786432 | tf_op jit(solution)/shard_map/all_to_all | solution.py:13
  12.1 1.6 %fusion.10 = f32[2048]{0:T(1024)S(1)} fusion(bf16[2048,256]{1,0:T(8,128)(2,1)} %param.4), kind=kLoop, calls=%fused_computation.14 | loop fusion | flops 1570816 | bytes 1056768 | tf_op jit(solution)/shard_map/reduce_sum | solution.py:41
  13.7 10.3 %all-to-all-done = bf16[16,32,320]{2,1,0:T(8,128)(2,1)S(1)} async-done(((bf16[16,32,320]{2,1,0:T(8,128)(2,1)}), bf16[16,32,320]{2,1,0:T(8,128)(2,1)S(1)}, u32[]{:S(2)}, u32[]{:S(2)}) %all-to-all-start) | async-done | bytes 327712 | tf_op jit(solution)/shard_map/all_to_all | solution.py:13
  24.0 2.4 %all_gather.3 = bf16[1024,320]{1,0:T(8,128)(2,1)S(1)} all-gather(bf16[512,320]{1,0:T(8,128)(2,1)S(1)} %bitcast.33), channel_id=1, replica_groups=mesh['x'=4,'h'=2,'l'=2,'z'=8,'c'=2] {'c'}, dimensions={0}, use_global_device_ids=true | all-gather | bytes 983040 | tf_op jit(solution)/shard_map/all_gather | solution.py:36
  26.3 2.5 %fusion.15 = f32[1024,2048]{1,0:T(8,128)S(1)} fusion(bf16[2048,256]{1,0:T(8,128)(2,1)} %param.4, bf16[1024,320]{1,0:T(8,128)(2,1)S(1)} %all_gather.3), kind=kOutput, calls=%fused_computation.27 | convolution fusion | flops 1073741824 | bytes 9961472 | tf_op jit(solution)/shard_map/nf,mf->nm/dot_general | solution.py:43
  28.8 0.0 copy-start
  28.8 0.2 fusion.12
  29.1 2.2 %fusion.7 = bf16[2048,64]{0,1:T(8,128)(2,1)S(1)} fusion(f32[1024,2048]{1,0:T(8,128)S(1)} %fusion.15, f32[1024]{0:T(1024)S(1)} %fusion.12, f32[2048]{0:T(1024)S(1)} %fusion.10, bf16[1024,320]{1,0:T(8,128)(2,1)S(1)} %all_gather.3), kind=kOutput, calls=%fused_computation.13 | convolution fusion | flops 279052288 | bytes 8925184 | tf_op jit(solution)/shard_map/dot_general | solution.py:45
  31.3 0.8 copy-done
  32.1 0.7 copy.17
  32.8 7.3 %all-to-all-start.1 = ((bf16[8,256,64]{1,2,0:T(8,128)(2,1)}), bf16[8,256,64]{1,2,0:T(8,128)(2,1)S(1)}, u32[]{:S(2)}, u32[]{:S(2)}) async-start(bf16[8,256,64]{1,2,0:T(8,128)(2,1)} %bitcast.32), calls=%async_computation.1 | async-start | bytes 524288 | tf_op jit(solution)/shard_map/all_to_all | solution.py:48
  40.0 6.4 %all-to-all-done.1 = bf16[8,256,64]{1,2,0:T(8,128)(2,1)S(1)} async-done(((bf16[8,256,64]{1,2,0:T(8,128)(2,1)}), bf16[8,256,64]{1,2,0:T(8,128)(2,1)S(1)}, u32[]{:S(2)}, u32[]{:S(2)}) %all-to-all-start.1) | async-done | bytes 262176 | tf_op jit(solution)/shard_map/all_to_all | solution.py:48
  46.5 0.8 fusion.20
  47.3 0.8 fusion.22
  48.1 0.7 broadcast_in_dim.5
  48.8 5.7 %all-to-all-start.2 = ((bf16[8,256,64]{1,2,0:T(8,128)(2,1)}), bf16[8,256,64]{1,2,0:T(8,128)(2,1)S(1)}, u32[]{:S(2)}, u32[]{:S(2)}) async-start(bf16[8,256,64]{1,2,0:T(8,128)(2,1)} %broadcast_in_dim.5), calls=%async_computation.2 | async-start | bytes 524288 | tf_op jit(solution)/shard_map/all_to_all | solution.py:13
  54.5 6.1 %all-to-all-done.2 = bf16[8,256,64]{1,2,0:T(8,128)(2,1)S(1)} async-done(((bf16[8,256,64]{1,2,0:T(8,128)(2,1)}), bf16[8,256,64]{1,2,0:T(8,128)(2,1)S(1)}, u32[]{:S(2)}, u32[]{:S(2)}) %all-to-all-start.2) | async-done | bytes 262176 | tf_op jit(solution)/shard_map/all_to_all | solution.py:13
  60.7 0.0 copy-start.1
  60.7 5.8 %convert_reduce_fusion = (f32[1024]{0:T(1024)S(1)}, f32[2048]{0:T(1024)S(1)}, bf16[2048,1024]{0,1:T(8,128)(2,1)S(1)}) fusion(f32[1024,2048]{1,0:T(8,128)} %copy-done, f32[1024]{0:T(1024)S(1)} %fusion.12, f32[2048]{0:T(1024)S(1)} %fusion.10, bf16[2048,64]{0,1:T(8,128)(2,1)S(1)} %bitcast.37, bf16[1024,320]{1,0:T(8,128)(2,1)S(1)} %all_gather.3), kind=kOutput, calls=%fused_computation | convolution fusion | flops 289403904 | bytes 13131776 | tf_op jit(solution)/shard_map/nr,mr->nm/dot_general | solution.py:53
  66.6 0.0 copy-start.2
  66.6 0.0 copy-done.1
  66.6 1.3 %fusion.11 = f32[1024,256]{1,0:T(8,128)S(1)} fusion(bf16[2048,1024]{0,1:T(8,128)(2,1)S(1)} %get-tuple-element.4, bf16[2048,256]{1,0:T(8,128)(2,1)S(1)} %copy-done.1, f32[1024]{0:T(1024)S(1)} %get-tuple-element.2, bf16[1024,320]{1,0:T(8,128)(2,1)S(1)} %all_gather.3), kind=kOutput, calls=%fused_computation.19 | convolution fusion | flops 1074790400 | bytes 6819840 | tf_op jit(solution)/shard_map/nm,nf->mf/dot_general | solution.py:58
  67.9 0.6 copy-done.2
  68.5 0.1 collective-permute-start
  68.6 1.5 %collective-permute-done = bf16[16,32,256]{2,1,0:T(8,128)(2,1)S(1)} collective-permute-done((bf16[16,32,256]{2,1,0:T(8,128)(2,1)S(1)}, bf16[16,32,256]{2,1,0:T(8,128)(2,1)S(1)}, u32[]{:S(2)}, u32[]{:S(2)}) %collective-permute-start) | collective-permute-done | bytes 262176 | tf_op jit(solution)/shard_map/ppermute | solution.py:62
  70.2 0.8 fusion.13
  70.9 5.6 %all-to-all-start.4 = ((bf16[16,32,256]{2,1,0:T(8,128)(2,1)}), bf16[16,32,256]{2,1,0:T(8,128)(2,1)S(1)}, u32[]{:S(2)}, u32[]{:S(2)}) async-start(bf16[16,32,256]{2,1,0:T(8,128)(2,1)} %fusion.13), calls=%async_computation.4 | async-start | bytes 524288 | tf_op jit(solution)/shard_map/all_to_all | solution.py:68
  76.5 4.8 %fusion.6 = bf16[2048,256]{1,0:T(8,128)(2,1)} fusion(bf16[2048,1024]{0,1:T(8,128)(2,1)} %copy-done.2, bf16[2048,256]{1,0:T(8,128)(2,1)S(1)} %copy-done.1, f32[2048]{0:T(1024)S(1)} %get-tuple-element.3, bf16[1024,320]{1,0:T(8,128)(2,1)S(1)} %all_gather.3), kind=kOutput, calls=%fused_computation.12 | convolution fusion | flops 1076363264 | bytes 6823936 | tf_op jit(solution)/shard_map/dot_general | solution.py:64
  81.3 4.9 %all-to-all-done.4 = bf16[16,32,256]{2,1,0:T(8,128)(2,1)S(1)} async-done(((bf16[16,32,256]{2,1,0:T(8,128)(2,1)}), bf16[16,32,256]{2,1,0:T(8,128)(2,1)S(1)}, u32[]{:S(2)}, u32[]{:S(2)}) %all-to-all-start.4) | async-done | bytes 262176 | tf_op jit(solution)/shard_map/all_to_all | solution.py:68
  86.2 6.1 %all-to-all-start.3 = ((bf16[8,256,256]{2,1,0:T(8,128)(2,1)}), bf16[8,256,256]{2,1,0:T(8,128)(2,1)S(1)}, u32[]{:S(2)}, u32[]{:S(2)}) async-start(bf16[8,256,256]{2,1,0:T(8,128)(2,1)} %bitcast.2), calls=%async_computation.3 | async-start | bytes 2097152 | tf_op jit(solution)/shard_map/all_to_all | solution.py:66
  92.3 0.7 convert_reduce_fusion.3
  93.0 12.5 %all-to-all-done.3 = bf16[8,256,256]{2,1,0:T(8,128)(2,1)S(1)} async-done(((bf16[8,256,256]{2,1,0:T(8,128)(2,1)}), bf16[8,256,256]{2,1,0:T(8,128)(2,1)S(1)}, u32[]{:S(2)}, u32[]{:S(2)}) %all-to-all-start.3) | async-done | bytes 1048608 | tf_op jit(solution)/shard_map/all_to_all | solution.py:66
  105.5 0.8 convert_reduce_fusion.2
  (6 shorter events, 0.1 us)
Async XLA Ops:
  2.1 21.8 %all-to-all-start = ((bf16[16,32,320]{2,1,0:T(8,128)(2,1)}), bf16[16,32,320]{2,1,0:T(8,128)(2,1)S(1)}, u32[]{:S(2)}, u32[]{:S(2)}) async-start(bf16[16,32,320]{2,1,0:T(8,128)(2,1)} %broadcast_in_dim.4), calls=%async_computation | async-start | bytes 786432 | tf_op jit(solution)/shard_map/all_to_all | solution.py:13
  28.8 3.2 %copy-start = (f32[1024,2048]{1,0:T(8,128)}, f32[1024,2048]{1,0:T(8,128)S(1)}, u32[]{:S(2)}) copy-start(f32[1024,2048]{1,0:T(8,128)S(1)} %fusion.15) | copy-start | bytes 25165828
  32.8 13.7 %all-to-all-start.1 = ((bf16[8,256,64]{1,2,0:T(8,128)(2,1)}), bf16[8,256,64]{1,2,0:T(8,128)(2,1)S(1)}, u32[]{:S(2)}, u32[]{:S(2)}) async-start(bf16[8,256,64]{1,2,0:T(8,128)(2,1)} %bitcast.32), calls=%async_computation.1 | async-start | bytes 524288 | tf_op jit(solution)/shard_map/all_to_all | solution.py:48
  48.8 11.8 %all-to-all-start.2 = ((bf16[8,256,64]{1,2,0:T(8,128)(2,1)}), bf16[8,256,64]{1,2,0:T(8,128)(2,1)S(1)}, u32[]{:S(2)}, u32[]{:S(2)}) async-start(bf16[8,256,64]{1,2,0:T(8,128)(2,1)} %broadcast_in_dim.5), calls=%async_computation.2 | async-start | bytes 524288 | tf_op jit(solution)/shard_map/all_to_all | solution.py:13
  60.7 5.9 %copy-start.1 = (bf16[2048,256]{1,0:T(8,128)(2,1)S(1)}, bf16[2048,256]{1,0:T(8,128)(2,1)}, u32[]{:S(2)}) copy-start(bf16[2048,256]{1,0:T(8,128)(2,1)} %param.4) | copy-start | bytes 3145732
  66.6 1.9 %copy-start.2 = (bf16[2048,1024]{0,1:T(8,128)(2,1)}, bf16[2048,1024]{0,1:T(8,128)(2,1)S(1)}, u32[]{:S(2)}) copy-start(bf16[2048,1024]{0,1:T(8,128)(2,1)S(1)} %get-tuple-element.4) | copy-start | bytes 12582916
  68.5 1.6 %collective-permute-start = (bf16[16,32,256]{2,1,0:T(8,128)(2,1)S(1)}, bf16[16,32,256]{2,1,0:T(8,128)(2,1)S(1)}, u32[]{:S(2)}, u32[]{:S(2)}) collective-permute-start(bf16[16,32,256]{2,1,0:T(8,128)(2,1)S(1)} %fusion.17), channel_id=1, source_target_pairs={{0,1},{1,0},{2,3},{3,2},{4,5},{5,4},{6,7},{7,6},{8,9},{9,8},{10,11... | collective-permute-start | bytes 786440 | tf_op jit(solution)/shard_map/ppermute | solution.py:62
  70.9 15.3 %all-to-all-start.4 = ((bf16[16,32,256]{2,1,0:T(8,128)(2,1)}), bf16[16,32,256]{2,1,0:T(8,128)(2,1)S(1)}, u32[]{:S(2)}, u32[]{:S(2)}) async-start(bf16[16,32,256]{2,1,0:T(8,128)(2,1)} %fusion.13), calls=%async_computation.4 | async-start | bytes 524288 | tf_op jit(solution)/shard_map/all_to_all | solution.py:68
  86.2 19.3 %all-to-all-start.3 = ((bf16[8,256,256]{2,1,0:T(8,128)(2,1)}), bf16[8,256,256]{2,1,0:T(8,128)(2,1)S(1)}, u32[]{:S(2)}, u32[]{:S(2)}) async-start(bf16[8,256,256]{2,1,0:T(8,128)(2,1)} %bitcast.2), calls=%async_computation.3 | async-start | bytes 2097152 | tf_op jit(solution)/shard_map/all_to_all | solution.py:66

commit v2 on v1

v2 whole, which is shorter than its diff:
```python
import jax
import jax.numpy as jnp
from jax import lax
from jax.sharding import Mesh, PartitionSpec as P

Y = ("h", "l")
F32 = jnp.float32
BF16 = jnp.bfloat16


def shift(block, axes, step):
    size = lax.axis_size(axes)
    return lax.ppermute(block, axes, [(i, (i + step) % size) for i in range(size)])


def spread(block, axes):
    return [block] + [shift(block, axes, s) for s in range(1, lax.axis_size(axes))]


def collect(pieces, axes, direction):
    total = pieces[0]
    for s in range(1, lax.axis_size(axes)):
        total = total + shift(pieces[s].astype(BF16), axes, direction * s).astype(F32)
    return total


def norm_backward(embed, upstream):
    scale = lax.rsqrt(jnp.mean(embed * embed, axis=1, keepdims=True) + 1e-06)
    normed = embed * scale
    grad = scale * (upstream - normed * jnp.mean(upstream * normed, axis=1, keepdims=True))
    return grad.astype(BF16)


def per_device(features, landmarks, whitening, cotangent):
    toks, width = features.shape
    rank = whitening.shape[1]
    n_x, n_h, n_y, n_z = lax.axis_size("x"), lax.axis_size("h"), lax.axis_size(Y), lax.axis_size("z")
    own = toks // (n_x * n_h)
    rows = landmarks.shape[0]
    gamma = 4.0 / width
    here, half = lax.axis_index("x"), lax.axis_index("h")

    both = jnp.concatenate([landmarks, whitening], axis=1)
    both = jnp.concatenate(spread(both, "z"), axis=0)
    both = jnp.concatenate(spread(both, Y), axis=0)
    both = jnp.concatenate(spread(both, "c"), axis=0)
    land_rows, white_rows = both[:, :width], both[:, width:]

    def taken(array):
        return jnp.concatenate(
            [lax.dynamic_slice_in_dim(array, (((here + s) % n_x) * n_h + half) * own, own, 0) for s in range(n_x)], axis=0
        )

    features, cotangent = taken(features), taken(cotangent)
    feat32 = features.astype(F32)
    land32 = land_rows.astype(F32)
    sq_feat = jnp.sum(feat32 * feat32, axis=1, keepdims=True)
    sq_land = jnp.sum(land32 * land32, axis=1)
    cross = jnp.einsum("nf,mf->nm", features, land_rows, preferred_element_type=F32)
    kernel = jnp.exp(-gamma * (sq_feat + sq_land[None, :] - 2.0 * cross))
    partial_embed = jnp.dot(kernel.astype(BF16), white_rows, preferred_element_type=F32)

    shares = partial_embed.astype(BF16)
    embed = partial_embed
    for s in range(1, n_x):
        embed = embed + jnp.roll(shift(shares, "x", s), -s * own, axis=0).astype(F32)
    dembed = norm_backward(embed, cotangent.astype(F32))

    dkernel = jnp.einsum("nr,mr->nm", dembed, white_rows, preferred_element_type=F32)
    coef = (-gamma * dkernel * kernel).astype(BF16)
    row_total = jnp.sum(coef, axis=1, keepdims=True, dtype=F32)
    col_total = jnp.sum(coef, axis=0, dtype=F32)

    pulled = jnp.einsum("nm,nf->mf", coef, features, preferred_element_type=F32)
    share = (2.0 * (col_total[:, None] * land32 - pulled)).reshape(2, n_y, n_z, rows, width)
    share = collect(share, "c", -1)
    share = collect(share, Y, -1)
    landmark_grad = collect(share, "z", -1)

    pulled = jnp.dot(coef, land_rows, preferred_element_type=F32)
    share = (2.0 * (row_total * feat32 - pulled)).reshape(n_x, own, width)
    feature_grad = collect(share, "x", 1)
    return (feature_grad, landmark_grad)


def solution(mesh):
    fine = Mesh(mesh.devices.reshape(4, 2, 2, 8, 2), ("x", "h", "l", "z", "c"))
    lm, tx = ("x", "h"), ("l", "z", "c")
    placed = (P(tx, None), P(lm + tx, None), P(lm + tx, None), P(tx, None))
    return jax.shard_map(
        per_device,
        mesh=fine,
        in_specs=placed,
        out_specs=(P(tx + lm, None), P(lm + tx, None)),
        check_vma=False,
    )
```

time: 108 us -> 97.2 us (0.900)
  the two profiles are of different devices: /device:TPU:24 before, /device:TPU:64 now
where the time goes in v2:
time: 97.2 us; the launch traced here: 96.9 us
  starting transfers between devices  53.7 us (55%)
  waiting for transfers between devices  23.5 us (24%)
  matrix products  10.5 us (11%)
  local copies, waits for them, and re-layouts  5.9 us (6%)
  other arithmetic  2.37 us (2%)
  between operations  1.01 us (1%)
    ppermute x28, starting transfers between devices, shift(): lax.ppermute(block, axes, [(i, (i + step) % size) for i in range(size)])  53.7 us
    ppermute x28, waiting for transfers between devices, shift(): lax.ppermute(block, axes, [(i, (i + step) % size) for i in range(size)])  23.5 us
    dot_general x1, matrix products, per_device(): jnp.einsum('nr,mr->nm', dembed, white_rows, preferred_element_type=F32)  4.21 us
    unnamed x15, local copies, waits for them, and re-layouts  2.65 us
    dot_general x1, matrix products, per_device(): jnp.dot(kernel.astype(BF16), white_rows, preferred_element_type=F32)  2.13 us
  transfers between devices with their start and end apart: 28, of which 10 were waited for; matrix products, arithmetic and copies ran while one was open for 4% of the time, Pallas kernels for 0%

profile of v2, /device:TPU:64, one launch (start us, length us, event | category | flops | bytes accessed | tf_op | source)
XLA Modules:
  0.0 96.9 jit_solution(18322902252899909184)
XLA Ops:
  0.6 0.7 constant_dynamic-update-slice_fusion.22
  1.4 0.7 constant_dynamic-update-slice_fusion.21
  2.1 2.0 %collective-permute-start = (bf16[32,320]{1,0:T(8,128)(2,1)S(1)}, bf16[32,320]{1,0:T(8,128)(2,1)S(1)}, u32[]{:S(2)}, u32[]{:S(2)}) collective-permute-start(bf16[32,320]{1,0:T(8,128)(2,1)S(1)} %get-tuple-element.67), channel_id=1, source_target_pairs={{0,2},{2,4},{4,6},{6,8},{8,10},{10,12},{12,14},{14,0},{1,3},{3,5},... | collective-permute-start | bytes 61448 | tf_op jit(solution)/shard_map/ppermute | solution.py:13
  4.2 3.6 %collective-permute-start.5 = (bf16[32,320]{1,0:T(8,128)(2,1)S(1)}, bf16[32,320]{1,0:T(8,128)(2,1)S(1)}, u32[]{:S(2)}, u32[]{:S(2)}) collective-permute-start(bf16[32,320]{1,0:T(8,128)(2,1)S(1)} %get-tuple-element.67), channel_id=1, source_target_pairs={{0,12},{2,14},{4,0},{6,2},{8,4},{10,6},{12,8},{14,10},{1,13},{3,15... | collective-permute-start | bytes 61448 | tf_op jit(solution)/shard_map/ppermute | solution.py:13
  7.7 2.8 %collective-permute-start.4 = (bf16[32,320]{1,0:T(8,128)(2,1)S(1)}, bf16[32,320]{1,0:T(8,128)(2,1)S(1)}, u32[]{:S(2)}, u32[]{:S(2)}) collective-permute-start(bf16[32,320]{1,0:T(8,128)(2,1)S(1)} %get-tuple-element.67), channel_id=1, source_target_pairs={{0,10},{2,12},{4,14},{6,0},{8,2},{10,4},{12,6},{14,8},{1,11},{3,13... | collective-permute-start | bytes 61448 | tf_op jit(solution)/shard_map/ppermute | solution.py:13
  10.6 1.7 %collective-permute-start.3 = (bf16[32,320]{1,0:T(8,128)(2,1)S(1)}, bf16[32,320]{1,0:T(8,128)(2,1)S(1)}, u32[]{:S(2)}, u32[]{:S(2)}) collective-permute-start(bf16[32,320]{1,0:T(8,128)(2,1)S(1)} %get-tuple-element.67), channel_id=1, source_target_pairs={{0,8},{2,10},{4,12},{6,14},{8,0},{10,2},{12,4},{14,6},{1,9},{3,11}... | collective-permute-start | bytes 61448 | tf_op jit(solution)/shard_map/ppermute | solution.py:13
  12.2 3.6 %collective-permute-start.1 = (bf16[32,320]{1,0:T(8,128)(2,1)S(1)}, bf16[32,320]{1,0:T(8,128)(2,1)S(1)}, u32[]{:S(2)}, u32[]{:S(2)}) collective-permute-start(bf16[32,320]{1,0:T(8,128)(2,1)S(1)} %get-tuple-element.67), channel_id=1, source_target_pairs={{0,4},{2,6},{4,8},{6,10},{8,12},{10,14},{12,0},{14,2},{1,5},{3,7},... | collective-permute-start | bytes 61448 | tf_op jit(solution)/shard_map/ppermute | solution.py:13
  15.8 2.1 %collective-permute-done.1 = bf16[32,320]{1,0:T(8,128)(2,1)S(1)} collective-permute-done((bf16[32,320]{1,0:T(8,128)(2,1)S(1)}, bf16[32,320]{1,0:T(8,128)(2,1)S(1)}, u32[]{:S(2)}, u32[]{:S(2)}) %collective-permute-start.1) | collective-permute-done | bytes 20512 | tf_op jit(solution)/shard_map/ppermute | solution.py:13
  17.9 5.3 %collective-permute-start.2 = (bf16[32,320]{1,0:T(8,128)(2,1)S(1)}, bf16[32,320]{1,0:T(8,128)(2,1)S(1)}, u32[]{:S(2)}, u32[]{:S(2)}) collective-permute-start(bf16[32,320]{1,0:T(8,128)(2,1)S(1)} %get-tuple-element.67), channel_id=1, source_target_pairs={{0,6},{2,8},{4,10},{6,12},{8,14},{10,0},{12,2},{14,4},{1,7},{3,9},... | collective-permute-start | bytes 61448 | tf_op jit(solution)/shard_map/ppermute | solution.py:13
  23.2 1.5 %collective-permute-done.2 = bf16[32,320]{1,0:T(8,128)(2,1)S(1)} collective-permute-done((bf16[32,320]{1,0:T(8,128)(2,1)S(1)}, bf16[32,320]{1,0:T(8,128)(2,1)S(1)}, u32[]{:S(2)}, u32[]{:S(2)}) %collective-permute-start.2) | collective-permute-done | bytes 20512 | tf_op jit(solution)/shard_map/ppermute | solution.py:13
  24.9 1.7 %collective-permute-start.7 = (bf16[256,320]{1,0:T(8,128)(2,1)S(1)}, bf16[256,320]{1,0:T(8,128)(2,1)S(1)}, u32[]{:S(2)}, u32[]{:S(2)}) collective-permute-start(bf16[256,320]{1,0:T(8,128)(2,1)S(1)} %get-tuple-element.41), channel_id=1, source_target_pairs={{0,16},{16,32},{32,48},{48,0},{1,17},{17,33},{33,49},{49,1},{2,18}... | collective-permute-start | bytes 491528 | tf_op jit(solution)/shard_map/ppermute | solution.py:13
  26.5 2.9 %collective-permute-start.8 = (bf16[256,320]{1,0:T(8,128)(2,1)S(1)}, bf16[256,320]{1,0:T(8,128)(2,1)S(1)}, u32[]{:S(2)}, u32[]{:S(2)}) collective-permute-start(bf16[256,320]{1,0:T(8,128)(2,1)S(1)} %get-tuple-element.41), channel_id=1, source_target_pairs={{0,32},{16,48},{32,0},{48,16},{1,33},{17,49},{33,1},{49,17},{2,34}... | collective-permute-start | bytes 491528 | tf_op jit(solution)/shard_map/ppermute | solution.py:13
  29.4 1.3 %collective-permute-start.9 = (bf16[256,320]{1,0:T(8,128)(2,1)S(1)}, bf16[256,320]{1,0:T(8,128)(2,1)S(1)}, u32[]{:S(2)}, u32[]{:S(2)}) collective-permute-start(bf16[256,320]{1,0:T(8,128)(2,1)S(1)} %get-tuple-element.41), channel_id=1, source_target_pairs={{0,48},{16,0},{32,16},{48,32},{1,49},{17,1},{33,17},{49,33},{2,50}... | collective-permute-start | bytes 491528 | tf_op jit(solution)/shard_map/ppermute | solution.py:13
  30.8 2.1 %collective-permute-done.7 = bf16[256,320]{1,0:T(8,128)(2,1)S(1)} collective-permute-done((bf16[256,320]{1,0:T(8,128)(2,1)S(1)}, bf16[256,320]{1,0:T(8,128)(2,1)S(1)}, u32[]{:S(2)}, u32[]{:S(2)}) %collective-permute-start.7) | collective-permute-done | bytes 163872 | tf_op jit(solution)/shard_map/ppermute | solution.py:13
  32.9 2.2 %collective-permute-done.8 = bf16[256,320]{1,0:T(8,128)(2,1)S(1)} collective-permute-done((bf16[256,320]{1,0:T(8,128)(2,1)S(1)}, bf16[256,320]{1,0:T(8,128)(2,1)S(1)}, u32[]{:S(2)}, u32[]{:S(2)}) %collective-permute-start.8) | collective-permute-done | bytes 163872 | tf_op jit(solution)/shard_map/ppermute | solution.py:13
  35.3 0.3 copy.6
  35.6 0.3 collective-permute-start.10
  35.9 1.1 %constant_dynamic-slice_fusion.7 = (bf16[256,256]{1,0:T(8,128)(2,1)S(1)}, bf16[256,256]{1,0:T(8,128)(2,1)S(1)}, bf16[256,256]{1,0:T(8,128)(2,1)S(1)}, bf16[256,256]{1,0:T(8,128)(2,1)S(1)}) fusion(bf16[2048,256]{1,0:T(8,128)(2,1)} %param.4, s32[]{:T(128)S(6)} %select_n.44, s32[]{:T(128)S(6)} %select_n.46, s32[]{:T(128)S(6)} %select_n.50, s32[]{:T(128)S(6)} %select_n.48), kind=kLoop, calls=%fused_computation.104 | loop fusion | bytes 1048592 | tf_op jit(solution)/shard_map/dynamic_slice | solution.py:51
  37.1 0.2 fusion.7
  37.3 0.8 collective-permute-done.10
  38.1 1.4 %copy.7 = bf16[1024,320]{1,0:T(8,128)(2,1)S(1)} copy(bf16[1024,320]{0,1:T(8,128)(2,1)} %collective-permute-done.10) | data formatting | bytes 1310720 | tf_op jit(solution)/shard_map/ppermute | solution.py:13
  39.7 0.3 fusion.3
  40.1 1.3 %fusion.9 = f32[1024,2048]{1,0:T(8,128)S(1)} fusion(bf16[2048,320]{1,0:T(8,128)(2,1)S(1)} %constant_dynamic-update-slice_fusion.23, bf16[256,256]{1,0:T(8,128)(2,1)S(1)} %get-tuple-element.12, bf16[256,256]{1,0:T(8,128)(2,1)S(1)} %get-tuple-element.13, bf16[256,256]{1,0:T(8,128)(2,1)S(1)} %get-tuple-element.11, bf16[256,256]{1,0:T(8,128)(2,1)S(1)} %get-tuple-element.10), kind=kOutput, calls=%fused_computation.19 | convolution fusion | flops 1075838976 | bytes 9961472 | tf_op jit(solution)/shard_map/nf,mf->nm/dot_general | solution.py:59
  41.4 2.1 %fusion.40 = (bf16[1024,64]{0,1:T(8,128)(2,1)S(1)}, f32[1024,64]{0,1:T(8,128)S(1)}) fusion(bf16[2048,320]{1,0:T(8,128)(2,1)S(1)} %constant_dynamic-update-slice_fusion.23, f32[1024,2048]{1,0:T(8,128)S(1)} %fusion.9, f32[2048]{0:T(1024)S(1)} %fusion.3, f32[1024]{0:T(1024)S(1)} %fusion.7), kind=kOutput, calls=%fused_computation.113 | convolution fusion | flops 278986752 | bytes 9318400 | tf_op jit(solution)/shard_map/dot_general | solution.py:61
  43.5 2.8 %collective-permute-start.13 = (bf16[1024,64]{0,1:T(8,128)(2,1)S(1)}, bf16[1024,64]{0,1:T(8,128)(2,1)S(1)}, u32[]{:S(2)}, u32[]{:S(2)}) collective-permute-start(bf16[1024,64]{0,1:T(8,128)(2,1)S(1)} %get-tuple-element.68), channel_id=1, source_target_pairs={{0,192},{64,0},{128,64},{192,128},{1,193},{65,1},{129,65},{193,129... | collective-permute-start | bytes 393224 | tf_op jit(solution)/shard_map/ppermute | solution.py:13
  46.3 2.3 %collective-permute-start.12 = (bf16[1024,64]{0,1:T(8,128)(2,1)S(1)}, bf16[1024,64]{0,1:T(8,128)(2,1)S(1)}, u32[]{:S(2)}, u32[]{:S(2)}) collective-permute-start(bf16[1024,64]{0,1:T(8,128)(2,1)S(1)} %get-tuple-element.68), channel_id=1, source_target_pairs={{0,128},{64,192},{128,0},{192,64},{1,129},{65,193},{129,1},{193,65... | collective-permute-start | bytes 393224 | tf_op jit(solution)/shard_map/ppermute | solution.py:13
  48.6 0.7 collective-permute-done.13
  49.4 6.2 %collective-permute-done.11 = bf16[1024,64]{0,1:T(8,128)(2,1)S(1)} collective-permute-done((bf16[1024,64]{0,1:T(8,128)(2,1)S(1)}, bf16[1024,64]{0,1:T(8,128)(2,1)S(1)}, u32[]{:S(2)}, u32[]{:S(2)}) %collective-permute-start.11) | collective-permute-done | bytes 131104 | tf_op jit(solution)/shard_map/ppermute | solution.py:13
  55.8 4.2 %convert_reduce_fusion = (f32[2048]{0:T(1024)S(1)}, f32[1024]{0:T(1024)S(1)}, bf16[1024,2048]{1,0:T(8,128)(2,1)S(1)}) fusion(f32[1024,2048]{1,0:T(8,128)S(1)} %fusion.9, f32[2048]{0:T(1024)S(1)} %fusion.3, f32[1024]{0:T(1024)S(1)} %fusion.7, bf16[2048,320]{1,0:T(8,128)(2,1)S(1)} %constant_dynamic-update-slice_fusion.23, f32[1024,64]{0,1:T(8,128)S(1)} %get-tuple-element.9, ...), kind=kOutput, calls=%fused_computation | convolution fusion | flops 290255872 | bytes 13533184 | tf_op jit(solution)/shard_map/nr,mr->nm/dot_general | solution.py:69
  60.0 1.6 %fusion.5 = f32[2048,256]{1,0:T(8,128)S(1)} fusion(f32[2048]{0:T(1024)S(1)} %get-tuple-element.2, bf16[2048,320]{1,0:T(8,128)(2,1)S(1)} %constant_dynamic-update-slice_fusion.23, bf16[1024,2048]{1,0:T(8,128)(2,1)S(1)} %get-tuple-element.70, bf16[256,256]{1,0:T(8,128)(2,1)S(1)} %get-tuple-element.12, bf16[256,256]{1,0:T(8,128)(2,1)S(1)} %get-tuple-element.13, ...), kind=kOutput, calls=%fused_computation.10 | convolution fusion | flops 1077936128 | bytes 7872512 | tf_op jit(solution)/shard_map/nm,nf->mf/dot_general | solution.py:74
  61.7 0.3 collective-permute-start.17
  62.0 1.0 %copy-done = f32[2048,256]{1,0:T(8,128)} copy-done((f32[2048,256]{1,0:T(8,128)}, f32[2048,256]{1,0:T(8,128)S(1)}, u32[]{:S(2)}) %copy-start) | copy-done | bytes 2097176
  63.0 1.3 %fusion.41 = (bf16[1024,256]{1,0:T(8,128)(2,1)S(1)}, f32[1024,256]{1,0:T(8,128)S(1)}) fusion(bf16[1024,2048]{1,0:T(8,128)(2,1)S(1)} %get-tuple-element.70, bf16[2048,320]{1,0:T(8,128)(2,1)S(1)} %constant_dynamic-update-slice_fusion.23, bf16[256,256]{1,0:T(8,128)(2,1)S(1)} %get-tuple-element.12, bf16[256,256]{1,0:T(8,128)(2,1)S(1)} %get-tuple-element.13, ...), kind=kOutput, calls=%fused_computation.114 | convolution fusion | flops 1076887552 | bytes 7344128 | tf_op jit(solution)/shard_map/dot_general | solution.py:80
  64.3 0.2 fusion.37
  64.5 2.5 %collective-permute-start.18 = (bf16[8,32,256]{2,1,0:T(8,128)(2,1)S(1)}, bf16[8,32,256]{2,1,0:T(8,128)(2,1)S(1)}, u32[]{:S(2)}, u32[]{:S(2)}) collective-permute-start(bf16[8,32,256]{2,1,0:T(8,128)(2,1)S(1)} %get-tuple-element.14), channel_id=1, source_target_pairs={{0,48},{16,0},{32,16},{48,32},{1,49},{17,1},{33,17},{49,33},{2,50}... | collective-permute-start | bytes 393224 | tf_op jit(solution)/shard_map/ppermute | solution.py:13
  67.0 2.4 %collective-permute-start.19 = (bf16[8,32,256]{2,1,0:T(8,128)(2,1)S(1)}, bf16[8,32,256]{2,1,0:T(8,128)(2,1)S(1)}, u32[]{:S(2)}, u32[]{:S(2)}) collective-permute-start(bf16[8,32,256]{2,1,0:T(8,128)(2,1)S(1)} %get-tuple-element.16), channel_id=1, source_target_pairs={{0,32},{16,48},{32,0},{48,16},{1,33},{17,49},{33,1},{49,17},{2,34}... | collective-permute-start | bytes 393224 | tf_op jit(solution)/shard_map/ppermute | solution.py:13
  69.5 3.2 %collective-permute-start.16 = (bf16[256,256]{1,0:T(8,128)(2,1)S(1)}, bf16[256,256]{1,0:T(8,128)(2,1)S(1)}, u32[]{:S(2)}, u32[]{:S(2)}) collective-permute-start(bf16[256,256]{1,0:T(8,128)(2,1)S(1)} %get-tuple-element.18), channel_id=1, source_target_pairs={{0,192},{64,0},{128,64},{192,128},{1,193},{65,1},{129,65},{193,129... | collective-permute-start | bytes 393224 | tf_op jit(solution)/shard_map/ppermute | solution.py:13
  72.8 3.2 %collective-permute-done.20 = bf16[8,32,256]{2,1,0:T(8,128)(2,1)S(1)} collective-permute-done((bf16[8,32,256]{2,1,0:T(8,128)(2,1)S(1)}, bf16[8,32,256]{2,1,0:T(8,128)(2,1)S(1)}, u32[]{:S(2)}, u32[]{:S(2)}) %collective-permute-start.20) | collective-permute-done | bytes 131104 | tf_op jit(solution)/shard_map/ppermute | solution.py:13
  76.0 2.6 %collective-permute-start.21 = (bf16[32,256]{1,0:T(8,128)(2,1)S(1)}, bf16[32,256]{1,0:T(8,128)(2,1)S(1)}, u32[]{:S(2)}, u32[]{:S(2)}) collective-permute-start(bf16[32,256]{1,0:T(8,128)(2,1)S(1)} %get-tuple-element.30), channel_id=1, source_target_pairs={{0,14},{2,0},{4,2},{6,4},{8,6},{10,8},{12,10},{14,12},{1,15},{3,1}... | collective-permute-start | bytes 49160 | tf_op jit(solution)/shard_map/ppermute | solution.py:13
  78.6 3.4 %collective-permute-start.26 = (bf16[32,256]{1,0:T(8,128)(2,1)S(1)}, bf16[32,256]{1,0:T(8,128)(2,1)S(1)}, u32[]{:S(2)}, u32[]{:S(2)}) collective-permute-start(bf16[32,256]{1,0:T(8,128)(2,1)S(1)} %get-tuple-element.32), channel_id=1, source_target_pairs={{0,4},{2,6},{4,8},{6,10},{8,12},{10,14},{12,0},{14,2},{1,5},{3,7},... | collective-permute-start | bytes 49160 | tf_op jit(solution)/shard_map/ppermute | solution.py:13
  82.1 1.9 %collective-permute-start.25 = (bf16[32,256]{1,0:T(8,128)(2,1)S(1)}, bf16[32,256]{1,0:T(8,128)(2,1)S(1)}, u32[]{:S(2)}, u32[]{:S(2)}) collective-permute-start(bf16[32,256]{1,0:T(8,128)(2,1)S(1)} %get-tuple-element.33), channel_id=1, source_target_pairs={{0,6},{2,8},{4,10},{6,12},{8,14},{10,0},{12,2},{14,4},{1,7},{3,9},... | collective-permute-start | bytes 49160 | tf_op jit(solution)/shard_map/ppermute | solution.py:13
  84.0 2.5 %collective-permute-start.24 = (bf16[32,256]{1,0:T(8,128)(2,1)S(1)}, bf16[32,256]{1,0:T(8,128)(2,1)S(1)}, u32[]{:S(2)}, u32[]{:S(2)}) collective-permute-start(bf16[32,256]{1,0:T(8,128)(2,1)S(1)} %get-tuple-element.34), channel_id=1, source_target_pairs={{0,8},{2,10},{4,12},{6,14},{8,0},{10,2},{12,4},{14,6},{1,9},{3,11}... | collective-permute-start | bytes 49160 | tf_op jit(solution)/shard_map/ppermute | solution.py:13
  86.6 3.9 %collective-permute-start.23 = (bf16[32,256]{1,0:T(8,128)(2,1)S(1)}, bf16[32,256]{1,0:T(8,128)(2,1)S(1)}, u32[]{:S(2)}, u32[]{:S(2)}) collective-permute-start(bf16[32,256]{1,0:T(8,128)(2,1)S(1)} %get-tuple-element.35), channel_id=1, source_target_pairs={{0,10},{2,12},{4,14},{6,0},{8,2},{10,4},{12,6},{14,8},{1,11},{3,13... | collective-permute-start | bytes 49160 | tf_op jit(solution)/shard_map/ppermute | solution.py:13
  90.4 0.4 collective-permute-start.22
  90.9 0.8 fusion.20
  91.7 1.7 %collective-permute-done.23 = bf16[32,256]{1,0:T(8,128)(2,1)S(1)} collective-permute-done((bf16[32,256]{1,0:T(8,128)(2,1)S(1)}, bf16[32,256]{1,0:T(8,128)(2,1)S(1)}, u32[]{:S(2)}, u32[]{:S(2)}) %collective-permute-start.23) | collective-permute-done | bytes 16416 | tf_op jit(solution)/shard_map/ppermute | solution.py:13
  93.3 3.0 %collective-permute-done.22 = bf16[32,256]{1,0:T(8,128)(2,1)S(1)} collective-permute-done((bf16[32,256]{1,0:T(8,128)(2,1)S(1)}, bf16[32,256]{1,0:T(8,128)(2,1)S(1)}, u32[]{:S(2)}, u32[]{:S(2)}) %collective-permute-start.22) | collective-permute-done | bytes 16416 | tf_op jit(solution)/shard_map/ppermute | solution.py:13
  96.3 0.6 fusion.30
  (55 shorter events, 1.1 us)
Async XLA Ops:
  2.1 10.2 %collective-permute-start = (bf16[32,320]{1,0:T(8,128)(2,1)S(1)}, bf16[32,320]{1,0:T(8,128)(2,1)S(1)}, u32[]{:S(2)}, u32[]{:S(2)}) collective-permute-start(bf16[32,320]{1,0:T(8,128)(2,1)S(1)} %get-tuple-element.67), channel_id=1, source_target_pairs={{0,2},{2,4},{4,6},{6,8},{8,10},{10,12},{12,14},{14,0},{1,3},{3,5},... | collective-permute-start | bytes 61448 | tf_op jit(solution)/shard_map/ppermute | solution.py:13
  4.1 20.8 %collective-permute-start.6 = (bf16[32,320]{1,0:T(8,128)(2,1)S(1)}, bf16[32,320]{1,0:T(8,128)(2,1)S(1)}, u32[]{:S(2)}, u32[]{:S(2)}) collective-permute-start(bf16[32,320]{1,0:T(8,128)(2,1)S(1)} %get-tuple-element.67), channel_id=1, source_target_pairs={{0,14},{2,0},{4,2},{6,4},{8,6},{10,8},{12,10},{14,12},{1,15},{3,1}... | collective-permute-start | bytes 61448 | tf_op jit(solution)/shard_map/ppermute | solution.py:13
  4.2 20.6 %collective-permute-start.5 = (bf16[32,320]{1,0:T(8,128)(2,1)S(1)}, bf16[32,320]{1,0:T(8,128)(2,1)S(1)}, u32[]{:S(2)}, u32[]{:S(2)}) collective-permute-start(bf16[32,320]{1,0:T(8,128)(2,1)S(1)} %get-tuple-element.67), channel_id=1, source_target_pairs={{0,12},{2,14},{4,0},{6,2},{8,4},{10,6},{12,8},{14,10},{1,13},{3,15... | collective-permute-start | bytes 61448 | tf_op jit(solution)/shard_map/ppermute | solution.py:13
  7.7 17.0 %collective-permute-start.4 = (bf16[32,320]{1,0:T(8,128)(2,1)S(1)}, bf16[32,320]{1,0:T(8,128)(2,1)S(1)}, u32[]{:S(2)}, u32[]{:S(2)}) collective-permute-start(bf16[32,320]{1,0:T(8,128)(2,1)S(1)} %get-tuple-element.67), channel_id=1, source_target_pairs={{0,10},{2,12},{4,14},{6,0},{8,2},{10,4},{12,6},{14,8},{1,11},{3,13... | collective-permute-start | bytes 61448 | tf_op jit(solution)/shard_map/ppermute | solution.py:13
  10.6 14.2 %collective-permute-start.3 = (bf16[32,320]{1,0:T(8,128)(2,1)S(1)}, bf16[32,320]{1,0:T(8,128)(2,1)S(1)}, u32[]{:S(2)}, u32[]{:S(2)}) collective-permute-start(bf16[32,320]{1,0:T(8,128)(2,1)S(1)} %get-tuple-element.67), channel_id=1, source_target_pairs={{0,8},{2,10},{4,12},{6,14},{8,0},{10,2},{12,4},{14,6},{1,9},{3,11}... | collective-permute-start | bytes 61448 | tf_op jit(solution)/shard_map/ppermute | solution.py:13
  12.2 5.7 %collective-permute-start.1 = (bf16[32,320]{1,0:T(8,128)(2,1)S(1)}, bf16[32,320]{1,0:T(8,128)(2,1)S(1)}, u32[]{:S(2)}, u32[]{:S(2)}) collective-permute-start(bf16[32,320]{1,0:T(8,128)(2,1)S(1)} %get-tuple-element.67), channel_id=1, source_target_pairs={{0,4},{2,6},{4,8},{6,10},{8,12},{10,14},{12,0},{14,2},{1,5},{3,7},... | collective-permute-start | bytes 61448 | tf_op jit(solution)/shard_map/ppermute | solution.py:13
  17.9 6.8 %collective-permute-start.2 = (bf16[32,320]{1,0:T(8,128)(2,1)S(1)}, bf16[32,320]{1,0:T(8,128)(2,1)S(1)}, u32[]{:S(2)}, u32[]{:S(2)}) collective-permute-start(bf16[32,320]{1,0:T(8,128)(2,1)S(1)} %get-tuple-element.67), channel_id=1, source_target_pairs={{0,6},{2,8},{4,10},{6,12},{8,14},{10,0},{12,2},{14,4},{1,7},{3,9},... | collective-permute-start | bytes 61448 | tf_op jit(solution)/shard_map/ppermute | solution.py:13
  24.9 8.0 %collective-permute-start.7 = (bf16[256,320]{1,0:T(8,128)(2,1)S(1)}, bf16[256,320]{1,0:T(8,128)(2,1)S(1)}, u32[]{:S(2)}, u32[]{:S(2)}) collective-permute-start(bf16[256,320]{1,0:T(8,128)(2,1)S(1)} %get-tuple-element.41), channel_id=1, source_target_pairs={{0,16},{16,32},{32,48},{48,0},{1,17},{17,33},{33,49},{49,1},{2,18}... | collective-permute-start | bytes 491528 | tf_op jit(solution)/shard_map/ppermute | solution.py:13
  26.5 8.7 %collective-permute-start.8 = (bf16[256,320]{1,0:T(8,128)(2,1)S(1)}, bf16[256,320]{1,0:T(8,128)(2,1)S(1)}, u32[]{:S(2)}, u32[]{:S(2)}) collective-permute-start(bf16[256,320]{1,0:T(8,128)(2,1)S(1)} %get-tuple-element.41), channel_id=1, source_target_pairs={{0,32},{16,48},{32,0},{48,16},{1,33},{17,49},{33,1},{49,17},{2,34}... | collective-permute-start | bytes 491528 | tf_op jit(solution)/shard_map/ppermute | solution.py:13
  29.4 5.8 %collective-permute-start.9 = (bf16[256,320]{1,0:T(8,128)(2,1)S(1)}, bf16[256,320]{1,0:T(8,128)(2,1)S(1)}, u32[]{:S(2)}, u32[]{:S(2)}) collective-permute-start(bf16[256,320]{1,0:T(8,128)(2,1)S(1)} %get-tuple-element.41), channel_id=1, source_target_pairs={{0,48},{16,0},{32,16},{48,32},{1,49},{17,1},{33,17},{49,33},{2,50}... | collective-permute-start | bytes 491528 | tf_op jit(solution)/shard_map/ppermute | solution.py:13
  35.6 2.5 %collective-permute-start.10 = (bf16[1024,320]{0,1:T(8,128)(2,1)S(1)}, bf16[1024,320]{0,1:T(8,128)(2,1)}, u32[]{:S(2)}, u32[]{:S(2)}) collective-permute-start(bf16[1024,320]{0,1:T(8,128)(2,1)S(1)} %copy.6), channel_id=1, source_target_pairs={{0,1},{1,0},{2,3},{3,2},{4,5},{5,4},{6,7},{7,6},{8,9},{9,8},{10,11... | collective-permute-start | bytes 1966088 | tf_op jit(solution)/shard_map/ppermute | solution.py:13
  41.3 7.3 %copy-start.1 = (bf16[2048,64]{0,1:T(8,128)(2,1)S(1)}, bf16[2048,64]{0,1:T(8,128)(2,1)}, u32[]{:S(2)}) copy-start(bf16[2048,64]{0,1:T(8,128)(2,1)} %param.7) | copy-start | bytes 786436
  43.5 5.9 %collective-permute-start.13 = (bf16[1024,64]{0,1:T(8,128)(2,1)S(1)}, bf16[1024,64]{0,1:T(8,128)(2,1)S(1)}, u32[]{:S(2)}, u32[]{:S(2)}) collective-permute-start(bf16[1024,64]{0,1:T(8,128)(2,1)S(1)} %get-tuple-element.68), channel_id=1, source_target_pairs={{0,192},{64,0},{128,64},{192,128},{1,193},{65,1},{129,65},{193,129... | collective-permute-start | bytes 393224 | tf_op jit(solution)/shard_map/ppermute | solution.py:13
  46.3 9.3 %collective-permute-start.11 = (bf16[1024,64]{0,1:T(8,128)(2,1)S(1)}, bf16[1024,64]{0,1:T(8,128)(2,1)S(1)}, u32[]{:S(2)}, u32[]{:S(2)}) collective-permute-start(bf16[1024,64]{0,1:T(8,128)(2,1)S(1)} %get-tuple-element.68), channel_id=1, source_target_pairs={{0,64},{64,128},{128,192},{192,0},{1,65},{65,129},{129,193},{193,1... | collective-permute-start | bytes 393224 | tf_op jit(solution)/shard_map/ppermute | solution.py:13
  46.3 9.3 %collective-permute-start.12 = (bf16[1024,64]{0,1:T(8,128)(2,1)S(1)}, bf16[1024,64]{0,1:T(8,128)(2,1)S(1)}, u32[]{:S(2)}, u32[]{:S(2)}) collective-permute-start(bf16[1024,64]{0,1:T(8,128)(2,1)S(1)} %get-tuple-element.68), channel_id=1, source_target_pairs={{0,128},{64,192},{128,0},{192,64},{1,129},{65,193},{129,1},{193,65... | collective-permute-start | bytes 393224 | tf_op jit(solution)/shard_map/ppermute | solution.py:13
  61.6 1.4 %copy-start = (f32[2048,256]{1,0:T(8,128)}, f32[2048,256]{1,0:T(8,128)S(1)}, u32[]{:S(2)}) copy-start(f32[2048,256]{1,0:T(8,128)S(1)} %fusion.5) | copy-start | bytes 6291460
  61.7 2.6 %collective-permute-start.17 = (bf16[4,8,32,256]{3,2,1,0:T(8,128)(2,1)S(1)}, bf16[4,8,32,256]{3,2,1,0:T(8,128)(2,1)S(1)}, u32[]{:S(2)}, u32[]{:S(2)}) collective-permute-start(bf16[4,8,32,256]{3,2,1,0:T(8,128)(2,1)S(1)} %bitcast.50), channel_id=1, source_target_pairs={{0,1},{1,0},{2,3},{3,2},{4,5},{5,4},{6,7},{7,6},{8,9},{9,8},{10,11... | collective-permute-start | bytes 1572872 | tf_op jit(solution)/shard_map/ppermute | solution.py:13
  63.0 1.3 %slice-start = ((f32[2048,256]{1,0:T(8,128)}), f32[1024,256]{1,0:T(8,128)S(1)}, s32[]{:S(2)}) async-start(f32[2048,256]{1,0:T(8,128)} %copy-done), calls=%async_computation | async-start | bytes 2097152 | tf_op jit(solution)/shard_map/slice | solution.py:21
  64.5 8.2 %collective-permute-start.18 = (bf16[8,32,256]{2,1,0:T(8,128)(2,1)S(1)}, bf16[8,32,256]{2,1,0:T(8,128)(2,1)S(1)}, u32[]{:S(2)}, u32[]{:S(2)}) collective-permute-start(bf16[8,32,256]{2,1,0:T(8,128)(2,1)S(1)} %get-tuple-element.14), channel_id=1, source_target_pairs={{0,48},{16,0},{32,16},{48,32},{1,49},{17,1},{33,17},{49,33},{2,50}... | collective-permute-start | bytes 393224 | tf_op jit(solution)/shard_map/ppermute | solution.py:13
  67.0 8.9 %collective-permute-start.20 = (bf16[8,32,256]{2,1,0:T(8,128)(2,1)S(1)}, bf16[8,32,256]{2,1,0:T(8,128)(2,1)S(1)}, u32[]{:S(2)}, u32[]{:S(2)}) collective-permute-start(bf16[8,32,256]{2,1,0:T(8,128)(2,1)S(1)} %get-tuple-element.15), channel_id=1, source_target_pairs={{0,16},{16,32},{32,48},{48,0},{1,17},{17,33},{33,49},{49,1},{2,18}... | collective-permute-start | bytes 393224 | tf_op jit(solution)/shard_map/ppermute | solution.py:13
  67.0 8.9 %collective-permute-start.19 = (bf16[8,32,256]{2,1,0:T(8,128)(2,1)S(1)}, bf16[8,32,256]{2,1,0:T(8,128)(2,1)S(1)}, u32[]{:S(2)}, u32[]{:S(2)}) collective-permute-start(bf16[8,32,256]{2,1,0:T(8,128)(2,1)S(1)} %get-tuple-element.16), channel_id=1, source_target_pairs={{0,32},{16,48},{32,0},{48,16},{1,33},{17,49},{33,1},{49,17},{2,34}... | collective-permute-start | bytes 393224 | tf_op jit(solution)/shard_map/ppermute | solution.py:13
  69.4 9.2 %collective-permute-start.14 = (bf16[256,256]{1,0:T(8,128)(2,1)S(1)}, bf16[256,256]{1,0:T(8,128)(2,1)S(1)}, u32[]{:S(2)}, u32[]{:S(2)}) collective-permute-start(bf16[256,256]{1,0:T(8,128)(2,1)S(1)} %get-tuple-element.17), channel_id=1, source_target_pairs={{0,64},{64,128},{128,192},{192,0},{1,65},{65,129},{129,193},{193,1... | collective-permute-start | bytes 393224 | tf_op jit(solution)/shard_map/ppermute | solution.py:13
  69.5 12.5 %collective-permute-start.16 = (bf16[256,256]{1,0:T(8,128)(2,1)S(1)}, bf16[256,256]{1,0:T(8,128)(2,1)S(1)}, u32[]{:S(2)}, u32[]{:S(2)}) collective-permute-start(bf16[256,256]{1,0:T(8,128)(2,1)S(1)} %get-tuple-element.18), channel_id=1, source_target_pairs={{0,192},{64,0},{128,64},{192,128},{1,193},{65,1},{129,65},{193,129... | collective-permute-start | bytes 393224 | tf_op jit(solution)/shard_map/ppermute | solution.py:13
  72.8 11.2 %collective-permute-start.15 = (bf16[256,256]{1,0:T(8,128)(2,1)S(1)}, bf16[256,256]{1,0:T(8,128)(2,1)S(1)}, u32[]{:S(2)}, u32[]{:S(2)}) collective-permute-start(bf16[256,256]{1,0:T(8,128)(2,1)S(1)} %get-tuple-element.19), channel_id=1, source_target_pairs={{0,128},{64,192},{128,0},{192,64},{1,129},{65,193},{129,1},{193,65... | collective-permute-start | bytes 393224 | tf_op jit(solution)/shard_map/ppermute | solution.py:13
  76.0 10.5 %collective-permute-start.21 = (bf16[32,256]{1,0:T(8,128)(2,1)S(1)}, bf16[32,256]{1,0:T(8,128)(2,1)S(1)}, u32[]{:S(2)}, u32[]{:S(2)}) collective-permute-start(bf16[32,256]{1,0:T(8,128)(2,1)S(1)} %get-tuple-element.30), channel_id=1, source_target_pairs={{0,14},{2,0},{4,2},{6,4},{8,6},{10,8},{12,10},{14,12},{1,15},{3,1}... | collective-permute-start | bytes 49160 | tf_op jit(solution)/shard_map/ppermute | solution.py:13
  78.6 11.8 %collective-permute-start.27 = (bf16[32,256]{1,0:T(8,128)(2,1)S(1)}, bf16[32,256]{1,0:T(8,128)(2,1)S(1)}, u32[]{:S(2)}, u32[]{:S(2)}) collective-permute-start(bf16[32,256]{1,0:T(8,128)(2,1)S(1)} %get-tuple-element.31), channel_id=1, source_target_pairs={{0,2},{2,4},{4,6},{6,8},{8,10},{10,12},{12,14},{14,0},{1,3},{3,5},... | collective-permute-start | bytes 49160 | tf_op jit(solution)/shard_map/ppermute | solution.py:13
  78.6 13.0 %collective-permute-start.26 = (bf16[32,256]{1,0:T(8,128)(2,1)S(1)}, bf16[32,256]{1,0:T(8,128)(2,1)S(1)}, u32[]{:S(2)}, u32[]{:S(2)}) collective-permute-start(bf16[32,256]{1,0:T(8,128)(2,1)S(1)} %get-tuple-element.32), channel_id=1, source_target_pairs={{0,4},{2,6},{4,8},{6,10},{8,12},{10,14},{12,0},{14,2},{1,5},{3,7},... | collective-permute-start | bytes 49160 | tf_op jit(solution)/shard_map/ppermute | solution.py:13
  82.1 9.6 %collective-permute-start.25 = (bf16[32,256]{1,0:T(8,128)(2,1)S(1)}, bf16[32,256]{1,0:T(8,128)(2,1)S(1)}, u32[]{:S(2)}, u32[]{:S(2)}) collective-permute-start(bf16[32,256]{1,0:T(8,128)(2,1)S(1)} %get-tuple-element.33), channel_id=1, source_target_pairs={{0,6},{2,8},{4,10},{6,12},{8,14},{10,0},{12,2},{14,4},{1,7},{3,9},... | collective-permute-start | bytes 49160 | tf_op jit(solution)/shard_map/ppermute | solution.py:13
  84.0 7.6 %collective-permute-start.24 = (bf16[32,256]{1,0:T(8,128)(2,1)S(1)}, bf16[32,256]{1,0:T(8,128)(2,1)S(1)}, u32[]{:S(2)}, u32[]{:S(2)}) collective-permute-start(bf16[32,256]{1,0:T(8,128)(2,1)S(1)} %get-tuple-element.34), channel_id=1, source_target_pairs={{0,8},{2,10},{4,12},{6,14},{8,0},{10,2},{12,4},{14,6},{1,9},{3,11}... | collective-permute-start | bytes 49160 | tf_op jit(solution)/shard_map/ppermute | solution.py:13
  86.6 6.7 %collective-permute-start.23 = (bf16[32,256]{1,0:T(8,128)(2,1)S(1)}, bf16[32,256]{1,0:T(8,128)(2,1)S(1)}, u32[]{:S(2)}, u32[]{:S(2)}) collective-permute-start(bf16[32,256]{1,0:T(8,128)(2,1)S(1)} %get-tuple-element.35), channel_id=1, source_target_pairs={{0,10},{2,12},{4,14},{6,0},{8,2},{10,4},{12,6},{14,8},{1,11},{3,13... | collective-permute-start | bytes 49160 | tf_op jit(solution)/shard_map/ppermute | solution.py:13
  90.4 5.8 %collective-permute-start.22 = (bf16[32,256]{1,0:T(8,128)(2,1)S(1)}, bf16[32,256]{1,0:T(8,128)(2,1)S(1)}, u32[]{:S(2)}, u32[]{:S(2)}) collective-permute-start(bf16[32,256]{1,0:T(8,128)(2,1)S(1)} %get-tuple-element.36), channel_id=1, source_target_pairs={{0,12},{2,14},{4,0},{6,2},{8,4},{10,6},{12,8},{14,10},{1,13},{3,15... | collective-permute-start | bytes 49160 | tf_op jit(solution)/shard_map/ppermute | solution.py:13

commit v3 on v2

--- a/solution.py
+++ b/solution.py
@@ -24,6 +24,14 @@
     return total
 
 
+def spread_at_once(block, axes):
+    return lax.all_to_all(jnp.broadcast_to(block[None], (lax.axis_size(axes),) + block.shape), axes, 0, 0, tiled=True)
+
+
+def collect_at_once(pieces, axes):
+    return jnp.sum(lax.all_to_all(pieces.astype(BF16), axes, 0, 0, tiled=True).astype(F32), axis=0)
+
+
 def norm_backward(embed, upstream):
     scale = lax.rsqrt(jnp.mean(embed * embed, axis=1, keepdims=True) + 1e-06)
     normed = embed * scale
@@ -41,7 +49,7 @@
     here, half = lax.axis_index("x"), lax.axis_index("h")
 
     both = jnp.concatenate([landmarks, whitening], axis=1)
-    both = jnp.concatenate(spread(both, "z"), axis=0)
+    both = spread_at_once(both, "z").reshape(n_z * rows, width + rank)
     both = jnp.concatenate(spread(both, Y), axis=0)
     both = jnp.concatenate(spread(both, "c"), axis=0)
     land_rows, white_rows = both[:, :width], both[:, width:]
@@ -75,7 +83,7 @@
     share = (2.0 * (col_total[:, None] * land32 - pulled)).reshape(2, n_y, n_z, rows, width)
     share = collect(share, "c", -1)
     share = collect(share, Y, -1)
-    landmark_grad = collect(share, "z", -1)
+    landmark_grad = collect_at_once(share, "z")
 
     pulled = jnp.dot(coef, land_rows, preferred_element_type=F32)
     share = (2.0 * (row_total * feat32 - pulled)).reshape(n_x, own, width)

time: 97.2 us -> 85.9 us (0.88)
  the two profiles are of different devices: /device:TPU:64 before, /device:TPU:24 now
where the time goes in v3:
time: 85.9 us; the launch traced here: 84.7 us
  waiting for transfers between devices  26.1 us (30%)
  starting transfers between devices  20.2 us (24%)
  blocking collectives  18.7 us (22%)
  matrix products  11.4 us (13%)
  other arithmetic  4.88 us (6%)
  local copies, waits for them, and re-layouts  2.3 us (3%)
  between operations  0.97 us (1%)
    all_to_all x1, blocking collectives, spread_at_once(): lax.all_to_all(jnp.broadcast_to(block[None], (lax.axis_size(axes),) + blo...  18.7 us
    ppermute x14, waiting for transfers between devices, shift(): lax.ppermute(block, axes, [(i, (i + step) % size) for i in range(size)])  18.7 us
    ppermute x14, starting transfers between devices, shift(): lax.ppermute(block, axes, [(i, (i + step) % size) for i in range(size)])  16.9 us
    all_to_all x1, waiting for transfers between devices, collect_at_once(): lax.all_to_all(pieces.astype(BF16), axes, 0, 0, tiled=True).astype(F32)  7.42 us
    dot_general x1, matrix products, per_device(): jnp.einsum('nr,mr->nm', dembed, white_rows, preferred_element_type=F32)  4.21 us
    all_to_all x1, starting transfers between devices, collect_at_once(): lax.all_to_all(pieces.astype(BF16), axes, 0, 0, tiled=True).astype(F32)  3.37 us
    dot_general x1, matrix products, per_device(): pulled = jnp.dot(coef, land_rows, preferred_element_type=F32)  2.23 us
    dot_general x1, matrix products, per_device(): jnp.dot(kernel.astype(BF16), white_rows, preferred_element_type=F32)  2.13 us
  transfers between devices with their start and end apart: 15, of which 8 were waited for; matrix products, arithmetic and copies ran while one was open for 6% of the time, Pallas kernels for 0%

profile of v3, /device:TPU:24, one launch (start us, length us, event | category | flops | bytes accessed | tf_op | source)
XLA Modules:
  0.0 84.7 jit_solution(5450746112365569247)
XLA Ops:
  0.6 0.8 pad_maximum_fusion.3
  1.5 18.7 %all_to_all.10 = bf16[8,32,320]{2,1,0:T(8,128)(2,1)S(1)} all-to-all(bf16[8,32,320]{2,1,0:T(8,128)(2,1)S(1)} %broadcast_in_dim.2), channel_id=1, replica_groups=mesh['x'=4,'h'=2,'l'=2,'z'=8,'c'=2] {'z'}, dimensions={0} | all-to-all | bytes 327680 | tf_op jit(solution)/shard_map/all_to_all | solution.py:28
  20.2 0.7 collective-permute-start.2
  21.0 0.9 %collective-permute-start.1 = (bf16[256,320]{1,0:T(8,128)(2,1)S(1)}, bf16[256,320]{1,0:T(8,128)(2,1)S(1)}, u32[]{:S(2)}, u32[]{:S(2)}) collective-permute-start(bf16[256,320]{1,0:T(8,128)(2,1)S(1)} %bitcast.23), channel_id=1, source_target_pairs={{0,32},{16,48},{32,0},{48,16},{1,33},{17,49},{33,1},{49,17},{2,34}... | collective-permute-start | bytes 491528 | tf_op jit(solution)/shard_map/ppermute | solution.py:13
  21.9 2.2 %collective-permute-start = (bf16[256,320]{1,0:T(8,128)(2,1)S(1)}, bf16[256,320]{1,0:T(8,128)(2,1)S(1)}, u32[]{:S(2)}, u32[]{:S(2)}) collective-permute-start(bf16[256,320]{1,0:T(8,128)(2,1)S(1)} %bitcast.24), channel_id=1, source_target_pairs={{0,16},{16,32},{32,48},{48,0},{1,17},{17,33},{33,49},{49,1},{2,18}... | collective-permute-start | bytes 491528 | tf_op jit(solution)/shard_map/ppermute | solution.py:13
  24.1 6.3 %collective-permute-done.2 = bf16[256,320]{1,0:T(8,128)(2,1)S(1)} collective-permute-done((bf16[256,320]{1,0:T(8,128)(2,1)S(1)}, bf16[256,320]{1,0:T(8,128)(2,1)S(1)}, u32[]{:S(2)}, u32[]{:S(2)}) %collective-permute-start.2) | collective-permute-done | bytes 163872 | tf_op jit(solution)/shard_map/ppermute | solution.py:13
  30.4 0.0 collective-permute-done.1
  30.4 0.7 collective-permute-done
  31.0 0.1 pad_maximum_fusion
  31.1 0.3 copy.6
  31.4 0.1 collective-permute-start.3
  31.6 0.2 fusion.7
  32.0 1.7 %collective-permute-done.3 = bf16[1024,320]{0,1:T(8,128)(2,1)} collective-permute-done((bf16[1024,320]{0,1:T(8,128)(2,1)S(1)}, bf16[1024,320]{0,1:T(8,128)(2,1)}, u32[]{:S(2)}, u32[]{:S(2)}) %collective-permute-start.3) | collective-permute-done | bytes 655392 | tf_op jit(solution)/shard_map/ppermute | solution.py:13
  33.7 1.4 %copy.7 = bf16[1024,320]{1,0:T(8,128)(2,1)S(1)} copy(bf16[1024,320]{0,1:T(8,128)(2,1)} %collective-permute-done.3) | data formatting | bytes 1310720 | tf_op jit(solution)/shard_map/ppermute | solution.py:13
  35.1 0.2 constant_dynamic-update-slice_fusion
  35.3 0.3 fusion.3
  35.7 1.3 %fusion.9 = f32[1024,2048]{1,0:T(8,128)S(1)} fusion(bf16[2048,320]{1,0:T(8,128)(2,1)S(1)} %constant_dynamic-update-slice_fusion, bf16[256,256]{1,0:T(8,128)(2,1)S(1)} %get-tuple-element.10, bf16[256,256]{1,0:T(8,128)(2,1)S(1)} %get-tuple-element.11, bf16[256,256]{1,0:T(8,128)(2,1)S(1)} %get-tuple-element.9, bf16[256,256]{1,0:T(8,128)(2,1)S(1)} %get-tuple-element.8), kind=kOutput, calls=%fused_computation.20 | convolution fusion | flops 1075838976 | bytes 9961472 | tf_op jit(solution)/shard_map/nf,mf->nm/dot_general | solution.py:67
  37.0 0.0 copy-start.1
  37.0 2.1 %fusion.32 = (bf16[1024,64]{0,1:T(8,128)(2,1)S(1)}, f32[1024,64]{0,1:T(8,128)S(1)}) fusion(bf16[2048,320]{1,0:T(8,128)(2,1)S(1)} %constant_dynamic-update-slice_fusion, f32[1024,2048]{1,0:T(8,128)S(1)} %fusion.9, f32[2048]{0:T(1024)S(1)} %fusion.3, f32[1024]{0:T(1024)S(1)} %fusion.7), kind=kOutput, calls=%fused_computation.70 | convolution fusion | flops 278986752 | bytes 9318400 | tf_op jit(solution)/shard_map/dot_general | solution.py:69
  39.1 2.8 %collective-permute-start.6 = (bf16[1024,64]{0,1:T(8,128)(2,1)S(1)}, bf16[1024,64]{0,1:T(8,128)(2,1)S(1)}, u32[]{:S(2)}, u32[]{:S(2)}) collective-permute-start(bf16[1024,64]{0,1:T(8,128)(2,1)S(1)} %get-tuple-element.24), channel_id=1, source_target_pairs={{0,192},{64,0},{128,64},{192,128},{1,193},{65,1},{129,65},{193,129... | collective-permute-start | bytes 393224 | tf_op jit(solution)/shard_map/ppermute | solution.py:13
  41.9 0.0 collective-permute-start.4
  41.9 2.3 %collective-permute-start.5 = (bf16[1024,64]{0,1:T(8,128)(2,1)S(1)}, bf16[1024,64]{0,1:T(8,128)(2,1)S(1)}, u32[]{:S(2)}, u32[]{:S(2)}) collective-permute-start(bf16[1024,64]{0,1:T(8,128)(2,1)S(1)} %get-tuple-element.24), channel_id=1, source_target_pairs={{0,128},{64,192},{128,0},{192,64},{1,129},{65,193},{129,1},{193,65... | collective-permute-start | bytes 393224 | tf_op jit(solution)/shard_map/ppermute | solution.py:13
  44.3 0.7 collective-permute-done.6
  45.0 6.2 %collective-permute-done.4 = bf16[1024,64]{0,1:T(8,128)(2,1)S(1)} collective-permute-done((bf16[1024,64]{0,1:T(8,128)(2,1)S(1)}, bf16[1024,64]{0,1:T(8,128)(2,1)S(1)}, u32[]{:S(2)}, u32[]{:S(2)}) %collective-permute-start.4) | collective-permute-done | bytes 131104 | tf_op jit(solution)/shard_map/ppermute | solution.py:13
  51.2 0.0 collective-permute-done.5
  51.3 0.1 multiply_reduce_fusion
  51.4 0.1 fusion.13
  51.4 4.2 %convert_reduce_fusion = (f32[2048]{0:T(1024)S(1)}, f32[1024]{0:T(1024)S(1)}, bf16[1024,2048]{1,0:T(8,128)(2,1)S(1)}) fusion(f32[1024,2048]{1,0:T(8,128)S(1)} %fusion.9, f32[2048]{0:T(1024)S(1)} %fusion.3, f32[1024]{0:T(1024)S(1)} %fusion.7, bf16[2048,320]{1,0:T(8,128)(2,1)S(1)} %constant_dynamic-update-slice_fusion, f32[1024,64]{0,1:T(8,128)S(1)} %get-tuple-element.7, ...), kind=kOutput, calls=%fused_computation | convolution fusion | flops 290255872 | bytes 13533184 | tf_op jit(solution)/shard_map/nr,mr->nm/dot_general | solution.py:77
  55.7 1.6 %fusion.5 = f32[2048,256]{1,0:T(8,128)S(1)} fusion(f32[2048]{0:T(1024)S(1)} %get-tuple-element.2, bf16[2048,320]{1,0:T(8,128)(2,1)S(1)} %constant_dynamic-update-slice_fusion, bf16[1024,2048]{1,0:T(8,128)(2,1)S(1)} %get-tuple-element.26, bf16[256,256]{1,0:T(8,128)(2,1)S(1)} %get-tuple-element.10, bf16[256,256]{1,0:T(8,128)(2,1)S(1)} %get-tuple-element.11, ...), kind=kOutput, calls=%fused_computation.10 | convolution fusion | flops 1077936128 | bytes 7872512 | tf_op jit(solution)/shard_map/nm,nf->mf/dot_general | solution.py:82
  57.2 0.1 slice.137
  57.3 0.1 collective-permute-start.10
  57.4 0.1 slice.103
  57.5 2.2 %fusion.33 = (bf16[1024,256]{1,0:T(8,128)(2,1)S(1)}, f32[1024,256]{1,0:T(8,128)}) fusion(bf16[1024,2048]{1,0:T(8,128)(2,1)S(1)} %get-tuple-element.26, bf16[2048,320]{1,0:T(8,128)(2,1)S(1)} %constant_dynamic-update-slice_fusion, bf16[256,256]{1,0:T(8,128)(2,1)S(1)} %get-tuple-element.10, bf16[256,256]{1,0:T(8,128)(2,1)S(1)} %get-tuple-element.11, ...), kind=kOutput, calls=%fused_computation.71 | convolution fusion | flops 1076887552 | bytes 7344128 | tf_op jit(solution)/shard_map/dot_general | solution.py:88
  59.7 0.2 fusion.29
  60.0 0.6 collective-permute-start.11
  60.6 2.7 %collective-permute-start.13 = (bf16[8,32,256]{2,1,0:T(8,128)(2,1)S(1)}, bf16[8,32,256]{2,1,0:T(8,128)(2,1)S(1)}, u32[]{:S(2)}, u32[]{:S(2)}) collective-permute-start(bf16[8,32,256]{2,1,0:T(8,128)(2,1)S(1)} %get-tuple-element.13), channel_id=1, source_target_pairs={{0,16},{16,32},{32,48},{48,0},{1,17},{17,33},{33,49},{49,1},{2,18}... | collective-permute-start | bytes 393224 | tf_op jit(solution)/shard_map/ppermute | solution.py:13
  63.3 0.8 collective-permute-start.12
  64.1 0.1 collective-permute-start.7
  64.2 3.2 %collective-permute-start.9 = (bf16[256,256]{1,0:T(8,128)(2,1)S(1)}, bf16[256,256]{1,0:T(8,128)(2,1)S(1)}, u32[]{:S(2)}, u32[]{:S(2)}) collective-permute-start(bf16[256,256]{1,0:T(8,128)(2,1)S(1)} %get-tuple-element.16), channel_id=1, source_target_pairs={{0,192},{64,0},{128,64},{192,128},{1,193},{65,1},{129,65},{193,129... | collective-permute-start | bytes 393224 | tf_op jit(solution)/shard_map/ppermute | solution.py:13
  67.4 0.0 collective-permute-done.11
  67.4 0.3 collective-permute-start.8
  67.7 1.6 %collective-permute-done.13 = bf16[8,32,256]{2,1,0:T(8,128)(2,1)S(1)} collective-permute-done((bf16[8,32,256]{2,1,0:T(8,128)(2,1)S(1)}, bf16[8,32,256]{2,1,0:T(8,128)(2,1)S(1)}, u32[]{:S(2)}, u32[]{:S(2)}) %collective-permute-start.13) | collective-permute-done | bytes 131104 | tf_op jit(solution)/shard_map/ppermute | solution.py:13
  69.2 1.5 %collective-permute-done.12 = bf16[8,32,256]{2,1,0:T(8,128)(2,1)S(1)} collective-permute-done((bf16[8,32,256]{2,1,0:T(8,128)(2,1)S(1)}, bf16[8,32,256]{2,1,0:T(8,128)(2,1)S(1)}, u32[]{:S(2)}, u32[]{:S(2)}) %collective-permute-start.12) | collective-permute-done | bytes 131104 | tf_op jit(solution)/shard_map/ppermute | solution.py:13
  70.8 0.7 fusion.19
  71.5 3.4 %all-to-all-start.1 = ((bf16[8,32,256]{2,1,0:T(8,128)(2,1)}), bf16[8,32,256]{2,1,0:T(8,128)(2,1)S(1)}, u32[]{:S(2)}, u32[]{:S(2)}) async-start(bf16[8,32,256]{2,1,0:T(8,128)(2,1)} %fusion.19), calls=%async_computation.1 | async-start | bytes 262144 | tf_op jit(solution)/shard_map/all_to_all | solution.py:32
  74.9 1.7 %fusion.21 = f32[256,256]{1,0:T(8,128)} fusion(f32[1024,256]{1,0:T(8,128)} %get-tuple-element.28, bf16[256,256]{1,0:T(8,128)(2,1)S(1)} %collective-permute-done.9, bf16[256,256]{1,0:T(8,128)(2,1)S(1)} %collective-permute-done.8, bf16[256,256]{1,0:T(8,128)(2,1)S(1)} %collective-permute-done.7), kind=kLoop, calls=%fused_computation.37 | loop fusion | flops 393216 | bytes 917504 | tf_op jit(solution)/shard_map/add | solution.py:23
  76.6 7.4 %all-to-all-done.1 = bf16[8,32,256]{2,1,0:T(8,128)(2,1)S(1)} async-done(((bf16[8,32,256]{2,1,0:T(8,128)(2,1)}), bf16[8,32,256]{2,1,0:T(8,128)(2,1)S(1)}, u32[]{:S(2)}, u32[]{:S(2)}) %all-to-all-start.1) | async-done | bytes 131104 | tf_op jit(solution)/shard_map/all_to_all | solution.py:32
  84.0 0.6 convert_reduce_fusion.2
  (23 shorter events, 0.3 us)
Async XLA Ops:
  0.6 30.9 %copy-start = (bf16[2048,256]{1,0:T(8,128)(2,1)S(1)}, bf16[2048,256]{1,0:T(8,128)(2,1)}, u32[]{:S(2)}) copy-start(bf16[2048,256]{1,0:T(8,128)(2,1)} %param.4) | copy-start | bytes 3145732
  20.2 10.1 %collective-permute-start.2 = (bf16[256,320]{1,0:T(8,128)(2,1)S(1)}, bf16[256,320]{1,0:T(8,128)(2,1)S(1)}, u32[]{:S(2)}, u32[]{:S(2)}) collective-permute-start(bf16[256,320]{1,0:T(8,128)(2,1)S(1)} %bitcast.22), channel_id=1, source_target_pairs={{0,48},{16,0},{32,16},{48,32},{1,49},{17,1},{33,17},{49,33},{2,50}... | collective-permute-start | bytes 491528 | tf_op jit(solution)/shard_map/ppermute | solution.py:13
  21.0 9.4 %collective-permute-start.1 = (bf16[256,320]{1,0:T(8,128)(2,1)S(1)}, bf16[256,320]{1,0:T(8,128)(2,1)S(1)}, u32[]{:S(2)}, u32[]{:S(2)}) collective-permute-start(bf16[256,320]{1,0:T(8,128)(2,1)S(1)} %bitcast.23), channel_id=1, source_target_pairs={{0,32},{16,48},{32,0},{48,16},{1,33},{17,49},{33,1},{49,17},{2,34}... | collective-permute-start | bytes 491528 | tf_op jit(solution)/shard_map/ppermute | solution.py:13
  21.9 9.1 %collective-permute-start = (bf16[256,320]{1,0:T(8,128)(2,1)S(1)}, bf16[256,320]{1,0:T(8,128)(2,1)S(1)}, u32[]{:S(2)}, u32[]{:S(2)}) collective-permute-start(bf16[256,320]{1,0:T(8,128)(2,1)S(1)} %bitcast.24), channel_id=1, source_target_pairs={{0,16},{16,32},{32,48},{48,0},{1,17},{17,33},{33,49},{49,1},{2,18}... | collective-permute-start | bytes 491528 | tf_op jit(solution)/shard_map/ppermute | solution.py:13
  31.4 2.3 %collective-permute-start.3 = (bf16[1024,320]{0,1:T(8,128)(2,1)S(1)}, bf16[1024,320]{0,1:T(8,128)(2,1)}, u32[]{:S(2)}, u32[]{:S(2)}) collective-permute-start(bf16[1024,320]{0,1:T(8,128)(2,1)S(1)} %copy.6), channel_id=1, source_target_pairs={{0,1},{1,0},{2,3},{3,2},{4,5},{5,4},{6,7},{7,6},{8,9},{9,8},{10,11... | collective-permute-start | bytes 1966088 | tf_op jit(solution)/shard_map/ppermute | solution.py:13
  37.0 7.3 %copy-start.1 = (bf16[2048,64]{0,1:T(8,128)(2,1)S(1)}, bf16[2048,64]{0,1:T(8,128)(2,1)}, u32[]{:S(2)}) copy-start(bf16[2048,64]{0,1:T(8,128)(2,1)} %param.7) | copy-start | bytes 786436
  39.1 5.9 %collective-permute-start.6 = (bf16[1024,64]{0,1:T(8,128)(2,1)S(1)}, bf16[1024,64]{0,1:T(8,128)(2,1)S(1)}, u32[]{:S(2)}, u32[]{:S(2)}) collective-permute-start(bf16[1024,64]{0,1:T(8,128)(2,1)S(1)} %get-tuple-element.24), channel_id=1, source_target_pairs={{0,192},{64,0},{128,64},{192,128},{1,193},{65,1},{129,65},{193,129... | collective-permute-start | bytes 393224 | tf_op jit(solution)/shard_map/ppermute | solution.py:13
  41.9 9.3 %collective-permute-start.4 = (bf16[1024,64]{0,1:T(8,128)(2,1)S(1)}, bf16[1024,64]{0,1:T(8,128)(2,1)S(1)}, u32[]{:S(2)}, u32[]{:S(2)}) collective-permute-start(bf16[1024,64]{0,1:T(8,128)(2,1)S(1)} %get-tuple-element.24), channel_id=1, source_target_pairs={{0,64},{64,128},{128,192},{192,0},{1,65},{65,129},{129,193},{193,1... | collective-permute-start | bytes 393224 | tf_op jit(solution)/shard_map/ppermute | solution.py:13
  41.9 9.3 %collective-permute-start.5 = (bf16[1024,64]{0,1:T(8,128)(2,1)S(1)}, bf16[1024,64]{0,1:T(8,128)(2,1)S(1)}, u32[]{:S(2)}, u32[]{:S(2)}) collective-permute-start(bf16[1024,64]{0,1:T(8,128)(2,1)S(1)} %get-tuple-element.24), channel_id=1, source_target_pairs={{0,128},{64,192},{128,0},{192,64},{1,129},{65,193},{129,1},{193,65... | collective-permute-start | bytes 393224 | tf_op jit(solution)/shard_map/ppermute | solution.py:13
  57.3 2.4 %collective-permute-start.10 = (bf16[4,8,32,256]{3,2,1,0:T(8,128)(2,1)S(1)}, bf16[4,8,32,256]{3,2,1,0:T(8,128)(2,1)S(1)}, u32[]{:S(2)}, u32[]{:S(2)}) collective-permute-start(bf16[4,8,32,256]{3,2,1,0:T(8,128)(2,1)S(1)} %bitcast.27), channel_id=1, source_target_pairs={{0,1},{1,0},{2,3},{3,2},{4,5},{5,4},{6,7},{7,6},{8,9},{9,8},{10,11... | collective-permute-start | bytes 1572872 | tf_op jit(solution)/shard_map/ppermute | solution.py:13
  60.0 7.5 %collective-permute-start.11 = (bf16[8,32,256]{2,1,0:T(8,128)(2,1)S(1)}, bf16[8,32,256]{2,1,0:T(8,128)(2,1)S(1)}, u32[]{:S(2)}, u32[]{:S(2)}) collective-permute-start(bf16[8,32,256]{2,1,0:T(8,128)(2,1)S(1)} %get-tuple-element.12), channel_id=1, source_target_pairs={{0,48},{16,0},{32,16},{48,32},{1,49},{17,1},{33,17},{49,33},{2,50}... | collective-permute-start | bytes 393224 | tf_op jit(solution)/shard_map/ppermute | solution.py:13
  60.6 8.7 %collective-permute-start.13 = (bf16[8,32,256]{2,1,0:T(8,128)(2,1)S(1)}, bf16[8,32,256]{2,1,0:T(8,128)(2,1)S(1)}, u32[]{:S(2)}, u32[]{:S(2)}) collective-permute-start(bf16[8,32,256]{2,1,0:T(8,128)(2,1)S(1)} %get-tuple-element.13), channel_id=1, source_target_pairs={{0,16},{16,32},{32,48},{48,0},{1,17},{17,33},{33,49},{49,1},{2,18}... | collective-permute-start | bytes 393224 | tf_op jit(solution)/shard_map/ppermute | solution.py:13
  63.3 7.5 %collective-permute-start.12 = (bf16[8,32,256]{2,1,0:T(8,128)(2,1)S(1)}, bf16[8,32,256]{2,1,0:T(8,128)(2,1)S(1)}, u32[]{:S(2)}, u32[]{:S(2)}) collective-permute-start(bf16[8,32,256]{2,1,0:T(8,128)(2,1)S(1)} %get-tuple-element.14), channel_id=1, source_target_pairs={{0,32},{16,48},{32,0},{48,16},{1,33},{17,49},{33,1},{49,17},{2,34}... | collective-permute-start | bytes 393224 | tf_op jit(solution)/shard_map/ppermute | solution.py:13
  64.1 10.8 %collective-permute-start.7 = (bf16[256,256]{1,0:T(8,128)(2,1)S(1)}, bf16[256,256]{1,0:T(8,128)(2,1)S(1)}, u32[]{:S(2)}, u32[]{:S(2)}) collective-permute-start(bf16[256,256]{1,0:T(8,128)(2,1)S(1)} %get-tuple-element.15), channel_id=1, source_target_pairs={{0,64},{64,128},{128,192},{192,0},{1,65},{65,129},{129,193},{193,1... | collective-permute-start | bytes 393224 | tf_op jit(solution)/shard_map/ppermute | solution.py:13
  64.2 10.7 %collective-permute-start.9 = (bf16[256,256]{1,0:T(8,128)(2,1)S(1)}, bf16[256,256]{1,0:T(8,128)(2,1)S(1)}, u32[]{:S(2)}, u32[]{:S(2)}) collective-permute-start(bf16[256,256]{1,0:T(8,128)(2,1)S(1)} %get-tuple-element.16), channel_id=1, source_target_pairs={{0,192},{64,0},{128,64},{192,128},{1,193},{65,1},{129,65},{193,129... | collective-permute-start | bytes 393224 | tf_op jit(solution)/shard_map/ppermute | solution.py:13
  67.4 7.5 %collective-permute-start.8 = (bf16[256,256]{1,0:T(8,128)(2,1)S(1)}, bf16[256,256]{1,0:T(8,128)(2,1)S(1)}, u32[]{:S(2)}, u32[]{:S(2)}) collective-permute-start(bf16[256,256]{1,0:T(8,128)(2,1)S(1)} %get-tuple-element.17), channel_id=1, source_target_pairs={{0,128},{64,192},{128,0},{192,64},{1,129},{65,193},{129,1},{193,65... | collective-permute-start | bytes 393224 | tf_op jit(solution)/shard_map/ppermute | solution.py:13
  71.5 12.5 %all-to-all-start.1 = ((bf16[8,32,256]{2,1,0:T(8,128)(2,1)}), bf16[8,32,256]{2,1,0:T(8,128)(2,1)S(1)}, u32[]{:S(2)}, u32[]{:S(2)}) async-start(bf16[8,32,256]{2,1,0:T(8,128)(2,1)} %fusion.19), calls=%async_computation.1 | async-start | bytes 262144 | tf_op jit(solution)/shard_map/all_to_all | solution.py:32

commit v4 on v3

v4 whole, which is shorter than its diff:
```python
import functools

import jax
import jax.numpy as jnp
from jax import lax
from jax.experimental import pallas as pl
from jax.experimental.pallas import tpu as pltpu
from jax.sharding import Mesh, PartitionSpec as P

Y = ("h", "l")
F32 = jnp.float32
BF16 = jnp.bfloat16
LOG2E = 1.4426950408889634
WHOLE = pl.BlockSpec(memory_space=pltpu.VMEM)
PARAMS = pltpu.CompilerParams(vmem_limit_bytes=20 * 2**20)


def forward_body(count, width, *refs):
    blocks, (feat_t, sq_feat, prior), (kern, embed) = refs[:count], refs[count:-2], refs[-2:]
    rows = blocks[0].shape[0]
    scale = 4.0 / width * LOG2E
    bias = sq_feat[...] * (-scale)
    total = prior[...]
    for i, block in enumerate(blocks):
        land, white = block[:, :width], block[:, width:]
        land32 = land.astype(F32)
        sq_land = jnp.sum(land32 * land32, axis=1, keepdims=True) * (-scale)
        cross = jnp.dot(land, feat_t[...], preferred_element_type=F32)
        value = jnp.exp2(cross * (2.0 * scale) + (bias + sq_land)).astype(BF16)
        kern[i * rows : (i + 1) * rows, :] = value
        total = total + lax.dot_general(white, value, (((0,), (0,)), ((), ())), preferred_element_type=F32)
    embed[...] = total


def forward(blocks, feat_t, sq_feat, prior):
    width, toks = feat_t.shape
    rows = sum(block.shape[0] for block in blocks)
    return pl.pallas_call(
        functools.partial(forward_body, len(blocks), width),
        out_shape=[jax.ShapeDtypeStruct((rows, toks), BF16), jax.ShapeDtypeStruct(prior.shape, F32)],
        in_specs=[WHOLE] * (len(blocks) + 3),
        out_specs=[WHOLE] * 2,
        compiler_params=PARAMS,
    )(*blocks, feat_t, sq_feat, prior)


def backward_body(count, width, *refs):
    blocks, (kern, dembed, feat, prior) = refs[:count], refs[count:-3]
    coef, land_grad, row_total = refs[-3:]
    rows = blocks[0].shape[0]
    total = prior[...]
    for i, block in enumerate(blocks):
        land, white = block[:, :width], block[:, width:]
        at = slice(i * rows, (i + 1) * rows)
        dkernel = jnp.dot(white, dembed[...], preferred_element_type=F32)
        value = (dkernel * kern[at, :].astype(F32)).astype(BF16)
        coef[at, :] = value
        value32 = value.astype(F32)
        total = total + jnp.sum(value32, axis=0, keepdims=True)
        col_total = jnp.sum(value32, axis=1, keepdims=True)
        pulled = jnp.dot(value, feat[...], preferred_element_type=F32)
        land_grad[at, :] = (2.0 * (col_total * land.astype(F32) - pulled)).astype(land_grad.dtype)
    row_total[...] = total


def backward(blocks, kern, dembed, feat, prior, kind):
    toks, width = feat.shape
    rows = kern.shape[0]
    return pl.pallas_call(
        functools.partial(backward_body, len(blocks), width),
        out_shape=[
            jax.ShapeDtypeStruct((rows, toks), BF16),
            jax.ShapeDtypeStruct((rows, width), kind),
            jax.ShapeDtypeStruct(prior.shape, F32),
        ],
        in_specs=[WHOLE] * (len(blocks) + 4),
        out_specs=[WHOLE] * 3,
        compiler_params=PARAMS,
    )(*blocks, kern, dembed, feat, prior)


def feature_body(count, coefs, width, *refs):
    blocks, coef, (feat_t, row_total), outs = refs[:count], refs[count : count + coefs], refs[count + coefs : count + coefs + 2], refs[count + coefs + 2 :]
    rows = blocks[0].shape[0]
    each = count // coefs
    step = feat_t.shape[1] // len(outs)
    pulled = None
    for i, block in enumerate(blocks):
        at = slice(i % each * rows, (i % each + 1) * rows)
        part = lax.dot_general(block[:, :width], coef[i // each][at, :], (((0,), (0,)), ((), ())), preferred_element_type=F32)
        pulled = part if pulled is None else pulled + part
    grad = 2.0 * (row_total[...] * feat_t[...].astype(F32) - pulled)
    for i, out in enumerate(outs):
        out[...] = grad[:, i * step : (i + 1) * step].astype(out.dtype)


def feature_share(blocks, coefs, feat_t, row_total, parts):
    width, toks = feat_t.shape
    kinds = [F32] + [BF16] * (parts - 1)
    return pl.pallas_call(
        functools.partial(feature_body, len(blocks), len(coefs), width),
        out_shape=[jax.ShapeDtypeStruct((width, toks // parts), kind) for kind in kinds],
        in_specs=[WHOLE] * (len(blocks) + len(coefs) + 2),
        out_specs=[WHOLE] * parts,
        compiler_params=PARAMS,
    )(*blocks, *coefs, feat_t, row_total)


def shift(block, axes, step):
    size = lax.axis_size(axes)
    return lax.ppermute(block, axes, [(i, (i + step) % size) for i in range(size)])


def spread(block, axes):
    return [block] + [shift(block, axes, s) for s in range(1, lax.axis_size(axes))]


def collect(pieces, axes, direction):
    total = pieces[0]
    for s in range(1, lax.axis_size(axes)):
        total = total + shift(pieces[s].astype(BF16), axes, direction * s).astype(F32)
    return total


def spread_at_once(block, axes):
    return lax.all_to_all(jnp.broadcast_to(block[None], (lax.axis_size(axes),) + block.shape), axes, 0, 0, tiled=True)


def collect_at_once(pieces, axes):
    return jnp.sum(lax.all_to_all(pieces.astype(BF16), axes, 0, 0, tiled=True).astype(F32), axis=0)


def norm_backward(embed, upstream, factor):
    scale = lax.rsqrt(jnp.mean(embed * embed, axis=0, keepdims=True) + 1e-06)
    normed = embed * scale
    grad = scale * (upstream - normed * jnp.mean(upstream * normed, axis=0, keepdims=True))
    return (factor * grad).astype(BF16)


def per_device(features, landmarks, whitening, cotangent):
    toks, width = features.shape
    rank = whitening.shape[1]
    n_x, n_h, n_y, n_z = lax.axis_size("x"), lax.axis_size("h"), lax.axis_size(Y), lax.axis_size("z")
    own = toks // (n_x * n_h)
    rows = landmarks.shape[0]
    gamma = 4.0 / width
    here, half = lax.axis_index("x"), lax.axis_index("h")

    def taken(array):
        return jnp.concatenate(
            [lax.dynamic_slice_in_dim(array, (((here + s) % n_x) * n_h + half) * own, own, 0) for s in range(n_x)], axis=0
        )

    features, cotangent = taken(features), taken(cotangent)
    feat_t, cot_t = features.T, cotangent.T.astype(F32)
    feat32 = features.astype(F32)
    sq_feat = jnp.sum(feat32 * feat32, axis=1)[None, :]

    both = jnp.concatenate([landmarks, whitening], axis=1)
    both = spread_at_once(both, "z").reshape(n_z * rows, width + rank)
    mine = spread(both, Y)
    theirs = [shift(block, "c", 1) for block in mine]

    kern_mine, embed = forward(mine, feat_t, sq_feat, jnp.zeros((rank, n_x * own), F32))
    kern_theirs, partial_embed = forward(theirs, feat_t, sq_feat, embed)

    shares = partial_embed.astype(BF16)
    embed = partial_embed
    for s in range(1, n_x):
        embed = embed + jnp.roll(shift(shares, "x", s), -s * own, axis=1).astype(F32)
    dembed = norm_backward(embed, cot_t, -gamma)

    no_total = jnp.zeros((1, n_x * own), F32)
    coef_theirs, land_theirs, row_total = backward(theirs, kern_theirs, dembed, features, no_total, BF16)
    coef_mine, land_mine, row_total = backward(mine, kern_mine, dembed, features, row_total, F32)
    share = (land_mine + shift(land_theirs, "c", 1).astype(F32)).reshape(n_y, n_z, rows, width)
    share = collect(share, Y, -1)

    feat_shares = feature_share(mine + theirs, [coef_mine, coef_theirs], feat_t, row_total, n_x)
    landmark_grad = collect_at_once(share, "z")
    feature_grad = collect(feat_shares, "x", 1).T
    return (feature_grad, landmark_grad)


def solution(mesh):
    fine = Mesh(mesh.devices.reshape(4, 2, 2, 8, 2), ("x", "h", "l", "z", "c"))
    lm, tx = ("x", "h"), ("l", "z", "c")
    placed = (P(tx, None), P(lm + tx, None), P(lm + tx, None), P(tx, None))
    return jax.shard_map(
        per_device,
        mesh=fine,
        in_specs=placed,
        out_specs=(P(tx + lm, None), P(lm + tx, None)),
        check_vma=False,
    )
```

time: 85.9 us -> 87.4 us (1.017)
  matrix products: 11.4 us -> 0 us
  Pallas kernels: 0 us -> 11.2 us
  local copies, waits for them, and re-layouts: 2.3 us -> 9.25 us
  waiting for transfers between devices: 26.1 us -> 21.6 us
    dot_general x5 -> x0, matrix products: 11.4 us -> none  [the longest x1 4.21 us: per_device(): jnp.einsum('nr,mr->nm', dembed, white_rows, preferred_element_type=F32)]
    pallas_call x0 -> x5, Pallas kernels: none -> 11.2 us  [the longest x2 4.56 us: forward(): pl.pallas_call(functools.partial(forward_body, len(blocks), width), out_s...]
    ppermute x14 -> x17, waiting for transfers between devices: 18.7 us -> 13.8 us  [shift(): lax.ppermute(block, axes, [(i, (i + step) % size) for i in range(size)])]
    slice x5, local copies, waits for them, and re-layouts: 0.04 us -> 4.2 us  [per_device(): jnp.roll(shift(shares, 'x', s), -s * own, axis=1).astype(F32)]
    unnamed x8 -> x19, local copies, waits for them, and re-layouts: 0.13 us -> 2.59 us
    dynamic_slice x2, local copies, waits for them, and re-layouts: 0.06 us -> 2.17 us  [taken(): lax.dynamic_slice_in_dim(array, ((here + s) % n_x * n_h + half) * own, ow...]
    add x1 -> x0, other arithmetic: 1.71 us -> none  [collect(): total + shift(pieces[s].astype(BF16), axes, direction * s).astype(F32)]
    ppermute x1 -> x0, local copies, waits for them, and re-layouts: 1.44 us -> none  [shift(): lax.ppermute(block, axes, [(i, (i + step) % size) for i in range(size)])]
  transfers between devices with their start and end apart: 15 -> 18, of which waited for: 8 -> 8; matrix products, arithmetic and copies ran while one was open for 6% -> 9% of each run, Pallas kernels for 0% -> 6%
where the time goes in v4:
time: 87.4 us; the launch traced here: 86.7 us
  waiting for transfers between devices  21.6 us (25%)
  starting transfers between devices  20.7 us (24%)
  blocking collectives  18.7 us (21%)
  Pallas kernels  11.2 us (13%)
  local copies, waits for them, and re-layouts  9.25 us (11%)
  other arithmetic  4.37 us (5%)
  between operations  0.92 us (1%)
    all_to_all x1, blocking collectives, spread_at_once(): lax.all_to_all(jnp.broadcast_to(block[None], (lax.axis_size(axes),) + blo...  18.7 us
    ppermute x17, starting transfers between devices, shift(): lax.ppermute(block, axes, [(i, (i + step) % size) for i in range(size)])  17.3 us
    ppermute x17, waiting for transfers between devices, shift(): lax.ppermute(block, axes, [(i, (i + step) % size) for i in range(size)])  13.8 us
    all_to_all x1, waiting for transfers between devices, collect_at_once(): lax.all_to_all(pieces.astype(BF16), axes, 0, 0, tiled=True).astype(F32)  7.82 us
    pallas_call x2, Pallas kernels, forward(): pl.pallas_call(functools.partial(forward_body, len(blocks), width), out_s...  4.56 us
    slice x5, local copies, waits for them, and re-layouts, per_device(): jnp.roll(shift(shares, 'x', s), -s * own, axis=1).astype(F32)  4.2 us
    pallas_call x2, Pallas kernels, backward(): pl.pallas_call(functools.partial(backward_body, len(blocks), width), out_...  4.14 us
    all_to_all x1, starting transfers between devices, collect_at_once(): lax.all_to_all(pieces.astype(BF16), axes, 0, 0, tiled=True).astype(F32)  3.37 us
  transfers between devices with their start and end apart: 18, of which 8 were waited for; matrix products, arithmetic and copies ran while one was open for 9% of the time, Pallas kernels for 6%

profile of v4, /device:TPU:24, one launch (start us, length us, event | category | flops | bytes accessed | tf_op | source)
XLA Modules:
  0.0 86.7 jit_solution(4994470659686081652)
XLA Ops:
  0.6 0.7 pad_maximum_fusion.2
  1.4 18.7 %all_to_all.10 = bf16[8,32,320]{2,1,0:T(8,128)(2,1)S(1)} all-to-all(bf16[8,32,320]{2,1,0:T(8,128)(2,1)S(1)} %broadcast_in_dim.8), channel_id=1, replica_groups=mesh['x'=4,'h'=2,'l'=2,'z'=8,'c'=2] {'z'}, dimensions={0} | all-to-all | bytes 327680 | tf_op jit(solution)/shard_map/all_to_all | solution.py:126
  20.1 0.7 collective-permute-start.2
  20.9 0.9 %collective-permute-start.1 = (bf16[256,320]{1,0:T(8,128)(2,1)S(1)}, bf16[256,320]{1,0:T(8,128)(2,1)S(1)}, u32[]{:S(2)}, u32[]{:S(2)}) collective-permute-start(bf16[256,320]{1,0:T(8,128)(2,1)S(1)} %bitcast.24), channel_id=1, source_target_pairs={{0,32},{16,48},{32,0},{48,16},{1,33},{17,49},{33,1},{49,17},{2,34}... | collective-permute-start | bytes 491528 | tf_op jit(solution)/shard_map/ppermute | solution.py:111
  21.8 2.2 %collective-permute-start = (bf16[256,320]{1,0:T(8,128)(2,1)S(1)}, bf16[256,320]{1,0:T(8,128)(2,1)S(1)}, u32[]{:S(2)}, u32[]{:S(2)}) collective-permute-start(bf16[256,320]{1,0:T(8,128)(2,1)S(1)} %bitcast.25), channel_id=1, source_target_pairs={{0,16},{16,32},{32,48},{48,0},{1,17},{17,33},{33,49},{49,1},{2,18}... | collective-permute-start | bytes 491528 | tf_op jit(solution)/shard_map/ppermute | solution.py:111
  24.0 6.3 %collective-permute-done.2.refs_3_ = bf16[256,320]{1,0:T(8,128)(2,1)S(1)} collective-permute-done((bf16[256,320]{1,0:T(8,128)(2,1)S(1)}, bf16[256,320]{1,0:T(8,128)(2,1)S(1)}, u32[]{:S(2)}, u32[]{:S(2)}) %collective-permute-start.2) | collective-permute-done | bytes 163872 | tf_op jit(solution)/shard_map/ppermute | solution.py:111
  30.3 0.5 collective-permute-start.5
  30.8 0.1 collective-permute-done.refs_1_
  30.9 1.2 %constant_dynamic-slice_fusion.7 = (bf16[256,256]{1,0:T(8,128)(2,1)S(1)}, bf16[256,256]{1,0:T(8,128)(2,1)S(1)}, bf16[256,256]{1,0:T(8,128)(2,1)S(1)}, bf16[256,256]{1,0:T(8,128)(2,1)S(1)}) fusion(bf16[2048,256]{1,0:T(8,128)(2,1)} %param.4, s32[]{:T(128)S(6)} %select_n.44, s32[]{:T(128)S(6)} %select_n.48, s32[]{:T(128)S(6)} %select_n.46, s32[]{:T(128)S(6)} %select_n.50), kind=kLoop, calls=%fused_computation.25 | loop fusion | bytes 1048592 | tf_op jit(solution)/shard_map/dynamic_slice | solution.py:151
  32.1 0.1 copy.13
  32.2 0.1 copy.15
  32.3 0.1 copy.14
  32.4 0.1 copy.16
  32.6 0.1 multiply_reduce_fusion
  32.7 1.7 %shard_map.59 = (bf16[1024,1024]{1,0:T(8,128)(2,1)S(1)}, f32[64,1024]{1,0:T(8,128)S(1)}) custom-call(bf16[256,320]{1,0:T(8,128)(2,1)S(1)} %bitcast.27, bf16[256,320]{1,0:T(8,128)(2,1)S(1)} %collective-permute-done.refs_1_, bf16[256,320]{1,0:T(8,128)(2,1)S(1)} %collective-permute-done.1.refs_2_, bf16[256,320]{1,0:T(8,128)(2,1)S(1)} %collective-permute-done.2.refs_3_, ...), custom_call_target="tpu_custom_call" | custom-call | tf_op jit(solution)/shard_map/pallas_call | solution.py:38
  34.5 2.9 %shard_map.60 = (bf16[1024,1024]{1,0:T(8,128)(2,1)S(1)}, f32[64,1024]{1,0:T(8,128)S(1)}) custom-call(bf16[256,320]{1,0:T(8,128)(2,1)} %collective-permute-done.3.refs_0_.refs_4_, bf16[256,320]{1,0:T(8,128)(2,1)} %collective-permute-done.4.refs_1_.refs_5_, bf16[256,320]{1,0:T(8,128)(2,1)} %collective-permute-done.5.refs_2_.refs_6_, ...), custom_call_target="tpu_custom_call" | custom-call | tf_op jit(solution)/shard_map/pallas_call | solution.py:38
  37.3 1.3 %copy-done = bf16[1024,1024]{1,0:T(8,128)(2,1)} copy-done((bf16[1024,1024]{1,0:T(8,128)(2,1)}, bf16[1024,1024]{1,0:T(8,128)(2,1)S(1)}, u32[]{:S(2)}) %copy-start) | copy-done | bytes 2097176
  38.7 0.7 convert_element_type.64
  39.4 2.8 %collective-permute-start.9 = (bf16[64,1024]{1,0:T(8,128)(2,1)}, bf16[64,1024]{1,0:T(8,128)(2,1)}, u32[]{:S(2)}, u32[]{:S(2)}) collective-permute-start(bf16[64,1024]{1,0:T(8,128)(2,1)} %convert_element_type.64), channel_id=1, source_target_pairs={{0,192},{64,0},{128,64},{192,128},{1,193},{65,1},{129,65},{193,129... | collective-permute-start | bytes 393224 | tf_op jit(solution)/shard_map/ppermute | solution.py:111
  42.2 2.3 %collective-permute-start.8 = (bf16[64,1024]{1,0:T(8,128)(2,1)}, bf16[64,1024]{1,0:T(8,128)(2,1)}, u32[]{:S(2)}, u32[]{:S(2)}) collective-permute-start(bf16[64,1024]{1,0:T(8,128)(2,1)} %convert_element_type.64), channel_id=1, source_target_pairs={{0,128},{64,192},{128,0},{192,64},{1,129},{65,193},{129,1},{193,65... | collective-permute-start | bytes 393224 | tf_op jit(solution)/shard_map/ppermute | solution.py:111
  44.5 0.2 copy.11.refs_6_
  44.7 1.0 %constant_dynamic-slice_fusion.3 = (bf16[256,64]{0,1:T(8,128)(2,1)S(1)}, bf16[256,64]{0,1:T(8,128)(2,1)S(1)}, bf16[256,64]{0,1:T(8,128)(2,1)S(1)}, bf16[256,64]{0,1:T(8,128)(2,1)S(1)}) fusion(bf16[2048,64]{0,1:T(8,128)(2,1)} %param.7, s32[]{:T(128)S(6)} %select_n.44, s32[]{:T(128)S(6)} %select_n.46, s32[]{:T(128)S(6)} %select_n.50, s32[]{:T(128)S(6)} %select_n.48), kind=kLoop, calls=%fused_computation.21 | loop fusion | bytes 262160 | tf_op jit(solution)/shard_map/dynamic_slice | solution.py:151
  45.7 0.2 collective-permute-done.9
  45.9 0.8 slice.57
  46.6 0.9 %slice.58 = bf16[64,768]{1,0:T(8,128)(2,1)S(1)} slice(bf16[64,1024]{1,0:T(8,128)(2,1)} %collective-permute-done.9), slice={[0:64], [0:768]} | slice | bytes 196608 | tf_op jit(solution)/shard_map/jit(_roll_static)/slice | solution.py:170
  47.5 4.6 %collective-permute-done.7 = bf16[64,1024]{1,0:T(8,128)(2,1)} collective-permute-done((bf16[64,1024]{1,0:T(8,128)(2,1)}, bf16[64,1024]{1,0:T(8,128)(2,1)}, u32[]{:S(2)}, u32[]{:S(2)}) %collective-permute-start.7) | collective-permute-done | bytes 131104 | tf_op jit(solution)/shard_map/ppermute | solution.py:111
  52.1 0.8 slice.54
  52.8 0.9 %slice.53 = bf16[64,768]{1,0:T(8,128)(2,1)S(1)} slice(bf16[64,1024]{1,0:T(8,128)(2,1)} %collective-permute-done.7), slice={[0:64], [256:1024]} | slice | bytes 196608 | tf_op jit(solution)/shard_map/jit(_roll_static)/slice | solution.py:170
  53.7 0.9 %fusion.6 = (bf16[64,512]{1,0:T(8,128)(2,1)S(1)}, bf16[64,512]{1,0:T(8,128)(2,1)S(1)}) fusion(bf16[64,1024]{1,0:T(8,128)(2,1)} %collective-permute-done.8), kind=kLoop, calls=%fused_computation.28 | loop fusion | bytes 262144 | tf_op jit(solution)/shard_map/jit(_roll_static)/slice | solution.py:170
  54.6 1.0 %multiply_reduce_fusion.1 = (f32[1024]{0:T(1024)S(1)}, f32[64,1024]{1,0:T(8,128)S(1)}) fusion(bf16[64,768]{1,0:T(8,128)(2,1)S(1)} %slice.58, bf16[64,256]{1,0:T(8,128)(2,1)S(1)} %slice.57, bf16[64,512]{1,0:T(8,128)(2,1)S(1)} %get-tuple-element.50, bf16[64,512]{1,0:T(8,128)(2,1)S(1)} %get-tuple-element.49, f32[64,1024]{1,0:T(8,128)} %copy-done.6, ...), kind=kLoop, calls=%fused_computation.12 | loop fusion | flops 1113088 | bytes 921600 | tf_op jit(solution)/shard_map/reduce_sum | solution.py:134
  55.9 2.7 %shard_map.61 = (bf16[1024,1024]{1,0:T(8,128)(2,1)S(1)}, bf16[1024,256]{1,0:T(8,128)(2,1)S(1)}, f32[1,1024]{1,0:T(1,128)S(1)}) custom-call(bf16[256,320]{1,0:T(8,128)(2,1)} %collective-permute-done.3.refs_0_.refs_4_, bf16[256,320]{1,0:T(8,128)(2,1)} %collective-permute-done.4.refs_1_.refs_5_, bf16[256,320]{1,0:T(8,128)(2,1)} %collective-permute-done.5.refs_2_.refs_6_, ...), custom_call_target="tpu_custom_call" | custom-call | tf_op jit(solution)/shard_map/pallas_call | solution.py:69
  58.6 0.3 collective-permute-start.13
  58.9 1.4 %shard_map.62 = (bf16[1024,1024]{1,0:T(8,128)(2,1)S(1)}, f32[1024,256]{1,0:T(8,128)S(1)}, f32[1,1024]{1,0:T(1,128)S(1)}) custom-call(bf16[256,320]{1,0:T(8,128)(2,1)S(1)} %bitcast.28, bf16[256,320]{1,0:T(8,128)(2,1)S(1)} %copy-done.5, bf16[256,320]{1,0:T(8,128)(2,1)S(1)} %copy-done.3, bf16[256,320]{1,0:T(8,128)(2,1)S(1)} %collective-permute-done.2.refs_3_, ...), custom_call_target="tpu_custom_call" | custom-call | tf_op jit(solution)/shard_map/pallas_call | solution.py:69
  60.3 0.4 collective-permute-done.13
  60.8 0.2 fusion.4
  61.0 2.7 %collective-permute-start.16 = (bf16[8,32,256]{2,1,0:T(8,128)(2,1)S(1)}, bf16[8,32,256]{2,1,0:T(8,128)(2,1)S(1)}, u32[]{:S(2)}, u32[]{:S(2)}) collective-permute-start(bf16[8,32,256]{2,1,0:T(8,128)(2,1)S(1)} %bitcast.35), channel_id=1, source_target_pairs={{0,16},{16,32},{32,48},{48,0},{1,17},{17,33},{33,49},{49,1},{2,18}... | collective-permute-start | bytes 393224 | tf_op jit(solution)/shard_map/ppermute | solution.py:111
  63.6 1.6 %collective-permute-start.15 = (bf16[8,32,256]{2,1,0:T(8,128)(2,1)S(1)}, bf16[8,32,256]{2,1,0:T(8,128)(2,1)S(1)}, u32[]{:S(2)}, u32[]{:S(2)}) collective-permute-start(bf16[8,32,256]{2,1,0:T(8,128)(2,1)S(1)} %bitcast.33), channel_id=1, source_target_pairs={{0,32},{16,48},{32,0},{48,16},{1,33},{17,49},{33,1},{49,17},{2,34}... | collective-permute-start | bytes 393224 | tf_op jit(solution)/shard_map/ppermute | solution.py:111
  65.2 2.5 %shard_map.63 = (f32[256,256]{1,0:T(8,128)S(1)}, bf16[256,256]{1,0:T(8,128)(2,1)S(1)}, bf16[256,256]{1,0:T(8,128)(2,1)S(1)}, bf16[256,256]{1,0:T(8,128)(2,1)S(1)}) custom-call(bf16[256,320]{1,0:T(8,128)(2,1)S(1)} %bitcast.29, bf16[256,320]{1,0:T(8,128)(2,1)S(1)} %copy-done.5, bf16[256,320]{1,0:T(8,128)(2,1)S(1)} %copy-done.3, ...), custom_call_target="tpu_custom_call" | custom-call | tf_op jit(solution)/shard_map/pallas_call | solution.py:100
  67.7 0.1 collective-permute-start.10
  67.8 1.0 %collective-permute-start.11 = (bf16[256,256]{1,0:T(8,128)(2,1)S(1)}, bf16[256,256]{1,0:T(8,128)(2,1)S(1)}, u32[]{:S(2)}, u32[]{:S(2)}) collective-permute-start(bf16[256,256]{1,0:T(8,128)(2,1)S(1)} %get-tuple-element.26), channel_id=1, source_target_pairs={{0,128},{64,192},{128,0},{192,64},{1,129},{65,193},{129,1},{193,65... | collective-permute-start | bytes 393224 | tf_op jit(solution)/shard_map/ppermute | solution.py:111
  68.8 2.3 %collective-permute-start.12 = (bf16[256,256]{1,0:T(8,128)(2,1)S(1)}, bf16[256,256]{1,0:T(8,128)(2,1)S(1)}, u32[]{:S(2)}, u32[]{:S(2)}) collective-permute-start(bf16[256,256]{1,0:T(8,128)(2,1)S(1)} %get-tuple-element.27), channel_id=1, source_target_pairs={{0,192},{64,0},{128,64},{192,128},{1,193},{65,1},{129,65},{193,129... | collective-permute-start | bytes 393224 | tf_op jit(solution)/shard_map/ppermute | solution.py:111
  71.1 1.8 %collective-permute-done.14 = bf16[8,32,256]{2,1,0:T(8,128)(2,1)S(1)} collective-permute-done((bf16[8,32,256]{2,1,0:T(8,128)(2,1)S(1)}, bf16[8,32,256]{2,1,0:T(8,128)(2,1)S(1)}, u32[]{:S(2)}, u32[]{:S(2)}) %collective-permute-start.14) | collective-permute-done | bytes 131104 | tf_op jit(solution)/shard_map/ppermute | solution.py:111
  72.9 0.7 add_convert_fusion
  73.6 3.4 %all-to-all-start.1 = ((bf16[8,32,256]{2,1,0:T(8,128)(2,1)}), bf16[8,32,256]{2,1,0:T(8,128)(2,1)S(1)}, u32[]{:S(2)}, u32[]{:S(2)}) async-start(bf16[8,32,256]{2,1,0:T(8,128)(2,1)} %add_convert_fusion), calls=%async_computation.1 | async-start | bytes 262144 | tf_op jit(solution)/shard_map/all_to_all | solution.py:130
  77.0 0.3 collective-permute-done.12
  77.4 0.8 copy.12
  78.3 7.8 %all-to-all-done.1 = bf16[8,32,256]{2,1,0:T(8,128)(2,1)S(1)} async-done(((bf16[8,32,256]{2,1,0:T(8,128)(2,1)}), bf16[8,32,256]{2,1,0:T(8,128)(2,1)S(1)}, u32[]{:S(2)}, u32[]{:S(2)}) %all-to-all-start.1) | async-done | bytes 131104 | tf_op jit(solution)/shard_map/all_to_all | solution.py:130
  86.1 0.6 convert_reduce_fusion
  (38 shorter events, 0.3 us)
Async XLA Ops:
  20.1 10.1 %collective-permute-start.2 = (bf16[256,320]{1,0:T(8,128)(2,1)S(1)}, bf16[256,320]{1,0:T(8,128)(2,1)S(1)}, u32[]{:S(2)}, u32[]{:S(2)}) collective-permute-start(bf16[256,320]{1,0:T(8,128)(2,1)S(1)} %bitcast.23), channel_id=1, source_target_pairs={{0,48},{16,0},{32,16},{48,32},{1,49},{17,1},{33,17},{49,33},{2,50}... | collective-permute-start | bytes 491528 | tf_op jit(solution)/shard_map/ppermute | solution.py:111
  20.9 9.4 %collective-permute-start.1 = (bf16[256,320]{1,0:T(8,128)(2,1)S(1)}, bf16[256,320]{1,0:T(8,128)(2,1)S(1)}, u32[]{:S(2)}, u32[]{:S(2)}) collective-permute-start(bf16[256,320]{1,0:T(8,128)(2,1)S(1)} %bitcast.24), channel_id=1, source_target_pairs={{0,32},{16,48},{32,0},{48,16},{1,33},{17,49},{33,1},{49,17},{2,34}... | collective-permute-start | bytes 491528 | tf_op jit(solution)/shard_map/ppermute | solution.py:111
  21.8 9.1 %collective-permute-start = (bf16[256,320]{1,0:T(8,128)(2,1)S(1)}, bf16[256,320]{1,0:T(8,128)(2,1)S(1)}, u32[]{:S(2)}, u32[]{:S(2)}) collective-permute-start(bf16[256,320]{1,0:T(8,128)(2,1)S(1)} %bitcast.25), channel_id=1, source_target_pairs={{0,16},{16,32},{32,48},{48,0},{1,17},{17,33},{33,49},{49,1},{2,18}... | collective-permute-start | bytes 491528 | tf_op jit(solution)/shard_map/ppermute | solution.py:111
  24.0 10.4 %collective-permute-start.3 = (bf16[256,320]{1,0:T(8,128)(2,1)S(1)}, bf16[256,320]{1,0:T(8,128)(2,1)}, u32[]{:S(2)}, u32[]{:S(2)}) collective-permute-start(bf16[256,320]{1,0:T(8,128)(2,1)S(1)} %bitcast.26), channel_id=1, source_target_pairs={{0,1},{1,0},{2,3},{3,2},{4,5},{5,4},{6,7},{7,6},{8,9},{9,8},{10,11... | collective-permute-start | bytes 491528 | tf_op jit(solution)/shard_map/ppermute | solution.py:111
  30.3 4.2 %collective-permute-start.6 = (bf16[256,320]{1,0:T(8,128)(2,1)S(1)}, bf16[256,320]{1,0:T(8,128)(2,1)}, u32[]{:S(2)}, u32[]{:S(2)}) collective-permute-start(bf16[256,320]{1,0:T(8,128)(2,1)S(1)} %collective-permute-done.2.refs_3_), channel_id=1, source_target_pairs={{0,1},{1,0},{2,3},{3,2},{4,5},{5,4},{6,7},{7,6},{8,9},{9,8},{10,11... | collective-permute-start | bytes 491528 | tf_op jit(solution)/shard_map/ppermute | solution.py:111
  30.3 4.1 %copy-start.2 = (bf16[256,320]{1,0:T(8,128)(2,1)}, bf16[256,320]{1,0:T(8,128)(2,1)S(1)}, u32[]{:S(2)}) copy-start(bf16[256,320]{1,0:T(8,128)(2,1)S(1)} %collective-permute-done.1.refs_2_) | copy-start | bytes 491524
  30.3 4.2 %collective-permute-start.5 = (bf16[256,320]{1,0:T(8,128)(2,1)S(1)}, bf16[256,320]{1,0:T(8,128)(2,1)}, u32[]{:S(2)}, u32[]{:S(2)}) collective-permute-start(bf16[256,320]{1,0:T(8,128)(2,1)S(1)} %collective-permute-done.1.refs_2_), channel_id=1, source_target_pairs={{0,1},{1,0},{2,3},{3,2},{4,5},{5,4},{6,7},{7,6},{8,9},{9,8},{10,11... | collective-permute-start | bytes 491528 | tf_op jit(solution)/shard_map/ppermute | solution.py:111
  30.9 3.5 %copy-start.4 = (bf16[256,320]{1,0:T(8,128)(2,1)}, bf16[256,320]{1,0:T(8,128)(2,1)S(1)}, u32[]{:S(2)}) copy-start(bf16[256,320]{1,0:T(8,128)(2,1)S(1)} %collective-permute-done.refs_1_) | copy-start | bytes 491524
  30.9 3.5 %collective-permute-start.4 = (bf16[256,320]{1,0:T(8,128)(2,1)S(1)}, bf16[256,320]{1,0:T(8,128)(2,1)}, u32[]{:S(2)}, u32[]{:S(2)}) collective-permute-start(bf16[256,320]{1,0:T(8,128)(2,1)S(1)} %collective-permute-done.refs_1_), channel_id=1, source_target_pairs={{0,1},{1,0},{2,3},{3,2},{4,5},{5,4},{6,7},{7,6},{8,9},{9,8},{10,11... | collective-permute-start | bytes 491528 | tf_op jit(solution)/shard_map/ppermute | solution.py:111
  37.3 1.3 %copy-start = (bf16[1024,1024]{1,0:T(8,128)(2,1)}, bf16[1024,1024]{1,0:T(8,128)(2,1)S(1)}, u32[]{:S(2)}) copy-start(bf16[1024,1024]{1,0:T(8,128)(2,1)S(1)} %get-tuple-element.19.refs_4_) | copy-start | bytes 6291460
  38.7 3.5 %copy-start.6 = (f32[64,1024]{1,0:T(8,128)}, f32[64,1024]{1,0:T(8,128)S(1)}, u32[]{:S(2)}) copy-start(f32[64,1024]{1,0:T(8,128)S(1)} %get-tuple-element.18) | copy-start | bytes 786436
  39.4 6.4 %collective-permute-start.9 = (bf16[64,1024]{1,0:T(8,128)(2,1)}, bf16[64,1024]{1,0:T(8,128)(2,1)}, u32[]{:S(2)}, u32[]{:S(2)}) collective-permute-start(bf16[64,1024]{1,0:T(8,128)(2,1)} %convert_element_type.64), channel_id=1, source_target_pairs={{0,192},{64,0},{128,64},{192,128},{1,193},{65,1},{129,65},{193,129... | collective-permute-start | bytes 393224 | tf_op jit(solution)/shard_map/ppermute | solution.py:111
  42.2 9.9 %collective-permute-start.7 = (bf16[64,1024]{1,0:T(8,128)(2,1)}, bf16[64,1024]{1,0:T(8,128)(2,1)}, u32[]{:S(2)}, u32[]{:S(2)}) collective-permute-start(bf16[64,1024]{1,0:T(8,128)(2,1)} %convert_element_type.64), channel_id=1, source_target_pairs={{0,64},{64,128},{128,192},{192,0},{1,65},{65,129},{129,193},{193,1... | collective-permute-start | bytes 393224 | tf_op jit(solution)/shard_map/ppermute | solution.py:111
  42.2 11.6 %collective-permute-start.8 = (bf16[64,1024]{1,0:T(8,128)(2,1)}, bf16[64,1024]{1,0:T(8,128)(2,1)}, u32[]{:S(2)}, u32[]{:S(2)}) collective-permute-start(bf16[64,1024]{1,0:T(8,128)(2,1)} %convert_element_type.64), channel_id=1, source_target_pairs={{0,128},{64,192},{128,0},{192,64},{1,129},{65,193},{129,1},{193,65... | collective-permute-start | bytes 393224 | tf_op jit(solution)/shard_map/ppermute | solution.py:111
  44.7 11.2 %copy-start.1 = (bf16[1024,1024]{1,0:T(8,128)(2,1)S(1)}, bf16[1024,1024]{1,0:T(8,128)(2,1)}, u32[]{:S(2)}) copy-start(bf16[1024,1024]{1,0:T(8,128)(2,1)} %copy-done) | copy-start | bytes 6291460
  55.7 3.1 %copy-start.3 = (bf16[256,320]{1,0:T(8,128)(2,1)S(1)}, bf16[256,320]{1,0:T(8,128)(2,1)}, u32[]{:S(2)}) copy-start(bf16[256,320]{1,0:T(8,128)(2,1)} %copy-done.2) | copy-start | bytes 491524
  55.7 3.1 %copy-start.5 = (bf16[256,320]{1,0:T(8,128)(2,1)S(1)}, bf16[256,320]{1,0:T(8,128)(2,1)}, u32[]{:S(2)}) copy-start(bf16[256,320]{1,0:T(8,128)(2,1)} %copy-done.4) | copy-start | bytes 491524
  58.6 2.2 %collective-permute-start.13 = (bf16[1024,256]{1,0:T(8,128)(2,1)S(1)}, bf16[1024,256]{1,0:T(8,128)(2,1)S(1)}, u32[]{:S(2)}, u32[]{:S(2)}) collective-permute-start(bf16[1024,256]{1,0:T(8,128)(2,1)S(1)} %get-tuple-element.29), channel_id=1, source_target_pairs={{0,1},{1,0},{2,3},{3,2},{4,5},{5,4},{6,7},{7,6},{8,9},{9,8},{10,11... | collective-permute-start | bytes 1572872 | tf_op jit(solution)/shard_map/ppermute | solution.py:111
  61.0 7.9 %collective-permute-start.16 = (bf16[8,32,256]{2,1,0:T(8,128)(2,1)S(1)}, bf16[8,32,256]{2,1,0:T(8,128)(2,1)S(1)}, u32[]{:S(2)}, u32[]{:S(2)}) collective-permute-start(bf16[8,32,256]{2,1,0:T(8,128)(2,1)S(1)} %bitcast.35), channel_id=1, source_target_pairs={{0,16},{16,32},{32,48},{48,0},{1,17},{17,33},{33,49},{49,1},{2,18}... | collective-permute-start | bytes 393224 | tf_op jit(solution)/shard_map/ppermute | solution.py:111
  63.6 9.3 %collective-permute-start.14 = (bf16[8,32,256]{2,1,0:T(8,128)(2,1)S(1)}, bf16[8,32,256]{2,1,0:T(8,128)(2,1)S(1)}, u32[]{:S(2)}, u32[]{:S(2)}) collective-permute-start(bf16[8,32,256]{2,1,0:T(8,128)(2,1)S(1)} %bitcast.34), channel_id=1, source_target_pairs={{0,48},{16,0},{32,16},{48,32},{1,49},{17,1},{33,17},{49,33},{2,50}... | collective-permute-start | bytes 393224 | tf_op jit(solution)/shard_map/ppermute | solution.py:111
  63.6 9.3 %collective-permute-start.15 = (bf16[8,32,256]{2,1,0:T(8,128)(2,1)S(1)}, bf16[8,32,256]{2,1,0:T(8,128)(2,1)S(1)}, u32[]{:S(2)}, u32[]{:S(2)}) collective-permute-start(bf16[8,32,256]{2,1,0:T(8,128)(2,1)S(1)} %bitcast.33), channel_id=1, source_target_pairs={{0,32},{16,48},{32,0},{48,16},{1,33},{17,49},{33,1},{49,17},{2,34}... | collective-permute-start | bytes 393224 | tf_op jit(solution)/shard_map/ppermute | solution.py:111
  67.7 9.3 %collective-permute-start.10 = (bf16[256,256]{1,0:T(8,128)(2,1)S(1)}, bf16[256,256]{1,0:T(8,128)(2,1)S(1)}, u32[]{:S(2)}, u32[]{:S(2)}) collective-permute-start(bf16[256,256]{1,0:T(8,128)(2,1)S(1)} %get-tuple-element.25), channel_id=1, source_target_pairs={{0,64},{64,128},{128,192},{192,0},{1,65},{65,129},{129,193},{193,1... | collective-permute-start | bytes 393224 | tf_op jit(solution)/shard_map/ppermute | solution.py:111
  67.8 9.3 %collective-permute-start.11 = (bf16[256,256]{1,0:T(8,128)(2,1)S(1)}, bf16[256,256]{1,0:T(8,128)(2,1)S(1)}, u32[]{:S(2)}, u32[]{:S(2)}) collective-permute-start(bf16[256,256]{1,0:T(8,128)(2,1)S(1)} %get-tuple-element.26), channel_id=1, source_target_pairs={{0,128},{64,192},{128,0},{192,64},{1,129},{65,193},{129,1},{193,65... | collective-permute-start | bytes 393224 | tf_op jit(solution)/shard_map/ppermute | solution.py:111
  68.8 8.6 %collective-permute-start.12 = (bf16[256,256]{1,0:T(8,128)(2,1)S(1)}, bf16[256,256]{1,0:T(8,128)(2,1)S(1)}, u32[]{:S(2)}, u32[]{:S(2)}) collective-permute-start(bf16[256,256]{1,0:T(8,128)(2,1)S(1)} %get-tuple-element.27), channel_id=1, source_target_pairs={{0,192},{64,0},{128,64},{192,128},{1,193},{65,1},{129,65},{193,129... | collective-permute-start | bytes 393224 | tf_op jit(solution)/shard_map/ppermute | solution.py:111
  73.6 12.4 %all-to-all-start.1 = ((bf16[8,32,256]{2,1,0:T(8,128)(2,1)}), bf16[8,32,256]{2,1,0:T(8,128)(2,1)S(1)}, u32[]{:S(2)}, u32[]{:S(2)}) async-start(bf16[8,32,256]{2,1,0:T(8,128)(2,1)} %add_convert_fusion), calls=%async_computation.1 | async-start | bytes 262144 | tf_op jit(solution)/shard_map/all_to_all | solution.py:130

commit v5 on v4

v5 whole, which is shorter than its diff:
```python
import functools

import jax
import jax.numpy as jnp
from jax import lax
from jax.experimental import pallas as pl
from jax.experimental.pallas import tpu as pltpu
from jax.sharding import Mesh, PartitionSpec as P

Y = ("h", "l")
F32 = jnp.float32
BF16 = jnp.bfloat16
LOG2E = 1.4426950408889634
WHOLE = pl.BlockSpec(memory_space=pltpu.VMEM)
PARAMS = pltpu.CompilerParams(vmem_limit_bytes=12 * 2**20)


def call(body, out_shape, *operands):
    return pl.pallas_call(
        body,
        out_shape=out_shape,
        in_specs=[WHOLE] * len(operands),
        out_specs=jax.tree.map(lambda _: WHOLE, out_shape),
        compiler_params=PARAMS,
    )(*operands)


def shaped(shape, kind):
    return jax.ShapeDtypeStruct(shape, kind)


def pack_body(quads, landmarks, whitening, out):
    rows = landmarks.shape[0]
    part = rows // quads
    white = whitening[...].astype(F32)
    white = jnp.concatenate([white[q * part : (q + 1) * part] for q in range(quads)], axis=1).astype(BF16)
    for i in range(out.shape[0]):
        out[i, :rows] = landmarks[...]
        out[i, rows:] = white


def pack(landmarks, whitening, copies):
    rows, width = landmarks.shape
    quads = width // whitening.shape[1]
    return call(functools.partial(pack_body, quads), shaped((copies, rows + rows // quads, width), BF16), landmarks, whitening)


def unpack(block, rank):
    count, packed, width = block.shape
    quads = width // rank
    rows = packed * quads // (quads + 1)
    land = block[:, :rows].reshape(count * rows, width)
    white = block[:, rows:].astype(F32)
    white = jnp.stack([white[:, :, q * rank : (q + 1) * rank] for q in range(quads)], axis=1)
    return land, white.reshape(count * rows, rank).astype(BF16)


def prepare_body(parts, places, features, cot_t, feat, feat_t, sq_feat, cot):
    own = features.shape[0] // parts
    for i, place in enumerate(places()):
        start = pl.multiple_of(place * own, own)
        to = slice(i * own, (i + 1) * own)
        some = features[pl.ds(start, own), :]
        turned = some.T
        turned32 = turned.astype(F32)
        feat[to, :] = some
        feat_t[:, to] = turned
        sq_feat[:, to] = jnp.sum(turned32 * turned32, axis=0, keepdims=True)
        cot[:, to] = cot_t[:, pl.ds(start, own)].astype(F32)


def prepare(features, cot_t, parts, places, count):
    toks, width = features.shape
    toks = toks // parts * count
    rank = cot_t.shape[0]
    shapes = [shaped((toks, width), BF16), shaped((width, toks), BF16), shaped((1, toks), F32), shaped((rank, toks), F32)]
    return call(functools.partial(prepare_body, parts, places), shapes, features, cot_t)


def forward_body(count, rank, first, *refs):
    blocks, (feat_t, sq_feat), (kern, *embeds) = refs[:count], refs[count : count + 2], refs[count + 2 + (not first) :]
    width = feat_t.shape[0]
    scale = 4.0 / width * LOG2E
    bias = sq_feat[...] * (-scale)
    total = None if first else refs[count + 2][...]
    for i, block in enumerate(blocks):
        land, white = unpack(block[...], rank)
        rows = land.shape[0]
        land32 = land.astype(F32)
        sq_land = jnp.sum(land32 * land32, axis=1, keepdims=True) * (-scale)
        cross = jnp.dot(land, feat_t[...], preferred_element_type=F32)
        value = jnp.exp2(cross * (2.0 * scale) + (bias + sq_land)).astype(BF16)
        kern[i * rows : (i + 1) * rows, :] = value
        part = lax.dot_general(white, value, (((0,), (0,)), ((), ())), preferred_element_type=F32)
        total = part if total is None else total + part
    for embed in embeds:
        embed[...] = total.astype(embed.dtype)


def forward(blocks, feat_t, sq_feat, prior, rows, rank):
    toks = feat_t.shape[1]
    shapes = [shaped((rows, toks), BF16), shaped((rank, toks), F32)] + [shaped((rank, toks), BF16)] * len(prior)
    return call(functools.partial(forward_body, len(blocks), rank, not prior), shapes, *blocks, feat_t, sq_feat, *prior)


def norm_body(factor, count, *refs):
    shares, cot, out = refs[:count], refs[count], refs[count + 1]
    own = cot.shape[1] // count
    for p in range(count):
        at = slice(p * own, (p + 1) * own)
        embed = shares[0][:, at]
        for s in range(1, count):
            t = (p + s) % count
            embed = embed + shares[s][:, t * own : (t + 1) * own].astype(F32)
        upstream = cot[:, at]
        scale = lax.rsqrt(jnp.mean(embed * embed, axis=0, keepdims=True) + 1e-06)
        normed = embed * scale
        grad = scale * (upstream - normed * jnp.mean(upstream * normed, axis=0, keepdims=True))
        out[:, at] = (factor * grad).astype(BF16)


def norm_backward(shares, cot, factor):
    return call(functools.partial(norm_body, factor, len(shares)), shaped(cot.shape, BF16), *shares, cot)


def backward_body(count, rank, first, *refs):
    blocks, (kern, dembed, feat) = refs[:count], refs[count : count + 3]
    coef, land_grad, row_total = refs[-3:]
    total = None if first else refs[count + 3][...]
    for i, block in enumerate(blocks):
        land, white = unpack(block[...], rank)
        rows = land.shape[0]
        at = slice(i * rows, (i + 1) * rows)
        dkernel = jnp.dot(white, dembed[...], preferred_element_type=F32)
        value = (dkernel * kern[at, :].astype(F32)).astype(BF16)
        coef[at, :] = value
        value32 = value.astype(F32)
        part = jnp.sum(value32, axis=0, keepdims=True)
        total = part if total is None else total + part
        col_total = jnp.sum(value32, axis=1, keepdims=True)
        pulled = jnp.dot(value, feat[...], preferred_element_type=F32)
        land_grad[at, :] = (2.0 * (col_total * land.astype(F32) - pulled)).astype(land_grad.dtype)
    row_total[...] = total


def backward(blocks, kern, dembed, feat, prior, kind):
    toks, width = feat.shape
    rows = kern.shape[0]
    shapes = [shaped((rows, toks), BF16), shaped((rows, width), kind), shaped((1, toks), F32)]
    body = functools.partial(backward_body, len(blocks), dembed.shape[0], not prior)
    return call(body, shapes, *blocks, kern, dembed, feat, *prior)


def feature_body(count, coefs, rank, *refs):
    blocks, coef, (feat_t, row_total), outs = refs[:count], refs[count : count + coefs], refs[count + coefs : count + coefs + 2], refs[count + coefs + 2 :]
    each = count // coefs
    step = feat_t.shape[1] // len(outs)
    pulled = None
    for i, block in enumerate(blocks):
        land, _ = unpack(block[...], rank)
        rows = land.shape[0]
        at = slice(i % each * rows, (i % each + 1) * rows)
        part = lax.dot_general(land, coef[i // each][at, :], (((0,), (0,)), ((), ())), preferred_element_type=F32)
        pulled = part if pulled is None else pulled + part
    grad = 2.0 * (row_total[...] * feat_t[...].astype(F32) - pulled)
    for i, out in enumerate(outs):
        out[...] = grad[:, i * step : (i + 1) * step].astype(out.dtype)


def feature_share(blocks, coefs, feat_t, row_total, parts, rank):
    width, toks = feat_t.shape
    shapes = [shaped((width, toks // parts), kind) for kind in [F32] + [BF16] * (parts - 1)]
    return call(functools.partial(feature_body, len(blocks), len(coefs), rank), shapes, *blocks, *coefs, feat_t, row_total)


def shift(block, axes, step):
    size = lax.axis_size(axes)
    return lax.ppermute(block, axes, [(i, (i + step) % size) for i in range(size)])


def spread(block, axes):
    return [block] + [shift(block, axes, s) for s in range(1, lax.axis_size(axes))]


def collect(pieces, axes, direction):
    total = pieces[0]
    for s in range(1, lax.axis_size(axes)):
        total = total + shift(pieces[s].astype(BF16), axes, direction * s).astype(F32)
    return total


def collect_at_once(pieces, axes):
    return jnp.sum(lax.all_to_all(pieces.astype(BF16), axes, 0, 0, tiled=True).astype(F32), axis=0)


def per_device(features, landmarks, whitening, cotangent):
    toks, width = features.shape
    rank = whitening.shape[1]
    n_x, n_h, n_y, n_z = lax.axis_size("x"), lax.axis_size("h"), lax.axis_size(Y), lax.axis_size("z")
    rows = landmarks.shape[0]
    gamma = 4.0 / width

    def places():
        here, half = lax.axis_index("x"), lax.axis_index("h")
        return [lax.rem(here + s, n_x) * n_h + half for s in range(n_x)]

    packed = lax.all_to_all(pack(landmarks, whitening, n_z), "z", 0, 0, tiled=True)
    feat, feat_t, sq_feat, cot = prepare(features, cotangent.T, n_x * n_h, places, n_x)
    packed, feat, feat_t, sq_feat, cot = lax.optimization_barrier((packed, feat, feat_t, sq_feat, cot))
    mine = spread(packed, Y)
    theirs = [shift(block, "c", 1) for block in mine]

    half_rows = n_y * n_z * rows
    kern_mine, embed = forward(mine, feat_t, sq_feat, [], half_rows, rank)
    kern_theirs, embed, share = forward(theirs, feat_t, sq_feat, [embed], half_rows, rank)
    dembed = norm_backward([embed] + [shift(share, "x", s) for s in range(1, n_x)], cot, -gamma)

    coef_theirs, land_theirs, row_total = backward(theirs, kern_theirs, dembed, feat, [], BF16)
    coef_mine, land_mine, row_total = backward(mine, kern_mine, dembed, feat, [row_total], F32)
    share = (land_mine + shift(land_theirs, "c", 1).astype(F32)).reshape(n_y, n_z, rows, width)
    share = collect(share, Y, -1)

    feat_shares = feature_share(mine + theirs, [coef_mine, coef_theirs], feat_t, row_total, n_x, rank)
    landmark_grad = collect_at_once(share, "z")
    feature_grad = collect(feat_shares, "x", 1).T
    return (feature_grad, landmark_grad)


def solution(mesh):
    fine = Mesh(mesh.devices.reshape(4, 2, 2, 8, 2), ("x", "h", "l", "z", "c"))
    lm, tx = ("x", "h"), ("l", "z", "c")
    placed = (P(tx, None), P(lm + tx, None), P(lm + tx, None), P(tx, None))
    return jax.shard_map(
        per_device,
        mesh=fine,
        in_specs=placed,
        out_specs=(P(tx + lm, None), P(lm + tx, None)),
        check_vma=False,
    )
```

time: 87.4 us -> 77 us (0.88)
  blocking collectives: 18.7 us -> 0 us
  waiting for transfers between devices: 21.6 us -> 31.9 us
  starting transfers between devices: 20.7 us -> 28.8 us
  local copies, waits for them, and re-layouts: 9.25 us -> 4.46 us
  other arithmetic: 4.37 us -> 1.6 us
  Pallas kernels: 11.2 us -> 9.03 us
    all_to_all x1 -> x0, blocking collectives: 18.7 us -> none  [spread_at_once(): lax.all_to_all(jnp.broadcast_to(block[None], (lax.axis_size(axes),) + blo...]
    all_to_all x0 -> x1, starting transfers between devices: none -> 8.47 us  [per_device(): lax.all_to_all(pack(landmarks, whitening, n_z), 'z', 0, 0, tiled=True)]
    all_to_all x0 -> x1, waiting for transfers between devices: none -> 7.34 us  [per_device(): lax.all_to_all(pack(landmarks, whitening, n_z), 'z', 0, 0, tiled=True)]
    slice x5 -> x0, local copies, waits for them, and re-layouts: 4.2 us -> none  [per_device(): jnp.roll(shift(shares, 'x', s), -s * own, axis=1).astype(F32)]
    ppermute x17, waiting for transfers between devices: 13.8 us -> 16.5 us  [shift(): lax.ppermute(block, axes, [(i, (i + step) % size) for i in range(size)])]
    dynamic_slice x2 -> x0, local copies, waits for them, and re-layouts: 2.17 us -> none  [taken(): lax.dynamic_slice_in_dim(array, ((here + s) % n_x * n_h + half) * own, ow...]
    pallas_call x5 -> x8, Pallas kernels: 11.2 us -> 9.03 us  [call(): pl.pallas_call(body, out_shape=out_shape, in_specs=[WHOLE] * len(operands...]
    unnamed x19 -> x9, local copies, waits for them, and re-layouts: 2.59 us -> 4.42 us
  transfers between devices with their start and end apart: 18 -> 19, of which waited for: 8 -> 9; matrix products, arithmetic and copies ran while one was open for 9% -> 2% of each run, Pallas kernels for 6% -> 6%
where the time goes in v5:
time: 77 us; the launch traced here: 76.6 us
  waiting for transfers between devices  31.9 us (41%)
  starting transfers between devices  28.8 us (37%)
  Pallas kernels  9.03 us (12%)
  local copies, waits for them, and re-layouts  4.46 us (6%)
  other arithmetic  1.6 us (2%)
  between operations  0.79 us (1%)
    ppermute x17, starting transfers between devices, shift(): lax.ppermute(block, axes, [(i, (i + step) % size) for i in range(size)])  17 us
    ppermute x17, waiting for transfers between devices, shift(): lax.ppermute(block, axes, [(i, (i + step) % size) for i in range(size)])  16.5 us
    pallas_call x8, Pallas kernels, call(): pl.pallas_call(body, out_shape=out_shape, in_specs=[WHOLE] * len(operands...  9.03 us
    all_to_all x1, starting transfers between devices, per_device(): lax.all_to_all(pack(landmarks, whitening, n_z), 'z', 0, 0, tiled=True)  8.47 us
    all_to_all x1, waiting for transfers between devices, collect_at_once(): lax.all_to_all(pieces.astype(BF16), axes, 0, 0, tiled=True).astype(F32)  8.06 us
    all_to_all x1, waiting for transfers between devices, per_device(): lax.all_to_all(pack(landmarks, whitening, n_z), 'z', 0, 0, tiled=True)  7.34 us
    unnamed x9, local copies, waits for them, and re-layouts  4.42 us
    all_to_all x1, starting transfers between devices, collect_at_once(): lax.all_to_all(pieces.astype(BF16), axes, 0, 0, tiled=True).astype(F32)  3.37 us
  transfers between devices with their start and end apart: 19, of which 9 were waited for; matrix products, arithmetic and copies ran while one was open for 2% of the time, Pallas kernels for 6%

profile of v5, /device:TPU:24, one launch (start us, length us, event | category | flops | bytes accessed | tf_op | source)
XLA Modules:
  0.0 76.6 jit_solution(3303013252738333040)
XLA Ops:
  0.6 0.7 copy-done.2
  1.4 0.7 copy-done.3
  2.0 0.7 shard_map.59
  2.8 8.5 %all-to-all-start = ((bf16[8,40,256]{2,1,0:T(8,128)(2,1)}), bf16[8,40,256]{2,1,0:T(8,128)(2,1)S(1)}, u32[]{:S(2)}, u32[]{:S(2)}) async-start(bf16[8,40,256]{2,1,0:T(8,128)(2,1)} %shard_map.59), calls=%async_computation | async-start | bytes 327680 | tf_op jit(solution)/shard_map/all_to_all | solution.py:207
  11.3 1.2 %copy-done = bf16[2048,256]{1,0:T(8,128)(2,1)S(1)} copy-done((bf16[2048,256]{1,0:T(8,128)(2,1)S(1)}, bf16[2048,256]{1,0:T(8,128)(2,1)}, u32[]{:S(2)}) %copy-start) | copy-done | bytes 1048600
  12.5 0.9 %copy-done.1 = bf16[2048,64]{0,1:T(8,128)(2,1)S(1)} copy-done((bf16[2048,64]{0,1:T(8,128)(2,1)S(1)}, bf16[2048,64]{0,1:T(8,128)(2,1)}, u32[]{:S(2)}) %copy-start.1) | copy-done | bytes 262168
  13.4 0.2 shard_map.60
  13.7 7.3 %all-to-all-done.refs_0_ = bf16[8,40,256]{2,1,0:T(8,128)(2,1)S(1)} async-done(((bf16[8,40,256]{2,1,0:T(8,128)(2,1)}), bf16[8,40,256]{2,1,0:T(8,128)(2,1)S(1)}, u32[]{:S(2)}, u32[]{:S(2)}) %all-to-all-start) | async-done | bytes 163872 | tf_op jit(solution)/shard_map/all_to_all | solution.py:207
  21.0 0.7 collective-permute-start.2
  21.8 0.9 %collective-permute-start.1 = (bf16[8,40,256]{2,1,0:T(8,128)(2,1)S(1)}, bf16[8,40,256]{2,1,0:T(8,128)(2,1)S(1)}, u32[]{:S(2)}, u32[]{:S(2)}) collective-permute-start(bf16[8,40,256]{2,1,0:T(8,128)(2,1)S(1)} %all-to-all-done.refs_0_), channel_id=1, source_target_pairs={{0,32},{16,48},{32,0},{48,16},{1,33},{17,49},{33,1},{49,17},{2,34}... | collective-permute-start | bytes 491528 | tf_op jit(solution)/shard_map/ppermute | solution.py:178
  22.7 2.2 %collective-permute-start = (bf16[8,40,256]{2,1,0:T(8,128)(2,1)S(1)}, bf16[8,40,256]{2,1,0:T(8,128)(2,1)S(1)}, u32[]{:S(2)}, u32[]{:S(2)}) collective-permute-start(bf16[8,40,256]{2,1,0:T(8,128)(2,1)S(1)} %all-to-all-done.refs_0_), channel_id=1, source_target_pairs={{0,16},{16,32},{32,48},{48,0},{1,17},{17,33},{33,49},{49,1},{2,18}... | collective-permute-start | bytes 491528 | tf_op jit(solution)/shard_map/ppermute | solution.py:178
  24.9 4.9 %collective-permute-done.2.refs_3_ = bf16[8,40,256]{2,1,0:T(8,128)(2,1)S(1)} collective-permute-done((bf16[8,40,256]{2,1,0:T(8,128)(2,1)S(1)}, bf16[8,40,256]{2,1,0:T(8,128)(2,1)S(1)}, u32[]{:S(2)}, u32[]{:S(2)}) %collective-permute-start.2) | collective-permute-done | bytes 163872 | tf_op jit(solution)/shard_map/ppermute | solution.py:178
  29.8 0.0 collective-permute-start.6
  29.8 0.0 collective-permute-done.1.refs_2_
  29.8 0.5 collective-permute-start.5
  30.3 0.1 collective-permute-done.refs_1_
  30.4 0.0 collective-permute-start.4
  30.4 1.7 %shard_map.61 = (bf16[1024,1024]{1,0:T(8,128)(2,1)S(1)}, f32[64,1024]{1,0:T(8,128)S(1)}) custom-call(bf16[8,40,256]{2,1,0:T(8,128)(2,1)S(1)} %all-to-all-done.refs_0_, bf16[8,40,256]{2,1,0:T(8,128)(2,1)S(1)} %collective-permute-done.refs_1_, bf16[8,40,256]{2,1,0:T(8,128)(2,1)S(1)} %collective-permute-done.1.refs_2_, ...), custom_call_target="tpu_custom_call" | custom-call | tf_op jit(solution)/shard_map/pallas_call | solution.py:19
  32.2 0.0 collective-permute-done.3.refs_0_.refs_4_
  32.2 0.0 collective-permute-done.6.refs_3_.refs_7_
  32.2 0.0 collective-permute-done.4.refs_1_.refs_5_
  32.2 1.8 %shard_map.62 = (bf16[1024,1024]{1,0:T(8,128)(2,1)S(1)}, f32[64,1024]{1,0:T(8,128)S(1)}, bf16[64,1024]{1,0:T(8,128)(2,1)S(1)}) custom-call(bf16[8,40,256]{2,1,0:T(8,128)(2,1)S(1)} %collective-permute-done.3.refs_0_.refs_4_, bf16[8,40,256]{2,1,0:T(8,128)(2,1)S(1)} %collective-permute-done.4.refs_1_.refs_5_, ...), custom_call_target="tpu_custom_call" | custom-call | tf_op jit(solution)/shard_map/pallas_call | solution.py:19
  34.0 2.8 %collective-permute-start.9 = (bf16[64,1024]{1,0:T(8,128)(2,1)S(1)}, bf16[64,1024]{1,0:T(8,128)(2,1)S(1)}, u32[]{:S(2)}, u32[]{:S(2)}) collective-permute-start(bf16[64,1024]{1,0:T(8,128)(2,1)S(1)} %get-tuple-element.36), channel_id=1, source_target_pairs={{0,192},{64,0},{128,64},{192,128},{1,193},{65,1},{129,65},{193,129... | collective-permute-start | bytes 393224 | tf_op jit(solution)/shard_map/ppermute | solution.py:178
  36.8 0.8 %collective-permute-start.8 = (bf16[64,1024]{1,0:T(8,128)(2,1)S(1)}, bf16[64,1024]{1,0:T(8,128)(2,1)S(1)}, u32[]{:S(2)}, u32[]{:S(2)}) collective-permute-start(bf16[64,1024]{1,0:T(8,128)(2,1)S(1)} %get-tuple-element.36), channel_id=1, source_target_pairs={{0,128},{64,192},{128,0},{192,64},{1,129},{65,193},{129,1},{193,65... | collective-permute-start | bytes 393224 | tf_op jit(solution)/shard_map/ppermute | solution.py:178
  37.6 0.9 %collective-permute-start.7 = (bf16[64,1024]{1,0:T(8,128)(2,1)S(1)}, bf16[64,1024]{1,0:T(8,128)(2,1)S(1)}, u32[]{:S(2)}, u32[]{:S(2)}) collective-permute-start(bf16[64,1024]{1,0:T(8,128)(2,1)S(1)} %get-tuple-element.36), channel_id=1, source_target_pairs={{0,64},{64,128},{128,192},{192,0},{1,65},{65,129},{129,193},{193,1... | collective-permute-start | bytes 393224 | tf_op jit(solution)/shard_map/ppermute | solution.py:178
  38.5 4.6 %collective-permute-done.9.refs_3_ = bf16[64,1024]{1,0:T(8,128)(2,1)S(1)} collective-permute-done((bf16[64,1024]{1,0:T(8,128)(2,1)S(1)}, bf16[64,1024]{1,0:T(8,128)(2,1)S(1)}, u32[]{:S(2)}, u32[]{:S(2)}) %collective-permute-start.9) | collective-permute-done | bytes 131104 | tf_op jit(solution)/shard_map/ppermute | solution.py:178
  43.1 1.6 %collective-permute-done.8.refs_2_ = bf16[64,1024]{1,0:T(8,128)(2,1)S(1)} collective-permute-done((bf16[64,1024]{1,0:T(8,128)(2,1)S(1)}, bf16[64,1024]{1,0:T(8,128)(2,1)S(1)}, u32[]{:S(2)}, u32[]{:S(2)}) %collective-permute-start.8) | collective-permute-done | bytes 131104 | tf_op jit(solution)/shard_map/ppermute | solution.py:178
  44.7 2.1 %collective-permute-done.7.refs_1_ = bf16[64,1024]{1,0:T(8,128)(2,1)S(1)} collective-permute-done((bf16[64,1024]{1,0:T(8,128)(2,1)S(1)}, bf16[64,1024]{1,0:T(8,128)(2,1)S(1)}, u32[]{:S(2)}, u32[]{:S(2)}) %collective-permute-start.7) | collective-permute-done | bytes 131104 | tf_op jit(solution)/shard_map/ppermute | solution.py:178
  46.7 0.2 shard_map.63.refs_5_
  46.9 1.6 %shard_map.64 = (bf16[1024,1024]{1,0:T(8,128)(2,1)S(1)}, bf16[1024,256]{1,0:T(8,128)(2,1)S(1)}, f32[1,1024]{1,0:T(1,128)S(1)}) custom-call(bf16[8,40,256]{2,1,0:T(8,128)(2,1)S(1)} %collective-permute-done.3.refs_0_.refs_4_, bf16[8,40,256]{2,1,0:T(8,128)(2,1)S(1)} %collective-permute-done.4.refs_1_.refs_5_, ...), custom_call_target="tpu_custom_call" | custom-call | tf_op jit(solution)/shard_map/pallas_call | solution.py:19
  48.5 0.3 collective-permute-start.13
  48.8 1.6 %shard_map.65 = (bf16[1024,1024]{1,0:T(8,128)(2,1)S(1)}, f32[1024,256]{1,0:T(8,128)S(1)}, f32[1,1024]{1,0:T(1,128)S(1)}) custom-call(bf16[8,40,256]{2,1,0:T(8,128)(2,1)S(1)} %all-to-all-done.refs_0_, bf16[8,40,256]{2,1,0:T(8,128)(2,1)S(1)} %collective-permute-done.refs_1_, bf16[8,40,256]{2,1,0:T(8,128)(2,1)S(1)} %collective-permute-done.1.refs_2_, ...), custom_call_target="tpu_custom_call" | custom-call | tf_op jit(solution)/shard_map/pallas_call | solution.py:19
  50.3 0.3 collective-permute-done.13
  50.7 0.2 fusion
  50.9 2.7 %collective-permute-start.16 = (bf16[8,32,256]{2,1,0:T(8,128)(2,1)S(1)}, bf16[8,32,256]{2,1,0:T(8,128)(2,1)S(1)}, u32[]{:S(2)}, u32[]{:S(2)}) collective-permute-start(bf16[8,32,256]{2,1,0:T(8,128)(2,1)S(1)} %bitcast.11), channel_id=1, source_target_pairs={{0,16},{16,32},{32,48},{48,0},{1,17},{17,33},{33,49},{49,1},{2,18}... | collective-permute-start | bytes 393224 | tf_op jit(solution)/shard_map/ppermute | solution.py:178
  53.6 0.0 collective-permute-start.14
  53.6 1.6 %collective-permute-start.15 = (bf16[8,32,256]{2,1,0:T(8,128)(2,1)S(1)}, bf16[8,32,256]{2,1,0:T(8,128)(2,1)S(1)}, u32[]{:S(2)}, u32[]{:S(2)}) collective-permute-start(bf16[8,32,256]{2,1,0:T(8,128)(2,1)S(1)} %bitcast.9), channel_id=1, source_target_pairs={{0,32},{16,48},{32,0},{48,16},{1,33},{17,49},{33,1},{49,17},{2,34}... | collective-permute-start | bytes 393224 | tf_op jit(solution)/shard_map/ppermute | solution.py:178
  55.1 1.3 %shard_map.66 = (f32[256,256]{1,0:T(8,128)S(1)}, bf16[256,256]{1,0:T(8,128)(2,1)S(1)}, bf16[256,256]{1,0:T(8,128)(2,1)S(1)}, bf16[256,256]{1,0:T(8,128)(2,1)S(1)}) custom-call(bf16[8,40,256]{2,1,0:T(8,128)(2,1)S(1)} %all-to-all-done.refs_0_, bf16[8,40,256]{2,1,0:T(8,128)(2,1)S(1)} %collective-permute-done.refs_1_, ...), custom_call_target="tpu_custom_call" | custom-call | tf_op jit(solution)/shard_map/pallas_call | solution.py:19
  56.4 0.1 collective-permute-start.10
  56.5 2.1 %collective-permute-start.11 = (bf16[256,256]{1,0:T(8,128)(2,1)S(1)}, bf16[256,256]{1,0:T(8,128)(2,1)S(1)}, u32[]{:S(2)}, u32[]{:S(2)}) collective-permute-start(bf16[256,256]{1,0:T(8,128)(2,1)S(1)} %get-tuple-element.46), channel_id=1, source_target_pairs={{0,128},{64,192},{128,0},{192,64},{1,129},{65,193},{129,1},{193,65... | collective-permute-start | bytes 393224 | tf_op jit(solution)/shard_map/ppermute | solution.py:178
  58.6 1.4 %collective-permute-start.12 = (bf16[256,256]{1,0:T(8,128)(2,1)S(1)}, bf16[256,256]{1,0:T(8,128)(2,1)S(1)}, u32[]{:S(2)}, u32[]{:S(2)}) collective-permute-start(bf16[256,256]{1,0:T(8,128)(2,1)S(1)} %get-tuple-element.47), channel_id=1, source_target_pairs={{0,192},{64,0},{128,64},{192,128},{1,193},{65,1},{129,65},{193,129... | collective-permute-start | bytes 393224 | tf_op jit(solution)/shard_map/ppermute | solution.py:178
  60.0 2.9 %collective-permute-done.14 = bf16[8,32,256]{2,1,0:T(8,128)(2,1)S(1)} collective-permute-done((bf16[8,32,256]{2,1,0:T(8,128)(2,1)S(1)}, bf16[8,32,256]{2,1,0:T(8,128)(2,1)S(1)}, u32[]{:S(2)}, u32[]{:S(2)}) %collective-permute-start.14) | collective-permute-done | bytes 131104 | tf_op jit(solution)/shard_map/ppermute | solution.py:178
  62.9 0.7 add_convert_fusion
  63.6 3.4 %all-to-all-start.1 = ((bf16[8,32,256]{2,1,0:T(8,128)(2,1)}), bf16[8,32,256]{2,1,0:T(8,128)(2,1)S(1)}, u32[]{:S(2)}, u32[]{:S(2)}) async-start(bf16[8,32,256]{2,1,0:T(8,128)(2,1)} %add_convert_fusion), calls=%async_computation.1 | async-start | bytes 262144 | tf_op jit(solution)/shard_map/all_to_all | solution.py:193
  67.0 0.1 add_bitcast_fusion
  67.1 0.8 %copy.6 = f32[256,256]{1,0:T(8,128)} copy(f32[256,256]{0,1:T(8,128)S(1)} %add_bitcast_fusion) | data formatting | bytes 524288
  67.9 8.1 %all-to-all-done.1 = bf16[8,32,256]{2,1,0:T(8,128)(2,1)S(1)} async-done(((bf16[8,32,256]{2,1,0:T(8,128)(2,1)}), bf16[8,32,256]{2,1,0:T(8,128)(2,1)S(1)}, u32[]{:S(2)}, u32[]{:S(2)}) %all-to-all-start.1) | async-done | bytes 131104 | tf_op jit(solution)/shard_map/all_to_all | solution.py:193
  76.0 0.6 convert_reduce_fusion
  (13 shorter events, 0.1 us)
Async XLA Ops:
  0.6 0.7 copy-start.2
  1.3 0.7 copy-start.3
  2.8 18.2 %all-to-all-start = ((bf16[8,40,256]{2,1,0:T(8,128)(2,1)}), bf16[8,40,256]{2,1,0:T(8,128)(2,1)S(1)}, u32[]{:S(2)}, u32[]{:S(2)}) async-start(bf16[8,40,256]{2,1,0:T(8,128)(2,1)} %shard_map.59), calls=%async_computation | async-start | bytes 327680 | tf_op jit(solution)/shard_map/all_to_all | solution.py:207
  11.3 1.2 %copy-start = (bf16[2048,256]{1,0:T(8,128)(2,1)S(1)}, bf16[2048,256]{1,0:T(8,128)(2,1)}, u32[]{:S(2)}) copy-start(bf16[2048,256]{1,0:T(8,128)(2,1)} %features.1) | copy-start | bytes 3145732
  12.5 0.9 %copy-start.1 = (bf16[2048,64]{0,1:T(8,128)(2,1)S(1)}, bf16[2048,64]{0,1:T(8,128)(2,1)}, u32[]{:S(2)}) copy-start(bf16[2048,64]{0,1:T(8,128)(2,1)} %param.7) | copy-start | bytes 786436
  21.0 8.8 %collective-permute-start.2 = (bf16[8,40,256]{2,1,0:T(8,128)(2,1)S(1)}, bf16[8,40,256]{2,1,0:T(8,128)(2,1)S(1)}, u32[]{:S(2)}, u32[]{:S(2)}) collective-permute-start(bf16[8,40,256]{2,1,0:T(8,128)(2,1)S(1)} %all-to-all-done.refs_0_), channel_id=1, source_target_pairs={{0,48},{16,0},{32,16},{48,32},{1,49},{17,1},{33,17},{49,33},{2,50}... | collective-permute-start | bytes 491528 | tf_op jit(solution)/shard_map/ppermute | solution.py:178
  21.8 8.0 %collective-permute-start.1 = (bf16[8,40,256]{2,1,0:T(8,128)(2,1)S(1)}, bf16[8,40,256]{2,1,0:T(8,128)(2,1)S(1)}, u32[]{:S(2)}, u32[]{:S(2)}) collective-permute-start(bf16[8,40,256]{2,1,0:T(8,128)(2,1)S(1)} %all-to-all-done.refs_0_), channel_id=1, source_target_pairs={{0,32},{16,48},{32,0},{48,16},{1,33},{17,49},{33,1},{49,17},{2,34}... | collective-permute-start | bytes 491528 | tf_op jit(solution)/shard_map/ppermute | solution.py:178
  22.7 7.7 %collective-permute-start = (bf16[8,40,256]{2,1,0:T(8,128)(2,1)S(1)}, bf16[8,40,256]{2,1,0:T(8,128)(2,1)S(1)}, u32[]{:S(2)}, u32[]{:S(2)}) collective-permute-start(bf16[8,40,256]{2,1,0:T(8,128)(2,1)S(1)} %all-to-all-done.refs_0_), channel_id=1, source_target_pairs={{0,16},{16,32},{32,48},{48,0},{1,17},{17,33},{33,49},{49,1},{2,18}... | collective-permute-start | bytes 491528 | tf_op jit(solution)/shard_map/ppermute | solution.py:178
  24.9 7.3 %collective-permute-start.3 = (bf16[8,40,256]{2,1,0:T(8,128)(2,1)S(1)}, bf16[8,40,256]{2,1,0:T(8,128)(2,1)S(1)}, u32[]{:S(2)}, u32[]{:S(2)}) collective-permute-start(bf16[8,40,256]{2,1,0:T(8,128)(2,1)S(1)} %all-to-all-done.refs_0_), channel_id=1, source_target_pairs={{0,1},{1,0},{2,3},{3,2},{4,5},{5,4},{6,7},{7,6},{8,9},{9,8},{10,11... | collective-permute-start | bytes 491528 | tf_op jit(solution)/shard_map/ppermute | solution.py:178
  29.8 2.4 %collective-permute-start.6 = (bf16[8,40,256]{2,1,0:T(8,128)(2,1)S(1)}, bf16[8,40,256]{2,1,0:T(8,128)(2,1)S(1)}, u32[]{:S(2)}, u32[]{:S(2)}) collective-permute-start(bf16[8,40,256]{2,1,0:T(8,128)(2,1)S(1)} %collective-permute-done.2.refs_3_), channel_id=1, source_target_pairs={{0,1},{1,0},{2,3},{3,2},{4,5},{5,4},{6,7},{7,6},{8,9},{9,8},{10,11... | collective-permute-start | bytes 491528 | tf_op jit(solution)/shard_map/ppermute | solution.py:178
  29.8 2.4 %collective-permute-start.5 = (bf16[8,40,256]{2,1,0:T(8,128)(2,1)S(1)}, bf16[8,40,256]{2,1,0:T(8,128)(2,1)S(1)}, u32[]{:S(2)}, u32[]{:S(2)}) collective-permute-start(bf16[8,40,256]{2,1,0:T(8,128)(2,1)S(1)} %collective-permute-done.1.refs_2_), channel_id=1, source_target_pairs={{0,1},{1,0},{2,3},{3,2},{4,5},{5,4},{6,7},{7,6},{8,9},{9,8},{10,11... | collective-permute-start | bytes 491528 | tf_op jit(solution)/shard_map/ppermute | solution.py:178
  30.4 1.8 %collective-permute-start.4 = (bf16[8,40,256]{2,1,0:T(8,128)(2,1)S(1)}, bf16[8,40,256]{2,1,0:T(8,128)(2,1)S(1)}, u32[]{:S(2)}, u32[]{:S(2)}) collective-permute-start(bf16[8,40,256]{2,1,0:T(8,128)(2,1)S(1)} %collective-permute-done.refs_1_), channel_id=1, source_target_pairs={{0,1},{1,0},{2,3},{3,2},{4,5},{5,4},{6,7},{7,6},{8,9},{9,8},{10,11... | collective-permute-start | bytes 491528 | tf_op jit(solution)/shard_map/ppermute | solution.py:178
  34.0 9.1 %collective-permute-start.9 = (bf16[64,1024]{1,0:T(8,128)(2,1)S(1)}, bf16[64,1024]{1,0:T(8,128)(2,1)S(1)}, u32[]{:S(2)}, u32[]{:S(2)}) collective-permute-start(bf16[64,1024]{1,0:T(8,128)(2,1)S(1)} %get-tuple-element.36), channel_id=1, source_target_pairs={{0,192},{64,0},{128,64},{192,128},{1,193},{65,1},{129,65},{193,129... | collective-permute-start | bytes 393224 | tf_op jit(solution)/shard_map/ppermute | solution.py:178
  36.8 7.9 %collective-permute-start.8 = (bf16[64,1024]{1,0:T(8,128)(2,1)S(1)}, bf16[64,1024]{1,0:T(8,128)(2,1)S(1)}, u32[]{:S(2)}, u32[]{:S(2)}) collective-permute-start(bf16[64,1024]{1,0:T(8,128)(2,1)S(1)} %get-tuple-element.36), channel_id=1, source_target_pairs={{0,128},{64,192},{128,0},{192,64},{1,129},{65,193},{129,1},{193,65... | collective-permute-start | bytes 393224 | tf_op jit(solution)/shard_map/ppermute | solution.py:178
  37.6 9.1 %collective-permute-start.7 = (bf16[64,1024]{1,0:T(8,128)(2,1)S(1)}, bf16[64,1024]{1,0:T(8,128)(2,1)S(1)}, u32[]{:S(2)}, u32[]{:S(2)}) collective-permute-start(bf16[64,1024]{1,0:T(8,128)(2,1)S(1)} %get-tuple-element.36), channel_id=1, source_target_pairs={{0,64},{64,128},{128,192},{192,0},{1,65},{65,129},{129,193},{193,1... | collective-permute-start | bytes 393224 | tf_op jit(solution)/shard_map/ppermute | solution.py:178
  48.5 2.2 %collective-permute-start.13 = (bf16[1024,256]{1,0:T(8,128)(2,1)S(1)}, bf16[1024,256]{1,0:T(8,128)(2,1)S(1)}, u32[]{:S(2)}, u32[]{:S(2)}) collective-permute-start(bf16[1024,256]{1,0:T(8,128)(2,1)S(1)} %get-tuple-element.49), channel_id=1, source_target_pairs={{0,1},{1,0},{2,3},{3,2},{4,5},{5,4},{6,7},{7,6},{8,9},{9,8},{10,11... | collective-permute-start | bytes 1572872 | tf_op jit(solution)/shard_map/ppermute | solution.py:178
  50.9 7.7 %collective-permute-start.16 = (bf16[8,32,256]{2,1,0:T(8,128)(2,1)S(1)}, bf16[8,32,256]{2,1,0:T(8,128)(2,1)S(1)}, u32[]{:S(2)}, u32[]{:S(2)}) collective-permute-start(bf16[8,32,256]{2,1,0:T(8,128)(2,1)S(1)} %bitcast.11), channel_id=1, source_target_pairs={{0,16},{16,32},{32,48},{48,0},{1,17},{17,33},{33,49},{49,1},{2,18}... | collective-permute-start | bytes 393224 | tf_op jit(solution)/shard_map/ppermute | solution.py:178
  53.6 9.3 %collective-permute-start.14 = (bf16[8,32,256]{2,1,0:T(8,128)(2,1)S(1)}, bf16[8,32,256]{2,1,0:T(8,128)(2,1)S(1)}, u32[]{:S(2)}, u32[]{:S(2)}) collective-permute-start(bf16[8,32,256]{2,1,0:T(8,128)(2,1)S(1)} %bitcast.10), channel_id=1, source_target_pairs={{0,48},{16,0},{32,16},{48,32},{1,49},{17,1},{33,17},{49,33},{2,50}... | collective-permute-start | bytes 393224 | tf_op jit(solution)/shard_map/ppermute | solution.py:178
  53.6 9.3 %collective-permute-start.15 = (bf16[8,32,256]{2,1,0:T(8,128)(2,1)S(1)}, bf16[8,32,256]{2,1,0:T(8,128)(2,1)S(1)}, u32[]{:S(2)}, u32[]{:S(2)}) collective-permute-start(bf16[8,32,256]{2,1,0:T(8,128)(2,1)S(1)} %bitcast.9), channel_id=1, source_target_pairs={{0,32},{16,48},{32,0},{48,16},{1,33},{17,49},{33,1},{49,17},{2,34}... | collective-permute-start | bytes 393224 | tf_op jit(solution)/shard_map/ppermute | solution.py:178
  56.4 10.6 %collective-permute-start.10 = (bf16[256,256]{1,0:T(8,128)(2,1)S(1)}, bf16[256,256]{1,0:T(8,128)(2,1)S(1)}, u32[]{:S(2)}, u32[]{:S(2)}) collective-permute-start(bf16[256,256]{1,0:T(8,128)(2,1)S(1)} %get-tuple-element.45), channel_id=1, source_target_pairs={{0,64},{64,128},{128,192},{192,0},{1,65},{65,129},{129,193},{193,1... | collective-permute-start | bytes 393224 | tf_op jit(solution)/shard_map/ppermute | solution.py:178
  56.5 10.5 %collective-permute-start.11 = (bf16[256,256]{1,0:T(8,128)(2,1)S(1)}, bf16[256,256]{1,0:T(8,128)(2,1)S(1)}, u32[]{:S(2)}, u32[]{:S(2)}) collective-permute-start(bf16[256,256]{1,0:T(8,128)(2,1)S(1)} %get-tuple-element.46), channel_id=1, source_target_pairs={{0,128},{64,192},{128,0},{192,64},{1,129},{65,193},{129,1},{193,65... | collective-permute-start | bytes 393224 | tf_op jit(solution)/shard_map/ppermute | solution.py:178
  58.6 8.4 %collective-permute-start.12 = (bf16[256,256]{1,0:T(8,128)(2,1)S(1)}, bf16[256,256]{1,0:T(8,128)(2,1)S(1)}, u32[]{:S(2)}, u32[]{:S(2)}) collective-permute-start(bf16[256,256]{1,0:T(8,128)(2,1)S(1)} %get-tuple-element.47), channel_id=1, source_target_pairs={{0,192},{64,0},{128,64},{192,128},{1,193},{65,1},{129,65},{193,129... | collective-permute-start | bytes 393224 | tf_op jit(solution)/shard_map/ppermute | solution.py:178
  63.6 12.4 %all-to-all-start.1 = ((bf16[8,32,256]{2,1,0:T(8,128)(2,1)}), bf16[8,32,256]{2,1,0:T(8,128)(2,1)S(1)}, u32[]{:S(2)}, u32[]{:S(2)}) async-start(bf16[8,32,256]{2,1,0:T(8,128)(2,1)} %add_convert_fusion), calls=%async_computation.1 | async-start | bytes 262144 | tf_op jit(solution)/shard_map/all_to_all | solution.py:193

commit v6 on v5

--- a/solution.py
+++ b/solution.py
@@ -7,6 +7,7 @@
 from jax.experimental.pallas import tpu as pltpu
 from jax.sharding import Mesh, PartitionSpec as P
 
+X = ("x",)
 Y = ("h", "l")
 F32 = jnp.float32
 BF16 = jnp.bfloat16
@@ -42,7 +43,11 @@
 def pack(landmarks, whitening, copies):
     rows, width = landmarks.shape
     quads = width // whitening.shape[1]
-    return call(functools.partial(pack_body, quads), shaped((copies, rows + rows // quads, width), BF16), landmarks, whitening)
+    return pl.pallas_call(
+        functools.partial(pack_body, quads),
+        out_shape=shaped((copies, rows + rows // quads, width), BF16),
+        compiler_params=PARAMS,
+    )(landmarks, whitening)
 
 
 def unpack(block, rank):
@@ -78,29 +83,31 @@
 
 
 def forward_body(count, rank, first, *refs):
-    blocks, (feat_t, sq_feat), (kern, *embeds) = refs[:count], refs[count : count + 2], refs[count + 2 + (not first) :]
+    blocks, (feat_t, sq_feat), outs = refs[:count], refs[count : count + 2], refs[count + 2 + (not first) :]
+    kerns, embeds = outs[:count], outs[count:]
     width = feat_t.shape[0]
     scale = 4.0 / width * LOG2E
     bias = sq_feat[...] * (-scale)
     total = None if first else refs[count + 2][...]
-    for i, block in enumerate(blocks):
+    for block, kern in zip(blocks, kerns):
         land, white = unpack(block[...], rank)
-        rows = land.shape[0]
         land32 = land.astype(F32)
         sq_land = jnp.sum(land32 * land32, axis=1, keepdims=True) * (-scale)
         cross = jnp.dot(land, feat_t[...], preferred_element_type=F32)
         value = jnp.exp2(cross * (2.0 * scale) + (bias + sq_land)).astype(BF16)
-        kern[i * rows : (i + 1) * rows, :] = value
+        kern[...] = value
         part = lax.dot_general(white, value, (((0,), (0,)), ((), ())), preferred_element_type=F32)
         total = part if total is None else total + part
     for embed in embeds:
         embed[...] = total.astype(embed.dtype)
 
 
-def forward(blocks, feat_t, sq_feat, prior, rows, rank):
-    toks = feat_t.shape[1]
-    shapes = [shaped((rows, toks), BF16), shaped((rank, toks), F32)] + [shaped((rank, toks), BF16)] * len(prior)
-    return call(functools.partial(forward_body, len(blocks), rank, not prior), shapes, *blocks, feat_t, sq_feat, *prior)
+def forward(blocks, feat_t, sq_feat, prior, rank):
+    width, toks = feat_t.shape
+    rows = [block.size // (width + rank) for block in blocks]
+    shapes = [shaped((n, toks), BF16) for n in rows] + [shaped((rank, toks), F32)] + [shaped((rank, toks), BF16)] * len(prior)
+    outs = call(functools.partial(forward_body, len(blocks), rank, not prior), shapes, *blocks, feat_t, sq_feat, *prior)
+    return outs[: len(blocks)], outs[len(blocks) :]
 
 
 def norm_body(factor, count, *refs):
@@ -110,7 +117,7 @@
         at = slice(p * own, (p + 1) * own)
         embed = shares[0][:, at]
         for s in range(1, count):
-            t = (p + s) % count
+            t = p ^ s
             embed = embed + shares[s][:, t * own : (t + 1) * own].astype(F32)
         upstream = cot[:, at]
         scale = lax.rsqrt(jnp.mean(embed * embed, axis=0, keepdims=True) + 1e-06)
@@ -124,15 +131,15 @@
 
 
 def backward_body(count, rank, first, *refs):
-    blocks, (kern, dembed, feat) = refs[:count], refs[count : count + 3]
+    blocks, kerns, (dembed, feat) = refs[:count], refs[count : 2 * count], refs[2 * count : 2 * count + 2]
     coef, land_grad, row_total = refs[-3:]
-    total = None if first else refs[count + 3][...]
+    total = None if first else refs[2 * count + 2][...]
     for i, block in enumerate(blocks):
         land, white = unpack(block[...], rank)
         rows = land.shape[0]
         at = slice(i * rows, (i + 1) * rows)
         dkernel = jnp.dot(white, dembed[...], preferred_element_type=F32)
-        value = (dkernel * kern[at, :].astype(F32)).astype(BF16)
+        value = (dkernel * kerns[i][...].astype(F32)).astype(BF16)
         coef[at, :] = value
         value32 = value.astype(F32)
         part = jnp.sum(value32, axis=0, keepdims=True)
@@ -143,12 +150,12 @@
     row_total[...] = total
 
 
-def backward(blocks, kern, dembed, feat, prior, kind):
+def backward(blocks, kerns, dembed, feat, prior, kind):
     toks, width = feat.shape
-    rows = kern.shape[0]
+    rows = sum(kern.shape[0] for kern in kerns)
     shapes = [shaped((rows, toks), BF16), shaped((rows, width), kind), shaped((1, toks), F32)]
     body = functools.partial(backward_body, len(blocks), dembed.shape[0], not prior)
-    return call(body, shapes, *blocks, kern, dembed, feat, *prior)
+    return call(body, shapes, *blocks, *kerns, dembed, feat, *prior)
 
 
 def feature_body(count, coefs, rank, *refs):
@@ -169,24 +176,31 @@
 
 def feature_share(blocks, coefs, feat_t, row_total, parts, rank):
     width, toks = feat_t.shape
-    shapes = [shaped((width, toks // parts), kind) for kind in [F32] + [BF16] * (parts - 1)]
+    shapes = [shaped((width, toks // parts), kind) for kind in [F32] * (parts // 2) + [BF16] * (parts // 2)]
     return call(functools.partial(feature_body, len(blocks), len(coefs), rank), shapes, *blocks, *coefs, feat_t, row_total)
 
 
-def shift(block, axes, step):
-    size = lax.axis_size(axes)
-    return lax.ppermute(block, axes, [(i, (i + step) % size) for i in range(size)])
-
-
-def spread(block, axes):
-    return [block] + [shift(block, axes, s) for s in range(1, lax.axis_size(axes))]
-
-
-def collect(pieces, axes, direction):
-    total = pieces[0]
-    for s in range(1, lax.axis_size(axes)):
-        total = total + shift(pieces[s].astype(BF16), axes, direction * s).astype(F32)
-    return total
+def partner(block, ring, which):
+    masks = (1, 3)
+    perm = [(2 * i + c, 2 * (i ^ masks[which ^ c]) + c) for i in range(lax.axis_size(ring)) for c in range(2)]
+    return lax.ppermute(block, ring + ("c",), perm)
+
+
+def other_core(block):
+    return lax.ppermute(block, "c", [(0, 1), (1, 0)])
+
+
+def spread(block, ring):
+    first = partner(block, ring, 0)
+    second = partner(block, ring, 1)
+    return [block, first, second, partner(first, ring, 1)]
+
+
+def collect(pieces, ring):
+    own, first, second, opposite = pieces
+    first = first + partner(opposite.astype(BF16), ring, 1).astype(F32)
+    own = own + partner(second.astype(BF16), ring, 1).astype(F32)
+    return own + partner(first.astype(BF16), ring, 0).astype(F32)
 
 
 def collect_at_once(pieces, axes):
@@ -201,28 +215,29 @@
     gamma = 4.0 / width
 
     def places():
-        here, half = lax.axis_index("x"), lax.axis_index("h")
-        return [lax.rem(here + s, n_x) * n_h + half for s in range(n_x)]
+        here, half, core = lax.axis_index("x"), lax.axis_index("h"), lax.axis_index("c")
+        members = [here, here ^ (1 + 2 * core), here ^ (3 - 2 * core), here ^ 2]
+        return [member * n_h + half for member in members]
 
     packed = lax.all_to_all(pack(landmarks, whitening, n_z), "z", 0, 0, tiled=True)
     feat, feat_t, sq_feat, cot = prepare(features, cotangent.T, n_x * n_h, places, n_x)
     packed, feat, feat_t, sq_feat, cot = lax.optimization_barrier((packed, feat, feat_t, sq_feat, cot))
     mine = spread(packed, Y)
-    theirs = [shift(block, "c", 1) for block in mine]
-
-    half_rows = n_y * n_z * rows
-    kern_mine, embed = forward(mine, feat_t, sq_feat, [], half_rows, rank)
-    kern_theirs, embed, share = forward(theirs, feat_t, sq_feat, [embed], half_rows, rank)
-    dembed = norm_backward([embed] + [shift(share, "x", s) for s in range(1, n_x)], cot, -gamma)
+    theirs = [other_core(block) for block in mine]
+
+    early, (embed,) = forward(mine[:3] + theirs[:3], feat_t, sq_feat, [], rank)
+    late, (embed, share) = forward(mine[3:] + theirs[3:], feat_t, sq_feat, [embed], rank)
+    kern_mine, kern_theirs = early[:3] + late[:1], early[3:] + late[1:]
+    dembed = norm_backward([embed] + spread(share, X)[1:], cot, -gamma)
 
     coef_theirs, land_theirs, row_total = backward(theirs, kern_theirs, dembed, feat, [], BF16)
     coef_mine, land_mine, row_total = backward(mine, kern_mine, dembed, feat, [row_total], F32)
-    share = (land_mine + shift(land_theirs, "c", 1).astype(F32)).reshape(n_y, n_z, rows, width)
-    share = collect(share, Y, -1)
+    land_share = (land_mine + other_core(land_theirs).astype(F32)).reshape(n_y, n_z, rows, width)
+    land_share = collect(land_share, Y)
 
     feat_shares = feature_share(mine + theirs, [coef_mine, coef_theirs], feat_t, row_total, n_x, rank)
-    landmark_grad = collect_at_once(share, "z")
-    feature_grad = collect(feat_shares, "x", 1).T
+    landmark_grad = collect_at_once(land_share, "z")
+    feature_grad = collect(feat_shares, X).T
     return (feature_grad, landmark_grad)
 
 

time: 77 us -> 84.3 us (1.095)
  the two profiles are of different devices: /device:TPU:24 before, /device:TPU:6 now
where the time goes in v6:
time: 84.3 us; the launch traced here: 83.9 us
  waiting for transfers between devices  41.5 us (49%)
  starting transfers between devices  26.5 us (31%)
  Pallas kernels  8.98 us (11%)
  local copies, waits for them, and re-layouts  4.47 us (5%)
  other arithmetic  1.61 us (2%)
    ppermute x12, waiting for transfers between devices, partner(): return lax.ppermute(block, ring + ('c',), perm)  26.1 us
    ppermute x12, starting transfers between devices, partner(): return lax.ppermute(block, ring + ('c',), perm)  13.9 us
    all_to_all x1, starting transfers between devices, per_device(): lax.all_to_all(pack(landmarks, whitening, n_z), 'z', 0, 0, tiled=True)  8.47 us
    pallas_call x7, Pallas kernels, call(): pl.pallas_call(body, out_shape=out_shape, in_specs=[WHOLE] * len(operands...  8.24 us
    all_to_all x1, waiting for transfers between devices, collect_at_once(): lax.all_to_all(pieces.astype(BF16), axes, 0, 0, tiled=True).astype(F32)  8.08 us
    all_to_all x1, waiting for transfers between devices, per_device(): lax.all_to_all(pack(landmarks, whitening, n_z), 'z', 0, 0, tiled=True)  7.35 us
    unnamed x9, local copies, waits for them, and re-layouts  4.42 us
    all_to_all x1, starting transfers between devices, collect_at_once(): lax.all_to_all(pieces.astype(BF16), axes, 0, 0, tiled=True).astype(F32)  3.37 us
  transfers between devices with their start and end apart: 19, of which 10 were waited for; matrix products, arithmetic and copies ran while one was open for 2% of the time, Pallas kernels for 7%

profile of v6, /device:TPU:6, one launch (start us, length us, event | category | flops | bytes accessed | tf_op | source)
XLA Modules:
  0.0 83.9 jit_solution(3807877245475505800)
XLA Ops:
  0.6 0.7 copy-done.2
  1.4 0.7 copy-done.3
  2.0 0.7 shard_map.59
  2.8 8.5 %all-to-all-start = ((bf16[8,40,256]{2,1,0:T(8,128)(2,1)}), bf16[8,40,256]{2,1,0:T(8,128)(2,1)S(1)}, u32[]{:S(2)}, u32[]{:S(2)}) async-start(bf16[8,40,256]{2,1,0:T(8,128)(2,1)} %shard_map.59), calls=%async_computation | async-start | bytes 327680 | tf_op jit(solution)/shard_map/all_to_all | solution.py:222
  11.3 1.2 %copy-done = bf16[2048,256]{1,0:T(8,128)(2,1)S(1)} copy-done((bf16[2048,256]{1,0:T(8,128)(2,1)S(1)}, bf16[2048,256]{1,0:T(8,128)(2,1)}, u32[]{:S(2)}) %copy-start) | copy-done | bytes 1048600
  12.5 0.9 %copy-done.1 = bf16[2048,64]{0,1:T(8,128)(2,1)S(1)} copy-done((bf16[2048,64]{0,1:T(8,128)(2,1)S(1)}, bf16[2048,64]{0,1:T(8,128)(2,1)}, u32[]{:S(2)}) %copy-start.1) | copy-done | bytes 262168
  13.4 0.2 shard_map.60
  13.7 7.3 %all-to-all-done.refs_0_ = bf16[8,40,256]{2,1,0:T(8,128)(2,1)S(1)} async-done(((bf16[8,40,256]{2,1,0:T(8,128)(2,1)}), bf16[8,40,256]{2,1,0:T(8,128)(2,1)S(1)}, u32[]{:S(2)}, u32[]{:S(2)}) %all-to-all-start) | async-done | bytes 163872 | tf_op jit(solution)/shard_map/all_to_all | solution.py:222
  21.0 1.6 %collective-permute-start = (bf16[8,40,256]{2,1,0:T(8,128)(2,1)S(1)}, bf16[8,40,256]{2,1,0:T(8,128)(2,1)S(1)}, u32[]{:S(2)}, u32[]{:S(2)}) collective-permute-start(bf16[8,40,256]{2,1,0:T(8,128)(2,1)S(1)} %all-to-all-done.refs_0_), channel_id=1, source_target_pairs={{0,16},{1,49},{16,0},{17,33},{32,48},{33,17},{48,32},{49,1},{2,18}... | collective-permute-start | bytes 491528 | tf_op jit(solution)/shard_map/ppermute | solution.py:186
  22.6 2.2 %collective-permute-start.1 = (bf16[8,40,256]{2,1,0:T(8,128)(2,1)S(1)}, bf16[8,40,256]{2,1,0:T(8,128)(2,1)S(1)}, u32[]{:S(2)}, u32[]{:S(2)}) collective-permute-start(bf16[8,40,256]{2,1,0:T(8,128)(2,1)S(1)} %all-to-all-done.refs_0_), channel_id=1, source_target_pairs={{0,48},{1,17},{16,32},{17,1},{32,16},{33,49},{48,0},{49,33},{2,50}... | collective-permute-start | bytes 491528 | tf_op jit(solution)/shard_map/ppermute | solution.py:186
  24.8 3.3 %collective-permute-done.refs_1_ = bf16[8,40,256]{2,1,0:T(8,128)(2,1)S(1)} collective-permute-done((bf16[8,40,256]{2,1,0:T(8,128)(2,1)S(1)}, bf16[8,40,256]{2,1,0:T(8,128)(2,1)S(1)}, u32[]{:S(2)}, u32[]{:S(2)}) %collective-permute-start) | collective-permute-done | bytes 163872 | tf_op jit(solution)/shard_map/ppermute | solution.py:186
  28.1 1.3 %collective-permute-start.2 = (bf16[8,40,256]{2,1,0:T(8,128)(2,1)S(1)}, bf16[8,40,256]{2,1,0:T(8,128)(2,1)S(1)}, u32[]{:S(2)}, u32[]{:S(2)}) collective-permute-start(bf16[8,40,256]{2,1,0:T(8,128)(2,1)S(1)} %collective-permute-done.refs_1_), channel_id=1, source_target_pairs={{0,48},{1,17},{16,32},{17,1},{32,16},{33,49},{48,0},{49,33},{2,50}... | collective-permute-start | bytes 491528 | tf_op jit(solution)/shard_map/ppermute | solution.py:186
  29.4 0.0 collective-permute-start.3
  29.4 0.0 collective-permute-done.1.refs_2_
  29.4 0.5 collective-permute-start.5
  29.9 0.0 collective-permute-start.4
  29.9 4.8 %collective-permute-done.2.refs_0_.refs_3_ = bf16[8,40,256]{2,1,0:T(8,128)(2,1)S(1)} collective-permute-done((bf16[8,40,256]{2,1,0:T(8,128)(2,1)S(1)}, bf16[8,40,256]{2,1,0:T(8,128)(2,1)S(1)}, u32[]{:S(2)}, u32[]{:S(2)}) %collective-permute-start.2) | collective-permute-done | bytes 163872 | tf_op jit(solution)/shard_map/ppermute | solution.py:186
  34.6 0.0 collective-permute-start.6
  34.6 0.0 collective-permute-done.4.refs_4_.refs_1_.refs_5_
  34.7 2.5 %shard_map.61 = (bf16[256,1024]{1,0:T(8,128)(2,1)S(1)}, bf16[256,1024]{1,0:T(8,128)(2,1)S(1)}, bf16[256,1024]{1,0:T(8,128)(2,1)S(1)}, bf16[256,1024]{1,0:T(8,128...) custom-call(bf16[8,40,256]{2,1,0:T(8,128)(2,1)S(1)} %all-to-all-done.refs_0_, ...), custom_call_target="tpu_custom_call" | custom-call | tf_op jit(solution)/shard_map/pallas_call | solution.py:20
  37.2 0.9 %shard_map.62 = (bf16[256,1024]{1,0:T(8,128)(2,1)S(1)}, bf16[256,1024]{1,0:T(8,128)(2,1)S(1)}, f32[64,1024]{1,0:T(8,128)S(1)}, bf16[64,1024]{1,0:T(8,128)(2,1)S(1)}) custom-call(bf16[8,40,256]{2,1,0:T(8,128)(2,1)S(1)} %collective-permute-done.2.refs_0_.refs_3_, bf16[8,40,256]{2,1,0:T(8,128)(2,1)S(1)} %collective-permute-done.6.refs_1_.refs_3_.refs_7_, ...), custom_call_target="tpu_custom_call" | custom-call | tf_op jit(solution)/shard_map/pallas_call | solution.py:20
  38.1 0.9 %collective-permute-start.7 = (bf16[64,1024]{1,0:T(8,128)(2,1)S(1)}, bf16[64,1024]{1,0:T(8,128)(2,1)S(1)}, u32[]{:S(2)}, u32[]{:S(2)}) collective-permute-start(bf16[64,1024]{1,0:T(8,128)(2,1)S(1)} %get-tuple-element.45), channel_id=1, source_target_pairs={{0,64},{1,193},{64,0},{65,129},{128,192},{129,65},{192,128},{193,1... | collective-permute-start | bytes 393224 | tf_op jit(solution)/shard_map/ppermute | solution.py:186
  39.1 1.1 %collective-permute-start.8 = (bf16[64,1024]{1,0:T(8,128)(2,1)S(1)}, bf16[64,1024]{1,0:T(8,128)(2,1)S(1)}, u32[]{:S(2)}, u32[]{:S(2)}) collective-permute-start(bf16[64,1024]{1,0:T(8,128)(2,1)S(1)} %get-tuple-element.45), channel_id=1, source_target_pairs={{0,192},{1,65},{64,128},{65,1},{128,64},{129,193},{192,0},{193,129... | collective-permute-start | bytes 393224 | tf_op jit(solution)/shard_map/ppermute | solution.py:186
  40.2 4.1 %collective-permute-done.7.refs_1_ = bf16[64,1024]{1,0:T(8,128)(2,1)S(1)} collective-permute-done((bf16[64,1024]{1,0:T(8,128)(2,1)S(1)}, bf16[64,1024]{1,0:T(8,128)(2,1)S(1)}, u32[]{:S(2)}, u32[]{:S(2)}) %collective-permute-start.7) | collective-permute-done | bytes 131104 | tf_op jit(solution)/shard_map/ppermute | solution.py:186
  44.3 0.0 collective-permute-start.9
  44.3 1.0 %collective-permute-done.8.refs_2_ = bf16[64,1024]{1,0:T(8,128)(2,1)S(1)} collective-permute-done((bf16[64,1024]{1,0:T(8,128)(2,1)S(1)}, bf16[64,1024]{1,0:T(8,128)(2,1)S(1)}, u32[]{:S(2)}, u32[]{:S(2)}) %collective-permute-start.8) | collective-permute-done | bytes 131104 | tf_op jit(solution)/shard_map/ppermute | solution.py:186
  45.3 5.2 %collective-permute-done.9.refs_3_ = bf16[64,1024]{1,0:T(8,128)(2,1)S(1)} collective-permute-done((bf16[64,1024]{1,0:T(8,128)(2,1)S(1)}, bf16[64,1024]{1,0:T(8,128)(2,1)S(1)}, u32[]{:S(2)}, u32[]{:S(2)}) %collective-permute-start.9) | collective-permute-done | bytes 131104 | tf_op jit(solution)/shard_map/ppermute | solution.py:186
  50.5 0.2 shard_map.63.refs_8_
  50.7 1.5 %shard_map.64 = (bf16[1024,1024]{1,0:T(8,128)(2,1)S(1)}, bf16[1024,256]{1,0:T(8,128)(2,1)S(1)}, f32[1,1024]{1,0:T(1,128)S(1)}) custom-call(bf16[8,40,256]{2,1,0:T(8,128)(2,1)S(1)} %collective-permute-done.3.refs_3_.refs_0_.refs_4_, bf16[8,40,256]{2,1,0:T(8,128)(2,1)S(1)} %collective-permute-done.4.refs_4_.refs_1_.refs_5_, ...), custom_call_target="tpu_custom_call" | custom-call | tf_op jit(solution)/shard_map/pallas_call | solution.py:20
  52.2 0.3 collective-permute-start.13
  52.5 1.5 %shard_map.65 = (bf16[1024,1024]{1,0:T(8,128)(2,1)S(1)}, f32[1024,256]{1,0:T(8,128)S(1)}, f32[1,1024]{1,0:T(1,128)S(1)}) custom-call(bf16[8,40,256]{2,1,0:T(8,128)(2,1)S(1)} %all-to-all-done.refs_0_, bf16[8,40,256]{2,1,0:T(8,128)(2,1)S(1)} %collective-permute-done.refs_1_, bf16[8,40,256]{2,1,0:T(8,128)(2,1)S(1)} %collective-permute-done.1.refs_2_, ...), custom_call_target="tpu_custom_call" | custom-call | tf_op jit(solution)/shard_map/pallas_call | solution.py:20
  54.1 1.3 %shard_map.66 = (f32[256,256]{1,0:T(8,128)S(1)}, f32[256,256]{1,0:T(8,128)S(1)}, bf16[256,256]{1,0:T(8,128)(2,1)S(1)}, bf16[256,256]{1,0:T(8,128)(2,1)S(1)}) custom-call(bf16[8,40,256]{2,1,0:T(8,128)(2,1)S(1)} %all-to-all-done.refs_0_, bf16[8,40,256]{2,1,0:T(8,128)(2,1)S(1)} %collective-permute-done.refs_1_, ...), custom_call_target="tpu_custom_call" | custom-call | tf_op jit(solution)/shard_map/pallas_call | solution.py:20
  55.3 0.1 collective-permute-start.10
  55.4 3.2 %collective-permute-start.11 = (bf16[256,256]{1,0:T(8,128)(2,1)S(1)}, bf16[256,256]{1,0:T(8,128)(2,1)S(1)}, u32[]{:S(2)}, u32[]{:S(2)}) collective-permute-start(bf16[256,256]{1,0:T(8,128)(2,1)S(1)} %get-tuple-element.59), channel_id=1, source_target_pairs={{0,192},{1,65},{64,128},{65,1},{128,64},{129,193},{192,0},{193,129... | collective-permute-start | bytes 393224 | tf_op jit(solution)/shard_map/ppermute | solution.py:186
  58.7 0.2 fusion
  58.9 1.3 %collective-permute-start.15 = (bf16[8,32,256]{2,1,0:T(8,128)(2,1)S(1)}, bf16[8,32,256]{2,1,0:T(8,128)(2,1)S(1)}, u32[]{:S(2)}, u32[]{:S(2)}) collective-permute-start(bf16[8,32,256]{2,1,0:T(8,128)(2,1)S(1)} %bitcast.11), channel_id=1, source_target_pairs={{0,48},{1,17},{16,32},{17,1},{32,16},{33,49},{48,0},{49,33},{2,50}... | collective-permute-start | bytes 393224 | tf_op jit(solution)/shard_map/ppermute | solution.py:186
  60.2 2.0 %collective-permute-start.14 = (bf16[8,32,256]{2,1,0:T(8,128)(2,1)S(1)}, bf16[8,32,256]{2,1,0:T(8,128)(2,1)S(1)}, u32[]{:S(2)}, u32[]{:S(2)}) collective-permute-start(bf16[8,32,256]{2,1,0:T(8,128)(2,1)S(1)} %bitcast.10), channel_id=1, source_target_pairs={{0,48},{1,17},{16,32},{17,1},{32,16},{33,49},{48,0},{49,33},{2,50}... | collective-permute-start | bytes 393224 | tf_op jit(solution)/shard_map/ppermute | solution.py:186
  62.2 2.9 %collective-permute-done.15 = bf16[8,32,256]{2,1,0:T(8,128)(2,1)S(1)} collective-permute-done((bf16[8,32,256]{2,1,0:T(8,128)(2,1)S(1)}, bf16[8,32,256]{2,1,0:T(8,128)(2,1)S(1)}, u32[]{:S(2)}, u32[]{:S(2)}) %collective-permute-start.15) | collective-permute-done | bytes 131104 | tf_op jit(solution)/shard_map/ppermute | solution.py:186
  65.2 0.1 collective-permute-start.16
  65.3 0.1 collective-permute-start.12
  65.4 1.9 %collective-permute-done.14 = bf16[8,32,256]{2,1,0:T(8,128)(2,1)S(1)} collective-permute-done((bf16[8,32,256]{2,1,0:T(8,128)(2,1)S(1)}, bf16[8,32,256]{2,1,0:T(8,128)(2,1)S(1)}, u32[]{:S(2)}, u32[]{:S(2)}) %collective-permute-start.14) | collective-permute-done | bytes 131104 | tf_op jit(solution)/shard_map/ppermute | solution.py:186
  67.3 2.9 %collective-permute-done.16 = bf16[8,32,256]{2,1,0:T(8,128)(2,1)S(1)} collective-permute-done((bf16[8,32,256]{2,1,0:T(8,128)(2,1)S(1)}, bf16[8,32,256]{2,1,0:T(8,128)(2,1)S(1)}, u32[]{:S(2)}, u32[]{:S(2)}) %collective-permute-start.16) | collective-permute-done | bytes 131104 | tf_op jit(solution)/shard_map/ppermute | solution.py:186
  70.2 0.7 add_convert_fusion
  70.9 3.4 %all-to-all-start.1 = ((bf16[8,32,256]{2,1,0:T(8,128)(2,1)}), bf16[8,32,256]{2,1,0:T(8,128)(2,1)S(1)}, u32[]{:S(2)}, u32[]{:S(2)}) async-start(bf16[8,32,256]{2,1,0:T(8,128)(2,1)} %add_convert_fusion), calls=%async_computation.1 | async-start | bytes 262144 | tf_op jit(solution)/shard_map/all_to_all | solution.py:207
  74.3 0.0 collective-permute-done.10
  74.4 0.8 copy.6
  75.2 8.1 %all-to-all-done.1 = bf16[8,32,256]{2,1,0:T(8,128)(2,1)S(1)} async-done(((bf16[8,32,256]{2,1,0:T(8,128)(2,1)}), bf16[8,32,256]{2,1,0:T(8,128)(2,1)S(1)}, u32[]{:S(2)}, u32[]{:S(2)}) %all-to-all-start.1) | async-done | bytes 131104 | tf_op jit(solution)/shard_map/all_to_all | solution.py:207
  83.3 0.6 convert_reduce_fusion
  (15 shorter events, 0.2 us)
Async XLA Ops:
  0.6 0.7 copy-start.2
  1.3 0.7 copy-start.3
  2.8 18.2 %all-to-all-start = ((bf16[8,40,256]{2,1,0:T(8,128)(2,1)}), bf16[8,40,256]{2,1,0:T(8,128)(2,1)S(1)}, u32[]{:S(2)}, u32[]{:S(2)}) async-start(bf16[8,40,256]{2,1,0:T(8,128)(2,1)} %shard_map.59), calls=%async_computation | async-start | bytes 327680 | tf_op jit(solution)/shard_map/all_to_all | solution.py:222
  11.3 1.2 %copy-start = (bf16[2048,256]{1,0:T(8,128)(2,1)S(1)}, bf16[2048,256]{1,0:T(8,128)(2,1)}, u32[]{:S(2)}) copy-start(bf16[2048,256]{1,0:T(8,128)(2,1)} %features.1) | copy-start | bytes 3145732
  12.5 0.9 %copy-start.1 = (bf16[2048,64]{0,1:T(8,128)(2,1)S(1)}, bf16[2048,64]{0,1:T(8,128)(2,1)}, u32[]{:S(2)}) copy-start(bf16[2048,64]{0,1:T(8,128)(2,1)} %param.7) | copy-start | bytes 786436
  21.0 7.1 %collective-permute-start = (bf16[8,40,256]{2,1,0:T(8,128)(2,1)S(1)}, bf16[8,40,256]{2,1,0:T(8,128)(2,1)S(1)}, u32[]{:S(2)}, u32[]{:S(2)}) collective-permute-start(bf16[8,40,256]{2,1,0:T(8,128)(2,1)S(1)} %all-to-all-done.refs_0_), channel_id=1, source_target_pairs={{0,16},{1,49},{16,0},{17,33},{32,48},{33,17},{48,32},{49,1},{2,18}... | collective-permute-start | bytes 491528 | tf_op jit(solution)/shard_map/ppermute | solution.py:186
  22.6 6.8 %collective-permute-start.1 = (bf16[8,40,256]{2,1,0:T(8,128)(2,1)S(1)}, bf16[8,40,256]{2,1,0:T(8,128)(2,1)S(1)}, u32[]{:S(2)}, u32[]{:S(2)}) collective-permute-start(bf16[8,40,256]{2,1,0:T(8,128)(2,1)S(1)} %all-to-all-done.refs_0_), channel_id=1, source_target_pairs={{0,48},{1,17},{16,32},{17,1},{32,16},{33,49},{48,0},{49,33},{2,50}... | collective-permute-start | bytes 491528 | tf_op jit(solution)/shard_map/ppermute | solution.py:186
  28.1 6.5 %collective-permute-start.2 = (bf16[8,40,256]{2,1,0:T(8,128)(2,1)S(1)}, bf16[8,40,256]{2,1,0:T(8,128)(2,1)S(1)}, u32[]{:S(2)}, u32[]{:S(2)}) collective-permute-start(bf16[8,40,256]{2,1,0:T(8,128)(2,1)S(1)} %collective-permute-done.refs_1_), channel_id=1, source_target_pairs={{0,48},{1,17},{16,32},{17,1},{32,16},{33,49},{48,0},{49,33},{2,50}... | collective-permute-start | bytes 491528 | tf_op jit(solution)/shard_map/ppermute | solution.py:186
  29.4 5.3 %collective-permute-start.3 = (bf16[8,40,256]{2,1,0:T(8,128)(2,1)S(1)}, bf16[8,40,256]{2,1,0:T(8,128)(2,1)S(1)}, u32[]{:S(2)}, u32[]{:S(2)}) collective-permute-start(bf16[8,40,256]{2,1,0:T(8,128)(2,1)S(1)} %all-to-all-done.refs_0_), channel_id=1, source_target_pairs={{0,1},{1,0},{2,3},{3,2},{4,5},{5,4},{6,7},{7,6},{8,9},{9,8},{10,11... | collective-permute-start | bytes 491528 | tf_op jit(solution)/shard_map/ppermute | solution.py:190
  29.4 5.3 %collective-permute-start.5 = (bf16[8,40,256]{2,1,0:T(8,128)(2,1)S(1)}, bf16[8,40,256]{2,1,0:T(8,128)(2,1)S(1)}, u32[]{:S(2)}, u32[]{:S(2)}) collective-permute-start(bf16[8,40,256]{2,1,0:T(8,128)(2,1)S(1)} %collective-permute-done.1.refs_2_), channel_id=1, source_target_pairs={{0,1},{1,0},{2,3},{3,2},{4,5},{5,4},{6,7},{7,6},{8,9},{9,8},{10,11... | collective-permute-start | bytes 491528 | tf_op jit(solution)/shard_map/ppermute | solution.py:190
  29.9 4.8 %collective-permute-start.4 = (bf16[8,40,256]{2,1,0:T(8,128)(2,1)S(1)}, bf16[8,40,256]{2,1,0:T(8,128)(2,1)S(1)}, u32[]{:S(2)}, u32[]{:S(2)}) collective-permute-start(bf16[8,40,256]{2,1,0:T(8,128)(2,1)S(1)} %collective-permute-done.refs_1_), channel_id=1, source_target_pairs={{0,1},{1,0},{2,3},{3,2},{4,5},{5,4},{6,7},{7,6},{8,9},{9,8},{10,11... | collective-permute-start | bytes 491528 | tf_op jit(solution)/shard_map/ppermute | solution.py:190
  34.6 2.6 %collective-permute-start.6 = (bf16[8,40,256]{2,1,0:T(8,128)(2,1)S(1)}, bf16[8,40,256]{2,1,0:T(8,128)(2,1)S(1)}, u32[]{:S(2)}, u32[]{:S(2)}) collective-permute-start(bf16[8,40,256]{2,1,0:T(8,128)(2,1)S(1)} %collective-permute-done.2.refs_0_.refs_3_), channel_id=1, source_target_pairs={{0,1},{1,0},{2,3},{3,2},{4,5},{5,4},{6,7},{7,6},{8,9},{9,8},{10,11... | collective-permute-start | bytes 491528 | tf_op jit(solution)/shard_map/ppermute | solution.py:190
  38.1 6.2 %collective-permute-start.7 = (bf16[64,1024]{1,0:T(8,128)(2,1)S(1)}, bf16[64,1024]{1,0:T(8,128)(2,1)S(1)}, u32[]{:S(2)}, u32[]{:S(2)}) collective-permute-start(bf16[64,1024]{1,0:T(8,128)(2,1)S(1)} %get-tuple-element.45), channel_id=1, source_target_pairs={{0,64},{1,193},{64,0},{65,129},{128,192},{129,65},{192,128},{193,1... | collective-permute-start | bytes 393224 | tf_op jit(solution)/shard_map/ppermute | solution.py:186
  39.1 6.3 %collective-permute-start.8 = (bf16[64,1024]{1,0:T(8,128)(2,1)S(1)}, bf16[64,1024]{1,0:T(8,128)(2,1)S(1)}, u32[]{:S(2)}, u32[]{:S(2)}) collective-permute-start(bf16[64,1024]{1,0:T(8,128)(2,1)S(1)} %get-tuple-element.45), channel_id=1, source_target_pairs={{0,192},{1,65},{64,128},{65,1},{128,64},{129,193},{192,0},{193,129... | collective-permute-start | bytes 393224 | tf_op jit(solution)/shard_map/ppermute | solution.py:186
  44.3 6.2 %collective-permute-start.9 = (bf16[64,1024]{1,0:T(8,128)(2,1)S(1)}, bf16[64,1024]{1,0:T(8,128)(2,1)S(1)}, u32[]{:S(2)}, u32[]{:S(2)}) collective-permute-start(bf16[64,1024]{1,0:T(8,128)(2,1)S(1)} %collective-permute-done.7.refs_1_), channel_id=1, source_target_pairs={{0,192},{1,65},{64,128},{65,1},{128,64},{129,193},{192,0},{193,129... | collective-permute-start | bytes 393224 | tf_op jit(solution)/shard_map/ppermute | solution.py:186
  52.2 6.4 %collective-permute-start.13 = (bf16[1024,256]{1,0:T(8,128)(2,1)S(1)}, bf16[1024,256]{1,0:T(8,128)(2,1)S(1)}, u32[]{:S(2)}, u32[]{:S(2)}) collective-permute-start(bf16[1024,256]{1,0:T(8,128)(2,1)S(1)} %get-tuple-element.61), channel_id=1, source_target_pairs={{0,1},{1,0},{2,3},{3,2},{4,5},{5,4},{6,7},{7,6},{8,9},{9,8},{10,11... | collective-permute-start | bytes 1572872 | tf_op jit(solution)/shard_map/ppermute | solution.py:190
  55.3 19.0 %collective-permute-start.10 = (bf16[256,256]{1,0:T(8,128)(2,1)S(1)}, bf16[256,256]{1,0:T(8,128)(2,1)S(1)}, u32[]{:S(2)}, u32[]{:S(2)}) collective-permute-start(bf16[256,256]{1,0:T(8,128)(2,1)S(1)} %get-tuple-element.57), channel_id=1, source_target_pairs={{0,192},{1,65},{64,128},{65,1},{128,64},{129,193},{192,0},{193,129... | collective-permute-start | bytes 393224 | tf_op jit(solution)/shard_map/ppermute | solution.py:186
  55.4 9.8 %collective-permute-start.11 = (bf16[256,256]{1,0:T(8,128)(2,1)S(1)}, bf16[256,256]{1,0:T(8,128)(2,1)S(1)}, u32[]{:S(2)}, u32[]{:S(2)}) collective-permute-start(bf16[256,256]{1,0:T(8,128)(2,1)S(1)} %get-tuple-element.59), channel_id=1, source_target_pairs={{0,192},{1,65},{64,128},{65,1},{128,64},{129,193},{192,0},{193,129... | collective-permute-start | bytes 393224 | tf_op jit(solution)/shard_map/ppermute | solution.py:186
  58.9 6.3 %collective-permute-start.15 = (bf16[8,32,256]{2,1,0:T(8,128)(2,1)S(1)}, bf16[8,32,256]{2,1,0:T(8,128)(2,1)S(1)}, u32[]{:S(2)}, u32[]{:S(2)}) collective-permute-start(bf16[8,32,256]{2,1,0:T(8,128)(2,1)S(1)} %bitcast.11), channel_id=1, source_target_pairs={{0,48},{1,17},{16,32},{17,1},{32,16},{33,49},{48,0},{49,33},{2,50}... | collective-permute-start | bytes 393224 | tf_op jit(solution)/shard_map/ppermute | solution.py:186
  60.2 7.1 %collective-permute-start.14 = (bf16[8,32,256]{2,1,0:T(8,128)(2,1)S(1)}, bf16[8,32,256]{2,1,0:T(8,128)(2,1)S(1)}, u32[]{:S(2)}, u32[]{:S(2)}) collective-permute-start(bf16[8,32,256]{2,1,0:T(8,128)(2,1)S(1)} %bitcast.10), channel_id=1, source_target_pairs={{0,48},{1,17},{16,32},{17,1},{32,16},{33,49},{48,0},{49,33},{2,50}... | collective-permute-start | bytes 393224 | tf_op jit(solution)/shard_map/ppermute | solution.py:186
  65.2 5.1 %collective-permute-start.16 = (bf16[8,32,256]{2,1,0:T(8,128)(2,1)S(1)}, bf16[8,32,256]{2,1,0:T(8,128)(2,1)S(1)}, u32[]{:S(2)}, u32[]{:S(2)}) collective-permute-start(bf16[8,32,256]{2,1,0:T(8,128)(2,1)S(1)} %add_convert_fusion.1), channel_id=1, source_target_pairs={{0,16},{1,49},{16,0},{17,33},{32,48},{33,17},{48,32},{49,1},{2,18}... | collective-permute-start | bytes 393224 | tf_op jit(solution)/shard_map/ppermute | solution.py:186
  65.3 9.0 %collective-permute-start.12 = (bf16[256,256]{1,0:T(8,128)(2,1)S(1)}, bf16[256,256]{1,0:T(8,128)(2,1)S(1)}, u32[]{:S(2)}, u32[]{:S(2)}) collective-permute-start(bf16[256,256]{1,0:T(8,128)(2,1)S(1)} %add_convert_fusion.2), channel_id=1, source_target_pairs={{0,64},{1,193},{64,0},{65,129},{128,192},{129,65},{192,128},{193,1... | collective-permute-start | bytes 393224 | tf_op jit(solution)/shard_map/ppermute | solution.py:186
  70.9 12.4 %all-to-all-start.1 = ((bf16[8,32,256]{2,1,0:T(8,128)(2,1)}), bf16[8,32,256]{2,1,0:T(8,128)(2,1)S(1)}, u32[]{:S(2)}, u32[]{:S(2)}) async-start(bf16[8,32,256]{2,1,0:T(8,128)(2,1)} %add_convert_fusion), calls=%async_computation.1 | async-start | bytes 262144 | tf_op jit(solution)/shard_map/all_to_all | solution.py:207

commit v7 on v5

v7 whole, which is shorter than its diff:
```python
import functools

import jax
import jax.numpy as jnp
from jax import lax
from jax.experimental import pallas as pl
from jax.experimental.pallas import tpu as pltpu
from jax.sharding import Mesh, PartitionSpec as P

X = ("x",)
Y = ("h", "l")
F32 = jnp.float32
BF16 = jnp.bfloat16
LOG2E = 1.4426950408889634
WHOLE = pl.BlockSpec(memory_space=pltpu.VMEM)
PARAMS = pltpu.CompilerParams(vmem_limit_bytes=12 * 2**20)


def call(body, out_shape, *operands):
    return pl.pallas_call(
        body,
        out_shape=out_shape,
        in_specs=[WHOLE] * len(operands),
        out_specs=jax.tree.map(lambda _: WHOLE, out_shape),
        compiler_params=PARAMS,
    )(*operands)


def shaped(shape, kind):
    return jax.ShapeDtypeStruct(shape, kind)


def pack_body(quads, landmarks, whitening, out, land, white, sems):
    fetches = [pltpu.make_async_copy(landmarks, land, sems.at[0]), pltpu.make_async_copy(whitening, white, sems.at[1])]
    for fetch in fetches:
        fetch.start()
    for fetch in fetches:
        fetch.wait()
    rows = land.shape[0]
    part = rows // quads
    white32 = white[...].astype(F32)
    beside = jnp.concatenate([white32[q * part : (q + 1) * part] for q in range(quads)], axis=1).astype(BF16)
    for i in range(out.shape[0]):
        out[i, :rows] = land[...]
        out[i, rows:] = beside


def pack(landmarks, whitening, copies):
    rows, width = landmarks.shape
    quads = width // whitening.shape[1]
    return pl.pallas_call(
        functools.partial(pack_body, quads),
        out_shape=shaped((copies, rows + rows // quads, width), BF16),
        in_specs=[pl.BlockSpec(memory_space=pltpu.HBM)] * 2,
        scratch_shapes=[
            pltpu.VMEM(landmarks.shape, BF16),
            pltpu.VMEM(whitening.shape, BF16),
            pltpu.SemaphoreType.DMA((2,)),
        ],
        compiler_params=PARAMS,
    )(*[pltpu.with_memory_space_constraint(array, pltpu.HBM) for array in (landmarks, whitening)])


def unpack(block, rank):
    count, packed, width = block.shape
    quads = width // rank
    rows = packed * quads // (quads + 1)
    land = block[:, :rows].reshape(count * rows, width)
    white = block[:, rows:].astype(F32)
    white = jnp.stack([white[:, :, q * rank : (q + 1) * rank] for q in range(quads)], axis=1)
    return land, white.reshape(count * rows, rank).astype(BF16)


def pieces_of(stacks, count):
    return [stack[i : i + count] for stack in stacks for i in range(0, stack.shape[0], count)]


def prepare_body(parts, places, features, cot_t, feat, feat_t, sq_feat, cot):
    own = features.shape[0] // parts
    for i, place in enumerate(places()):
        start = pl.multiple_of(place * own, own)
        to = slice(i * own, (i + 1) * own)
        some = features[pl.ds(start, own), :]
        turned = some.T
        turned32 = turned.astype(F32)
        feat[to, :] = some
        feat_t[:, to] = turned
        sq_feat[:, to] = jnp.sum(turned32 * turned32, axis=0, keepdims=True)
        cot[:, to] = cot_t[:, pl.ds(start, own)].astype(F32)


def prepare(features, cot_t, parts, places, count):
    toks, width = features.shape
    toks = toks // parts * count
    rank = cot_t.shape[0]
    shapes = [shaped((toks, width), BF16), shaped((width, toks), BF16), shaped((1, toks), F32), shaped((rank, toks), F32)]
    return call(functools.partial(prepare_body, parts, places), shapes, features, cot_t)


def forward_body(count, members, rank, first, *refs):
    blocks, (feat_t, sq_feat), (kern, *embeds) = refs[:count], refs[count : count + 2], refs[count + 2 + (not first) :]
    width = feat_t.shape[0]
    scale = 4.0 / width * LOG2E
    bias = sq_feat[...] * (-scale)
    total = None if first else refs[count + 2][...]
    for i, block in enumerate(pieces_of(blocks, members)):
        land, white = unpack(block, rank)
        rows = land.shape[0]
        land32 = land.astype(F32)
        sq_land = jnp.sum(land32 * land32, axis=1, keepdims=True) * (-scale)
        cross = jnp.dot(land, feat_t[...], preferred_element_type=F32)
        value = jnp.exp2(cross * (2.0 * scale) + (bias + sq_land)).astype(BF16)
        kern[i * rows : (i + 1) * rows, :] = value
        part = lax.dot_general(white, value, (((0,), (0,)), ((), ())), preferred_element_type=F32)
        total = part if total is None else total + part
    for embed in embeds:
        embed[...] = total.astype(embed.dtype)


def forward(blocks, members, feat_t, sq_feat, prior, rows, rank):
    toks = feat_t.shape[1]
    shapes = [shaped((rows, toks), BF16), shaped((rank, toks), F32)] + [shaped((rank, toks), BF16)] * len(prior)
    return call(functools.partial(forward_body, len(blocks), members, rank, not prior), shapes, *blocks, feat_t, sq_feat, *prior)


def moved(ref, place, places, bit):
    own = ref.shape[1] // places
    start = (place ^ bit) * own
    return ref[:, start : start + own].astype(F32)


def pair_sum_body(places, share, other, total, rounded):
    own = share.shape[1] // places
    for p in range(places):
        at = slice(p * own, (p + 1) * own)
        total[:, at] = share[:, at] + moved(other, p, places, 1)
    rounded[...] = total[...].astype(BF16)


def pair_sum(share, other, places):
    shapes = [shaped(share.shape, F32), shaped(share.shape, BF16)]
    return call(functools.partial(pair_sum_body, places), shapes, share, other)


def norm_body(factor, places, share, other, cot, out):
    own = cot.shape[1] // places
    for p in range(places):
        at = slice(p * own, (p + 1) * own)
        embed = share[:, at] + moved(other, p, places, 2)
        upstream = cot[:, at]
        scale = lax.rsqrt(jnp.mean(embed * embed, axis=0, keepdims=True) + 1e-06)
        normed = embed * scale
        grad = scale * (upstream - normed * jnp.mean(upstream * normed, axis=0, keepdims=True))
        out[:, at] = (factor * grad).astype(BF16)


def norm_backward(share, other, cot, factor, places):
    return call(functools.partial(norm_body, factor, places), shaped(cot.shape, BF16), share, other, cot)


def backward_body(count, members, rank, first, *refs):
    blocks, (kern, dembed, feat) = refs[:count], refs[count : count + 3]
    coef, land_grad, row_total = refs[-3:]
    total = None if first else refs[count + 3][...]
    for i, block in enumerate(pieces_of(blocks, members)):
        land, white = unpack(block, rank)
        rows = land.shape[0]
        at = slice(i * rows, (i + 1) * rows)
        dkernel = jnp.dot(white, dembed[...], preferred_element_type=F32)
        value = (dkernel * kern[at, :].astype(F32)).astype(BF16)
        coef[at, :] = value
        value32 = value.astype(F32)
        part = jnp.sum(value32, axis=0, keepdims=True)
        total = part if total is None else total + part
        col_total = jnp.sum(value32, axis=1, keepdims=True)
        pulled = jnp.dot(value, feat[...], preferred_element_type=F32)
        land_grad[at, :] = (2.0 * (col_total * land.astype(F32) - pulled)).astype(land_grad.dtype)
    row_total[...] = total


def backward(blocks, members, kern, dembed, feat, prior, kind):
    toks, width = feat.shape
    rows = kern.shape[0]
    shapes = [shaped((rows, toks), BF16), shaped((rows, width), kind), shaped((1, toks), F32)]
    body = functools.partial(backward_body, len(blocks), members, dembed.shape[0], not prior)
    return call(body, shapes, *blocks, kern, dembed, feat, *prior)


def feature_body(count, members, coefs, rank, *refs):
    blocks, coef, (feat_t, row_total), outs = refs[:count], refs[count : count + coefs], refs[count + coefs : count + coefs + 2], refs[count + coefs + 2 :]
    pieces = pieces_of(blocks, members)
    each = len(pieces) // coefs
    pulled = None
    for i, block in enumerate(pieces):
        land, _ = unpack(block, rank)
        rows = land.shape[0]
        at = slice(i % each * rows, (i % each + 1) * rows)
        part = lax.dot_general(land, coef[i // each][at, :], (((0,), (0,)), ((), ())), preferred_element_type=F32)
        pulled = part if pulled is None else pulled + part
    grad = 2.0 * (row_total[...] * feat_t[...].astype(F32) - pulled)
    start = 0
    for out in outs:
        out[...] = grad[:, start : start + out.shape[1]].astype(out.dtype)
        start += out.shape[1]


def feature_share(blocks, members, coefs, feat_t, row_total, rank):
    width, toks = feat_t.shape
    shapes = [shaped((width, toks // 2), kind) for kind in (F32, BF16)]
    body = functools.partial(feature_body, len(blocks), members, len(coefs), rank)
    return call(body, shapes, *blocks, *coefs, feat_t, row_total)


def shift(block, axes, step):
    size = lax.axis_size(axes)
    return lax.ppermute(block, axes, [(i, (i + step) % size) for i in range(size)])


def partner(block, ring, which):
    masks = (1, 3)
    perm = [(2 * i + c, 2 * (i ^ masks[which ^ c]) + c) for i in range(lax.axis_size(ring)) for c in range(2)]
    return lax.ppermute(block, ring + ("c",), perm)


def spread(block, axes):
    return [block] + [shift(block, axes, s) for s in range(1, lax.axis_size(axes))]


def collect(pieces, axes, direction):
    total = pieces[0]
    for s in range(1, lax.axis_size(axes)):
        total = total + shift(pieces[s].astype(BF16), axes, direction * s).astype(F32)
    return total


def collect_at_once(pieces, axes):
    return jnp.sum(lax.all_to_all(pieces.astype(BF16), axes, 0, 0, tiled=True).astype(F32), axis=0)


def per_device(features, landmarks, whitening, cotangent):
    toks, width = features.shape
    rank = whitening.shape[1]
    n_x, n_h, n_y, n_z = lax.axis_size("x"), lax.axis_size("h"), lax.axis_size(Y), lax.axis_size("z")
    rows = landmarks.shape[0]
    gamma = 4.0 / width

    def places():
        here, half, core = lax.axis_index("x"), lax.axis_index("h"), lax.axis_index("c")
        members = [here, here ^ (1 + 2 * core), here ^ (3 - 2 * core), here ^ 2]
        return [member * n_h + half for member in members]

    packed = lax.all_to_all(pack(landmarks, whitening, n_z), "z", 0, 0, tiled=True)
    feat, feat_t, sq_feat, cot = prepare(features, cotangent.T, n_x * n_h, places, n_x)
    packed, feat, feat_t, sq_feat, cot = lax.optimization_barrier((packed, feat, feat_t, sq_feat, cot))
    mine = spread(packed, Y)
    theirs = [shift(jnp.concatenate(mine, axis=0), "c", 1)]

    half_rows = n_y * n_z * rows
    kern_mine, embed = forward(mine, n_z, feat_t, sq_feat, [], half_rows, rank)
    kern_theirs, embed, share = forward(theirs, n_z, feat_t, sq_feat, [embed], half_rows, rank)
    embed, share = pair_sum(embed, partner(share, X, 0), n_x)
    dembed = norm_backward(embed, partner(share, X, 1), cot, -gamma, n_x)

    coef_theirs, land_theirs, row_total = backward(theirs, n_z, kern_theirs, dembed, feat, [], BF16)
    coef_mine, land_mine, row_total = backward(mine, n_z, kern_mine, dembed, feat, [row_total], F32)
    land_share = (land_mine + shift(land_theirs, "c", 1).astype(F32)).reshape(n_y, n_z, rows, width)
    land_share = collect(land_share, Y, -1)

    near, far = feature_share(mine + theirs, n_z, [coef_mine, coef_theirs], feat_t, row_total, rank)
    land_share, far = lax.optimization_barrier((land_share.astype(BF16), partner(far, X, 1)))
    landmark_grad = collect_at_once(land_share, "z")
    near = near + far.astype(F32)
    own = near.shape[1] // 2
    feature_grad = (near[:, :own] + partner(near[:, own:].astype(BF16), X, 0).astype(F32)).T
    return (feature_grad, landmark_grad)


def solution(mesh):
    fine = Mesh(mesh.devices.reshape(4, 2, 2, 8, 2), ("x", "h", "l", "z", "c"))
    lm, tx = ("x", "h"), ("l", "z", "c")
    placed = (P(tx, None), P(lm + tx, None), P(lm + tx, None), P(tx, None))
    return jax.shard_map(
        per_device,
        mesh=fine,
        in_specs=placed,
        out_specs=(P(tx + lm, None), P(lm + tx, None)),
        check_vma=False,
    )
```

time: 77 us -> 78.8 us (1.023)
  the two profiles are of different devices: /device:TPU:24 before, /device:TPU:20 now
where the time goes in v7:
time: 78.8 us; the launch traced here: 78.4 us
  waiting for transfers between devices  35.3 us (45%)
  starting transfers between devices  27.8 us (35%)
  Pallas kernels  9.75 us (12%)
  local copies, waits for them, and re-layouts  3.07 us (4%)
  other arithmetic  1.67 us (2%)
    ppermute x4, waiting for transfers between devices, partner(): return lax.ppermute(block, ring + ('c',), perm)  11.8 us
    ppermute x8, starting transfers between devices, shift(): lax.ppermute(block, axes, [(i, (i + step) % size) for i in range(size)])  9.76 us
    all_to_all x1, starting transfers between devices, per_device(): lax.all_to_all(pack(landmarks, whitening, n_z), 'z', 0, 0, tiled=True)  8.48 us
    pallas_call x8, Pallas kernels, call(): pl.pallas_call(body, out_shape=out_shape, in_specs=[WHOLE] * len(operands...  8.27 us
    all_to_all x1, waiting for transfers between devices, collect_at_once(): lax.all_to_all(pieces.astype(BF16), axes, 0, 0, tiled=True).astype(F32)  8.1 us
    ppermute x8, waiting for transfers between devices, shift(): lax.ppermute(block, axes, [(i, (i + step) % size) for i in range(size)])  8.04 us
    all_to_all x1, waiting for transfers between devices, per_device(): lax.all_to_all(pack(landmarks, whitening, n_z), 'z', 0, 0, tiled=True)  7.35 us
    ppermute x4, starting transfers between devices, partner(): return lax.ppermute(block, ring + ('c',), perm)  6.23 us
  transfers between devices with their start and end apart: 14, of which 12 were waited for; matrix products, arithmetic and copies ran while one was open for 2% of the time, Pallas kernels for 6%

profile of v7, /device:TPU:20, one launch (start us, length us, event | category | flops | bytes accessed | tf_op | source)
XLA Modules:
  0.0 78.4 jit_solution(6671499105215298880)
XLA Ops:
  0.6 1.5 %shard_map.59 = bf16[8,40,256]{2,1,0:T(8,128)(2,1)} custom-call(bf16[32,256]{1,0:T(8,128)(2,1)} %landmarks.1, bf16[32,64]{1,0:T(8,128)(2,1)} %whitening.1), custom_call_target="tpu_custom_call" | custom-call | tf_op jit(solution)/shard_map/pallas_call | solution.py:51
  2.1 8.5 %all-to-all-start = ((bf16[8,40,256]{2,1,0:T(8,128)(2,1)}), bf16[8,40,256]{2,1,0:T(8,128)(2,1)S(1)}, u32[]{:S(2)}, u32[]{:S(2)}) async-start(bf16[8,40,256]{2,1,0:T(8,128)(2,1)} %shard_map.59), calls=%async_computation | async-start | bytes 327680 | tf_op jit(solution)/shard_map/all_to_all | solution.py:252
  10.6 0.0 copy-start
  10.6 1.2 %copy-done = bf16[2048,256]{1,0:T(8,128)(2,1)S(1)} copy-done((bf16[2048,256]{1,0:T(8,128)(2,1)S(1)}, bf16[2048,256]{1,0:T(8,128)(2,1)}, u32[]{:S(2)}) %copy-start) | copy-done | bytes 1048600
  11.8 0.0 copy-start.1
  11.8 0.9 %copy-done.1 = bf16[2048,64]{0,1:T(8,128)(2,1)S(1)} copy-done((bf16[2048,64]{0,1:T(8,128)(2,1)S(1)}, bf16[2048,64]{0,1:T(8,128)(2,1)}, u32[]{:S(2)}) %copy-start.1) | copy-done | bytes 262168
  12.8 0.2 shard_map.60
  13.0 7.3 %all-to-all-done.refs_0_ = bf16[8,40,256]{2,1,0:T(8,128)(2,1)S(1)} async-done(((bf16[8,40,256]{2,1,0:T(8,128)(2,1)}), bf16[8,40,256]{2,1,0:T(8,128)(2,1)S(1)}, u32[]{:S(2)}, u32[]{:S(2)}) %all-to-all-start) | async-done | bytes 163872 | tf_op jit(solution)/shard_map/all_to_all | solution.py:252
  20.4 0.4 collective-permute-start.2
  20.8 2.9 %collective-permute-start.1 = (bf16[8,40,256]{2,1,0:T(8,128)(2,1)S(1)}, bf16[8,40,256]{2,1,0:T(8,128)(2,1)S(1)}, u32[]{:S(2)}, u32[]{:S(2)}) collective-permute-start(bf16[8,40,256]{2,1,0:T(8,128)(2,1)S(1)} %all-to-all-done.refs_0_), channel_id=1, source_target_pairs={{0,32},{16,48},{32,0},{48,16},{1,33},{17,49},{33,1},{49,17},{2,34}... | collective-permute-start | bytes 491528 | tf_op jit(solution)/shard_map/ppermute | solution.py:216
  23.7 0.0 collective-permute-start
  23.7 2.4 %collective-permute-done.2.refs_3_ = bf16[8,40,256]{2,1,0:T(8,128)(2,1)S(1)} collective-permute-done((bf16[8,40,256]{2,1,0:T(8,128)(2,1)S(1)}, bf16[8,40,256]{2,1,0:T(8,128)(2,1)S(1)}, u32[]{:S(2)}, u32[]{:S(2)}) %collective-permute-start.2) | collective-permute-done | bytes 163872 | tf_op jit(solution)/shard_map/ppermute | solution.py:216
  26.2 1.7 %collective-permute-done.1.refs_2_ = bf16[8,40,256]{2,1,0:T(8,128)(2,1)S(1)} collective-permute-done((bf16[8,40,256]{2,1,0:T(8,128)(2,1)S(1)}, bf16[8,40,256]{2,1,0:T(8,128)(2,1)S(1)}, u32[]{:S(2)}, u32[]{:S(2)}) %collective-permute-start.1) | collective-permute-done | bytes 163872 | tf_op jit(solution)/shard_map/ppermute | solution.py:216
  27.9 1.7 %collective-permute-done.refs_1_ = bf16[8,40,256]{2,1,0:T(8,128)(2,1)S(1)} collective-permute-done((bf16[8,40,256]{2,1,0:T(8,128)(2,1)S(1)}, bf16[8,40,256]{2,1,0:T(8,128)(2,1)S(1)}, u32[]{:S(2)}, u32[]{:S(2)}) %collective-permute-start) | collective-permute-done | bytes 163872 | tf_op jit(solution)/shard_map/ppermute | solution.py:216
  29.6 0.1 pad_maximum_fusion
  29.7 0.1 collective-permute-start.3
  29.8 1.7 %shard_map.61 = (bf16[1024,1024]{1,0:T(8,128)(2,1)S(1)}, f32[64,1024]{1,0:T(8,128)S(1)}) custom-call(bf16[8,40,256]{2,1,0:T(8,128)(2,1)S(1)} %all-to-all-done.refs_0_, bf16[8,40,256]{2,1,0:T(8,128)(2,1)S(1)} %collective-permute-done.refs_1_, bf16[8,40,256]{2,1,0:T(8,128)(2,1)S(1)} %collective-permute-done.1.refs_2_, ...), custom_call_target="tpu_custom_call" | custom-call | tf_op jit(solution)/shard_map/pallas_call | solution.py:20
  31.5 0.4 collective-permute-done.3.refs_0_.refs_4_
  31.9 1.8 %shard_map.62 = (bf16[1024,1024]{1,0:T(8,128)(2,1)S(1)}, f32[64,1024]{1,0:T(8,128)S(1)}, bf16[64,1024]{1,0:T(8,128)(2,1)S(1)}) custom-call(bf16[32,40,256]{2,1,0:T(8,128)(2,1)S(1)} %collective-permute-done.3.refs_0_.refs_4_, bf16[256,1024]{1,0:T(8,128)(2,1)S(1)} %get-tuple-element.33.refs_4_.refs_1_.refs_7_, ...), custom_call_target="tpu_custom_call" | custom-call | tf_op jit(solution)/shard_map/pallas_call | solution.py:20
  33.6 1.3 %collective-permute-start.4 = (bf16[64,1024]{1,0:T(8,128)(2,1)S(1)}, bf16[64,1024]{1,0:T(8,128)(2,1)S(1)}, u32[]{:S(2)}, u32[]{:S(2)}) collective-permute-start(bf16[64,1024]{1,0:T(8,128)(2,1)S(1)} %get-tuple-element.38), channel_id=1, source_target_pairs={{0,64},{1,193},{64,0},{65,129},{128,192},{129,65},{192,128},{193,1... | collective-permute-start | bytes 393224 | tf_op jit(solution)/shard_map/ppermute | solution.py:222
  34.9 3.8 %collective-permute-done.4.other = bf16[64,1024]{1,0:T(8,128)(2,1)S(1)} collective-permute-done((bf16[64,1024]{1,0:T(8,128)(2,1)S(1)}, bf16[64,1024]{1,0:T(8,128)(2,1)S(1)}, u32[]{:S(2)}, u32[]{:S(2)}) %collective-permute-start.4) | collective-permute-done | bytes 131104 | tf_op jit(solution)/shard_map/ppermute | solution.py:222
  38.7 0.6 collective-permute-start.5
  39.3 4.4 %collective-permute-done.5.other = bf16[64,1024]{1,0:T(8,128)(2,1)S(1)} collective-permute-done((bf16[64,1024]{1,0:T(8,128)(2,1)S(1)}, bf16[64,1024]{1,0:T(8,128)(2,1)S(1)}, u32[]{:S(2)}, u32[]{:S(2)}) %collective-permute-start.5) | collective-permute-done | bytes 131104 | tf_op jit(solution)/shard_map/ppermute | solution.py:222
  43.8 0.2 shard_map.64.refs_2_.refs_5_
  43.9 1.5 %shard_map.65 = (bf16[1024,1024]{1,0:T(8,128)(2,1)S(1)}, bf16[1024,256]{1,0:T(8,128)(2,1)S(1)}, f32[1,1024]{1,0:T(1,128)S(1)}) custom-call(bf16[32,40,256]{2,1,0:T(8,128)(2,1)S(1)} %collective-permute-done.3.refs_0_.refs_4_, bf16[1024,1024]{1,0:T(8,128)(2,1)S(1)} %get-tuple-element.43.refs_1_, bf16[64,1024]{1,0:T(8,128)(2,1)S(1)} %shard_map.64.refs_2_.refs_5_, ...), custom_call_target="tpu_custom_call" | custom-call | tf_op jit(solution)/shard_map/pallas_call | solution.py:20
  45.5 0.1 collective-permute-start.6
  45.6 1.5 %shard_map.66 = (bf16[1024,1024]{1,0:T(8,128)(2,1)S(1)}, f32[1024,256]{1,0:T(8,128)S(1)}, f32[1,1024]{1,0:T(1,128)S(1)}) custom-call(bf16[8,40,256]{2,1,0:T(8,128)(2,1)S(1)} %all-to-all-done.refs_0_, bf16[8,40,256]{2,1,0:T(8,128)(2,1)S(1)} %collective-permute-done.refs_1_, bf16[8,40,256]{2,1,0:T(8,128)(2,1)S(1)} %collective-permute-done.1.refs_2_, ...), custom_call_target="tpu_custom_call" | custom-call | tf_op jit(solution)/shard_map/pallas_call | solution.py:20
  47.1 0.3 collective-permute-done.6
  47.5 0.1 fusion.1
  47.6 1.5 %collective-permute-start.9 = (bf16[8,32,256]{2,1,0:T(8,128)(2,1)S(1)}, bf16[8,32,256]{2,1,0:T(8,128)(2,1)S(1)}, u32[]{:S(2)}, u32[]{:S(2)}) collective-permute-start(bf16[8,32,256]{2,1,0:T(8,128)(2,1)S(1)} %bitcast.11), channel_id=1, source_target_pairs={{0,16},{16,32},{32,48},{48,0},{1,17},{17,33},{33,49},{49,1},{2,18}... | collective-permute-start | bytes 393224 | tf_op jit(solution)/shard_map/ppermute | solution.py:216
  49.2 0.6 collective-permute-start.7
  49.7 4.1 %collective-permute-start.8 = (bf16[8,32,256]{2,1,0:T(8,128)(2,1)S(1)}, bf16[8,32,256]{2,1,0:T(8,128)(2,1)S(1)}, u32[]{:S(2)}, u32[]{:S(2)}) collective-permute-start(bf16[8,32,256]{2,1,0:T(8,128)(2,1)S(1)} %bitcast.9), channel_id=1, source_target_pairs={{0,32},{16,48},{32,0},{48,16},{1,33},{17,49},{33,1},{49,17},{2,34}... | collective-permute-start | bytes 393224 | tf_op jit(solution)/shard_map/ppermute | solution.py:216
  53.9 1.3 %shard_map.67 = (f32[256,512]{1,0:T(8,128)S(1)}, bf16[256,512]{1,0:T(8,128)(2,1)S(1)}) custom-call(bf16[8,40,256]{2,1,0:T(8,128)(2,1)S(1)} %all-to-all-done.refs_0_, bf16[8,40,256]{2,1,0:T(8,128)(2,1)S(1)} %collective-permute-done.refs_1_, bf16[8,40,256]{2,1,0:T(8,128)(2,1)S(1)} %collective-permute-done.1.refs_2_, ...), custom_call_target="tpu_custom_call" | custom-call | tf_op jit(solution)/shard_map/pallas_call | solution.py:20
  55.1 0.6 collective-permute-start.10
  55.8 0.0 collective-permute-done.9
  55.8 0.3 collective-permute-done.7
  56.1 1.1 %collective-permute-done.8 = bf16[8,32,256]{2,1,0:T(8,128)(2,1)S(1)} collective-permute-done((bf16[8,32,256]{2,1,0:T(8,128)(2,1)S(1)}, bf16[8,32,256]{2,1,0:T(8,128)(2,1)S(1)}, u32[]{:S(2)}, u32[]{:S(2)}) %collective-permute-start.8) | collective-permute-done | bytes 131104 | tf_op jit(solution)/shard_map/ppermute | solution.py:216
  57.3 0.7 add_convert_fusion
  58.0 3.6 %collective-permute-done.10 = bf16[256,512]{1,0:T(8,128)(2,1)S(1)} collective-permute-done((bf16[256,512]{1,0:T(8,128)(2,1)S(1)}, bf16[256,512]{1,0:T(8,128)(2,1)S(1)}, u32[]{:S(2)}, u32[]{:S(2)}) %collective-permute-start.10) | collective-permute-done | bytes 262176 | tf_op jit(solution)/shard_map/ppermute | solution.py:222
  61.6 0.1 convert_add_fusion.1
  61.7 3.7 %collective-permute-start.11 = (bf16[256,256]{1,0:T(8,128)(2,1)S(1)}, bf16[256,256]{1,0:T(8,128)(2,1)S(1)}, u32[]{:S(2)}, u32[]{:S(2)}) collective-permute-start(bf16[256,256]{1,0:T(8,128)(2,1)S(1)} %slice.42), channel_id=1, source_target_pairs={{0,64},{1,193},{64,0},{65,129},{128,192},{129,65},{192,128},{193,1... | collective-permute-start | bytes 393224 | tf_op jit(solution)/shard_map/ppermute | solution.py:222
  65.4 3.4 %all-to-all-start.1 = ((bf16[8,32,256]{2,1,0:T(8,128)(2,1)}), bf16[8,32,256]{2,1,0:T(8,128)(2,1)S(1)}, u32[]{:S(2)}, u32[]{:S(2)}) async-start(bf16[8,32,256]{2,1,0:T(8,128)(2,1)} %add_convert_fusion), calls=%async_computation.1 | async-start | bytes 262144 | tf_op jit(solution)/shard_map/all_to_all | solution.py:237
  68.8 0.0 collective-permute-done.11
  68.8 0.8 %copy.6 = f32[256,256]{1,0:T(8,128)} copy(f32[256,256]{0,1:T(8,128)S(1)} %fusion) | data formatting | bytes 524288
  69.7 8.1 %all-to-all-done.1 = bf16[8,32,256]{2,1,0:T(8,128)(2,1)S(1)} async-done(((bf16[8,32,256]{2,1,0:T(8,128)(2,1)}), bf16[8,32,256]{2,1,0:T(8,128)(2,1)S(1)}, u32[]{:S(2)}, u32[]{:S(2)}) %all-to-all-start.1) | async-done | bytes 131104 | tf_op jit(solution)/shard_map/all_to_all | solution.py:237
  77.8 0.6 convert_reduce_fusion
  (5 shorter events, 0.1 us)
Async XLA Ops:
  2.1 18.2 %all-to-all-start = ((bf16[8,40,256]{2,1,0:T(8,128)(2,1)}), bf16[8,40,256]{2,1,0:T(8,128)(2,1)S(1)}, u32[]{:S(2)}, u32[]{:S(2)}) async-start(bf16[8,40,256]{2,1,0:T(8,128)(2,1)} %shard_map.59), calls=%async_computation | async-start | bytes 327680 | tf_op jit(solution)/shard_map/all_to_all | solution.py:252
  10.6 1.2 %copy-start = (bf16[2048,256]{1,0:T(8,128)(2,1)S(1)}, bf16[2048,256]{1,0:T(8,128)(2,1)}, u32[]{:S(2)}) copy-start(bf16[2048,256]{1,0:T(8,128)(2,1)} %features.1) | copy-start | bytes 3145732
  11.8 0.9 %copy-start.1 = (bf16[2048,64]{0,1:T(8,128)(2,1)S(1)}, bf16[2048,64]{0,1:T(8,128)(2,1)}, u32[]{:S(2)}) copy-start(bf16[2048,64]{0,1:T(8,128)(2,1)} %param.7) | copy-start | bytes 786436
  20.4 5.8 %collective-permute-start.2 = (bf16[8,40,256]{2,1,0:T(8,128)(2,1)S(1)}, bf16[8,40,256]{2,1,0:T(8,128)(2,1)S(1)}, u32[]{:S(2)}, u32[]{:S(2)}) collective-permute-start(bf16[8,40,256]{2,1,0:T(8,128)(2,1)S(1)} %all-to-all-done.refs_0_), channel_id=1, source_target_pairs={{0,48},{16,0},{32,16},{48,32},{1,49},{17,1},{33,17},{49,33},{2,50}... | collective-permute-start | bytes 491528 | tf_op jit(solution)/shard_map/ppermute | solution.py:216
  20.8 7.1 %collective-permute-start.1 = (bf16[8,40,256]{2,1,0:T(8,128)(2,1)S(1)}, bf16[8,40,256]{2,1,0:T(8,128)(2,1)S(1)}, u32[]{:S(2)}, u32[]{:S(2)}) collective-permute-start(bf16[8,40,256]{2,1,0:T(8,128)(2,1)S(1)} %all-to-all-done.refs_0_), channel_id=1, source_target_pairs={{0,32},{16,48},{32,0},{48,16},{1,33},{17,49},{33,1},{49,17},{2,34}... | collective-permute-start | bytes 491528 | tf_op jit(solution)/shard_map/ppermute | solution.py:216
  23.7 5.9 %collective-permute-start = (bf16[8,40,256]{2,1,0:T(8,128)(2,1)S(1)}, bf16[8,40,256]{2,1,0:T(8,128)(2,1)S(1)}, u32[]{:S(2)}, u32[]{:S(2)}) collective-permute-start(bf16[8,40,256]{2,1,0:T(8,128)(2,1)S(1)} %all-to-all-done.refs_0_), channel_id=1, source_target_pairs={{0,16},{16,32},{32,48},{48,0},{1,17},{17,33},{33,49},{49,1},{2,18}... | collective-permute-start | bytes 491528 | tf_op jit(solution)/shard_map/ppermute | solution.py:216
  29.7 2.2 %collective-permute-start.3 = (bf16[32,40,256]{2,1,0:T(8,128)(2,1)S(1)}, bf16[32,40,256]{2,1,0:T(8,128)(2,1)S(1)}, u32[]{:S(2)}, u32[]{:S(2)}) collective-permute-start(bf16[32,40,256]{2,1,0:T(8,128)(2,1)S(1)} %pad_maximum_fusion), channel_id=1, source_target_pairs={{0,1},{1,0},{2,3},{3,2},{4,5},{5,4},{6,7},{7,6},{8,9},{9,8},{10,11... | collective-permute-start | bytes 1966088 | tf_op jit(solution)/shard_map/ppermute | solution.py:216
  33.6 5.1 %collective-permute-start.4 = (bf16[64,1024]{1,0:T(8,128)(2,1)S(1)}, bf16[64,1024]{1,0:T(8,128)(2,1)S(1)}, u32[]{:S(2)}, u32[]{:S(2)}) collective-permute-start(bf16[64,1024]{1,0:T(8,128)(2,1)S(1)} %get-tuple-element.38), channel_id=1, source_target_pairs={{0,64},{1,193},{64,0},{65,129},{128,192},{129,65},{192,128},{193,1... | collective-permute-start | bytes 393224 | tf_op jit(solution)/shard_map/ppermute | solution.py:222
  38.7 5.1 %collective-permute-start.5 = (bf16[64,1024]{1,0:T(8,128)(2,1)S(1)}, bf16[64,1024]{1,0:T(8,128)(2,1)S(1)}, u32[]{:S(2)}, u32[]{:S(2)}) collective-permute-start(bf16[64,1024]{1,0:T(8,128)(2,1)S(1)} %get-tuple-element.40), channel_id=1, source_target_pairs={{0,192},{1,65},{64,128},{65,1},{128,64},{129,193},{192,0},{193,129... | collective-permute-start | bytes 393224 | tf_op jit(solution)/shard_map/ppermute | solution.py:222
  45.5 2.0 %collective-permute-start.6 = (bf16[1024,256]{1,0:T(8,128)(2,1)S(1)}, bf16[1024,256]{1,0:T(8,128)(2,1)S(1)}, u32[]{:S(2)}, u32[]{:S(2)}) collective-permute-start(bf16[1024,256]{1,0:T(8,128)(2,1)S(1)} %get-tuple-element.50), channel_id=1, source_target_pairs={{0,1},{1,0},{2,3},{3,2},{4,5},{5,4},{6,7},{7,6},{8,9},{9,8},{10,11... | collective-permute-start | bytes 1572872 | tf_op jit(solution)/shard_map/ppermute | solution.py:216
  47.6 8.1 %collective-permute-start.9 = (bf16[8,32,256]{2,1,0:T(8,128)(2,1)S(1)}, bf16[8,32,256]{2,1,0:T(8,128)(2,1)S(1)}, u32[]{:S(2)}, u32[]{:S(2)}) collective-permute-start(bf16[8,32,256]{2,1,0:T(8,128)(2,1)S(1)} %bitcast.11), channel_id=1, source_target_pairs={{0,16},{16,32},{32,48},{48,0},{1,17},{17,33},{33,49},{49,1},{2,18}... | collective-permute-start | bytes 393224 | tf_op jit(solution)/shard_map/ppermute | solution.py:216
  49.2 6.9 %collective-permute-start.7 = (bf16[8,32,256]{2,1,0:T(8,128)(2,1)S(1)}, bf16[8,32,256]{2,1,0:T(8,128)(2,1)S(1)}, u32[]{:S(2)}, u32[]{:S(2)}) collective-permute-start(bf16[8,32,256]{2,1,0:T(8,128)(2,1)S(1)} %bitcast.10), channel_id=1, source_target_pairs={{0,48},{16,0},{32,16},{48,32},{1,49},{17,1},{33,17},{49,33},{2,50}... | collective-permute-start | bytes 393224 | tf_op jit(solution)/shard_map/ppermute | solution.py:216
  49.7 7.5 %collective-permute-start.8 = (bf16[8,32,256]{2,1,0:T(8,128)(2,1)S(1)}, bf16[8,32,256]{2,1,0:T(8,128)(2,1)S(1)}, u32[]{:S(2)}, u32[]{:S(2)}) collective-permute-start(bf16[8,32,256]{2,1,0:T(8,128)(2,1)S(1)} %bitcast.9), channel_id=1, source_target_pairs={{0,32},{16,48},{32,0},{48,16},{1,33},{17,49},{33,1},{49,17},{2,34}... | collective-permute-start | bytes 393224 | tf_op jit(solution)/shard_map/ppermute | solution.py:216
  55.1 6.5 %collective-permute-start.10 = (bf16[256,512]{1,0:T(8,128)(2,1)S(1)}, bf16[256,512]{1,0:T(8,128)(2,1)S(1)}, u32[]{:S(2)}, u32[]{:S(2)}) collective-permute-start(bf16[256,512]{1,0:T(8,128)(2,1)S(1)} %get-tuple-element.51), channel_id=1, source_target_pairs={{0,192},{1,65},{64,128},{65,1},{128,64},{129,193},{192,0},{193,129... | collective-permute-start | bytes 786440 | tf_op jit(solution)/shard_map/ppermute | solution.py:222
  61.7 7.1 %collective-permute-start.11 = (bf16[256,256]{1,0:T(8,128)(2,1)S(1)}, bf16[256,256]{1,0:T(8,128)(2,1)S(1)}, u32[]{:S(2)}, u32[]{:S(2)}) collective-permute-start(bf16[256,256]{1,0:T(8,128)(2,1)S(1)} %slice.42), channel_id=1, source_target_pairs={{0,64},{1,193},{64,0},{65,129},{128,192},{129,65},{192,128},{193,1... | collective-permute-start | bytes 393224 | tf_op jit(solution)/shard_map/ppermute | solution.py:222
  65.4 12.4 %all-to-all-start.1 = ((bf16[8,32,256]{2,1,0:T(8,128)(2,1)}), bf16[8,32,256]{2,1,0:T(8,128)(2,1)S(1)}, u32[]{:S(2)}, u32[]{:S(2)}) async-start(bf16[8,32,256]{2,1,0:T(8,128)(2,1)} %add_convert_fusion), calls=%async_computation.1 | async-start | bytes 262144 | tf_op jit(solution)/shard_map/all_to_all | solution.py:237

commit v8 on v7

--- a/solution.py
+++ b/solution.py
@@ -119,43 +119,24 @@
 
 def forward(blocks, members, feat_t, sq_feat, prior, rows, rank):
     toks = feat_t.shape[1]
-    shapes = [shaped((rows, toks), BF16), shaped((rank, toks), F32)] + [shaped((rank, toks), BF16)] * len(prior)
+    shapes = [shaped((rows, toks), BF16), shaped((rank, toks), BF16 if prior else F32)]
     return call(functools.partial(forward_body, len(blocks), members, rank, not prior), shapes, *blocks, feat_t, sq_feat, *prior)
 
 
-def moved(ref, place, places, bit):
-    own = ref.shape[1] // places
-    start = (place ^ bit) * own
-    return ref[:, start : start + own].astype(F32)
-
-
-def pair_sum_body(places, share, other, total, rounded):
-    own = share.shape[1] // places
-    for p in range(places):
-        at = slice(p * own, (p + 1) * own)
-        total[:, at] = share[:, at] + moved(other, p, places, 1)
-    rounded[...] = total[...].astype(BF16)
-
-
-def pair_sum(share, other, places):
-    shapes = [shaped(share.shape, F32), shaped(share.shape, BF16)]
-    return call(functools.partial(pair_sum_body, places), shapes, share, other)
-
-
-def norm_body(factor, places, share, other, cot, out):
-    own = cot.shape[1] // places
-    for p in range(places):
-        at = slice(p * own, (p + 1) * own)
-        embed = share[:, at] + moved(other, p, places, 2)
-        upstream = cot[:, at]
-        scale = lax.rsqrt(jnp.mean(embed * embed, axis=0, keepdims=True) + 1e-06)
-        normed = embed * scale
-        grad = scale * (upstream - normed * jnp.mean(upstream * normed, axis=0, keepdims=True))
-        out[:, at] = (factor * grad).astype(BF16)
-
-
-def norm_backward(share, other, cot, factor, places):
-    return call(functools.partial(norm_body, factor, places), shaped(cot.shape, BF16), share, other, cot)
+def norm_body(factor, shares, cot, out):
+    places = shares.shape[0]
+    embed = shares[0].astype(F32)
+    for s in range(1, places):
+        embed = embed + shares[s].astype(F32)
+    upstream = cot[...]
+    scale = lax.rsqrt(jnp.mean(embed * embed, axis=0, keepdims=True) + 1e-06)
+    normed = embed * scale
+    grad = scale * (upstream - normed * jnp.mean(upstream * normed, axis=0, keepdims=True))
+    out[...] = (factor * grad).astype(BF16)
+
+
+def norm_backward(shares, cot, factor):
+    return call(functools.partial(norm_body, factor), shaped(cot.shape, BF16), shares, cot)
 
 
 def backward_body(count, members, rank, first, *refs):
@@ -187,7 +168,7 @@
 
 
 def feature_body(count, members, coefs, rank, *refs):
-    blocks, coef, (feat_t, row_total), outs = refs[:count], refs[count : count + coefs], refs[count + coefs : count + coefs + 2], refs[count + coefs + 2 :]
+    blocks, coef, (feat_t, row_total), outs = refs[:count], refs[count : count + coefs], refs[count + coefs : count + coefs + 2], refs[-1]
     pieces = pieces_of(blocks, members)
     each = len(pieces) // coefs
     pulled = None
@@ -198,15 +179,14 @@
         part = lax.dot_general(land, coef[i // each][at, :], (((0,), (0,)), ((), ())), preferred_element_type=F32)
         pulled = part if pulled is None else pulled + part
     grad = 2.0 * (row_total[...] * feat_t[...].astype(F32) - pulled)
-    start = 0
-    for out in outs:
-        out[...] = grad[:, start : start + out.shape[1]].astype(out.dtype)
-        start += out.shape[1]
-
-
-def feature_share(blocks, members, coefs, feat_t, row_total, rank):
+    groups, _, own = outs.shape
+    for i in range(groups):
+        outs[i] = grad[:, i * own : (i + 1) * own].astype(BF16)
+
+
+def feature_share(blocks, members, coefs, feat_t, row_total, rank, groups):
     width, toks = feat_t.shape
-    shapes = [shaped((width, toks // 2), kind) for kind in (F32, BF16)]
+    shapes = shaped((groups, width, toks // groups), BF16)
     body = functools.partial(feature_body, len(blocks), members, len(coefs), rank)
     return call(body, shapes, *blocks, *coefs, feat_t, row_total)
 
@@ -214,23 +194,6 @@
 def shift(block, axes, step):
     size = lax.axis_size(axes)
     return lax.ppermute(block, axes, [(i, (i + step) % size) for i in range(size)])
-
-
-def partner(block, ring, which):
-    masks = (1, 3)
-    perm = [(2 * i + c, 2 * (i ^ masks[which ^ c]) + c) for i in range(lax.axis_size(ring)) for c in range(2)]
-    return lax.ppermute(block, ring + ("c",), perm)
-
-
-def spread(block, axes):
-    return [block] + [shift(block, axes, s) for s in range(1, lax.axis_size(axes))]
-
-
-def collect(pieces, axes, direction):
-    total = pieces[0]
-    for s in range(1, lax.axis_size(axes)):
-        total = total + shift(pieces[s].astype(BF16), axes, direction * s).astype(F32)
-    return total
 
 
 def collect_at_once(pieces, axes):
@@ -245,33 +208,27 @@
     gamma = 4.0 / width
 
     def places():
-        here, half, core = lax.axis_index("x"), lax.axis_index("h"), lax.axis_index("c")
-        members = [here, here ^ (1 + 2 * core), here ^ (3 - 2 * core), here ^ 2]
-        return [member * n_h + half for member in members]
-
-    packed = lax.all_to_all(pack(landmarks, whitening, n_z), "z", 0, 0, tiled=True)
+        return [s * n_h + lax.axis_index("h") for s in range(n_x)]
+
+    packed = lax.all_to_all(pack(landmarks, whitening, n_y * n_z), Y + ("z",), 0, 0, tiled=True)
     feat, feat_t, sq_feat, cot = prepare(features, cotangent.T, n_x * n_h, places, n_x)
     packed, feat, feat_t, sq_feat, cot = lax.optimization_barrier((packed, feat, feat_t, sq_feat, cot))
-    mine = spread(packed, Y)
-    theirs = [shift(jnp.concatenate(mine, axis=0), "c", 1)]
+    mine, theirs = [packed], [shift(packed, "c", 1)]
 
     half_rows = n_y * n_z * rows
     kern_mine, embed = forward(mine, n_z, feat_t, sq_feat, [], half_rows, rank)
-    kern_theirs, embed, share = forward(theirs, n_z, feat_t, sq_feat, [embed], half_rows, rank)
-    embed, share = pair_sum(embed, partner(share, X, 0), n_x)
-    dembed = norm_backward(embed, partner(share, X, 1), cot, -gamma, n_x)
+    kern_theirs, share = forward(theirs, n_z, feat_t, sq_feat, [embed], half_rows, rank)
+    shares = lax.all_to_all(jnp.broadcast_to(share[None], (n_x,) + share.shape), "x", 0, 0, tiled=True)
+    dembed = norm_backward(shares, cot, -gamma)
 
     coef_theirs, land_theirs, row_total = backward(theirs, n_z, kern_theirs, dembed, feat, [], BF16)
     coef_mine, land_mine, row_total = backward(mine, n_z, kern_mine, dembed, feat, [row_total], F32)
     land_share = (land_mine + shift(land_theirs, "c", 1).astype(F32)).reshape(n_y, n_z, rows, width)
-    land_share = collect(land_share, Y, -1)
-
-    near, far = feature_share(mine + theirs, n_z, [coef_mine, coef_theirs], feat_t, row_total, rank)
-    land_share, far = lax.optimization_barrier((land_share.astype(BF16), partner(far, X, 1)))
+    land_share = collect_at_once(land_share, Y)
+
+    feat_share = feature_share(mine + theirs, n_z, [coef_mine, coef_theirs], feat_t, row_total, rank, n_x)
     landmark_grad = collect_at_once(land_share, "z")
-    near = near + far.astype(F32)
-    own = near.shape[1] // 2
-    feature_grad = (near[:, :own] + partner(near[:, own:].astype(BF16), X, 0).astype(F32)).T
+    feature_grad = collect_at_once(feat_share, "x").T
     return (feature_grad, landmark_grad)
 
 

time: 78.8 us -> 98.9 us (1.26)
  the two profiles are of different devices: /device:TPU:20 before, /device:TPU:24 now
where the time goes in v8:
time: 98.9 us; the launch traced here: 97.5 us
  waiting for transfers between devices  37.6 us (38%)
  starting transfers between devices  24.6 us (25%)
  blocking collectives  13.9 us (14%)
  Pallas kernels  10.8 us (11%)
  local copies, waits for them, and re-layouts  7.43 us (8%)
  other arithmetic  2.41 us (2%)
    all_to_all x3, waiting for transfers between devices, collect_at_once(): lax.all_to_all(pieces.astype(BF16), axes, 0, 0, tiled=True).astype(F32)  20.1 us
    all_to_all x1, waiting for transfers between devices, per_device(): lax.all_to_all(pack(landmarks, whitening, n_y * n_z), Y + ('z',), 0, 0, t...  17.1 us
    all_to_all x1, blocking collectives, per_device(): lax.all_to_all(jnp.broadcast_to(share[None], (n_x,) + share.shape), 'x',...  13.9 us
    all_to_all x3, starting transfers between devices, collect_at_once(): lax.all_to_all(pieces.astype(BF16), axes, 0, 0, tiled=True).astype(F32)  13 us
    all_to_all x1, starting transfers between devices, per_device(): lax.all_to_all(pack(landmarks, whitening, n_y * n_z), Y + ('z',), 0, 0, t...  11.5 us
    pallas_call x7, Pallas kernels, call(): pl.pallas_call(body, out_shape=out_shape, in_specs=[WHOLE] * len(operands...  9.04 us
    unnamed x17, local copies, waits for them, and re-layouts  7.37 us
  transfers between devices with their start and end apart: 6, of which 5 were waited for; matrix products, arithmetic and copies ran while one was open for 2% of the time, Pallas kernels for 6%

profile of v8, /device:TPU:24, one launch (start us, length us, event | category | flops | bytes accessed | tf_op | source)
XLA Modules:
  0.0 97.5 jit_solution(576076599604059026)
XLA Ops:
  0.6 0.0 copy-start.5
  0.6 0.0 copy-start.4
  0.7 1.8 %shard_map.59 = bf16[32,40,256]{2,1,0:T(8,128)(2,1)} custom-call(bf16[32,256]{1,0:T(8,128)(2,1)} %landmarks.1, bf16[32,64]{1,0:T(8,128)(2,1)} %whitening.1), custom_call_target="tpu_custom_call" | custom-call | tf_op jit(solution)/shard_map/pallas_call | solution.py:51
  2.4 11.5 %all-to-all-start = ((bf16[32,40,256]{2,1,0:T(8,128)(2,1)}), bf16[32,40,256]{2,1,0:T(8,128)(2,1)S(1)}, u32[]{:S(2)}, u32[]{:S(2)}) async-start(bf16[32,40,256]{2,1,0:T(8,128)(2,1)} %shard_map.59), calls=%async_computation | async-start | bytes 1310720 | tf_op jit(solution)/shard_map/all_to_all | solution.py:213
  14.0 0.0 copy-done.5
  14.0 0.0 copy-done.4
  14.0 0.3 shard_map.60
  14.2 0.0 copy-start.6
  14.3 0.7 copy-done.6
  14.9 17.1 %all-to-all-done.refs_0_ = bf16[32,40,256]{2,1,0:T(8,128)(2,1)S(1)} async-done(((bf16[32,40,256]{2,1,0:T(8,128)(2,1)}), bf16[32,40,256]{2,1,0:T(8,128)(2,1)S(1)}, u32[]{:S(2)}, u32[]{:S(2)}) %all-to-all-start) | async-done | bytes 655392 | tf_op jit(solution)/shard_map/all_to_all | solution.py:213
  32.1 0.0 copy-start.7
  32.1 0.0 collective-permute-start
  32.1 1.7 %shard_map.61 = (bf16[1024,1024]{1,0:T(8,128)(2,1)S(1)}, f32[64,1024]{1,0:T(8,128)S(1)}) custom-call(bf16[32,40,256]{2,1,0:T(8,128)(2,1)S(1)} %all-to-all-done.refs_0_, bf16[256,1024]{1,0:T(8,128)(2,1)S(1)} %get-tuple-element.26.refs_1_.refs_4_, f32[1,1024]{1,0:T(1,128)S(1)} %get-tuple-element.27.refs_2_), custom_call_target="tpu_custom_call" | custom-call | tf_op jit(solution)/shard_map/pallas_call | solution.py:20
  33.8 0.4 collective-permute-done.refs_0_.refs_1_
  34.2 1.8 %shard_map.62 = (bf16[1024,1024]{1,0:T(8,128)(2,1)S(1)}, bf16[64,1024]{1,0:T(8,128)(2,1)S(1)}) custom-call(bf16[32,40,256]{2,1,0:T(8,128)(2,1)S(1)} %collective-permute-done.refs_0_.refs_1_, bf16[256,1024]{1,0:T(8,128)(2,1)S(1)} %get-tuple-element.26.refs_1_.refs_4_, f32[1,1024]{1,0:T(1,128)S(1)} %get-tuple-element.27.refs_2_, ...), custom_call_target="tpu_custom_call" | custom-call | tf_op jit(solution)/shard_map/pallas_call | solution.py:20
  35.9 0.1 broadcast_in_dim.2
  36.0 13.9 %all_to_all.25.shares = bf16[4,64,1024]{2,1,0:T(8,128)(2,1)S(1)} all-to-all(bf16[4,64,1024]{2,1,0:T(8,128)(2,1)S(1)} %broadcast_in_dim.2), channel_id=1, replica_groups=mesh['x'=4,'h'=2,'l'=2,'z'=8,'c'=2] {'x'}, dimensions={0} | all-to-all | bytes 1048576 | tf_op jit(solution)/shard_map/all_to_all | solution.py:221
  49.9 0.0 copy-done.7
  49.9 0.2 shard_map.63.refs_2_
  50.0 1.5 %shard_map.64 = (bf16[1024,1024]{1,0:T(8,128)(2,1)S(1)}, bf16[1024,256]{1,0:T(8,128)(2,1)S(1)}, f32[1,1024]{1,0:T(1,128)S(1)}) custom-call(bf16[32,40,256]{2,1,0:T(8,128)(2,1)S(1)} %collective-permute-done.refs_0_.refs_1_, bf16[1024,1024]{1,0:T(8,128)(2,1)S(1)} %get-tuple-element.33.refs_1_, bf16[64,1024]{1,0:T(8,128)(2,1)S(1)} %shard_map.63.refs_2_, ...), custom_call_target="tpu_custom_call" | custom-call | tf_op jit(solution)/shard_map/pallas_call | solution.py:20
  51.6 0.0 copy-start
  51.6 1.3 %copy-done = bf16[1024,1024]{1,0:T(8,128)(2,1)} copy-done((bf16[1024,1024]{1,0:T(8,128)(2,1)}, bf16[1024,1024]{1,0:T(8,128)(2,1)S(1)}, u32[]{:S(2)}) %copy-start) | copy-done | bytes 2097176
  52.9 0.0 collective-permute-start.1
  52.9 1.5 %shard_map.65 = (bf16[1024,1024]{1,0:T(8,128)(2,1)S(1)}, f32[1024,256]{1,0:T(8,128)S(1)}, f32[1,1024]{1,0:T(1,128)S(1)}) custom-call(bf16[32,40,256]{2,1,0:T(8,128)(2,1)S(1)} %all-to-all-done.refs_0_, bf16[1024,1024]{1,0:T(8,128)(2,1)S(1)} %get-tuple-element.28.refs_1_, bf16[64,1024]{1,0:T(8,128)(2,1)S(1)} %shard_map.63.refs_2_, ...), custom_call_target="tpu_custom_call" | custom-call | tf_op jit(solution)/shard_map/pallas_call | solution.py:20
  54.4 0.0 copy-start.2
  54.4 1.3 %copy-done.2 = bf16[1024,1024]{1,0:T(8,128)(2,1)} copy-done((bf16[1024,1024]{1,0:T(8,128)(2,1)}, bf16[1024,1024]{1,0:T(8,128)(2,1)S(1)}, u32[]{:S(2)}) %copy-start.2) | copy-done | bytes 2097176
  55.8 0.0 collective-permute-done.1
  55.8 1.0 add_convert_fusion
  56.7 6.0 %all-to-all-start.3 = ((bf16[4,8,32,256]{3,2,1,0:T(8,128)(2,1)}), bf16[4,8,32,256]{3,2,1,0:T(8,128)(2,1)S(1)}, u32[]{:S(2)}, u32[]{:S(2)}) async-start(bf16[4,8,32,256]{3,2,1,0:T(8,128)(2,1)} %bitcast.2), calls=%async_computation.3 | async-start | bytes 1048576 | tf_op jit(solution)/shard_map/all_to_all | solution.py:200
  62.7 0.0 copy-start.1
  62.7 1.6 %copy-done.1 = bf16[1024,1024]{1,0:T(8,128)(2,1)S(1)} copy-done((bf16[1024,1024]{1,0:T(8,128)(2,1)S(1)}, bf16[1024,1024]{1,0:T(8,128)(2,1)}, u32[]{:S(2)}) %copy-start.1) | copy-done | bytes 2097176
  64.3 0.0 copy-start.3
  64.3 1.6 %copy-done.3 = bf16[1024,1024]{1,0:T(8,128)(2,1)S(1)} copy-done((bf16[1024,1024]{1,0:T(8,128)(2,1)S(1)}, bf16[1024,1024]{1,0:T(8,128)(2,1)}, u32[]{:S(2)}) %copy-start.3) | copy-done | bytes 2097176
  65.9 2.1 %shard_map.66 = bf16[4,256,256]{2,1,0:T(8,128)(2,1)} custom-call(bf16[32,40,256]{2,1,0:T(8,128)(2,1)S(1)} %all-to-all-done.refs_0_, bf16[32,40,256]{2,1,0:T(8,128)(2,1)S(1)} %collective-permute-done.refs_0_.refs_1_, bf16[1024,1024]{1,0:T(8,128)(2,1)S(1)} %copy-done.3, bf16[1024,1024]{1,0:T(8,128)(2,1)S(1)} %copy-done.1, ...), custom_call_target="tpu_custom_call" | custom-call | tf_op jit(solution)/shard_map/pallas_call | solution.py:20
  68.0 3.1 %all-to-all-done.3 = bf16[4,8,32,256]{3,2,1,0:T(8,128)(2,1)S(1)} async-done(((bf16[4,8,32,256]{3,2,1,0:T(8,128)(2,1)}), bf16[4,8,32,256]{3,2,1,0:T(8,128)(2,1)S(1)}, u32[]{:S(2)}, u32[]{:S(2)}) %all-to-all-start.3) | async-done | bytes 524320 | tf_op jit(solution)/shard_map/all_to_all | solution.py:200
  71.1 3.5 %all-to-all-start.2 = ((bf16[4,256,256]{2,1,0:T(8,128)(2,1)}), bf16[4,256,256]{2,1,0:T(8,128)(2,1)S(1)}, u32[]{:S(2)}, u32[]{:S(2)}) async-start(bf16[4,256,256]{2,1,0:T(8,128)(2,1)} %shard_map.66), calls=%async_computation.2 | async-start | bytes 1048576 | tf_op jit(solution)/shard_map/all_to_all | solution.py:200
  74.6 0.7 reduce_sum.31
  75.3 8.9 %all-to-all-done.2 = bf16[4,256,256]{2,1,0:T(8,128)(2,1)S(1)} async-done(((bf16[4,256,256]{2,1,0:T(8,128)(2,1)}), bf16[4,256,256]{2,1,0:T(8,128)(2,1)S(1)}, u32[]{:S(2)}, u32[]{:S(2)}) %all-to-all-start.2) | async-done | bytes 524320 | tf_op jit(solution)/shard_map/all_to_all | solution.py:200
  84.2 3.6 %all-to-all-start.4 = ((bf16[8,32,256]{2,1,0:T(8,128)(2,1)}), bf16[8,32,256]{2,1,0:T(8,128)(2,1)S(1)}, u32[]{:S(2)}, u32[]{:S(2)}) async-start(bf16[8,32,256]{2,1,0:T(8,128)(2,1)} %reduce_sum.31), calls=%async_computation.4 | async-start | bytes 262144 | tf_op jit(solution)/shard_map/all_to_all | solution.py:200
  87.8 0.1 convert_reduce_fusion
  87.8 0.8 copy.7
  88.7 8.2 %all-to-all-done.4 = bf16[8,32,256]{2,1,0:T(8,128)(2,1)S(1)} async-done(((bf16[8,32,256]{2,1,0:T(8,128)(2,1)}), bf16[8,32,256]{2,1,0:T(8,128)(2,1)S(1)}, u32[]{:S(2)}, u32[]{:S(2)}) %all-to-all-start.4) | async-done | bytes 131104 | tf_op jit(solution)/shard_map/all_to_all | solution.py:200
  96.8 0.6 convert_reduce_fusion.1
Async XLA Ops:
  0.6 13.3 %copy-start.5 = (bf16[2048,64]{0,1:T(8,128)(2,1)S(1)}, bf16[2048,64]{0,1:T(8,128)(2,1)}, u32[]{:S(2)}) copy-start(bf16[2048,64]{0,1:T(8,128)(2,1)} %param.7) | copy-start | bytes 786436
  0.6 13.3 %copy-start.4 = (bf16[2048,256]{1,0:T(8,128)(2,1)S(1)}, bf16[2048,256]{1,0:T(8,128)(2,1)}, u32[]{:S(2)}) copy-start(bf16[2048,256]{1,0:T(8,128)(2,1)} %features.1) | copy-start | bytes 3145732
  2.4 29.6 %all-to-all-start = ((bf16[32,40,256]{2,1,0:T(8,128)(2,1)}), bf16[32,40,256]{2,1,0:T(8,128)(2,1)S(1)}, u32[]{:S(2)}, u32[]{:S(2)}) async-start(bf16[32,40,256]{2,1,0:T(8,128)(2,1)} %shard_map.59), calls=%async_computation | async-start | bytes 1310720 | tf_op jit(solution)/shard_map/all_to_all | solution.py:213
  14.2 0.7 copy-start.6
  32.1 17.8 %copy-start.7 = (f32[64,1024]{1,0:T(8,128)S(1)}, f32[64,1024]{1,0:T(8,128)}, u32[]{:S(2)}) copy-start(f32[64,1024]{1,0:T(8,128)} %copy-done.6) | copy-start | bytes 786436
  32.1 2.1 %collective-permute-start = (bf16[32,40,256]{2,1,0:T(8,128)(2,1)S(1)}, bf16[32,40,256]{2,1,0:T(8,128)(2,1)S(1)}, u32[]{:S(2)}, u32[]{:S(2)}) collective-permute-start(bf16[32,40,256]{2,1,0:T(8,128)(2,1)S(1)} %all-to-all-done.refs_0_), channel_id=1, source_target_pairs={{0,1},{1,0},{2,3},{3,2},{4,5},{5,4},{6,7},{7,6},{8,9},{9,8},{10,11... | collective-permute-start | bytes 1966088 | tf_op jit(solution)/shard_map/ppermute | solution.py:196
  51.6 1.3 %copy-start = (bf16[1024,1024]{1,0:T(8,128)(2,1)}, bf16[1024,1024]{1,0:T(8,128)(2,1)S(1)}, u32[]{:S(2)}) copy-start(bf16[1024,1024]{1,0:T(8,128)(2,1)S(1)} %get-tuple-element.36.refs_3_) | copy-start | bytes 6291460
  52.9 2.9 %collective-permute-start.1 = (bf16[1024,256]{1,0:T(8,128)(2,1)S(1)}, bf16[1024,256]{1,0:T(8,128)(2,1)S(1)}, u32[]{:S(2)}, u32[]{:S(2)}) collective-permute-start(bf16[1024,256]{1,0:T(8,128)(2,1)S(1)} %get-tuple-element.39), channel_id=1, source_target_pairs={{0,1},{1,0},{2,3},{3,2},{4,5},{5,4},{6,7},{7,6},{8,9},{9,8},{10,11... | collective-permute-start | bytes 1572872 | tf_op jit(solution)/shard_map/ppermute | solution.py:196
  54.4 1.3 %copy-start.2 = (bf16[1024,1024]{1,0:T(8,128)(2,1)}, bf16[1024,1024]{1,0:T(8,128)(2,1)S(1)}, u32[]{:S(2)}) copy-start(bf16[1024,1024]{1,0:T(8,128)(2,1)S(1)} %get-tuple-element.35.refs_2_) | copy-start | bytes 6291460
  56.7 14.3 %all-to-all-start.3 = ((bf16[4,8,32,256]{3,2,1,0:T(8,128)(2,1)}), bf16[4,8,32,256]{3,2,1,0:T(8,128)(2,1)S(1)}, u32[]{:S(2)}, u32[]{:S(2)}) async-start(bf16[4,8,32,256]{3,2,1,0:T(8,128)(2,1)} %bitcast.2), calls=%async_computation.3 | async-start | bytes 1048576 | tf_op jit(solution)/shard_map/all_to_all | solution.py:200
  62.7 1.6 %copy-start.1 = (bf16[1024,1024]{1,0:T(8,128)(2,1)S(1)}, bf16[1024,1024]{1,0:T(8,128)(2,1)}, u32[]{:S(2)}) copy-start(bf16[1024,1024]{1,0:T(8,128)(2,1)} %copy-done) | copy-start | bytes 6291460
  64.3 1.6 %copy-start.3 = (bf16[1024,1024]{1,0:T(8,128)(2,1)S(1)}, bf16[1024,1024]{1,0:T(8,128)(2,1)}, u32[]{:S(2)}) copy-start(bf16[1024,1024]{1,0:T(8,128)(2,1)} %copy-done.2) | copy-start | bytes 6291460
  71.1 13.1 %all-to-all-start.2 = ((bf16[4,256,256]{2,1,0:T(8,128)(2,1)}), bf16[4,256,256]{2,1,0:T(8,128)(2,1)S(1)}, u32[]{:S(2)}, u32[]{:S(2)}) async-start(bf16[4,256,256]{2,1,0:T(8,128)(2,1)} %shard_map.66), calls=%async_computation.2 | async-start | bytes 1048576 | tf_op jit(solution)/shard_map/all_to_all | solution.py:200
  84.2 12.7 %all-to-all-start.4 = ((bf16[8,32,256]{2,1,0:T(8,128)(2,1)}), bf16[8,32,256]{2,1,0:T(8,128)(2,1)S(1)}, u32[]{:S(2)}, u32[]{:S(2)}) async-start(bf16[8,32,256]{2,1,0:T(8,128)(2,1)} %reduce_sum.31), calls=%async_computation.4 | async-start | bytes 262144 | tf_op jit(solution)/shard_map/all_to_all | solution.py:200

commit v9 on v7

--- a/solution.py
+++ b/solution.py
@@ -71,10 +71,6 @@
     return land, white.reshape(count * rows, rank).astype(BF16)
 
 
-def pieces_of(stacks, count):
-    return [stack[i : i + count] for stack in stacks for i in range(0, stack.shape[0], count)]
-
-
 def prepare_body(parts, places, features, cot_t, feat, feat_t, sq_feat, cot):
     own = features.shape[0] // parts
     for i, place in enumerate(places()):
@@ -97,30 +93,32 @@
     return call(functools.partial(prepare_body, parts, places), shapes, features, cot_t)
 
 
-def forward_body(count, members, rank, first, *refs):
-    blocks, (feat_t, sq_feat), (kern, *embeds) = refs[:count], refs[count : count + 2], refs[count + 2 + (not first) :]
+def forward_body(count, rank, first, *refs):
+    blocks, (feat_t, sq_feat), outs = refs[:count], refs[count : count + 2], refs[count + 2 + (not first) :]
+    kerns, embeds = outs[:count], outs[count:]
     width = feat_t.shape[0]
     scale = 4.0 / width * LOG2E
     bias = sq_feat[...] * (-scale)
     total = None if first else refs[count + 2][...]
-    for i, block in enumerate(pieces_of(blocks, members)):
-        land, white = unpack(block, rank)
-        rows = land.shape[0]
+    for block, kern in zip(blocks, kerns):
+        land, white = unpack(block[...], rank)
         land32 = land.astype(F32)
         sq_land = jnp.sum(land32 * land32, axis=1, keepdims=True) * (-scale)
         cross = jnp.dot(land, feat_t[...], preferred_element_type=F32)
         value = jnp.exp2(cross * (2.0 * scale) + (bias + sq_land)).astype(BF16)
-        kern[i * rows : (i + 1) * rows, :] = value
+        kern[...] = value
         part = lax.dot_general(white, value, (((0,), (0,)), ((), ())), preferred_element_type=F32)
         total = part if total is None else total + part
     for embed in embeds:
         embed[...] = total.astype(embed.dtype)
 
 
-def forward(blocks, members, feat_t, sq_feat, prior, rows, rank):
-    toks = feat_t.shape[1]
-    shapes = [shaped((rows, toks), BF16), shaped((rank, toks), F32)] + [shaped((rank, toks), BF16)] * len(prior)
-    return call(functools.partial(forward_body, len(blocks), members, rank, not prior), shapes, *blocks, feat_t, sq_feat, *prior)
+def forward(blocks, feat_t, sq_feat, prior, last, rank):
+    width, toks = feat_t.shape
+    shapes = [shaped((block.size // (width + rank), toks), BF16) for block in blocks]
+    shapes += [shaped((rank, toks), kind) for kind in ([F32, BF16] if last else [F32])]
+    outs = call(functools.partial(forward_body, len(blocks), rank, not prior), shapes, *blocks, feat_t, sq_feat, *prior)
+    return outs[: len(blocks)], outs[len(blocks) :]
 
 
 def moved(ref, place, places, bit):
@@ -158,16 +156,16 @@
     return call(functools.partial(norm_body, factor, places), shaped(cot.shape, BF16), share, other, cot)
 
 
-def backward_body(count, members, rank, first, *refs):
-    blocks, (kern, dembed, feat) = refs[:count], refs[count : count + 3]
+def backward_body(count, rank, first, *refs):
+    blocks, kerns, (dembed, feat) = refs[:count], refs[count : 2 * count], refs[2 * count : 2 * count + 2]
     coef, land_grad, row_total = refs[-3:]
-    total = None if first else refs[count + 3][...]
-    for i, block in enumerate(pieces_of(blocks, members)):
-        land, white = unpack(block, rank)
+    total = None if first else refs[2 * count + 2][...]
+    for i, block in enumerate(blocks):
+        land, white = unpack(block[...], rank)
         rows = land.shape[0]
         at = slice(i * rows, (i + 1) * rows)
         dkernel = jnp.dot(white, dembed[...], preferred_element_type=F32)
-        value = (dkernel * kern[at, :].astype(F32)).astype(BF16)
+        value = (dkernel * kerns[i][...].astype(F32)).astype(BF16)
         coef[at, :] = value
         value32 = value.astype(F32)
         part = jnp.sum(value32, axis=0, keepdims=True)
@@ -178,21 +176,20 @@
     row_total[...] = total
 
 
-def backward(blocks, members, kern, dembed, feat, prior, kind):
+def backward(blocks, kerns, dembed, feat, prior, kind):
     toks, width = feat.shape
-    rows = kern.shape[0]
+    rows = sum(kern.shape[0] for kern in kerns)
     shapes = [shaped((rows, toks), BF16), shaped((rows, width), kind), shaped((1, toks), F32)]
-    body = functools.partial(backward_body, len(blocks), members, dembed.shape[0], not prior)
-    return call(body, shapes, *blocks, kern, dembed, feat, *prior)
-
-
-def feature_body(count, members, coefs, rank, *refs):
+    body = functools.partial(backward_body, len(blocks), dembed.shape[0], not prior)
+    return call(body, shapes, *blocks, *kerns, dembed, feat, *prior)
+
+
+def feature_body(count, coefs, rank, *refs):
     blocks, coef, (feat_t, row_total), outs = refs[:count], refs[count : count + coefs], refs[count + coefs : count + coefs + 2], refs[count + coefs + 2 :]
-    pieces = pieces_of(blocks, members)
-    each = len(pieces) // coefs
+    each = count // coefs
     pulled = None
-    for i, block in enumerate(pieces):
-        land, _ = unpack(block, rank)
+    for i, block in enumerate(blocks):
+        land, _ = unpack(block[...], rank)
         rows = land.shape[0]
         at = slice(i % each * rows, (i % each + 1) * rows)
         part = lax.dot_general(land, coef[i // each][at, :], (((0,), (0,)), ((), ())), preferred_element_type=F32)
@@ -204,10 +201,10 @@
         start += out.shape[1]
 
 
-def feature_share(blocks, members, coefs, feat_t, row_total, rank):
+def feature_share(blocks, coefs, feat_t, row_total, parts, rank):
     width, toks = feat_t.shape
-    shapes = [shaped((width, toks // 2), kind) for kind in (F32, BF16)]
-    body = functools.partial(feature_body, len(blocks), members, len(coefs), rank)
+    shapes = [shaped((width, toks // parts), kind) for kind in [F32] + [BF16] * (parts - 1)]
+    body = functools.partial(feature_body, len(blocks), len(coefs), rank)
     return call(body, shapes, *blocks, *coefs, feat_t, row_total)
 
 
@@ -253,25 +250,34 @@
     feat, feat_t, sq_feat, cot = prepare(features, cotangent.T, n_x * n_h, places, n_x)
     packed, feat, feat_t, sq_feat, cot = lax.optimization_barrier((packed, feat, feat_t, sq_feat, cot))
     mine = spread(packed, Y)
-    theirs = [shift(jnp.concatenate(mine, axis=0), "c", 1)]
-
-    half_rows = n_y * n_z * rows
-    kern_mine, embed = forward(mine, n_z, feat_t, sq_feat, [], half_rows, rank)
-    kern_theirs, embed, share = forward(theirs, n_z, feat_t, sq_feat, [embed], half_rows, rank)
+    theirs = [shift(packed, "c", 1)] + [None] * (n_y - 1)
+
+    order = (0, 3, 1, 2)
+    kern_mine, kern_theirs = {}, {}
+    embed = []
+    for step in range(n_y + 1):
+        todo = [(kern_theirs, theirs, order[step - 1])] * (step > 0) + [(kern_mine, mine, order[step % n_y])] * (step < n_y)
+        kerns, embed = forward([blocks[s] for _, blocks, s in todo], feat_t, sq_feat, embed, step == n_y, rank)
+        for (where, _, s), kern in zip(todo, kerns):
+            where[s] = kern
+        if step + 1 < n_y:
+            s = order[step + 1]
+            mine[s], embed = lax.optimization_barrier((mine[s], embed))
+            theirs[s] = shift(mine[s], "c", 1)
+    kern_mine, kern_theirs = [kern_mine[s] for s in range(n_y)], [kern_theirs[s] for s in range(n_y)]
+    embed, share = embed
     embed, share = pair_sum(embed, partner(share, X, 0), n_x)
     dembed = norm_backward(embed, partner(share, X, 1), cot, -gamma, n_x)
 
-    coef_theirs, land_theirs, row_total = backward(theirs, n_z, kern_theirs, dembed, feat, [], BF16)
-    coef_mine, land_mine, row_total = backward(mine, n_z, kern_mine, dembed, feat, [row_total], F32)
+    coef_theirs, land_theirs, row_total = backward(theirs, kern_theirs, dembed, feat, [], BF16)
+    coef_mine, land_mine, row_total = backward(mine, kern_mine, dembed, feat, [row_total], F32)
     land_share = (land_mine + shift(land_theirs, "c", 1).astype(F32)).reshape(n_y, n_z, rows, width)
     land_share = collect(land_share, Y, -1)
 
-    near, far = feature_share(mine + theirs, n_z, [coef_mine, coef_theirs], feat_t, row_total, rank)
-    land_share, far = lax.optimization_barrier((land_share.astype(BF16), partner(far, X, 1)))
+    own, first, second, opposite = feature_share(mine + theirs, [coef_mine, coef_theirs], feat_t, row_total, n_x, rank)
     landmark_grad = collect_at_once(land_share, "z")
-    near = near + far.astype(F32)
-    own = near.shape[1] // 2
-    feature_grad = (near[:, :own] + partner(near[:, own:].astype(BF16), X, 0).astype(F32)).T
+    arrived = [partner(first, X, 0), partner(second, X, 1), shift(opposite, "x", 2)]
+    feature_grad = (own + sum(share.astype(F32) for share in arrived)).T
     return (feature_grad, landmark_grad)
 
 

time: 78.8 us -> 77.4 us (0.982)
  the two profiles are of different devices: /device:TPU:20 before, /device:TPU:24 now
where the time goes in v9:
time: 77.4 us; the launch traced here: 76.5 us
  waiting for transfers between devices  34.2 us (44%)
  starting transfers between devices  26.9 us (35%)
  Pallas kernels  10.1 us (13%)
  local copies, waits for them, and re-layouts  3.05 us (4%)
  other arithmetic  1.54 us (2%)
    ppermute x12, waiting for transfers between devices, shift(): lax.ppermute(block, axes, [(i, (i + step) % size) for i in range(size)])  11.9 us
    pallas_call x11, Pallas kernels, call(): pl.pallas_call(body, out_shape=out_shape, in_specs=[WHOLE] * len(operands...  8.6 us
    all_to_all x1, starting transfers between devices, per_device(): lax.all_to_all(pack(landmarks, whitening, n_z), 'z', 0, 0, tiled=True)  8.48 us
    all_to_all x1, waiting for transfers between devices, collect_at_once(): lax.all_to_all(pieces.astype(BF16), axes, 0, 0, tiled=True).astype(F32)  8.06 us
    ppermute x12, starting transfers between devices, shift(): lax.ppermute(block, axes, [(i, (i + step) % size) for i in range(size)])  7.72 us
    ppermute x4, starting transfers between devices, partner(): return lax.ppermute(block, ring + ('c',), perm)  7.35 us
    all_to_all x1, waiting for transfers between devices, per_device(): lax.all_to_all(pack(landmarks, whitening, n_z), 'z', 0, 0, tiled=True)  7.35 us
    ppermute x4, waiting for transfers between devices, partner(): return lax.ppermute(block, ring + ('c',), perm)  6.91 us
  transfers between devices with their start and end apart: 18, of which 10 were waited for; matrix products, arithmetic and copies ran while one was open for 2% of the time, Pallas kernels for 8%

profile of v9, /device:TPU:24, one launch (start us, length us, event | category | flops | bytes accessed | tf_op | source)
XLA Modules:
  0.0 76.5 jit_solution(8907504216524098638)
XLA Ops:
  0.6 1.5 %shard_map.59 = bf16[8,40,256]{2,1,0:T(8,128)(2,1)} custom-call(bf16[32,256]{1,0:T(8,128)(2,1)} %landmarks.1, bf16[32,64]{1,0:T(8,128)(2,1)} %whitening.1), custom_call_target="tpu_custom_call" | custom-call | tf_op jit(solution)/shard_map/pallas_call | solution.py:51
  2.1 8.5 %all-to-all-start = ((bf16[8,40,256]{2,1,0:T(8,128)(2,1)}), bf16[8,40,256]{2,1,0:T(8,128)(2,1)S(1)}, u32[]{:S(2)}, u32[]{:S(2)}) async-start(bf16[8,40,256]{2,1,0:T(8,128)(2,1)} %shard_map.59), calls=%async_computation | async-start | bytes 327680 | tf_op jit(solution)/shard_map/all_to_all | solution.py:249
  10.6 1.2 %copy-done = bf16[2048,256]{1,0:T(8,128)(2,1)S(1)} copy-done((bf16[2048,256]{1,0:T(8,128)(2,1)S(1)}, bf16[2048,256]{1,0:T(8,128)(2,1)}, u32[]{:S(2)}) %copy-start) | copy-done | bytes 1048600
  11.8 0.9 %copy-done.1 = bf16[2048,64]{0,1:T(8,128)(2,1)S(1)} copy-done((bf16[2048,64]{0,1:T(8,128)(2,1)S(1)}, bf16[2048,64]{0,1:T(8,128)(2,1)}, u32[]{:S(2)}) %copy-start.1) | copy-done | bytes 262168
  12.8 0.2 shard_map.60
  13.0 7.3 %all-to-all-done.refs_0_ = bf16[8,40,256]{2,1,0:T(8,128)(2,1)S(1)} async-done(((bf16[8,40,256]{2,1,0:T(8,128)(2,1)}), bf16[8,40,256]{2,1,0:T(8,128)(2,1)S(1)}, u32[]{:S(2)}, u32[]{:S(2)}) %all-to-all-start) | async-done | bytes 163872 | tf_op jit(solution)/shard_map/all_to_all | solution.py:249
  20.4 0.7 collective-permute-start.2
  21.1 0.0 collective-permute-start.1
  21.1 2.5 %collective-permute-start = (bf16[8,40,256]{2,1,0:T(8,128)(2,1)S(1)}, bf16[8,40,256]{2,1,0:T(8,128)(2,1)S(1)}, u32[]{:S(2)}, u32[]{:S(2)}) collective-permute-start(bf16[8,40,256]{2,1,0:T(8,128)(2,1)S(1)} %all-to-all-done.refs_0_), channel_id=1, source_target_pairs={{0,16},{16,32},{32,48},{48,0},{1,17},{17,33},{33,49},{49,1},{2,18}... | collective-permute-start | bytes 491528 | tf_op jit(solution)/shard_map/ppermute | solution.py:213
  23.6 0.5 shard_map.61
  24.1 2.8 %collective-permute-done.2.refs_1_.refs_3_ = bf16[8,40,256]{2,1,0:T(8,128)(2,1)S(1)} collective-permute-done((bf16[8,40,256]{2,1,0:T(8,128)(2,1)S(1)}, bf16[8,40,256]{2,1,0:T(8,128)(2,1)S(1)}, u32[]{:S(2)}, u32[]{:S(2)}) %collective-permute-start.2) | collective-permute-done | bytes 163872 | tf_op jit(solution)/shard_map/ppermute | solution.py:213
  26.9 0.0 collective-permute-start.4
  26.9 0.0 collective-permute-start.3
  26.9 0.0 collective-permute-done.1.refs_0_.refs_4_
  26.9 0.9 %shard_map.62 = (bf16[256,1024]{1,0:T(8,128)(2,1)S(1)}, bf16[256,1024]{1,0:T(8,128)(2,1)S(1)}, f32[64,1024]{1,0:T(8,128)S(1)}) custom-call(bf16[8,40,256]{2,1,0:T(8,128)(2,1)S(1)} %collective-permute-done.1.refs_0_.refs_4_, bf16[8,40,256]{2,1,0:T(8,128)(2,1)S(1)} %collective-permute-done.2.refs_1_.refs_3_, ...), custom_call_target="tpu_custom_call" | custom-call | tf_op jit(solution)/shard_map/pallas_call | solution.py:20
  27.9 3.4 %collective-permute-done.refs_1_ = bf16[8,40,256]{2,1,0:T(8,128)(2,1)S(1)} collective-permute-done((bf16[8,40,256]{2,1,0:T(8,128)(2,1)S(1)}, bf16[8,40,256]{2,1,0:T(8,128)(2,1)S(1)}, u32[]{:S(2)}, u32[]{:S(2)}) %collective-permute-start) | collective-permute-done | bytes 163872 | tf_op jit(solution)/shard_map/ppermute | solution.py:213
  31.3 0.0 collective-permute-start.5
  31.3 0.0 collective-permute-done.4.refs_0_.refs_3_.refs_7_
  31.3 0.9 %shard_map.63 = (bf16[256,1024]{1,0:T(8,128)(2,1)S(1)}, bf16[256,1024]{1,0:T(8,128)(2,1)S(1)}, f32[64,1024]{1,0:T(8,128)S(1)}) custom-call(bf16[8,40,256]{2,1,0:T(8,128)(2,1)S(1)} %collective-permute-done.4.refs_0_.refs_3_.refs_7_, bf16[8,40,256]{2,1,0:T(8,128)(2,1)S(1)} %collective-permute-done.refs_1_, ...), custom_call_target="tpu_custom_call" | custom-call | tf_op jit(solution)/shard_map/pallas_call | solution.py:20
  32.2 2.8 %collective-permute-done.3.refs_1_.refs_2_ = bf16[8,40,256]{2,1,0:T(8,128)(2,1)S(1)} collective-permute-done((bf16[8,40,256]{2,1,0:T(8,128)(2,1)S(1)}, bf16[8,40,256]{2,1,0:T(8,128)(2,1)S(1)}, u32[]{:S(2)}, u32[]{:S(2)}) %collective-permute-start.3) | collective-permute-done | bytes 163872 | tf_op jit(solution)/shard_map/ppermute | solution.py:213
  35.0 0.0 collective-permute-start.6
  35.0 0.9 %shard_map.64 = (bf16[256,1024]{1,0:T(8,128)(2,1)S(1)}, bf16[256,1024]{1,0:T(8,128)(2,1)S(1)}, f32[64,1024]{1,0:T(8,128)S(1)}) custom-call(bf16[8,40,256]{2,1,0:T(8,128)(2,1)S(1)} %collective-permute-done.5.refs_0_.refs_1_.refs_5_, bf16[8,40,256]{2,1,0:T(8,128)(2,1)S(1)} %collective-permute-done.3.refs_1_.refs_2_, ...), custom_call_target="tpu_custom_call" | custom-call | tf_op jit(solution)/shard_map/pallas_call | solution.py:20
  36.0 0.5 collective-permute-done.6.refs_0_.refs_2_.refs_6_
  36.4 0.5 shard_map.65
  36.9 1.6 %collective-permute-start.7 = (bf16[64,1024]{1,0:T(8,128)(2,1)S(1)}, bf16[64,1024]{1,0:T(8,128)(2,1)S(1)}, u32[]{:S(2)}, u32[]{:S(2)}) collective-permute-start(bf16[64,1024]{1,0:T(8,128)(2,1)S(1)} %get-tuple-element.65), channel_id=1, source_target_pairs={{0,64},{1,193},{64,0},{65,129},{128,192},{129,65},{192,128},{193,1... | collective-permute-start | bytes 393224 | tf_op jit(solution)/shard_map/ppermute | solution.py:219
  38.5 3.5 %collective-permute-done.7.other = bf16[64,1024]{1,0:T(8,128)(2,1)S(1)} collective-permute-done((bf16[64,1024]{1,0:T(8,128)(2,1)S(1)}, bf16[64,1024]{1,0:T(8,128)(2,1)S(1)}, u32[]{:S(2)}, u32[]{:S(2)}) %collective-permute-start.7) | collective-permute-done | bytes 131104 | tf_op jit(solution)/shard_map/ppermute | solution.py:219
  42.0 2.8 %collective-permute-start.8 = (bf16[64,1024]{1,0:T(8,128)(2,1)S(1)}, bf16[64,1024]{1,0:T(8,128)(2,1)S(1)}, u32[]{:S(2)}, u32[]{:S(2)}) collective-permute-start(bf16[64,1024]{1,0:T(8,128)(2,1)S(1)} %get-tuple-element.67), channel_id=1, source_target_pairs={{0,192},{1,65},{64,128},{65,1},{128,64},{129,193},{192,0},{193,129... | collective-permute-start | bytes 393224 | tf_op jit(solution)/shard_map/ppermute | solution.py:219
  44.9 3.4 %collective-permute-done.8.other = bf16[64,1024]{1,0:T(8,128)(2,1)S(1)} collective-permute-done((bf16[64,1024]{1,0:T(8,128)(2,1)S(1)}, bf16[64,1024]{1,0:T(8,128)(2,1)S(1)}, u32[]{:S(2)}, u32[]{:S(2)}) %collective-permute-start.8) | collective-permute-done | bytes 131104 | tf_op jit(solution)/shard_map/ppermute | solution.py:219
  48.3 0.1 shard_map.67.refs_8_
  48.4 1.5 %shard_map.68 = (bf16[1024,1024]{1,0:T(8,128)(2,1)S(1)}, bf16[1024,256]{1,0:T(8,128)(2,1)S(1)}, f32[1,1024]{1,0:T(1,128)S(1)}) custom-call(bf16[8,40,256]{2,1,0:T(8,128)(2,1)S(1)} %collective-permute-done.1.refs_0_.refs_4_, bf16[8,40,256]{2,1,0:T(8,128)(2,1)S(1)} %collective-permute-done.5.refs_0_.refs_1_.refs_5_, ...), custom_call_target="tpu_custom_call" | custom-call | tf_op jit(solution)/shard_map/pallas_call | solution.py:20
  50.0 0.3 collective-permute-start.12
  50.3 1.5 %shard_map.69 = (bf16[1024,1024]{1,0:T(8,128)(2,1)S(1)}, f32[1024,256]{1,0:T(8,128)S(1)}, f32[1,1024]{1,0:T(1,128)S(1)}) custom-call(bf16[8,40,256]{2,1,0:T(8,128)(2,1)S(1)} %all-to-all-done.refs_0_, bf16[8,40,256]{2,1,0:T(8,128)(2,1)S(1)} %collective-permute-done.refs_1_, bf16[8,40,256]{2,1,0:T(8,128)(2,1)S(1)} %collective-permute-done.3.refs_1_.refs_2_, ...), custom_call_target="tpu_custom_call" | custom-call | tf_op jit(solution)/shard_map/pallas_call | solution.py:20
  51.8 0.3 collective-permute-done.12
  52.2 0.1 fusion
  52.3 1.2 %collective-permute-start.15 = (bf16[8,32,256]{2,1,0:T(8,128)(2,1)S(1)}, bf16[8,32,256]{2,1,0:T(8,128)(2,1)S(1)}, u32[]{:S(2)}, u32[]{:S(2)}) collective-permute-start(bf16[8,32,256]{2,1,0:T(8,128)(2,1)S(1)} %bitcast.11), channel_id=1, source_target_pairs={{0,16},{16,32},{32,48},{48,0},{1,17},{17,33},{33,49},{49,1},{2,18}... | collective-permute-start | bytes 393224 | tf_op jit(solution)/shard_map/ppermute | solution.py:213
  53.5 0.9 %collective-permute-start.13 = (bf16[8,32,256]{2,1,0:T(8,128)(2,1)S(1)}, bf16[8,32,256]{2,1,0:T(8,128)(2,1)S(1)}, u32[]{:S(2)}, u32[]{:S(2)}) collective-permute-start(bf16[8,32,256]{2,1,0:T(8,128)(2,1)S(1)} %bitcast.10), channel_id=1, source_target_pairs={{0,48},{16,0},{32,16},{48,32},{1,49},{17,1},{33,17},{49,33},{2,50}... | collective-permute-start | bytes 393224 | tf_op jit(solution)/shard_map/ppermute | solution.py:213
  54.4 0.6 collective-permute-start.14
  55.0 1.3 %shard_map.70 = (f32[256,256]{1,0:T(8,128)S(1)}, bf16[256,256]{1,0:T(8,128)(2,1)S(1)}, bf16[256,256]{1,0:T(8,128)(2,1)S(1)}, bf16[256,256]{1,0:T(8,128)(2,1)S(1)}) custom-call(bf16[8,40,256]{2,1,0:T(8,128)(2,1)S(1)} %all-to-all-done.refs_0_, bf16[8,40,256]{2,1,0:T(8,128)(2,1)S(1)} %collective-permute-done.refs_1_, ...), custom_call_target="tpu_custom_call" | custom-call | tf_op jit(solution)/shard_map/pallas_call | solution.py:20
  56.3 0.4 collective-permute-start.9
  56.7 2.6 %collective-permute-start.10 = (bf16[256,256]{1,0:T(8,128)(2,1)S(1)}, bf16[256,256]{1,0:T(8,128)(2,1)S(1)}, u32[]{:S(2)}, u32[]{:S(2)}) collective-permute-start(bf16[256,256]{1,0:T(8,128)(2,1)S(1)} %get-tuple-element.80), channel_id=1, source_target_pairs={{0,192},{1,65},{64,128},{65,1},{128,64},{129,193},{192,0},{193,129... | collective-permute-start | bytes 393224 | tf_op jit(solution)/shard_map/ppermute | solution.py:219
  59.3 1.5 %collective-permute-start.11 = (bf16[256,256]{1,0:T(8,128)(2,1)S(1)}, bf16[256,256]{1,0:T(8,128)(2,1)S(1)}, u32[]{:S(2)}, u32[]{:S(2)}) collective-permute-start(bf16[256,256]{1,0:T(8,128)(2,1)S(1)} %get-tuple-element.81), channel_id=1, source_target_pairs={{0,128},{64,192},{128,0},{192,64},{1,129},{65,193},{129,1},{193,65... | collective-permute-start | bytes 393224 | tf_op jit(solution)/shard_map/ppermute | solution.py:213
  60.7 2.1 %collective-permute-done.13 = bf16[8,32,256]{2,1,0:T(8,128)(2,1)S(1)} collective-permute-done((bf16[8,32,256]{2,1,0:T(8,128)(2,1)S(1)}, bf16[8,32,256]{2,1,0:T(8,128)(2,1)S(1)}, u32[]{:S(2)}, u32[]{:S(2)}) %collective-permute-start.13) | collective-permute-done | bytes 131104 | tf_op jit(solution)/shard_map/ppermute | solution.py:213
  62.8 0.7 add_convert_fusion
  63.5 3.4 %all-to-all-start.1 = ((bf16[8,32,256]{2,1,0:T(8,128)(2,1)}), bf16[8,32,256]{2,1,0:T(8,128)(2,1)S(1)}, u32[]{:S(2)}, u32[]{:S(2)}) async-start(bf16[8,32,256]{2,1,0:T(8,128)(2,1)} %add_convert_fusion), calls=%async_computation.1 | async-start | bytes 262144 | tf_op jit(solution)/shard_map/all_to_all | solution.py:234
  66.9 0.1 add_bitcast_fusion
  67.0 0.8 %copy.6 = f32[256,256]{1,0:T(8,128)} copy(f32[256,256]{0,1:T(8,128)S(1)} %add_bitcast_fusion) | data formatting | bytes 524288
  67.8 8.1 %all-to-all-done.1 = bf16[8,32,256]{2,1,0:T(8,128)(2,1)S(1)} async-done(((bf16[8,32,256]{2,1,0:T(8,128)(2,1)}), bf16[8,32,256]{2,1,0:T(8,128)(2,1)S(1)}, u32[]{:S(2)}, u32[]{:S(2)}) %all-to-all-start.1) | async-done | bytes 131104 | tf_op jit(solution)/shard_map/all_to_all | solution.py:234
  75.9 0.6 convert_reduce_fusion
  (11 shorter events, 0.1 us)
Async XLA Ops:
  2.1 18.2 %all-to-all-start = ((bf16[8,40,256]{2,1,0:T(8,128)(2,1)}), bf16[8,40,256]{2,1,0:T(8,128)(2,1)S(1)}, u32[]{:S(2)}, u32[]{:S(2)}) async-start(bf16[8,40,256]{2,1,0:T(8,128)(2,1)} %shard_map.59), calls=%async_computation | async-start | bytes 327680 | tf_op jit(solution)/shard_map/all_to_all | solution.py:249
  10.6 1.2 %copy-start = (bf16[2048,256]{1,0:T(8,128)(2,1)S(1)}, bf16[2048,256]{1,0:T(8,128)(2,1)}, u32[]{:S(2)}) copy-start(bf16[2048,256]{1,0:T(8,128)(2,1)} %features.1) | copy-start | bytes 3145732
  11.8 0.9 %copy-start.1 = (bf16[2048,64]{0,1:T(8,128)(2,1)S(1)}, bf16[2048,64]{0,1:T(8,128)(2,1)}, u32[]{:S(2)}) copy-start(bf16[2048,64]{0,1:T(8,128)(2,1)} %param.7) | copy-start | bytes 786436
  20.4 6.5 %collective-permute-start.2 = (bf16[8,40,256]{2,1,0:T(8,128)(2,1)S(1)}, bf16[8,40,256]{2,1,0:T(8,128)(2,1)S(1)}, u32[]{:S(2)}, u32[]{:S(2)}) collective-permute-start(bf16[8,40,256]{2,1,0:T(8,128)(2,1)S(1)} %all-to-all-done.refs_0_), channel_id=1, source_target_pairs={{0,48},{16,0},{32,16},{48,32},{1,49},{17,1},{33,17},{49,33},{2,50}... | collective-permute-start | bytes 491528 | tf_op jit(solution)/shard_map/ppermute | solution.py:213
  21.1 5.8 %collective-permute-start.1 = (bf16[8,40,256]{2,1,0:T(8,128)(2,1)S(1)}, bf16[8,40,256]{2,1,0:T(8,128)(2,1)S(1)}, u32[]{:S(2)}, u32[]{:S(2)}) collective-permute-start(bf16[8,40,256]{2,1,0:T(8,128)(2,1)S(1)} %all-to-all-done.refs_0_), channel_id=1, source_target_pairs={{0,1},{1,0},{2,3},{3,2},{4,5},{5,4},{6,7},{7,6},{8,9},{9,8},{10,11... | collective-permute-start | bytes 491528 | tf_op jit(solution)/shard_map/ppermute | solution.py:213
  21.1 10.2 %collective-permute-start = (bf16[8,40,256]{2,1,0:T(8,128)(2,1)S(1)}, bf16[8,40,256]{2,1,0:T(8,128)(2,1)S(1)}, u32[]{:S(2)}, u32[]{:S(2)}) collective-permute-start(bf16[8,40,256]{2,1,0:T(8,128)(2,1)S(1)} %all-to-all-done.refs_0_), channel_id=1, source_target_pairs={{0,16},{16,32},{32,48},{48,0},{1,17},{17,33},{33,49},{49,1},{2,18}... | collective-permute-start | bytes 491528 | tf_op jit(solution)/shard_map/ppermute | solution.py:213
  26.9 4.4 %collective-permute-start.4 = (bf16[8,40,256]{2,1,0:T(8,128)(2,1)S(1)}, bf16[8,40,256]{2,1,0:T(8,128)(2,1)S(1)}, u32[]{:S(2)}, u32[]{:S(2)}) collective-permute-start(bf16[8,40,256]{2,1,0:T(8,128)(2,1)S(1)} %collective-permute-done.2.refs_1_.refs_3_), channel_id=1, source_target_pairs={{0,1},{1,0},{2,3},{3,2},{4,5},{5,4},{6,7},{7,6},{8,9},{9,8},{10,11... | collective-permute-start | bytes 491528 | tf_op jit(solution)/shard_map/ppermute | solution.py:213
  26.9 8.1 %collective-permute-start.3 = (bf16[8,40,256]{2,1,0:T(8,128)(2,1)S(1)}, bf16[8,40,256]{2,1,0:T(8,128)(2,1)S(1)}, u32[]{:S(2)}, u32[]{:S(2)}) collective-permute-start(bf16[8,40,256]{2,1,0:T(8,128)(2,1)S(1)} %all-to-all-done.refs_0_), channel_id=1, source_target_pairs={{0,32},{16,48},{32,0},{48,16},{1,33},{17,49},{33,1},{49,17},{2,34}... | collective-permute-start | bytes 491528 | tf_op jit(solution)/shard_map/ppermute | solution.py:213
  31.3 3.7 %collective-permute-start.5 = (bf16[8,40,256]{2,1,0:T(8,128)(2,1)S(1)}, bf16[8,40,256]{2,1,0:T(8,128)(2,1)S(1)}, u32[]{:S(2)}, u32[]{:S(2)}) collective-permute-start(bf16[8,40,256]{2,1,0:T(8,128)(2,1)S(1)} %collective-permute-done.refs_1_), channel_id=1, source_target_pairs={{0,1},{1,0},{2,3},{3,2},{4,5},{5,4},{6,7},{7,6},{8,9},{9,8},{10,11... | collective-permute-start | bytes 491528 | tf_op jit(solution)/shard_map/ppermute | solution.py:213
  35.0 1.4 %collective-permute-start.6 = (bf16[8,40,256]{2,1,0:T(8,128)(2,1)S(1)}, bf16[8,40,256]{2,1,0:T(8,128)(2,1)S(1)}, u32[]{:S(2)}, u32[]{:S(2)}) collective-permute-start(bf16[8,40,256]{2,1,0:T(8,128)(2,1)S(1)} %collective-permute-done.3.refs_1_.refs_2_), channel_id=1, source_target_pairs={{0,1},{1,0},{2,3},{3,2},{4,5},{5,4},{6,7},{7,6},{8,9},{9,8},{10,11... | collective-permute-start | bytes 491528 | tf_op jit(solution)/shard_map/ppermute | solution.py:213
  36.9 5.1 %collective-permute-start.7 = (bf16[64,1024]{1,0:T(8,128)(2,1)S(1)}, bf16[64,1024]{1,0:T(8,128)(2,1)S(1)}, u32[]{:S(2)}, u32[]{:S(2)}) collective-permute-start(bf16[64,1024]{1,0:T(8,128)(2,1)S(1)} %get-tuple-element.65), channel_id=1, source_target_pairs={{0,64},{1,193},{64,0},{65,129},{128,192},{129,65},{192,128},{193,1... | collective-permute-start | bytes 393224 | tf_op jit(solution)/shard_map/ppermute | solution.py:219
  42.0 6.3 %collective-permute-start.8 = (bf16[64,1024]{1,0:T(8,128)(2,1)S(1)}, bf16[64,1024]{1,0:T(8,128)(2,1)S(1)}, u32[]{:S(2)}, u32[]{:S(2)}) collective-permute-start(bf16[64,1024]{1,0:T(8,128)(2,1)S(1)} %get-tuple-element.67), channel_id=1, source_target_pairs={{0,192},{1,65},{64,128},{65,1},{128,64},{129,193},{192,0},{193,129... | collective-permute-start | bytes 393224 | tf_op jit(solution)/shard_map/ppermute | solution.py:219
  50.0 2.2 %collective-permute-start.12 = (bf16[1024,256]{1,0:T(8,128)(2,1)S(1)}, bf16[1024,256]{1,0:T(8,128)(2,1)S(1)}, u32[]{:S(2)}, u32[]{:S(2)}) collective-permute-start(bf16[1024,256]{1,0:T(8,128)(2,1)S(1)} %get-tuple-element.83), channel_id=1, source_target_pairs={{0,1},{1,0},{2,3},{3,2},{4,5},{5,4},{6,7},{7,6},{8,9},{9,8},{10,11... | collective-permute-start | bytes 1572872 | tf_op jit(solution)/shard_map/ppermute | solution.py:213
  52.3 7.0 %collective-permute-start.15 = (bf16[8,32,256]{2,1,0:T(8,128)(2,1)S(1)}, bf16[8,32,256]{2,1,0:T(8,128)(2,1)S(1)}, u32[]{:S(2)}, u32[]{:S(2)}) collective-permute-start(bf16[8,32,256]{2,1,0:T(8,128)(2,1)S(1)} %bitcast.11), channel_id=1, source_target_pairs={{0,16},{16,32},{32,48},{48,0},{1,17},{17,33},{33,49},{49,1},{2,18}... | collective-permute-start | bytes 393224 | tf_op jit(solution)/shard_map/ppermute | solution.py:213
  53.5 9.3 %collective-permute-start.13 = (bf16[8,32,256]{2,1,0:T(8,128)(2,1)S(1)}, bf16[8,32,256]{2,1,0:T(8,128)(2,1)S(1)}, u32[]{:S(2)}, u32[]{:S(2)}) collective-permute-start(bf16[8,32,256]{2,1,0:T(8,128)(2,1)S(1)} %bitcast.10), channel_id=1, source_target_pairs={{0,48},{16,0},{32,16},{48,32},{1,49},{17,1},{33,17},{49,33},{2,50}... | collective-permute-start | bytes 393224 | tf_op jit(solution)/shard_map/ppermute | solution.py:213
  54.4 8.4 %collective-permute-start.14 = (bf16[8,32,256]{2,1,0:T(8,128)(2,1)S(1)}, bf16[8,32,256]{2,1,0:T(8,128)(2,1)S(1)}, u32[]{:S(2)}, u32[]{:S(2)}) collective-permute-start(bf16[8,32,256]{2,1,0:T(8,128)(2,1)S(1)} %bitcast.9), channel_id=1, source_target_pairs={{0,32},{16,48},{32,0},{48,16},{1,33},{17,49},{33,1},{49,17},{2,34}... | collective-permute-start | bytes 393224 | tf_op jit(solution)/shard_map/ppermute | solution.py:213
  56.3 10.6 %collective-permute-start.9 = (bf16[256,256]{1,0:T(8,128)(2,1)S(1)}, bf16[256,256]{1,0:T(8,128)(2,1)S(1)}, u32[]{:S(2)}, u32[]{:S(2)}) collective-permute-start(bf16[256,256]{1,0:T(8,128)(2,1)S(1)} %get-tuple-element.79), channel_id=1, source_target_pairs={{0,64},{1,193},{64,0},{65,129},{128,192},{129,65},{192,128},{193,1... | collective-permute-start | bytes 393224 | tf_op jit(solution)/shard_map/ppermute | solution.py:219
  56.7 10.2 %collective-permute-start.10 = (bf16[256,256]{1,0:T(8,128)(2,1)S(1)}, bf16[256,256]{1,0:T(8,128)(2,1)S(1)}, u32[]{:S(2)}, u32[]{:S(2)}) collective-permute-start(bf16[256,256]{1,0:T(8,128)(2,1)S(1)} %get-tuple-element.80), channel_id=1, source_target_pairs={{0,192},{1,65},{64,128},{65,1},{128,64},{129,193},{192,0},{193,129... | collective-permute-start | bytes 393224 | tf_op jit(solution)/shard_map/ppermute | solution.py:219
  59.3 7.6 %collective-permute-start.11 = (bf16[256,256]{1,0:T(8,128)(2,1)S(1)}, bf16[256,256]{1,0:T(8,128)(2,1)S(1)}, u32[]{:S(2)}, u32[]{:S(2)}) collective-permute-start(bf16[256,256]{1,0:T(8,128)(2,1)S(1)} %get-tuple-element.81), channel_id=1, source_target_pairs={{0,128},{64,192},{128,0},{192,64},{1,129},{65,193},{129,1},{193,65... | collective-permute-start | bytes 393224 | tf_op jit(solution)/shard_map/ppermute | solution.py:213
  63.5 12.4 %all-to-all-start.1 = ((bf16[8,32,256]{2,1,0:T(8,128)(2,1)}), bf16[8,32,256]{2,1,0:T(8,128)(2,1)S(1)}, u32[]{:S(2)}, u32[]{:S(2)}) async-start(bf16[8,32,256]{2,1,0:T(8,128)(2,1)} %add_convert_fusion), calls=%async_computation.1 | async-start | bytes 262144 | tf_op jit(solution)/shard_map/all_to_all | solution.py:234

commit v10 on v7

--- a/solution.py
+++ b/solution.py
@@ -71,8 +71,10 @@
     return land, white.reshape(count * rows, rank).astype(BF16)
 
 
-def pieces_of(stacks, count):
-    return [stack[i : i + count] for stack in stacks for i in range(0, stack.shape[0], count)]
+def pieces_of(stacks, members):
+    for stack in stacks:
+        for i in range(0, stack.shape[0], members):
+            yield stack[i : i + members]
 
 
 def prepare_body(parts, places, features, cot_t, feat, feat_t, sq_feat, cot):
@@ -98,29 +100,33 @@
 
 
 def forward_body(count, members, rank, first, *refs):
-    blocks, (feat_t, sq_feat), (kern, *embeds) = refs[:count], refs[count : count + 2], refs[count + 2 + (not first) :]
+    stacks, (feat_t, sq_feat), outs = refs[:count], refs[count : count + 2], refs[count + 2 + (not first) :]
+    blocks = sum(stack.shape[0] for stack in stacks) // members
+    kerns, embeds = outs[:blocks], outs[blocks:]
     width = feat_t.shape[0]
     scale = 4.0 / width * LOG2E
     bias = sq_feat[...] * (-scale)
     total = None if first else refs[count + 2][...]
-    for i, block in enumerate(pieces_of(blocks, members)):
+    for block, kern in zip(pieces_of(stacks, members), kerns):
         land, white = unpack(block, rank)
-        rows = land.shape[0]
         land32 = land.astype(F32)
         sq_land = jnp.sum(land32 * land32, axis=1, keepdims=True) * (-scale)
         cross = jnp.dot(land, feat_t[...], preferred_element_type=F32)
         value = jnp.exp2(cross * (2.0 * scale) + (bias + sq_land)).astype(BF16)
-        kern[i * rows : (i + 1) * rows, :] = value
+        kern[...] = value
         part = lax.dot_general(white, value, (((0,), (0,)), ((), ())), preferred_element_type=F32)
         total = part if total is None else total + part
     for embed in embeds:
         embed[...] = total.astype(embed.dtype)
 
 
-def forward(blocks, members, feat_t, sq_feat, prior, rows, rank):
-    toks = feat_t.shape[1]
-    shapes = [shaped((rows, toks), BF16), shaped((rank, toks), F32)] + [shaped((rank, toks), BF16)] * len(prior)
-    return call(functools.partial(forward_body, len(blocks), members, rank, not prior), shapes, *blocks, feat_t, sq_feat, *prior)
+def forward(blocks, members, feat_t, sq_feat, prior, last, rank):
+    width, toks = feat_t.shape
+    count = sum(block.shape[0] for block in blocks) // members
+    rows = sum(block.size for block in blocks) // (width + rank) // count
+    shapes = [shaped((rows, toks), BF16)] * count + [shaped((rank, toks), kind) for kind in ([F32, BF16] if last else [F32])]
+    outs = call(functools.partial(forward_body, len(blocks), members, rank, not prior), shapes, *blocks, feat_t, sq_feat, *prior)
+    return outs[:count], outs[count:]
 
 
 def moved(ref, place, places, bit):
@@ -159,15 +165,17 @@
 
 
 def backward_body(count, members, rank, first, *refs):
-    blocks, (kern, dembed, feat) = refs[:count], refs[count : count + 3]
+    stacks, refs = refs[:count], refs[count:]
+    blocks = sum(stack.shape[0] for stack in stacks) // members
+    kerns, (dembed, feat) = refs[:blocks], refs[blocks : blocks + 2]
     coef, land_grad, row_total = refs[-3:]
-    total = None if first else refs[count + 3][...]
-    for i, block in enumerate(pieces_of(blocks, members)):
+    total = None if first else refs[blocks + 2][...]
+    for i, block in enumerate(pieces_of(stacks, members)):
         land, white = unpack(block, rank)
         rows = land.shape[0]
         at = slice(i * rows, (i + 1) * rows)
         dkernel = jnp.dot(white, dembed[...], preferred_element_type=F32)
-        value = (dkernel * kern[at, :].astype(F32)).astype(BF16)
+        value = (dkernel * kerns[i][...].astype(F32)).astype(BF16)
         coef[at, :] = value
         value32 = value.astype(F32)
         part = jnp.sum(value32, axis=0, keepdims=True)
@@ -178,20 +186,19 @@
     row_total[...] = total
 
 
-def backward(blocks, members, kern, dembed, feat, prior, kind):
+def backward(blocks, members, kerns, dembed, feat, prior, kind):
     toks, width = feat.shape
-    rows = kern.shape[0]
+    rows = sum(kern.shape[0] for kern in kerns)
     shapes = [shaped((rows, toks), BF16), shaped((rows, width), kind), shaped((1, toks), F32)]
     body = functools.partial(backward_body, len(blocks), members, dembed.shape[0], not prior)
-    return call(body, shapes, *blocks, kern, dembed, feat, *prior)
+    return call(body, shapes, *blocks, *kerns, dembed, feat, *prior)
 
 
 def feature_body(count, members, coefs, rank, *refs):
-    blocks, coef, (feat_t, row_total), outs = refs[:count], refs[count : count + coefs], refs[count + coefs : count + coefs + 2], refs[count + coefs + 2 :]
-    pieces = pieces_of(blocks, members)
-    each = len(pieces) // coefs
+    stacks, coef, (feat_t, row_total), outs = refs[:count], refs[count : count + coefs], refs[count + coefs : count + coefs + 2], refs[count + coefs + 2 :]
+    each = sum(stack.shape[0] for stack in stacks) // members // coefs
     pulled = None
-    for i, block in enumerate(pieces):
+    for i, block in enumerate(pieces_of(stacks, members)):
         land, _ = unpack(block, rank)
         rows = land.shape[0]
         at = slice(i % each * rows, (i % each + 1) * rows)
@@ -204,9 +211,9 @@
         start += out.shape[1]
 
 
-def feature_share(blocks, members, coefs, feat_t, row_total, rank):
+def feature_share(blocks, members, coefs, feat_t, row_total, parts, rank):
     width, toks = feat_t.shape
-    shapes = [shaped((width, toks // 2), kind) for kind in (F32, BF16)]
+    shapes = [shaped((width, toks // parts), kind) for kind in [F32] + [BF16] * (parts - 1)]
     body = functools.partial(feature_body, len(blocks), members, len(coefs), rank)
     return call(body, shapes, *blocks, *coefs, feat_t, row_total)
 
@@ -253,11 +260,14 @@
     feat, feat_t, sq_feat, cot = prepare(features, cotangent.T, n_x * n_h, places, n_x)
     packed, feat, feat_t, sq_feat, cot = lax.optimization_barrier((packed, feat, feat_t, sq_feat, cot))
     mine = spread(packed, Y)
+
+    kern_own, embed = forward(mine[:1], n_z, feat_t, sq_feat, [], False, rank)
+    *arrived, embed = lax.optimization_barrier((*mine[1:], *embed))
+    mine = mine[:1] + arrived
     theirs = [shift(jnp.concatenate(mine, axis=0), "c", 1)]
-
-    half_rows = n_y * n_z * rows
-    kern_mine, embed = forward(mine, n_z, feat_t, sq_feat, [], half_rows, rank)
-    kern_theirs, embed, share = forward(theirs, n_z, feat_t, sq_feat, [embed], half_rows, rank)
+    kern_mine, embed = forward(arrived, n_z, feat_t, sq_feat, [embed], False, rank)
+    kern_theirs, (embed, share) = forward(theirs, n_z, feat_t, sq_feat, embed, True, rank)
+    kern_mine = kern_own + kern_mine
     embed, share = pair_sum(embed, partner(share, X, 0), n_x)
     dembed = norm_backward(embed, partner(share, X, 1), cot, -gamma, n_x)
 
@@ -266,12 +276,10 @@
     land_share = (land_mine + shift(land_theirs, "c", 1).astype(F32)).reshape(n_y, n_z, rows, width)
     land_share = collect(land_share, Y, -1)
 
-    near, far = feature_share(mine + theirs, n_z, [coef_mine, coef_theirs], feat_t, row_total, rank)
-    land_share, far = lax.optimization_barrier((land_share.astype(BF16), partner(far, X, 1)))
+    own, first, second, opposite = feature_share(mine + theirs, n_z, [coef_mine, coef_theirs], feat_t, row_total, n_x, rank)
     landmark_grad = collect_at_once(land_share, "z")
-    near = near + far.astype(F32)
-    own = near.shape[1] // 2
-    feature_grad = (near[:, :own] + partner(near[:, own:].astype(BF16), X, 0).astype(F32)).T
+    arrived = [partner(first, X, 0), partner(second, X, 1), shift(opposite, "x", 2)]
+    feature_grad = (own + sum(share.astype(F32) for share in arrived)).T
     return (feature_grad, landmark_grad)
 
 

time: 78.8 us -> 75.4 us (0.957)
  the two profiles are of different devices: /device:TPU:20 before, /device:TPU:24 now
where the time goes in v10:
time: 75.4 us; the launch traced here: 74.8 us
  waiting for transfers between devices  30.3 us (40%)
  starting transfers between devices  29.1 us (39%)
  Pallas kernels  9.91 us (13%)
  local copies, waits for them, and re-layouts  3.05 us (4%)
  other arithmetic  1.63 us (2%)
  between operations  0.77 us (1%)
    ppermute x9, starting transfers between devices, shift(): lax.ppermute(block, axes, [(i, (i + step) % size) for i in range(size)])  9.93 us
    all_to_all x1, starting transfers between devices, per_device(): lax.all_to_all(pack(landmarks, whitening, n_z), 'z', 0, 0, tiled=True)  8.48 us
    pallas_call x9, Pallas kernels, call(): pl.pallas_call(body, out_shape=out_shape, in_specs=[WHOLE] * len(operands...  8.44 us
    all_to_all x1, waiting for transfers between devices, collect_at_once(): lax.all_to_all(pieces.astype(BF16), axes, 0, 0, tiled=True).astype(F32)  8.06 us
    ppermute x9, waiting for transfers between devices, shift(): lax.ppermute(block, axes, [(i, (i + step) % size) for i in range(size)])  7.96 us
    ppermute x4, starting transfers between devices, partner(): return lax.ppermute(block, ring + ('c',), perm)  7.36 us
    all_to_all x1, waiting for transfers between devices, per_device(): lax.all_to_all(pack(landmarks, whitening, n_z), 'z', 0, 0, tiled=True)  7.35 us
    ppermute x4, waiting for transfers between devices, partner(): return lax.ppermute(block, ring + ('c',), perm)  6.9 us
  transfers between devices with their start and end apart: 15, of which 9 were waited for; matrix products, arithmetic and copies ran while one was open for 2% of the time, Pallas kernels for 7%

profile of v10, /device:TPU:24, one launch (start us, length us, event | category | flops | bytes accessed | tf_op | source)
XLA Modules:
  0.0 74.8 jit_solution(94420791777872926)
XLA Ops:
  0.6 1.5 %shard_map.59 = bf16[8,40,256]{2,1,0:T(8,128)(2,1)} custom-call(bf16[32,256]{1,0:T(8,128)(2,1)} %landmarks.1, bf16[32,64]{1,0:T(8,128)(2,1)} %whitening.1), custom_call_target="tpu_custom_call" | custom-call | tf_op jit(solution)/shard_map/pallas_call | solution.py:51
  2.1 8.5 %all-to-all-start = ((bf16[8,40,256]{2,1,0:T(8,128)(2,1)}), bf16[8,40,256]{2,1,0:T(8,128)(2,1)S(1)}, u32[]{:S(2)}, u32[]{:S(2)}) async-start(bf16[8,40,256]{2,1,0:T(8,128)(2,1)} %shard_map.59), calls=%async_computation | async-start | bytes 327680 | tf_op jit(solution)/shard_map/all_to_all | solution.py:259
  10.6 0.0 copy-start
  10.6 1.2 %copy-done = bf16[2048,256]{1,0:T(8,128)(2,1)S(1)} copy-done((bf16[2048,256]{1,0:T(8,128)(2,1)S(1)}, bf16[2048,256]{1,0:T(8,128)(2,1)}, u32[]{:S(2)}) %copy-start) | copy-done | bytes 1048600
  11.8 0.9 %copy-done.1 = bf16[2048,64]{0,1:T(8,128)(2,1)S(1)} copy-done((bf16[2048,64]{0,1:T(8,128)(2,1)S(1)}, bf16[2048,64]{0,1:T(8,128)(2,1)}, u32[]{:S(2)}) %copy-start.1) | copy-done | bytes 262168
  12.8 0.2 shard_map.60
  13.0 7.3 %all-to-all-done.refs_0_ = bf16[8,40,256]{2,1,0:T(8,128)(2,1)S(1)} async-done(((bf16[8,40,256]{2,1,0:T(8,128)(2,1)}), bf16[8,40,256]{2,1,0:T(8,128)(2,1)S(1)}, u32[]{:S(2)}, u32[]{:S(2)}) %all-to-all-start) | async-done | bytes 163872 | tf_op jit(solution)/shard_map/all_to_all | solution.py:259
  20.4 0.7 collective-permute-start.2
  21.1 0.9 %collective-permute-start.1 = (bf16[8,40,256]{2,1,0:T(8,128)(2,1)S(1)}, bf16[8,40,256]{2,1,0:T(8,128)(2,1)S(1)}, u32[]{:S(2)}, u32[]{:S(2)}) collective-permute-start(bf16[8,40,256]{2,1,0:T(8,128)(2,1)S(1)} %all-to-all-done.refs_0_), channel_id=1, source_target_pairs={{0,32},{16,48},{32,0},{48,16},{1,33},{17,49},{33,1},{49,17},{2,34}... | collective-permute-start | bytes 491528 | tf_op jit(solution)/shard_map/ppermute | solution.py:223
  22.0 2.2 %collective-permute-start = (bf16[8,40,256]{2,1,0:T(8,128)(2,1)S(1)}, bf16[8,40,256]{2,1,0:T(8,128)(2,1)S(1)}, u32[]{:S(2)}, u32[]{:S(2)}) collective-permute-start(bf16[8,40,256]{2,1,0:T(8,128)(2,1)S(1)} %all-to-all-done.refs_0_), channel_id=1, source_target_pairs={{0,16},{16,32},{32,48},{48,0},{1,17},{17,33},{33,49},{49,1},{2,18}... | collective-permute-start | bytes 491528 | tf_op jit(solution)/shard_map/ppermute | solution.py:223
  24.2 0.5 shard_map.61
  24.7 4.4 %collective-permute-done.2.refs_2_.refs_3_ = bf16[8,40,256]{2,1,0:T(8,128)(2,1)S(1)} collective-permute-done((bf16[8,40,256]{2,1,0:T(8,128)(2,1)S(1)}, bf16[8,40,256]{2,1,0:T(8,128)(2,1)S(1)}, u32[]{:S(2)}, u32[]{:S(2)}) %collective-permute-start.2) | collective-permute-done | bytes 163872 | tf_op jit(solution)/shard_map/ppermute | solution.py:223
  29.1 0.0 collective-permute-done.1.refs_1_.refs_2_
  29.1 0.6 collective-permute-done.refs_0_.refs_1_
  29.8 0.1 pad_maximum_fusion
  29.9 0.1 collective-permute-start.3
  30.0 1.4 %shard_map.62 = (bf16[256,1024]{1,0:T(8,128)(2,1)S(1)}, bf16[256,1024]{1,0:T(8,128)(2,1)S(1)}, bf16[256,1024]{1,0:T(8,128)(2,1)S(1)}, f32[64,1024]{1,0:T(8,128)S(1)}) custom-call(bf16[8,40,256]{2,1,0:T(8,128)(2,1)S(1)} %collective-permute-done.refs_0_.refs_1_, bf16[8,40,256]{2,1,0:T(8,128)(2,1)S(1)} %collective-permute-done.1.refs_1_.refs_2_, ...), custom_call_target="tpu_custom_call" | custom-call | tf_op jit(solution)/shard_map/pallas_call | solution.py:20
  31.3 0.7 collective-permute-done.3.refs_0_.refs_4_
  32.0 1.8 %shard_map.63 = (bf16[256,1024]{1,0:T(8,128)(2,1)S(1)}, bf16[256,1024]{1,0:T(8,128)(2,1)S(1)}, bf16[256,1024]{1,0:T(8,128)(2,1)S(1)}, bf16[256,1024]{1,0:T(8,128...) custom-call(bf16[32,40,256]{2,1,0:T(8,128)(2,1)S(1)} %collective-permute-done.3.refs_0_.refs_4_, ...), custom_call_target="tpu_custom_call" | custom-call | tf_op jit(solution)/shard_map/pallas_call | solution.py:20
  33.8 1.6 %collective-permute-start.4 = (bf16[64,1024]{1,0:T(8,128)(2,1)S(1)}, bf16[64,1024]{1,0:T(8,128)(2,1)S(1)}, u32[]{:S(2)}, u32[]{:S(2)}) collective-permute-start(bf16[64,1024]{1,0:T(8,128)(2,1)S(1)} %get-tuple-element.57), channel_id=1, source_target_pairs={{0,64},{1,193},{64,0},{65,129},{128,192},{129,65},{192,128},{193,1... | collective-permute-start | bytes 393224 | tf_op jit(solution)/shard_map/ppermute | solution.py:229
  35.4 3.5 %collective-permute-done.4.other = bf16[64,1024]{1,0:T(8,128)(2,1)S(1)} collective-permute-done((bf16[64,1024]{1,0:T(8,128)(2,1)S(1)}, bf16[64,1024]{1,0:T(8,128)(2,1)S(1)}, u32[]{:S(2)}, u32[]{:S(2)}) %collective-permute-start.4) | collective-permute-done | bytes 131104 | tf_op jit(solution)/shard_map/ppermute | solution.py:229
  38.9 2.8 %collective-permute-start.5 = (bf16[64,1024]{1,0:T(8,128)(2,1)S(1)}, bf16[64,1024]{1,0:T(8,128)(2,1)S(1)}, u32[]{:S(2)}, u32[]{:S(2)}) collective-permute-start(bf16[64,1024]{1,0:T(8,128)(2,1)S(1)} %get-tuple-element.59), channel_id=1, source_target_pairs={{0,192},{1,65},{64,128},{65,1},{128,64},{129,193},{192,0},{193,129... | collective-permute-start | bytes 393224 | tf_op jit(solution)/shard_map/ppermute | solution.py:229
  41.8 3.4 %collective-permute-done.5.other = bf16[64,1024]{1,0:T(8,128)(2,1)S(1)} collective-permute-done((bf16[64,1024]{1,0:T(8,128)(2,1)S(1)}, bf16[64,1024]{1,0:T(8,128)(2,1)S(1)}, u32[]{:S(2)}, u32[]{:S(2)}) %collective-permute-start.5) | collective-permute-done | bytes 131104 | tf_op jit(solution)/shard_map/ppermute | solution.py:229
  45.2 0.1 shard_map.65.refs_5_.refs_8_
  45.3 1.5 %shard_map.66 = (bf16[1024,1024]{1,0:T(8,128)(2,1)S(1)}, bf16[1024,256]{1,0:T(8,128)(2,1)S(1)}, f32[1,1024]{1,0:T(1,128)S(1)}) custom-call(bf16[32,40,256]{2,1,0:T(8,128)(2,1)S(1)} %collective-permute-done.3.refs_0_.refs_4_, bf16[256,1024]{1,0:T(8,128)(2,1)S(1)} %get-tuple-element.62.refs_1_, bf16[256,1024]{1,0:T(8,128)(2,1)S(1)} %get-tuple-element.63.refs_2_, ...), custom_call_target="tpu_custom_call" | custom-call | tf_op jit(solution)/shard_map/pallas_call | solution.py:20
  46.9 0.1 collective-permute-start.9
  47.0 1.6 %shard_map.67 = (bf16[1024,1024]{1,0:T(8,128)(2,1)S(1)}, f32[1024,256]{1,0:T(8,128)S(1)}, f32[1,1024]{1,0:T(1,128)S(1)}) custom-call(bf16[8,40,256]{2,1,0:T(8,128)(2,1)S(1)} %all-to-all-done.refs_0_, bf16[8,40,256]{2,1,0:T(8,128)(2,1)S(1)} %collective-permute-done.refs_0_.refs_1_, bf16[8,40,256]{2,1,0:T(8,128)(2,1)S(1)} %collective-permute-done.1.refs_1_.refs_2_, ...), custom_call_target="tpu_custom_call" | custom-call | tf_op jit(solution)/shard_map/pallas_call | solution.py:20
  48.5 0.3 collective-permute-done.9
  48.9 0.1 fusion
  49.0 2.7 %collective-permute-start.12 = (bf16[8,32,256]{2,1,0:T(8,128)(2,1)S(1)}, bf16[8,32,256]{2,1,0:T(8,128)(2,1)S(1)}, u32[]{:S(2)}, u32[]{:S(2)}) collective-permute-start(bf16[8,32,256]{2,1,0:T(8,128)(2,1)S(1)} %bitcast.11), channel_id=1, source_target_pairs={{0,16},{16,32},{32,48},{48,0},{1,17},{17,33},{33,49},{49,1},{2,18}... | collective-permute-start | bytes 393224 | tf_op jit(solution)/shard_map/ppermute | solution.py:223
  51.7 0.0 collective-permute-start.10
  51.7 1.7 %collective-permute-start.11 = (bf16[8,32,256]{2,1,0:T(8,128)(2,1)S(1)}, bf16[8,32,256]{2,1,0:T(8,128)(2,1)S(1)}, u32[]{:S(2)}, u32[]{:S(2)}) collective-permute-start(bf16[8,32,256]{2,1,0:T(8,128)(2,1)S(1)} %bitcast.9), channel_id=1, source_target_pairs={{0,32},{16,48},{32,0},{48,16},{1,33},{17,49},{33,1},{49,17},{2,34}... | collective-permute-start | bytes 393224 | tf_op jit(solution)/shard_map/ppermute | solution.py:223
  53.5 1.3 %shard_map.68 = (f32[256,256]{1,0:T(8,128)S(1)}, bf16[256,256]{1,0:T(8,128)(2,1)S(1)}, bf16[256,256]{1,0:T(8,128)(2,1)S(1)}, bf16[256,256]{1,0:T(8,128)(2,1)S(1)}) custom-call(bf16[8,40,256]{2,1,0:T(8,128)(2,1)S(1)} %all-to-all-done.refs_0_, bf16[8,40,256]{2,1,0:T(8,128)(2,1)S(1)} %collective-permute-done.refs_0_.refs_1_, ...), custom_call_target="tpu_custom_call" | custom-call | tf_op jit(solution)/shard_map/pallas_call | solution.py:20
  54.7 0.4 collective-permute-start.6
  55.1 2.6 %collective-permute-start.7 = (bf16[256,256]{1,0:T(8,128)(2,1)S(1)}, bf16[256,256]{1,0:T(8,128)(2,1)S(1)}, u32[]{:S(2)}, u32[]{:S(2)}) collective-permute-start(bf16[256,256]{1,0:T(8,128)(2,1)S(1)} %get-tuple-element.72), channel_id=1, source_target_pairs={{0,192},{1,65},{64,128},{65,1},{128,64},{129,193},{192,0},{193,129... | collective-permute-start | bytes 393224 | tf_op jit(solution)/shard_map/ppermute | solution.py:229
  57.7 0.0 collective-permute-done.12
  57.7 1.5 %collective-permute-start.8 = (bf16[256,256]{1,0:T(8,128)(2,1)S(1)}, bf16[256,256]{1,0:T(8,128)(2,1)S(1)}, u32[]{:S(2)}, u32[]{:S(2)}) collective-permute-start(bf16[256,256]{1,0:T(8,128)(2,1)S(1)} %get-tuple-element.73), channel_id=1, source_target_pairs={{0,128},{64,192},{128,0},{192,64},{1,129},{65,193},{129,1},{193,65... | collective-permute-start | bytes 393224 | tf_op jit(solution)/shard_map/ppermute | solution.py:223
  59.2 1.9 %collective-permute-done.10 = bf16[8,32,256]{2,1,0:T(8,128)(2,1)S(1)} collective-permute-done((bf16[8,32,256]{2,1,0:T(8,128)(2,1)S(1)}, bf16[8,32,256]{2,1,0:T(8,128)(2,1)S(1)}, u32[]{:S(2)}, u32[]{:S(2)}) %collective-permute-start.10) | collective-permute-done | bytes 131104 | tf_op jit(solution)/shard_map/ppermute | solution.py:223
  61.0 0.0 collective-permute-done.11
  61.0 0.7 add_convert_fusion
  61.8 3.4 %all-to-all-start.1 = ((bf16[8,32,256]{2,1,0:T(8,128)(2,1)}), bf16[8,32,256]{2,1,0:T(8,128)(2,1)S(1)}, u32[]{:S(2)}, u32[]{:S(2)}) async-start(bf16[8,32,256]{2,1,0:T(8,128)(2,1)} %add_convert_fusion), calls=%async_computation.1 | async-start | bytes 262144 | tf_op jit(solution)/shard_map/all_to_all | solution.py:244
  65.1 0.0 collective-permute-done.6
  65.2 0.0 collective-permute-done.7
  65.2 0.0 collective-permute-done.8
  65.2 0.1 add_bitcast_fusion
  65.2 0.8 %copy.6 = f32[256,256]{1,0:T(8,128)} copy(f32[256,256]{0,1:T(8,128)S(1)} %add_bitcast_fusion) | data formatting | bytes 524288
  66.1 8.1 %all-to-all-done.1 = bf16[8,32,256]{2,1,0:T(8,128)(2,1)S(1)} async-done(((bf16[8,32,256]{2,1,0:T(8,128)(2,1)}), bf16[8,32,256]{2,1,0:T(8,128)(2,1)S(1)}, u32[]{:S(2)}, u32[]{:S(2)}) %all-to-all-start.1) | async-done | bytes 131104 | tf_op jit(solution)/shard_map/all_to_all | solution.py:244
  74.1 0.6 convert_reduce_fusion
  (4 shorter events, 0.1 us)
Async XLA Ops:
  2.1 18.2 %all-to-all-start = ((bf16[8,40,256]{2,1,0:T(8,128)(2,1)}), bf16[8,40,256]{2,1,0:T(8,128)(2,1)S(1)}, u32[]{:S(2)}, u32[]{:S(2)}) async-start(bf16[8,40,256]{2,1,0:T(8,128)(2,1)} %shard_map.59), calls=%async_computation | async-start | bytes 327680 | tf_op jit(solution)/shard_map/all_to_all | solution.py:259
  10.6 1.2 %copy-start = (bf16[2048,256]{1,0:T(8,128)(2,1)S(1)}, bf16[2048,256]{1,0:T(8,128)(2,1)}, u32[]{:S(2)}) copy-start(bf16[2048,256]{1,0:T(8,128)(2,1)} %features.1) | copy-start | bytes 3145732
  11.8 0.9 %copy-start.1 = (bf16[2048,64]{0,1:T(8,128)(2,1)S(1)}, bf16[2048,64]{0,1:T(8,128)(2,1)}, u32[]{:S(2)}) copy-start(bf16[2048,64]{0,1:T(8,128)(2,1)} %param.7) | copy-start | bytes 786436
  20.4 8.8 %collective-permute-start.2 = (bf16[8,40,256]{2,1,0:T(8,128)(2,1)S(1)}, bf16[8,40,256]{2,1,0:T(8,128)(2,1)S(1)}, u32[]{:S(2)}, u32[]{:S(2)}) collective-permute-start(bf16[8,40,256]{2,1,0:T(8,128)(2,1)S(1)} %all-to-all-done.refs_0_), channel_id=1, source_target_pairs={{0,48},{16,0},{32,16},{48,32},{1,49},{17,1},{33,17},{49,33},{2,50}... | collective-permute-start | bytes 491528 | tf_op jit(solution)/shard_map/ppermute | solution.py:223
  21.1 8.0 %collective-permute-start.1 = (bf16[8,40,256]{2,1,0:T(8,128)(2,1)S(1)}, bf16[8,40,256]{2,1,0:T(8,128)(2,1)S(1)}, u32[]{:S(2)}, u32[]{:S(2)}) collective-permute-start(bf16[8,40,256]{2,1,0:T(8,128)(2,1)S(1)} %all-to-all-done.refs_0_), channel_id=1, source_target_pairs={{0,32},{16,48},{32,0},{48,16},{1,33},{17,49},{33,1},{49,17},{2,34}... | collective-permute-start | bytes 491528 | tf_op jit(solution)/shard_map/ppermute | solution.py:223
  22.0 7.7 %collective-permute-start = (bf16[8,40,256]{2,1,0:T(8,128)(2,1)S(1)}, bf16[8,40,256]{2,1,0:T(8,128)(2,1)S(1)}, u32[]{:S(2)}, u32[]{:S(2)}) collective-permute-start(bf16[8,40,256]{2,1,0:T(8,128)(2,1)S(1)} %all-to-all-done.refs_0_), channel_id=1, source_target_pairs={{0,16},{16,32},{32,48},{48,0},{1,17},{17,33},{33,49},{49,1},{2,18}... | collective-permute-start | bytes 491528 | tf_op jit(solution)/shard_map/ppermute | solution.py:223
  29.9 2.2 %collective-permute-start.3 = (bf16[32,40,256]{2,1,0:T(8,128)(2,1)S(1)}, bf16[32,40,256]{2,1,0:T(8,128)(2,1)S(1)}, u32[]{:S(2)}, u32[]{:S(2)}) collective-permute-start(bf16[32,40,256]{2,1,0:T(8,128)(2,1)S(1)} %pad_maximum_fusion), channel_id=1, source_target_pairs={{0,1},{1,0},{2,3},{3,2},{4,5},{5,4},{6,7},{7,6},{8,9},{9,8},{10,11... | collective-permute-start | bytes 1966088 | tf_op jit(solution)/shard_map/ppermute | solution.py:223
  33.8 5.1 %collective-permute-start.4 = (bf16[64,1024]{1,0:T(8,128)(2,1)S(1)}, bf16[64,1024]{1,0:T(8,128)(2,1)S(1)}, u32[]{:S(2)}, u32[]{:S(2)}) collective-permute-start(bf16[64,1024]{1,0:T(8,128)(2,1)S(1)} %get-tuple-element.57), channel_id=1, source_target_pairs={{0,64},{1,193},{64,0},{65,129},{128,192},{129,65},{192,128},{193,1... | collective-permute-start | bytes 393224 | tf_op jit(solution)/shard_map/ppermute | solution.py:229
  38.9 6.3 %collective-permute-start.5 = (bf16[64,1024]{1,0:T(8,128)(2,1)S(1)}, bf16[64,1024]{1,0:T(8,128)(2,1)S(1)}, u32[]{:S(2)}, u32[]{:S(2)}) collective-permute-start(bf16[64,1024]{1,0:T(8,128)(2,1)S(1)} %get-tuple-element.59), channel_id=1, source_target_pairs={{0,192},{1,65},{64,128},{65,1},{128,64},{129,193},{192,0},{193,129... | collective-permute-start | bytes 393224 | tf_op jit(solution)/shard_map/ppermute | solution.py:229
  46.9 2.0 %collective-permute-start.9 = (bf16[1024,256]{1,0:T(8,128)(2,1)S(1)}, bf16[1024,256]{1,0:T(8,128)(2,1)S(1)}, u32[]{:S(2)}, u32[]{:S(2)}) collective-permute-start(bf16[1024,256]{1,0:T(8,128)(2,1)S(1)} %get-tuple-element.75), channel_id=1, source_target_pairs={{0,1},{1,0},{2,3},{3,2},{4,5},{5,4},{6,7},{7,6},{8,9},{9,8},{10,11... | collective-permute-start | bytes 1572872 | tf_op jit(solution)/shard_map/ppermute | solution.py:223
  49.0 8.7 %collective-permute-start.12 = (bf16[8,32,256]{2,1,0:T(8,128)(2,1)S(1)}, bf16[8,32,256]{2,1,0:T(8,128)(2,1)S(1)}, u32[]{:S(2)}, u32[]{:S(2)}) collective-permute-start(bf16[8,32,256]{2,1,0:T(8,128)(2,1)S(1)} %bitcast.11), channel_id=1, source_target_pairs={{0,16},{16,32},{32,48},{48,0},{1,17},{17,33},{33,49},{49,1},{2,18}... | collective-permute-start | bytes 393224 | tf_op jit(solution)/shard_map/ppermute | solution.py:223
  51.7 9.3 %collective-permute-start.10 = (bf16[8,32,256]{2,1,0:T(8,128)(2,1)S(1)}, bf16[8,32,256]{2,1,0:T(8,128)(2,1)S(1)}, u32[]{:S(2)}, u32[]{:S(2)}) collective-permute-start(bf16[8,32,256]{2,1,0:T(8,128)(2,1)S(1)} %bitcast.10), channel_id=1, source_target_pairs={{0,48},{16,0},{32,16},{48,32},{1,49},{17,1},{33,17},{49,33},{2,50}... | collective-permute-start | bytes 393224 | tf_op jit(solution)/shard_map/ppermute | solution.py:223
  51.7 9.3 %collective-permute-start.11 = (bf16[8,32,256]{2,1,0:T(8,128)(2,1)S(1)}, bf16[8,32,256]{2,1,0:T(8,128)(2,1)S(1)}, u32[]{:S(2)}, u32[]{:S(2)}) collective-permute-start(bf16[8,32,256]{2,1,0:T(8,128)(2,1)S(1)} %bitcast.9), channel_id=1, source_target_pairs={{0,32},{16,48},{32,0},{48,16},{1,33},{17,49},{33,1},{49,17},{2,34}... | collective-permute-start | bytes 393224 | tf_op jit(solution)/shard_map/ppermute | solution.py:223
  54.7 10.4 %collective-permute-start.6 = (bf16[256,256]{1,0:T(8,128)(2,1)S(1)}, bf16[256,256]{1,0:T(8,128)(2,1)S(1)}, u32[]{:S(2)}, u32[]{:S(2)}) collective-permute-start(bf16[256,256]{1,0:T(8,128)(2,1)S(1)} %get-tuple-element.71), channel_id=1, source_target_pairs={{0,64},{1,193},{64,0},{65,129},{128,192},{129,65},{192,128},{193,1... | collective-permute-start | bytes 393224 | tf_op jit(solution)/shard_map/ppermute | solution.py:229
  55.1 10.1 %collective-permute-start.7 = (bf16[256,256]{1,0:T(8,128)(2,1)S(1)}, bf16[256,256]{1,0:T(8,128)(2,1)S(1)}, u32[]{:S(2)}, u32[]{:S(2)}) collective-permute-start(bf16[256,256]{1,0:T(8,128)(2,1)S(1)} %get-tuple-element.72), channel_id=1, source_target_pairs={{0,192},{1,65},{64,128},{65,1},{128,64},{129,193},{192,0},{193,129... | collective-permute-start | bytes 393224 | tf_op jit(solution)/shard_map/ppermute | solution.py:229
  57.7 7.5 %collective-permute-start.8 = (bf16[256,256]{1,0:T(8,128)(2,1)S(1)}, bf16[256,256]{1,0:T(8,128)(2,1)S(1)}, u32[]{:S(2)}, u32[]{:S(2)}) collective-permute-start(bf16[256,256]{1,0:T(8,128)(2,1)S(1)} %get-tuple-element.73), channel_id=1, source_target_pairs={{0,128},{64,192},{128,0},{192,64},{1,129},{65,193},{129,1},{193,65... | collective-permute-start | bytes 393224 | tf_op jit(solution)/shard_map/ppermute | solution.py:223
  61.8 12.4 %all-to-all-start.1 = ((bf16[8,32,256]{2,1,0:T(8,128)(2,1)}), bf16[8,32,256]{2,1,0:T(8,128)(2,1)S(1)}, u32[]{:S(2)}, u32[]{:S(2)}) async-start(bf16[8,32,256]{2,1,0:T(8,128)(2,1)} %add_convert_fusion), calls=%async_computation.1 | async-start | bytes 262144 | tf_op jit(solution)/shard_map/all_to_all | solution.py:244

commit v11 on v10

--- a/solution.py
+++ b/solution.py
@@ -107,14 +107,18 @@
     scale = 4.0 / width * LOG2E
     bias = sq_feat[...] * (-scale)
     total = None if first else refs[count + 2][...]
+    whites, values = [], []
     for block, kern in zip(pieces_of(stacks, members), kerns):
         land, white = unpack(block, rank)
         land32 = land.astype(F32)
         sq_land = jnp.sum(land32 * land32, axis=1, keepdims=True) * (-scale)
         cross = jnp.dot(land, feat_t[...], preferred_element_type=F32)
-        value = jnp.exp2(cross * (2.0 * scale) + (bias + sq_land)).astype(BF16)
+        value = jnp.exp2(cross * (2.0 * scale) + (bias + sq_land))
         kern[...] = value
-        part = lax.dot_general(white, value, (((0,), (0,)), ((), ())), preferred_element_type=F32)
+        values.append(value.astype(BF16))
+        whites.append(white.T)
+    for white, value in zip(whites, values):
+        part = jnp.dot(white, value, preferred_element_type=F32)
         total = part if total is None else total + part
     for embed in embeds:
         embed[...] = total.astype(embed.dtype)
@@ -124,7 +128,7 @@
     width, toks = feat_t.shape
     count = sum(block.shape[0] for block in blocks) // members
     rows = sum(block.size for block in blocks) // (width + rank) // count
-    shapes = [shaped((rows, toks), BF16)] * count + [shaped((rank, toks), kind) for kind in ([F32, BF16] if last else [F32])]
+    shapes = [shaped((rows, toks), F32)] * count + [shaped((rank, toks), kind) for kind in ([F32, BF16] if last else [F32])]
     outs = call(functools.partial(forward_body, len(blocks), members, rank, not prior), shapes, *blocks, feat_t, sq_feat, *prior)
     return outs[:count], outs[count:]
 
@@ -175,9 +179,9 @@
         rows = land.shape[0]
         at = slice(i * rows, (i + 1) * rows)
         dkernel = jnp.dot(white, dembed[...], preferred_element_type=F32)
-        value = (dkernel * kerns[i][...].astype(F32)).astype(BF16)
+        value32 = dkernel * kerns[i][...]
+        value = value32.astype(BF16)
         coef[at, :] = value
-        value32 = value.astype(F32)
         part = jnp.sum(value32, axis=0, keepdims=True)
         total = part if total is None else total + part
         col_total = jnp.sum(value32, axis=1, keepdims=True)

time: 75.4 us -> 75.2 us (level)
  transfers between devices with their start and end apart: 15 -> 15, of which waited for: 9 -> 9; matrix products, arithmetic and copies ran while one was open for 2% -> 2% of each run, Pallas kernels for 7% -> 6%
where the time goes in v11:
time: 75.2 us; the launch traced here: 74.6 us
  waiting for transfers between devices  30.7 us (41%)
  starting transfers between devices  29 us (39%)
  Pallas kernels  9.41 us (13%)
  local copies, waits for them, and re-layouts  3.05 us (4%)
  other arithmetic  1.69 us (2%)
  between operations  0.78 us (1%)
    ppermute x9, starting transfers between devices, shift(): lax.ppermute(block, axes, [(i, (i + step) % size) for i in range(size)])  9.74 us
    all_to_all x1, starting transfers between devices, per_device(): lax.all_to_all(pack(landmarks, whitening, n_z), 'z', 0, 0, tiled=True)  8.48 us
    ppermute x9, waiting for transfers between devices, shift(): lax.ppermute(block, axes, [(i, (i + step) % size) for i in range(size)])  8.37 us
    all_to_all x1, waiting for transfers between devices, collect_at_once(): lax.all_to_all(pieces.astype(BF16), axes, 0, 0, tiled=True).astype(F32)  8.06 us
    pallas_call x9, Pallas kernels, call(): pl.pallas_call(body, out_shape=out_shape, in_specs=[WHOLE] * len(operands...  7.93 us
    ppermute x4, starting transfers between devices, partner(): return lax.ppermute(block, ring + ('c',), perm)  7.37 us
    all_to_all x1, waiting for transfers between devices, per_device(): lax.all_to_all(pack(landmarks, whitening, n_z), 'z', 0, 0, tiled=True)  7.35 us
    ppermute x4, waiting for transfers between devices, partner(): return lax.ppermute(block, ring + ('c',), perm)  6.91 us
  transfers between devices with their start and end apart: 15, of which 9 were waited for; matrix products, arithmetic and copies ran while one was open for 2% of the time, Pallas kernels for 6%

profile of v11, /device:TPU:24, one launch (start us, length us, event | category | flops | bytes accessed | tf_op | source)
XLA Modules:
  0.0 74.6 jit_solution(1159363653594501659)
XLA Ops:
  0.6 1.5 %shard_map.59 = bf16[8,40,256]{2,1,0:T(8,128)(2,1)} custom-call(bf16[32,256]{1,0:T(8,128)(2,1)} %landmarks.1, bf16[32,64]{1,0:T(8,128)(2,1)} %whitening.1), custom_call_target="tpu_custom_call" | custom-call | tf_op jit(solution)/shard_map/pallas_call | solution.py:51
  2.1 8.5 %all-to-all-start = ((bf16[8,40,256]{2,1,0:T(8,128)(2,1)}), bf16[8,40,256]{2,1,0:T(8,128)(2,1)S(1)}, u32[]{:S(2)}, u32[]{:S(2)}) async-start(bf16[8,40,256]{2,1,0:T(8,128)(2,1)} %shard_map.59), calls=%async_computation | async-start | bytes 327680 | tf_op jit(solution)/shard_map/all_to_all | solution.py:263
  10.6 0.0 copy-start
  10.6 1.2 %copy-done = bf16[2048,256]{1,0:T(8,128)(2,1)S(1)} copy-done((bf16[2048,256]{1,0:T(8,128)(2,1)S(1)}, bf16[2048,256]{1,0:T(8,128)(2,1)}, u32[]{:S(2)}) %copy-start) | copy-done | bytes 1048600
  11.8 0.9 %copy-done.1 = bf16[2048,64]{0,1:T(8,128)(2,1)S(1)} copy-done((bf16[2048,64]{0,1:T(8,128)(2,1)S(1)}, bf16[2048,64]{0,1:T(8,128)(2,1)}, u32[]{:S(2)}) %copy-start.1) | copy-done | bytes 262168
  12.8 0.2 shard_map.60
  13.0 7.3 %all-to-all-done.refs_0_ = bf16[8,40,256]{2,1,0:T(8,128)(2,1)S(1)} async-done(((bf16[8,40,256]{2,1,0:T(8,128)(2,1)}), bf16[8,40,256]{2,1,0:T(8,128)(2,1)S(1)}, u32[]{:S(2)}, u32[]{:S(2)}) %all-to-all-start) | async-done | bytes 163872 | tf_op jit(solution)/shard_map/all_to_all | solution.py:263
  20.4 0.7 collective-permute-start.2
  21.1 0.9 %collective-permute-start.1 = (bf16[8,40,256]{2,1,0:T(8,128)(2,1)S(1)}, bf16[8,40,256]{2,1,0:T(8,128)(2,1)S(1)}, u32[]{:S(2)}, u32[]{:S(2)}) collective-permute-start(bf16[8,40,256]{2,1,0:T(8,128)(2,1)S(1)} %all-to-all-done.refs_0_), channel_id=1, source_target_pairs={{0,32},{16,48},{32,0},{48,16},{1,33},{17,49},{33,1},{49,17},{2,34}... | collective-permute-start | bytes 491528 | tf_op jit(solution)/shard_map/ppermute | solution.py:227
  22.0 2.2 %collective-permute-start = (bf16[8,40,256]{2,1,0:T(8,128)(2,1)S(1)}, bf16[8,40,256]{2,1,0:T(8,128)(2,1)S(1)}, u32[]{:S(2)}, u32[]{:S(2)}) collective-permute-start(bf16[8,40,256]{2,1,0:T(8,128)(2,1)S(1)} %all-to-all-done.refs_0_), channel_id=1, source_target_pairs={{0,16},{16,32},{32,48},{48,0},{1,17},{17,33},{33,49},{49,1},{2,18}... | collective-permute-start | bytes 491528 | tf_op jit(solution)/shard_map/ppermute | solution.py:227
  24.2 0.5 shard_map.61
  24.7 4.4 %collective-permute-done.2.refs_2_.refs_3_ = bf16[8,40,256]{2,1,0:T(8,128)(2,1)S(1)} collective-permute-done((bf16[8,40,256]{2,1,0:T(8,128)(2,1)S(1)}, bf16[8,40,256]{2,1,0:T(8,128)(2,1)S(1)}, u32[]{:S(2)}, u32[]{:S(2)}) %collective-permute-start.2) | collective-permute-done | bytes 163872 | tf_op jit(solution)/shard_map/ppermute | solution.py:227
  29.1 0.0 collective-permute-done.1.refs_1_.refs_2_
  29.1 0.6 collective-permute-done.refs_0_.refs_1_
  29.8 0.1 pad_maximum_fusion
  29.9 0.1 collective-permute-start.3
  30.0 1.1 %shard_map.62 = (f32[256,1024]{1,0:T(8,128)S(1)}, f32[256,1024]{1,0:T(8,128)S(1)}, f32[256,1024]{1,0:T(8,128)S(1)}, f32[64,1024]{1,0:T(8,128)S(1)}) custom-call(bf16[8,40,256]{2,1,0:T(8,128)(2,1)S(1)} %collective-permute-done.refs_0_.refs_1_, bf16[8,40,256]{2,1,0:T(8,128)(2,1)S(1)} %collective-permute-done.1.refs_1_.refs_2_, ...), custom_call_target="tpu_custom_call" | custom-call | tf_op jit(solution)/shard_map/pallas_call | solution.py:20
  31.1 0.9 %collective-permute-done.3.refs_0_.refs_4_ = bf16[32,40,256]{2,1,0:T(8,128)(2,1)S(1)} collective-permute-done((bf16[32,40,256]{2,1,0:T(8,128)(2,1)S(1)}, bf16[32,40,256]{2,1,0:T(8,128)(2,1)S(1)}, u32[]{:S(2)}, u32[]{:S(2)}) %collective-permute-start.3) | collective-permute-done | bytes 655392 | tf_op jit(solution)/shard_map/ppermute | solution.py:227
  32.0 1.5 %shard_map.63 = (f32[256,1024]{1,0:T(8,128)S(1)}, f32[256,1024]{1,0:T(8,128)S(1)}, f32[256,1024]{1,0:T(8,128)S(1)}, f32[256,1024]{1,0:T(8,128)S(1)}, f32[64,1024...) custom-call(bf16[32,40,256]{2,1,0:T(8,128)(2,1)S(1)} %collective-permute-done.3.refs_0_.refs_4_, ...), custom_call_target="tpu_custom_call" | custom-call | tf_op jit(solution)/shard_map/pallas_call | solution.py:20
  33.6 1.6 %collective-permute-start.4 = (bf16[64,1024]{1,0:T(8,128)(2,1)S(1)}, bf16[64,1024]{1,0:T(8,128)(2,1)S(1)}, u32[]{:S(2)}, u32[]{:S(2)}) collective-permute-start(bf16[64,1024]{1,0:T(8,128)(2,1)S(1)} %get-tuple-element.57), channel_id=1, source_target_pairs={{0,64},{1,193},{64,0},{65,129},{128,192},{129,65},{192,128},{193,1... | collective-permute-start | bytes 393224 | tf_op jit(solution)/shard_map/ppermute | solution.py:233
  35.2 3.5 %collective-permute-done.4.other = bf16[64,1024]{1,0:T(8,128)(2,1)S(1)} collective-permute-done((bf16[64,1024]{1,0:T(8,128)(2,1)S(1)}, bf16[64,1024]{1,0:T(8,128)(2,1)S(1)}, u32[]{:S(2)}, u32[]{:S(2)}) %collective-permute-start.4) | collective-permute-done | bytes 131104 | tf_op jit(solution)/shard_map/ppermute | solution.py:233
  38.7 2.8 %collective-permute-start.5 = (bf16[64,1024]{1,0:T(8,128)(2,1)S(1)}, bf16[64,1024]{1,0:T(8,128)(2,1)S(1)}, u32[]{:S(2)}, u32[]{:S(2)}) collective-permute-start(bf16[64,1024]{1,0:T(8,128)(2,1)S(1)} %get-tuple-element.59), channel_id=1, source_target_pairs={{0,192},{1,65},{64,128},{65,1},{128,64},{129,193},{192,0},{193,129... | collective-permute-start | bytes 393224 | tf_op jit(solution)/shard_map/ppermute | solution.py:233
  41.5 3.4 %collective-permute-done.5.other = bf16[64,1024]{1,0:T(8,128)(2,1)S(1)} collective-permute-done((bf16[64,1024]{1,0:T(8,128)(2,1)S(1)}, bf16[64,1024]{1,0:T(8,128)(2,1)S(1)}, u32[]{:S(2)}, u32[]{:S(2)}) %collective-permute-start.5) | collective-permute-done | bytes 131104 | tf_op jit(solution)/shard_map/ppermute | solution.py:233
  45.0 0.1 shard_map.65.refs_5_.refs_8_
  45.1 1.5 %shard_map.66 = (bf16[1024,1024]{1,0:T(8,128)(2,1)S(1)}, bf16[1024,256]{1,0:T(8,128)(2,1)S(1)}, f32[1,1024]{1,0:T(1,128)S(1)}) custom-call(bf16[32,40,256]{2,1,0:T(8,128)(2,1)S(1)} %collective-permute-done.3.refs_0_.refs_4_, f32[256,1024]{1,0:T(8,128)S(1)} %get-tuple-element.62.refs_1_, f32[256,1024]{1,0:T(8,128)S(1)} %get-tuple-element.63.refs_2_, ...), custom_call_target="tpu_custom_call" | custom-call | tf_op jit(solution)/shard_map/pallas_call | solution.py:20
  46.6 0.1 collective-permute-start.9
  46.7 1.5 %shard_map.67 = (bf16[1024,1024]{1,0:T(8,128)(2,1)S(1)}, f32[1024,256]{1,0:T(8,128)S(1)}, f32[1,1024]{1,0:T(1,128)S(1)}) custom-call(bf16[8,40,256]{2,1,0:T(8,128)(2,1)S(1)} %all-to-all-done.refs_0_, bf16[8,40,256]{2,1,0:T(8,128)(2,1)S(1)} %collective-permute-done.refs_0_.refs_1_, bf16[8,40,256]{2,1,0:T(8,128)(2,1)S(1)} %collective-permute-done.1.refs_1_.refs_2_, ...), custom_call_target="tpu_custom_call" | custom-call | tf_op jit(solution)/shard_map/pallas_call | solution.py:20
  48.2 0.4 collective-permute-done.9
  48.6 0.2 fusion
  48.8 2.7 %collective-permute-start.12 = (bf16[8,32,256]{2,1,0:T(8,128)(2,1)S(1)}, bf16[8,32,256]{2,1,0:T(8,128)(2,1)S(1)}, u32[]{:S(2)}, u32[]{:S(2)}) collective-permute-start(bf16[8,32,256]{2,1,0:T(8,128)(2,1)S(1)} %bitcast.11), channel_id=1, source_target_pairs={{0,16},{16,32},{32,48},{48,0},{1,17},{17,33},{33,49},{49,1},{2,18}... | collective-permute-start | bytes 393224 | tf_op jit(solution)/shard_map/ppermute | solution.py:227
  51.5 0.0 collective-permute-start.10
  51.5 1.6 %collective-permute-start.11 = (bf16[8,32,256]{2,1,0:T(8,128)(2,1)S(1)}, bf16[8,32,256]{2,1,0:T(8,128)(2,1)S(1)}, u32[]{:S(2)}, u32[]{:S(2)}) collective-permute-start(bf16[8,32,256]{2,1,0:T(8,128)(2,1)S(1)} %bitcast.9), channel_id=1, source_target_pairs={{0,32},{16,48},{32,0},{48,16},{1,33},{17,49},{33,1},{49,17},{2,34}... | collective-permute-start | bytes 393224 | tf_op jit(solution)/shard_map/ppermute | solution.py:227
  53.1 1.3 %shard_map.68 = (f32[256,256]{1,0:T(8,128)S(1)}, bf16[256,256]{1,0:T(8,128)(2,1)S(1)}, bf16[256,256]{1,0:T(8,128)(2,1)S(1)}, bf16[256,256]{1,0:T(8,128)(2,1)S(1)}) custom-call(bf16[8,40,256]{2,1,0:T(8,128)(2,1)S(1)} %all-to-all-done.refs_0_, bf16[8,40,256]{2,1,0:T(8,128)(2,1)S(1)} %collective-permute-done.refs_0_.refs_1_, ...), custom_call_target="tpu_custom_call" | custom-call | tf_op jit(solution)/shard_map/pallas_call | solution.py:20
  54.4 0.4 collective-permute-start.6
  54.7 2.6 %collective-permute-start.7 = (bf16[256,256]{1,0:T(8,128)(2,1)S(1)}, bf16[256,256]{1,0:T(8,128)(2,1)S(1)}, u32[]{:S(2)}, u32[]{:S(2)}) collective-permute-start(bf16[256,256]{1,0:T(8,128)(2,1)S(1)} %get-tuple-element.72), channel_id=1, source_target_pairs={{0,192},{1,65},{64,128},{65,1},{128,64},{129,193},{192,0},{193,129... | collective-permute-start | bytes 393224 | tf_op jit(solution)/shard_map/ppermute | solution.py:233
  57.3 0.0 collective-permute-done.12
  57.3 1.5 %collective-permute-start.8 = (bf16[256,256]{1,0:T(8,128)(2,1)S(1)}, bf16[256,256]{1,0:T(8,128)(2,1)S(1)}, u32[]{:S(2)}, u32[]{:S(2)}) collective-permute-start(bf16[256,256]{1,0:T(8,128)(2,1)S(1)} %get-tuple-element.73), channel_id=1, source_target_pairs={{0,128},{64,192},{128,0},{192,64},{1,129},{65,193},{129,1},{193,65... | collective-permute-start | bytes 393224 | tf_op jit(solution)/shard_map/ppermute | solution.py:227
  58.8 2.0 %collective-permute-done.10 = bf16[8,32,256]{2,1,0:T(8,128)(2,1)S(1)} collective-permute-done((bf16[8,32,256]{2,1,0:T(8,128)(2,1)S(1)}, bf16[8,32,256]{2,1,0:T(8,128)(2,1)S(1)}, u32[]{:S(2)}, u32[]{:S(2)}) %collective-permute-start.10) | collective-permute-done | bytes 131104 | tf_op jit(solution)/shard_map/ppermute | solution.py:227
  60.8 0.0 collective-permute-done.11
  60.8 0.7 add_convert_fusion
  61.5 3.4 %all-to-all-start.1 = ((bf16[8,32,256]{2,1,0:T(8,128)(2,1)}), bf16[8,32,256]{2,1,0:T(8,128)(2,1)S(1)}, u32[]{:S(2)}, u32[]{:S(2)}) async-start(bf16[8,32,256]{2,1,0:T(8,128)(2,1)} %add_convert_fusion), calls=%async_computation.1 | async-start | bytes 262144 | tf_op jit(solution)/shard_map/all_to_all | solution.py:248
  64.9 0.0 collective-permute-done.6
  64.9 0.0 collective-permute-done.7
  64.9 0.0 collective-permute-done.8
  65.0 0.1 add_bitcast_fusion
  65.0 0.8 %copy.6 = f32[256,256]{1,0:T(8,128)} copy(f32[256,256]{0,1:T(8,128)S(1)} %add_bitcast_fusion) | data formatting | bytes 524288
  65.9 8.1 %all-to-all-done.1 = bf16[8,32,256]{2,1,0:T(8,128)(2,1)S(1)} async-done(((bf16[8,32,256]{2,1,0:T(8,128)(2,1)}), bf16[8,32,256]{2,1,0:T(8,128)(2,1)S(1)}, u32[]{:S(2)}, u32[]{:S(2)}) %all-to-all-start.1) | async-done | bytes 131104 | tf_op jit(solution)/shard_map/all_to_all | solution.py:248
  73.9 0.6 convert_reduce_fusion
  (4 shorter events, 0.1 us)
Async XLA Ops:
  2.1 18.2 %all-to-all-start = ((bf16[8,40,256]{2,1,0:T(8,128)(2,1)}), bf16[8,40,256]{2,1,0:T(8,128)(2,1)S(1)}, u32[]{:S(2)}, u32[]{:S(2)}) async-start(bf16[8,40,256]{2,1,0:T(8,128)(2,1)} %shard_map.59), calls=%async_computation | async-start | bytes 327680 | tf_op jit(solution)/shard_map/all_to_all | solution.py:263
  10.6 1.2 %copy-start = (bf16[2048,256]{1,0:T(8,128)(2,1)S(1)}, bf16[2048,256]{1,0:T(8,128)(2,1)}, u32[]{:S(2)}) copy-start(bf16[2048,256]{1,0:T(8,128)(2,1)} %features.1) | copy-start | bytes 3145732
  11.8 0.9 %copy-start.1 = (bf16[2048,64]{0,1:T(8,128)(2,1)S(1)}, bf16[2048,64]{0,1:T(8,128)(2,1)}, u32[]{:S(2)}) copy-start(bf16[2048,64]{0,1:T(8,128)(2,1)} %param.7) | copy-start | bytes 786436
  20.4 8.8 %collective-permute-start.2 = (bf16[8,40,256]{2,1,0:T(8,128)(2,1)S(1)}, bf16[8,40,256]{2,1,0:T(8,128)(2,1)S(1)}, u32[]{:S(2)}, u32[]{:S(2)}) collective-permute-start(bf16[8,40,256]{2,1,0:T(8,128)(2,1)S(1)} %all-to-all-done.refs_0_), channel_id=1, source_target_pairs={{0,48},{16,0},{32,16},{48,32},{1,49},{17,1},{33,17},{49,33},{2,50}... | collective-permute-start | bytes 491528 | tf_op jit(solution)/shard_map/ppermute | solution.py:227
  21.1 8.0 %collective-permute-start.1 = (bf16[8,40,256]{2,1,0:T(8,128)(2,1)S(1)}, bf16[8,40,256]{2,1,0:T(8,128)(2,1)S(1)}, u32[]{:S(2)}, u32[]{:S(2)}) collective-permute-start(bf16[8,40,256]{2,1,0:T(8,128)(2,1)S(1)} %all-to-all-done.refs_0_), channel_id=1, source_target_pairs={{0,32},{16,48},{32,0},{48,16},{1,33},{17,49},{33,1},{49,17},{2,34}... | collective-permute-start | bytes 491528 | tf_op jit(solution)/shard_map/ppermute | solution.py:227
  22.0 7.7 %collective-permute-start = (bf16[8,40,256]{2,1,0:T(8,128)(2,1)S(1)}, bf16[8,40,256]{2,1,0:T(8,128)(2,1)S(1)}, u32[]{:S(2)}, u32[]{:S(2)}) collective-permute-start(bf16[8,40,256]{2,1,0:T(8,128)(2,1)S(1)} %all-to-all-done.refs_0_), channel_id=1, source_target_pairs={{0,16},{16,32},{32,48},{48,0},{1,17},{17,33},{33,49},{49,1},{2,18}... | collective-permute-start | bytes 491528 | tf_op jit(solution)/shard_map/ppermute | solution.py:227
  29.9 2.2 %collective-permute-start.3 = (bf16[32,40,256]{2,1,0:T(8,128)(2,1)S(1)}, bf16[32,40,256]{2,1,0:T(8,128)(2,1)S(1)}, u32[]{:S(2)}, u32[]{:S(2)}) collective-permute-start(bf16[32,40,256]{2,1,0:T(8,128)(2,1)S(1)} %pad_maximum_fusion), channel_id=1, source_target_pairs={{0,1},{1,0},{2,3},{3,2},{4,5},{5,4},{6,7},{7,6},{8,9},{9,8},{10,11... | collective-permute-start | bytes 1966088 | tf_op jit(solution)/shard_map/ppermute | solution.py:227
  33.6 5.1 %collective-permute-start.4 = (bf16[64,1024]{1,0:T(8,128)(2,1)S(1)}, bf16[64,1024]{1,0:T(8,128)(2,1)S(1)}, u32[]{:S(2)}, u32[]{:S(2)}) collective-permute-start(bf16[64,1024]{1,0:T(8,128)(2,1)S(1)} %get-tuple-element.57), channel_id=1, source_target_pairs={{0,64},{1,193},{64,0},{65,129},{128,192},{129,65},{192,128},{193,1... | collective-permute-start | bytes 393224 | tf_op jit(solution)/shard_map/ppermute | solution.py:233
  38.7 6.3 %collective-permute-start.5 = (bf16[64,1024]{1,0:T(8,128)(2,1)S(1)}, bf16[64,1024]{1,0:T(8,128)(2,1)S(1)}, u32[]{:S(2)}, u32[]{:S(2)}) collective-permute-start(bf16[64,1024]{1,0:T(8,128)(2,1)S(1)} %get-tuple-element.59), channel_id=1, source_target_pairs={{0,192},{1,65},{64,128},{65,1},{128,64},{129,193},{192,0},{193,129... | collective-permute-start | bytes 393224 | tf_op jit(solution)/shard_map/ppermute | solution.py:233
  46.6 2.0 %collective-permute-start.9 = (bf16[1024,256]{1,0:T(8,128)(2,1)S(1)}, bf16[1024,256]{1,0:T(8,128)(2,1)S(1)}, u32[]{:S(2)}, u32[]{:S(2)}) collective-permute-start(bf16[1024,256]{1,0:T(8,128)(2,1)S(1)} %get-tuple-element.75), channel_id=1, source_target_pairs={{0,1},{1,0},{2,3},{3,2},{4,5},{5,4},{6,7},{7,6},{8,9},{9,8},{10,11... | collective-permute-start | bytes 1572872 | tf_op jit(solution)/shard_map/ppermute | solution.py:227
  48.8 8.5 %collective-permute-start.12 = (bf16[8,32,256]{2,1,0:T(8,128)(2,1)S(1)}, bf16[8,32,256]{2,1,0:T(8,128)(2,1)S(1)}, u32[]{:S(2)}, u32[]{:S(2)}) collective-permute-start(bf16[8,32,256]{2,1,0:T(8,128)(2,1)S(1)} %bitcast.11), channel_id=1, source_target_pairs={{0,16},{16,32},{32,48},{48,0},{1,17},{17,33},{33,49},{49,1},{2,18}... | collective-permute-start | bytes 393224 | tf_op jit(solution)/shard_map/ppermute | solution.py:227
  51.5 9.3 %collective-permute-start.10 = (bf16[8,32,256]{2,1,0:T(8,128)(2,1)S(1)}, bf16[8,32,256]{2,1,0:T(8,128)(2,1)S(1)}, u32[]{:S(2)}, u32[]{:S(2)}) collective-permute-start(bf16[8,32,256]{2,1,0:T(8,128)(2,1)S(1)} %bitcast.10), channel_id=1, source_target_pairs={{0,48},{16,0},{32,16},{48,32},{1,49},{17,1},{33,17},{49,33},{2,50}... | collective-permute-start | bytes 393224 | tf_op jit(solution)/shard_map/ppermute | solution.py:227
  51.5 9.3 %collective-permute-start.11 = (bf16[8,32,256]{2,1,0:T(8,128)(2,1)S(1)}, bf16[8,32,256]{2,1,0:T(8,128)(2,1)S(1)}, u32[]{:S(2)}, u32[]{:S(2)}) collective-permute-start(bf16[8,32,256]{2,1,0:T(8,128)(2,1)S(1)} %bitcast.9), channel_id=1, source_target_pairs={{0,32},{16,48},{32,0},{48,16},{1,33},{17,49},{33,1},{49,17},{2,34}... | collective-permute-start | bytes 393224 | tf_op jit(solution)/shard_map/ppermute | solution.py:227
  54.4 10.6 %collective-permute-start.6 = (bf16[256,256]{1,0:T(8,128)(2,1)S(1)}, bf16[256,256]{1,0:T(8,128)(2,1)S(1)}, u32[]{:S(2)}, u32[]{:S(2)}) collective-permute-start(bf16[256,256]{1,0:T(8,128)(2,1)S(1)} %get-tuple-element.71), channel_id=1, source_target_pairs={{0,64},{1,193},{64,0},{65,129},{128,192},{129,65},{192,128},{193,1... | collective-permute-start | bytes 393224 | tf_op jit(solution)/shard_map/ppermute | solution.py:233
  54.7 10.2 %collective-permute-start.7 = (bf16[256,256]{1,0:T(8,128)(2,1)S(1)}, bf16[256,256]{1,0:T(8,128)(2,1)S(1)}, u32[]{:S(2)}, u32[]{:S(2)}) collective-permute-start(bf16[256,256]{1,0:T(8,128)(2,1)S(1)} %get-tuple-element.72), channel_id=1, source_target_pairs={{0,192},{1,65},{64,128},{65,1},{128,64},{129,193},{192,0},{193,129... | collective-permute-start | bytes 393224 | tf_op jit(solution)/shard_map/ppermute | solution.py:233
  57.3 7.6 %collective-permute-start.8 = (bf16[256,256]{1,0:T(8,128)(2,1)S(1)}, bf16[256,256]{1,0:T(8,128)(2,1)S(1)}, u32[]{:S(2)}, u32[]{:S(2)}) collective-permute-start(bf16[256,256]{1,0:T(8,128)(2,1)S(1)} %get-tuple-element.73), channel_id=1, source_target_pairs={{0,128},{64,192},{128,0},{192,64},{1,129},{65,193},{129,1},{193,65... | collective-permute-start | bytes 393224 | tf_op jit(solution)/shard_map/ppermute | solution.py:227
  61.5 12.4 %all-to-all-start.1 = ((bf16[8,32,256]{2,1,0:T(8,128)(2,1)}), bf16[8,32,256]{2,1,0:T(8,128)(2,1)S(1)}, u32[]{:S(2)}, u32[]{:S(2)}) async-start(bf16[8,32,256]{2,1,0:T(8,128)(2,1)} %add_convert_fusion), calls=%async_computation.1 | async-start | bytes 262144 | tf_op jit(solution)/shard_map/all_to_all | solution.py:248

commit v12 on v11

--- a/solution.py
+++ b/solution.py
@@ -152,7 +152,7 @@
     return call(functools.partial(pair_sum_body, places), shapes, share, other)
 
 
-def norm_body(factor, places, share, other, cot, out):
+def norm_backward(factor, places, share, other, cot, out):
     own = cot.shape[1] // places
     for p in range(places):
         at = slice(p * own, (p + 1) * own)
@@ -162,10 +162,6 @@
         normed = embed * scale
         grad = scale * (upstream - normed * jnp.mean(upstream * normed, axis=0, keepdims=True))
         out[:, at] = (factor * grad).astype(BF16)
-
-
-def norm_backward(share, other, cot, factor, places):
-    return call(functools.partial(norm_body, factor, places), shaped(cot.shape, BF16), share, other, cot)
 
 
 def backward_body(count, members, rank, first, *refs):
@@ -190,12 +186,28 @@
     row_total[...] = total
 
 
-def backward(blocks, members, kerns, dembed, feat, prior, kind):
+def backward_first_body(count, members, rank, factor, places, *refs):
+    *ins, share, other, cot, feat, coef, land_grad, row_total, dembed = refs
+    norm_backward(factor, places, share, other, cot, dembed)
+    backward_body(count, members, rank, True, *ins, dembed, feat, coef, land_grad, row_total)
+
+
+def backward_shapes(kerns, feat, kind):
     toks, width = feat.shape
     rows = sum(kern.shape[0] for kern in kerns)
-    shapes = [shaped((rows, toks), BF16), shaped((rows, width), kind), shaped((1, toks), F32)]
-    body = functools.partial(backward_body, len(blocks), members, dembed.shape[0], not prior)
-    return call(body, shapes, *blocks, *kerns, dembed, feat, *prior)
+    return [shaped((rows, toks), BF16), shaped((rows, width), kind), shaped((1, toks), F32)]
+
+
+def backward_first(blocks, members, kerns, shares, cot, feat, factor, places):
+    rank = cot.shape[0]
+    body = functools.partial(backward_first_body, len(blocks), members, rank, factor, places)
+    shapes = backward_shapes(kerns, feat, BF16) + [shaped(cot.shape, BF16)]
+    return call(body, shapes, *blocks, *kerns, *shares, cot, feat)
+
+
+def backward(blocks, members, kerns, dembed, feat, prior):
+    body = functools.partial(backward_body, len(blocks), members, dembed.shape[0], False)
+    return call(body, backward_shapes(kerns, feat, F32), *blocks, *kerns, dembed, feat, prior)
 
 
 def feature_body(count, members, coefs, rank, *refs):
@@ -273,10 +285,9 @@
     kern_theirs, (embed, share) = forward(theirs, n_z, feat_t, sq_feat, embed, True, rank)
     kern_mine = kern_own + kern_mine
     embed, share = pair_sum(embed, partner(share, X, 0), n_x)
-    dembed = norm_backward(embed, partner(share, X, 1), cot, -gamma, n_x)
-
-    coef_theirs, land_theirs, row_total = backward(theirs, n_z, kern_theirs, dembed, feat, [], BF16)
-    coef_mine, land_mine, row_total = backward(mine, n_z, kern_mine, dembed, feat, [row_total], F32)
+    shares = [embed, partner(share, X, 1)]
+    coef_theirs, land_theirs, row_total, dembed = backward_first(theirs, n_z, kern_theirs, shares, cot, feat, -gamma, n_x)
+    coef_mine, land_mine, row_total = backward(mine, n_z, kern_mine, dembed, feat, row_total)
     land_share = (land_mine + shift(land_theirs, "c", 1).astype(F32)).reshape(n_y, n_z, rows, width)
     land_share = collect(land_share, Y, -1)
 

time: 75.2 us -> 75 us (level)
    pallas_call x9 -> x8, Pallas kernels: 7.93 us -> 7.76 us  [call(): pl.pallas_call(body, out_shape=out_shape, in_specs=[WHOLE] * len(operands...]
where the time goes in v12:
time: 75 us; the launch traced here: 74.4 us
  waiting for transfers between devices  30.7 us (41%)
  starting transfers between devices  29 us (39%)
  Pallas kernels  9.24 us (12%)
  local copies, waits for them, and re-layouts  3.05 us (4%)
  other arithmetic  1.65 us (2%)
  between operations  0.78 us (1%)
    ppermute x9, starting transfers between devices, shift(): lax.ppermute(block, axes, [(i, (i + step) % size) for i in range(size)])  9.75 us
    all_to_all x1, starting transfers between devices, per_device(): lax.all_to_all(pack(landmarks, whitening, n_z), 'z', 0, 0, tiled=True)  8.48 us
    ppermute x9, waiting for transfers between devices, shift(): lax.ppermute(block, axes, [(i, (i + step) % size) for i in range(size)])  8.38 us
    all_to_all x1, waiting for transfers between devices, collect_at_once(): lax.all_to_all(pieces.astype(BF16), axes, 0, 0, tiled=True).astype(F32)  8.06 us
    pallas_call x8, Pallas kernels, call(): pl.pallas_call(body, out_shape=out_shape, in_specs=[WHOLE] * len(operands...  7.76 us
    ppermute x4, starting transfers between devices, partner(): return lax.ppermute(block, ring + ('c',), perm)  7.37 us
    all_to_all x1, waiting for transfers between devices, per_device(): lax.all_to_all(pack(landmarks, whitening, n_z), 'z', 0, 0, tiled=True)  7.35 us
    ppermute x4, waiting for transfers between devices, partner(): return lax.ppermute(block, ring + ('c',), perm)  6.9 us
  transfers between devices with their start and end apart: 15, of which 9 were waited for; matrix products, arithmetic and copies ran while one was open for 2% of the time, Pallas kernels for 6%

profile of v12, /device:TPU:24, one launch (start us, length us, event | category | flops | bytes accessed | tf_op | source)
XLA Modules:
  0.0 74.4 jit_solution(15385650606650752852)
XLA Ops:
  0.6 1.5 %shard_map.59 = bf16[8,40,256]{2,1,0:T(8,128)(2,1)} custom-call(bf16[32,256]{1,0:T(8,128)(2,1)} %landmarks.1, bf16[32,64]{1,0:T(8,128)(2,1)} %whitening.1), custom_call_target="tpu_custom_call" | custom-call | tf_op jit(solution)/shard_map/pallas_call | solution.py:51
  2.1 8.5 %all-to-all-start = ((bf16[8,40,256]{2,1,0:T(8,128)(2,1)}), bf16[8,40,256]{2,1,0:T(8,128)(2,1)S(1)}, u32[]{:S(2)}, u32[]{:S(2)}) async-start(bf16[8,40,256]{2,1,0:T(8,128)(2,1)} %shard_map.59), calls=%async_computation | async-start | bytes 327680 | tf_op jit(solution)/shard_map/all_to_all | solution.py:275
  10.6 0.0 copy-start
  10.6 1.2 %copy-done = bf16[2048,256]{1,0:T(8,128)(2,1)S(1)} copy-done((bf16[2048,256]{1,0:T(8,128)(2,1)S(1)}, bf16[2048,256]{1,0:T(8,128)(2,1)}, u32[]{:S(2)}) %copy-start) | copy-done | bytes 1048600
  11.8 0.0 copy-start.1
  11.8 0.9 %copy-done.1 = bf16[2048,64]{0,1:T(8,128)(2,1)S(1)} copy-done((bf16[2048,64]{0,1:T(8,128)(2,1)S(1)}, bf16[2048,64]{0,1:T(8,128)(2,1)}, u32[]{:S(2)}) %copy-start.1) | copy-done | bytes 262168
  12.8 0.2 shard_map.60
  13.0 7.3 %all-to-all-done.refs_0_ = bf16[8,40,256]{2,1,0:T(8,128)(2,1)S(1)} async-done(((bf16[8,40,256]{2,1,0:T(8,128)(2,1)}), bf16[8,40,256]{2,1,0:T(8,128)(2,1)S(1)}, u32[]{:S(2)}, u32[]{:S(2)}) %all-to-all-start) | async-done | bytes 163872 | tf_op jit(solution)/shard_map/all_to_all | solution.py:275
  20.4 0.7 collective-permute-start.2
  21.1 0.9 %collective-permute-start.1 = (bf16[8,40,256]{2,1,0:T(8,128)(2,1)S(1)}, bf16[8,40,256]{2,1,0:T(8,128)(2,1)S(1)}, u32[]{:S(2)}, u32[]{:S(2)}) collective-permute-start(bf16[8,40,256]{2,1,0:T(8,128)(2,1)S(1)} %all-to-all-done.refs_0_), channel_id=1, source_target_pairs={{0,32},{16,48},{32,0},{48,16},{1,33},{17,49},{33,1},{49,17},{2,34}... | collective-permute-start | bytes 491528 | tf_op jit(solution)/shard_map/ppermute | solution.py:239
  22.0 2.2 %collective-permute-start = (bf16[8,40,256]{2,1,0:T(8,128)(2,1)S(1)}, bf16[8,40,256]{2,1,0:T(8,128)(2,1)S(1)}, u32[]{:S(2)}, u32[]{:S(2)}) collective-permute-start(bf16[8,40,256]{2,1,0:T(8,128)(2,1)S(1)} %all-to-all-done.refs_0_), channel_id=1, source_target_pairs={{0,16},{16,32},{32,48},{48,0},{1,17},{17,33},{33,49},{49,1},{2,18}... | collective-permute-start | bytes 491528 | tf_op jit(solution)/shard_map/ppermute | solution.py:239
  24.2 0.5 shard_map.61
  24.7 4.4 %collective-permute-done.2.refs_2_.refs_3_ = bf16[8,40,256]{2,1,0:T(8,128)(2,1)S(1)} collective-permute-done((bf16[8,40,256]{2,1,0:T(8,128)(2,1)S(1)}, bf16[8,40,256]{2,1,0:T(8,128)(2,1)S(1)}, u32[]{:S(2)}, u32[]{:S(2)}) %collective-permute-start.2) | collective-permute-done | bytes 163872 | tf_op jit(solution)/shard_map/ppermute | solution.py:239
  29.1 0.0 collective-permute-done.1.refs_1_.refs_2_
  29.1 0.6 collective-permute-done.refs_0_.refs_1_
  29.8 0.1 pad_maximum_fusion
  29.9 0.1 collective-permute-start.3
  30.0 1.2 %shard_map.62 = (f32[256,1024]{1,0:T(8,128)S(1)}, f32[256,1024]{1,0:T(8,128)S(1)}, f32[256,1024]{1,0:T(8,128)S(1)}, f32[64,1024]{1,0:T(8,128)S(1)}) custom-call(bf16[8,40,256]{2,1,0:T(8,128)(2,1)S(1)} %collective-permute-done.refs_0_.refs_1_, bf16[8,40,256]{2,1,0:T(8,128)(2,1)S(1)} %collective-permute-done.1.refs_1_.refs_2_, ...), custom_call_target="tpu_custom_call" | custom-call | tf_op jit(solution)/shard_map/pallas_call | solution.py:20
  31.1 0.9 %collective-permute-done.3.refs_0_.refs_4_ = bf16[32,40,256]{2,1,0:T(8,128)(2,1)S(1)} collective-permute-done((bf16[32,40,256]{2,1,0:T(8,128)(2,1)S(1)}, bf16[32,40,256]{2,1,0:T(8,128)(2,1)S(1)}, u32[]{:S(2)}, u32[]{:S(2)}) %collective-permute-start.3) | collective-permute-done | bytes 655392 | tf_op jit(solution)/shard_map/ppermute | solution.py:239
  32.0 1.5 %shard_map.63 = (f32[256,1024]{1,0:T(8,128)S(1)}, f32[256,1024]{1,0:T(8,128)S(1)}, f32[256,1024]{1,0:T(8,128)S(1)}, f32[256,1024]{1,0:T(8,128)S(1)}, f32[64,1024...) custom-call(bf16[32,40,256]{2,1,0:T(8,128)(2,1)S(1)} %collective-permute-done.3.refs_0_.refs_4_, ...), custom_call_target="tpu_custom_call" | custom-call | tf_op jit(solution)/shard_map/pallas_call | solution.py:20
  33.6 1.6 %collective-permute-start.4 = (bf16[64,1024]{1,0:T(8,128)(2,1)S(1)}, bf16[64,1024]{1,0:T(8,128)(2,1)S(1)}, u32[]{:S(2)}, u32[]{:S(2)}) collective-permute-start(bf16[64,1024]{1,0:T(8,128)(2,1)S(1)} %get-tuple-element.62), channel_id=1, source_target_pairs={{0,64},{1,193},{64,0},{65,129},{128,192},{129,65},{192,128},{193,1... | collective-permute-start | bytes 393224 | tf_op jit(solution)/shard_map/ppermute | solution.py:245
  35.2 3.5 %collective-permute-done.4.other = bf16[64,1024]{1,0:T(8,128)(2,1)S(1)} collective-permute-done((bf16[64,1024]{1,0:T(8,128)(2,1)S(1)}, bf16[64,1024]{1,0:T(8,128)(2,1)S(1)}, u32[]{:S(2)}, u32[]{:S(2)}) %collective-permute-start.4) | collective-permute-done | bytes 131104 | tf_op jit(solution)/shard_map/ppermute | solution.py:245
  38.7 2.8 %collective-permute-start.5 = (bf16[64,1024]{1,0:T(8,128)(2,1)S(1)}, bf16[64,1024]{1,0:T(8,128)(2,1)S(1)}, u32[]{:S(2)}, u32[]{:S(2)}) collective-permute-start(bf16[64,1024]{1,0:T(8,128)(2,1)S(1)} %get-tuple-element.64), channel_id=1, source_target_pairs={{0,192},{1,65},{64,128},{65,1},{128,64},{129,193},{192,0},{193,129... | collective-permute-start | bytes 393224 | tf_op jit(solution)/shard_map/ppermute | solution.py:245
  41.5 3.4 %collective-permute-done.5.refs_6_ = bf16[64,1024]{1,0:T(8,128)(2,1)S(1)} collective-permute-done((bf16[64,1024]{1,0:T(8,128)(2,1)S(1)}, bf16[64,1024]{1,0:T(8,128)(2,1)S(1)}, u32[]{:S(2)}, u32[]{:S(2)}) %collective-permute-start.5) | collective-permute-done | bytes 131104 | tf_op jit(solution)/shard_map/ppermute | solution.py:245
  44.9 1.5 %shard_map.65 = (bf16[1024,1024]{1,0:T(8,128)(2,1)S(1)}, bf16[1024,256]{1,0:T(8,128)(2,1)S(1)}, f32[1,1024]{1,0:T(1,128)S(1)}, bf16[64,1024]{1,0:T(8,128)(2,1)S(1)}) custom-call(bf16[32,40,256]{2,1,0:T(8,128)(2,1)S(1)} %collective-permute-done.3.refs_0_.refs_4_, f32[256,1024]{1,0:T(8,128)S(1)} %get-tuple-element.57.refs_1_, ...), custom_call_target="tpu_custom_call" | custom-call | tf_op jit(solution)/shard_map/pallas_call | solution.py:20
  46.5 0.1 collective-permute-start.9
  46.6 1.5 %shard_map.66 = (bf16[1024,1024]{1,0:T(8,128)(2,1)S(1)}, f32[1024,256]{1,0:T(8,128)S(1)}, f32[1,1024]{1,0:T(1,128)S(1)}) custom-call(bf16[8,40,256]{2,1,0:T(8,128)(2,1)S(1)} %all-to-all-done.refs_0_, bf16[8,40,256]{2,1,0:T(8,128)(2,1)S(1)} %collective-permute-done.refs_0_.refs_1_, bf16[8,40,256]{2,1,0:T(8,128)(2,1)S(1)} %collective-permute-done.1.refs_1_.refs_2_, ...), custom_call_target="tpu_custom_call" | custom-call | tf_op jit(solution)/shard_map/pallas_call | solution.py:20
  48.1 0.4 collective-permute-done.9
  48.5 0.1 fusion
  48.6 2.7 %collective-permute-start.12 = (bf16[8,32,256]{2,1,0:T(8,128)(2,1)S(1)}, bf16[8,32,256]{2,1,0:T(8,128)(2,1)S(1)}, u32[]{:S(2)}, u32[]{:S(2)}) collective-permute-start(bf16[8,32,256]{2,1,0:T(8,128)(2,1)S(1)} %bitcast.11), channel_id=1, source_target_pairs={{0,16},{16,32},{32,48},{48,0},{1,17},{17,33},{33,49},{49,1},{2,18}... | collective-permute-start | bytes 393224 | tf_op jit(solution)/shard_map/ppermute | solution.py:239
  51.3 0.0 collective-permute-start.10
  51.3 1.6 %collective-permute-start.11 = (bf16[8,32,256]{2,1,0:T(8,128)(2,1)S(1)}, bf16[8,32,256]{2,1,0:T(8,128)(2,1)S(1)}, u32[]{:S(2)}, u32[]{:S(2)}) collective-permute-start(bf16[8,32,256]{2,1,0:T(8,128)(2,1)S(1)} %bitcast.9), channel_id=1, source_target_pairs={{0,32},{16,48},{32,0},{48,16},{1,33},{17,49},{33,1},{49,17},{2,34}... | collective-permute-start | bytes 393224 | tf_op jit(solution)/shard_map/ppermute | solution.py:239
  52.9 1.3 %shard_map.67 = (f32[256,256]{1,0:T(8,128)S(1)}, bf16[256,256]{1,0:T(8,128)(2,1)S(1)}, bf16[256,256]{1,0:T(8,128)(2,1)S(1)}, bf16[256,256]{1,0:T(8,128)(2,1)S(1)}) custom-call(bf16[8,40,256]{2,1,0:T(8,128)(2,1)S(1)} %all-to-all-done.refs_0_, bf16[8,40,256]{2,1,0:T(8,128)(2,1)S(1)} %collective-permute-done.refs_0_.refs_1_, ...), custom_call_target="tpu_custom_call" | custom-call | tf_op jit(solution)/shard_map/pallas_call | solution.py:20
  54.2 0.4 collective-permute-start.6
  54.5 2.6 %collective-permute-start.7 = (bf16[256,256]{1,0:T(8,128)(2,1)S(1)}, bf16[256,256]{1,0:T(8,128)(2,1)S(1)}, u32[]{:S(2)}, u32[]{:S(2)}) collective-permute-start(bf16[256,256]{1,0:T(8,128)(2,1)S(1)} %get-tuple-element.74), channel_id=1, source_target_pairs={{0,192},{1,65},{64,128},{65,1},{128,64},{129,193},{192,0},{193,129... | collective-permute-start | bytes 393224 | tf_op jit(solution)/shard_map/ppermute | solution.py:245
  57.1 0.0 collective-permute-done.12
  57.1 1.5 %collective-permute-start.8 = (bf16[256,256]{1,0:T(8,128)(2,1)S(1)}, bf16[256,256]{1,0:T(8,128)(2,1)S(1)}, u32[]{:S(2)}, u32[]{:S(2)}) collective-permute-start(bf16[256,256]{1,0:T(8,128)(2,1)S(1)} %get-tuple-element.75), channel_id=1, source_target_pairs={{0,128},{64,192},{128,0},{192,64},{1,129},{65,193},{129,1},{193,65... | collective-permute-start | bytes 393224 | tf_op jit(solution)/shard_map/ppermute | solution.py:239
  58.6 2.0 %collective-permute-done.10 = bf16[8,32,256]{2,1,0:T(8,128)(2,1)S(1)} collective-permute-done((bf16[8,32,256]{2,1,0:T(8,128)(2,1)S(1)}, bf16[8,32,256]{2,1,0:T(8,128)(2,1)S(1)}, u32[]{:S(2)}, u32[]{:S(2)}) %collective-permute-start.10) | collective-permute-done | bytes 131104 | tf_op jit(solution)/shard_map/ppermute | solution.py:239
  60.6 0.0 collective-permute-done.11
  60.6 0.7 add_convert_fusion
  61.4 3.4 %all-to-all-start.1 = ((bf16[8,32,256]{2,1,0:T(8,128)(2,1)}), bf16[8,32,256]{2,1,0:T(8,128)(2,1)S(1)}, u32[]{:S(2)}, u32[]{:S(2)}) async-start(bf16[8,32,256]{2,1,0:T(8,128)(2,1)} %add_convert_fusion), calls=%async_computation.1 | async-start | bytes 262144 | tf_op jit(solution)/shard_map/all_to_all | solution.py:260
  64.7 0.0 collective-permute-done.6
  64.7 0.0 collective-permute-done.7
  64.8 0.0 collective-permute-done.8
  64.8 0.1 add_bitcast_fusion
  64.8 0.8 %copy.6 = f32[256,256]{1,0:T(8,128)} copy(f32[256,256]{0,1:T(8,128)S(1)} %add_bitcast_fusion) | data formatting | bytes 524288
  65.7 8.1 %all-to-all-done.1 = bf16[8,32,256]{2,1,0:T(8,128)(2,1)S(1)} async-done(((bf16[8,32,256]{2,1,0:T(8,128)(2,1)}), bf16[8,32,256]{2,1,0:T(8,128)(2,1)S(1)}, u32[]{:S(2)}, u32[]{:S(2)}) %all-to-all-start.1) | async-done | bytes 131104 | tf_op jit(solution)/shard_map/all_to_all | solution.py:260
  73.7 0.6 convert_reduce_fusion
  (3 shorter events, 0.1 us)
Async XLA Ops:
  2.1 18.2 %all-to-all-start = ((bf16[8,40,256]{2,1,0:T(8,128)(2,1)}), bf16[8,40,256]{2,1,0:T(8,128)(2,1)S(1)}, u32[]{:S(2)}, u32[]{:S(2)}) async-start(bf16[8,40,256]{2,1,0:T(8,128)(2,1)} %shard_map.59), calls=%async_computation | async-start | bytes 327680 | tf_op jit(solution)/shard_map/all_to_all | solution.py:275
  10.6 1.2 %copy-start = (bf16[2048,256]{1,0:T(8,128)(2,1)S(1)}, bf16[2048,256]{1,0:T(8,128)(2,1)}, u32[]{:S(2)}) copy-start(bf16[2048,256]{1,0:T(8,128)(2,1)} %features.1) | copy-start | bytes 3145732
  11.8 0.9 %copy-start.1 = (bf16[2048,64]{0,1:T(8,128)(2,1)S(1)}, bf16[2048,64]{0,1:T(8,128)(2,1)}, u32[]{:S(2)}) copy-start(bf16[2048,64]{0,1:T(8,128)(2,1)} %param.7) | copy-start | bytes 786436
  20.4 8.8 %collective-permute-start.2 = (bf16[8,40,256]{2,1,0:T(8,128)(2,1)S(1)}, bf16[8,40,256]{2,1,0:T(8,128)(2,1)S(1)}, u32[]{:S(2)}, u32[]{:S(2)}) collective-permute-start(bf16[8,40,256]{2,1,0:T(8,128)(2,1)S(1)} %all-to-all-done.refs_0_), channel_id=1, source_target_pairs={{0,48},{16,0},{32,16},{48,32},{1,49},{17,1},{33,17},{49,33},{2,50}... | collective-permute-start | bytes 491528 | tf_op jit(solution)/shard_map/ppermute | solution.py:239
  21.1 8.0 %collective-permute-start.1 = (bf16[8,40,256]{2,1,0:T(8,128)(2,1)S(1)}, bf16[8,40,256]{2,1,0:T(8,128)(2,1)S(1)}, u32[]{:S(2)}, u32[]{:S(2)}) collective-permute-start(bf16[8,40,256]{2,1,0:T(8,128)(2,1)S(1)} %all-to-all-done.refs_0_), channel_id=1, source_target_pairs={{0,32},{16,48},{32,0},{48,16},{1,33},{17,49},{33,1},{49,17},{2,34}... | collective-permute-start | bytes 491528 | tf_op jit(solution)/shard_map/ppermute | solution.py:239
  22.0 7.7 %collective-permute-start = (bf16[8,40,256]{2,1,0:T(8,128)(2,1)S(1)}, bf16[8,40,256]{2,1,0:T(8,128)(2,1)S(1)}, u32[]{:S(2)}, u32[]{:S(2)}) collective-permute-start(bf16[8,40,256]{2,1,0:T(8,128)(2,1)S(1)} %all-to-all-done.refs_0_), channel_id=1, source_target_pairs={{0,16},{16,32},{32,48},{48,0},{1,17},{17,33},{33,49},{49,1},{2,18}... | collective-permute-start | bytes 491528 | tf_op jit(solution)/shard_map/ppermute | solution.py:239
  29.9 2.2 %collective-permute-start.3 = (bf16[32,40,256]{2,1,0:T(8,128)(2,1)S(1)}, bf16[32,40,256]{2,1,0:T(8,128)(2,1)S(1)}, u32[]{:S(2)}, u32[]{:S(2)}) collective-permute-start(bf16[32,40,256]{2,1,0:T(8,128)(2,1)S(1)} %pad_maximum_fusion), channel_id=1, source_target_pairs={{0,1},{1,0},{2,3},{3,2},{4,5},{5,4},{6,7},{7,6},{8,9},{9,8},{10,11... | collective-permute-start | bytes 1966088 | tf_op jit(solution)/shard_map/ppermute | solution.py:239
  33.6 5.1 %collective-permute-start.4 = (bf16[64,1024]{1,0:T(8,128)(2,1)S(1)}, bf16[64,1024]{1,0:T(8,128)(2,1)S(1)}, u32[]{:S(2)}, u32[]{:S(2)}) collective-permute-start(bf16[64,1024]{1,0:T(8,128)(2,1)S(1)} %get-tuple-element.62), channel_id=1, source_target_pairs={{0,64},{1,193},{64,0},{65,129},{128,192},{129,65},{192,128},{193,1... | collective-permute-start | bytes 393224 | tf_op jit(solution)/shard_map/ppermute | solution.py:245
  38.7 6.3 %collective-permute-start.5 = (bf16[64,1024]{1,0:T(8,128)(2,1)S(1)}, bf16[64,1024]{1,0:T(8,128)(2,1)S(1)}, u32[]{:S(2)}, u32[]{:S(2)}) collective-permute-start(bf16[64,1024]{1,0:T(8,128)(2,1)S(1)} %get-tuple-element.64), channel_id=1, source_target_pairs={{0,192},{1,65},{64,128},{65,1},{128,64},{129,193},{192,0},{193,129... | collective-permute-start | bytes 393224 | tf_op jit(solution)/shard_map/ppermute | solution.py:245
  46.5 2.0 %collective-permute-start.9 = (bf16[1024,256]{1,0:T(8,128)(2,1)S(1)}, bf16[1024,256]{1,0:T(8,128)(2,1)S(1)}, u32[]{:S(2)}, u32[]{:S(2)}) collective-permute-start(bf16[1024,256]{1,0:T(8,128)(2,1)S(1)} %get-tuple-element.77), channel_id=1, source_target_pairs={{0,1},{1,0},{2,3},{3,2},{4,5},{5,4},{6,7},{7,6},{8,9},{9,8},{10,11... | collective-permute-start | bytes 1572872 | tf_op jit(solution)/shard_map/ppermute | solution.py:239
  48.6 8.5 %collective-permute-start.12 = (bf16[8,32,256]{2,1,0:T(8,128)(2,1)S(1)}, bf16[8,32,256]{2,1,0:T(8,128)(2,1)S(1)}, u32[]{:S(2)}, u32[]{:S(2)}) collective-permute-start(bf16[8,32,256]{2,1,0:T(8,128)(2,1)S(1)} %bitcast.11), channel_id=1, source_target_pairs={{0,16},{16,32},{32,48},{48,0},{1,17},{17,33},{33,49},{49,1},{2,18}... | collective-permute-start | bytes 393224 | tf_op jit(solution)/shard_map/ppermute | solution.py:239
  51.3 9.3 %collective-permute-start.10 = (bf16[8,32,256]{2,1,0:T(8,128)(2,1)S(1)}, bf16[8,32,256]{2,1,0:T(8,128)(2,1)S(1)}, u32[]{:S(2)}, u32[]{:S(2)}) collective-permute-start(bf16[8,32,256]{2,1,0:T(8,128)(2,1)S(1)} %bitcast.10), channel_id=1, source_target_pairs={{0,48},{16,0},{32,16},{48,32},{1,49},{17,1},{33,17},{49,33},{2,50}... | collective-permute-start | bytes 393224 | tf_op jit(solution)/shard_map/ppermute | solution.py:239
  51.3 9.3 %collective-permute-start.11 = (bf16[8,32,256]{2,1,0:T(8,128)(2,1)S(1)}, bf16[8,32,256]{2,1,0:T(8,128)(2,1)S(1)}, u32[]{:S(2)}, u32[]{:S(2)}) collective-permute-start(bf16[8,32,256]{2,1,0:T(8,128)(2,1)S(1)} %bitcast.9), channel_id=1, source_target_pairs={{0,32},{16,48},{32,0},{48,16},{1,33},{17,49},{33,1},{49,17},{2,34}... | collective-permute-start | bytes 393224 | tf_op jit(solution)/shard_map/ppermute | solution.py:239
  54.2 10.6 %collective-permute-start.6 = (bf16[256,256]{1,0:T(8,128)(2,1)S(1)}, bf16[256,256]{1,0:T(8,128)(2,1)S(1)}, u32[]{:S(2)}, u32[]{:S(2)}) collective-permute-start(bf16[256,256]{1,0:T(8,128)(2,1)S(1)} %get-tuple-element.73), channel_id=1, source_target_pairs={{0,64},{1,193},{64,0},{65,129},{128,192},{129,65},{192,128},{193,1... | collective-permute-start | bytes 393224 | tf_op jit(solution)/shard_map/ppermute | solution.py:245
  54.5 10.2 %collective-permute-start.7 = (bf16[256,256]{1,0:T(8,128)(2,1)S(1)}, bf16[256,256]{1,0:T(8,128)(2,1)S(1)}, u32[]{:S(2)}, u32[]{:S(2)}) collective-permute-start(bf16[256,256]{1,0:T(8,128)(2,1)S(1)} %get-tuple-element.74), channel_id=1, source_target_pairs={{0,192},{1,65},{64,128},{65,1},{128,64},{129,193},{192,0},{193,129... | collective-permute-start | bytes 393224 | tf_op jit(solution)/shard_map/ppermute | solution.py:245
  57.1 7.6 %collective-permute-start.8 = (bf16[256,256]{1,0:T(8,128)(2,1)S(1)}, bf16[256,256]{1,0:T(8,128)(2,1)S(1)}, u32[]{:S(2)}, u32[]{:S(2)}) collective-permute-start(bf16[256,256]{1,0:T(8,128)(2,1)S(1)} %get-tuple-element.75), channel_id=1, source_target_pairs={{0,128},{64,192},{128,0},{192,64},{1,129},{65,193},{129,1},{193,65... | collective-permute-start | bytes 393224 | tf_op jit(solution)/shard_map/ppermute | solution.py:239
  61.4 12.4 %all-to-all-start.1 = ((bf16[8,32,256]{2,1,0:T(8,128)(2,1)}), bf16[8,32,256]{2,1,0:T(8,128)(2,1)S(1)}, u32[]{:S(2)}, u32[]{:S(2)}) async-start(bf16[8,32,256]{2,1,0:T(8,128)(2,1)} %add_convert_fusion), calls=%async_computation.1 | async-start | bytes 262144 | tf_op jit(solution)/shard_map/all_to_all | solution.py:260

commit v13 on v11

--- a/solution.py
+++ b/solution.py
@@ -9,6 +9,7 @@
 
 X = ("x",)
 Y = ("h", "l")
+SHIFTS = (3, 1, 2)
 F32 = jnp.float32
 BF16 = jnp.bfloat16
 LOG2E = 1.4426950408889634
@@ -234,13 +235,13 @@
 
 
 def spread(block, axes):
-    return [block] + [shift(block, axes, s) for s in range(1, lax.axis_size(axes))]
-
-
-def collect(pieces, axes, direction):
+    return [block] + [shift(block, axes, s) for s in SHIFTS]
+
+
+def collect(pieces, axes):
     total = pieces[0]
-    for s in range(1, lax.axis_size(axes)):
-        total = total + shift(pieces[s].astype(BF16), axes, direction * s).astype(F32)
+    for i, s in enumerate(SHIFTS):
+        total = total + shift(pieces[i + 1].astype(BF16), axes, -s).astype(F32)
     return total
 
 
@@ -278,7 +279,7 @@
     coef_theirs, land_theirs, row_total = backward(theirs, n_z, kern_theirs, dembed, feat, [], BF16)
     coef_mine, land_mine, row_total = backward(mine, n_z, kern_mine, dembed, feat, [row_total], F32)
     land_share = (land_mine + shift(land_theirs, "c", 1).astype(F32)).reshape(n_y, n_z, rows, width)
-    land_share = collect(land_share, Y, -1)
+    land_share = collect(land_share, Y)
 
     own, first, second, opposite = feature_share(mine + theirs, n_z, [coef_mine, coef_theirs], feat_t, row_total, n_x, rank)
     landmark_grad = collect_at_once(land_share, "z")

time: 75.2 us -> 74 us (0.984)
  starting transfers between devices: 29 us -> 27.3 us
    ppermute x9, starting transfers between devices: 9.74 us -> 8.08 us  [shift(): lax.ppermute(block, axes, [(i, (i + step) % size) for i in range(size)])]
  transfers between devices with their start and end apart: 15 -> 15, of which waited for: 9 -> 11; matrix products, arithmetic and copies ran while one was open for 2% -> 2% of each run, Pallas kernels for 6% -> 6%
where the time goes in v13:
time: 74 us; the launch traced here: 73.5 us
  waiting for transfers between devices  31.3 us (42%)
  starting transfers between devices  27.3 us (37%)
  Pallas kernels  9.41 us (13%)
  local copies, waits for them, and re-layouts  3.05 us (4%)
  other arithmetic  1.69 us (2%)
  between operations  0.76 us (1%)
    ppermute x9, waiting for transfers between devices, shift(): lax.ppermute(block, axes, [(i, (i + step) % size) for i in range(size)])  8.89 us
    all_to_all x1, starting transfers between devices, per_device(): lax.all_to_all(pack(landmarks, whitening, n_z), 'z', 0, 0, tiled=True)  8.48 us
    all_to_all x1, waiting for transfers between devices, collect_at_once(): lax.all_to_all(pieces.astype(BF16), axes, 0, 0, tiled=True).astype(F32)  8.14 us
    ppermute x9, starting transfers between devices, shift(): lax.ppermute(block, axes, [(i, (i + step) % size) for i in range(size)])  8.08 us
    pallas_call x9, Pallas kernels, call(): pl.pallas_call(body, out_shape=out_shape, in_specs=[WHOLE] * len(operands...  7.93 us
    ppermute x4, starting transfers between devices, partner(): return lax.ppermute(block, ring + ('c',), perm)  7.36 us
    all_to_all x1, waiting for transfers between devices, per_device(): lax.all_to_all(pack(landmarks, whitening, n_z), 'z', 0, 0, tiled=True)  7.35 us
    ppermute x4, waiting for transfers between devices, partner(): return lax.ppermute(block, ring + ('c',), perm)  6.9 us
  transfers between devices with their start and end apart: 15, of which 11 were waited for; matrix products, arithmetic and copies ran while one was open for 2% of the time, Pallas kernels for 6%

profile of v13, /device:TPU:24, one launch (start us, length us, event | category | flops | bytes accessed | tf_op | source)
XLA Modules:
  0.0 73.5 jit_solution(15141984706322011197)
XLA Ops:
  0.6 1.5 %shard_map.59 = bf16[8,40,256]{2,1,0:T(8,128)(2,1)} custom-call(bf16[32,256]{1,0:T(8,128)(2,1)} %landmarks.1, bf16[32,64]{1,0:T(8,128)(2,1)} %whitening.1), custom_call_target="tpu_custom_call" | custom-call | tf_op jit(solution)/shard_map/pallas_call | solution.py:52
  2.1 8.5 %all-to-all-start = ((bf16[8,40,256]{2,1,0:T(8,128)(2,1)}), bf16[8,40,256]{2,1,0:T(8,128)(2,1)S(1)}, u32[]{:S(2)}, u32[]{:S(2)}) async-start(bf16[8,40,256]{2,1,0:T(8,128)(2,1)} %shard_map.59), calls=%async_computation | async-start | bytes 327680 | tf_op jit(solution)/shard_map/all_to_all | solution.py:264
  10.6 0.0 copy-start
  10.6 1.2 %copy-done = bf16[2048,256]{1,0:T(8,128)(2,1)S(1)} copy-done((bf16[2048,256]{1,0:T(8,128)(2,1)S(1)}, bf16[2048,256]{1,0:T(8,128)(2,1)}, u32[]{:S(2)}) %copy-start) | copy-done | bytes 1048600
  11.8 0.9 %copy-done.1 = bf16[2048,64]{0,1:T(8,128)(2,1)S(1)} copy-done((bf16[2048,64]{0,1:T(8,128)(2,1)S(1)}, bf16[2048,64]{0,1:T(8,128)(2,1)}, u32[]{:S(2)}) %copy-start.1) | copy-done | bytes 262168
  12.8 0.2 shard_map.60
  13.0 7.3 %all-to-all-done.refs_0_ = bf16[8,40,256]{2,1,0:T(8,128)(2,1)S(1)} async-done(((bf16[8,40,256]{2,1,0:T(8,128)(2,1)}), bf16[8,40,256]{2,1,0:T(8,128)(2,1)S(1)}, u32[]{:S(2)}, u32[]{:S(2)}) %all-to-all-start) | async-done | bytes 163872 | tf_op jit(solution)/shard_map/all_to_all | solution.py:264
  20.4 1.2 %collective-permute-start.2 = (bf16[8,40,256]{2,1,0:T(8,128)(2,1)S(1)}, bf16[8,40,256]{2,1,0:T(8,128)(2,1)S(1)}, u32[]{:S(2)}, u32[]{:S(2)}) collective-permute-start(bf16[8,40,256]{2,1,0:T(8,128)(2,1)S(1)} %all-to-all-done.refs_0_), channel_id=1, source_target_pairs={{0,32},{16,48},{32,0},{48,16},{1,33},{17,49},{33,1},{49,17},{2,34}... | collective-permute-start | bytes 491528 | tf_op jit(solution)/shard_map/ppermute | solution.py:228
  21.6 2.2 %collective-permute-start.1 = (bf16[8,40,256]{2,1,0:T(8,128)(2,1)S(1)}, bf16[8,40,256]{2,1,0:T(8,128)(2,1)S(1)}, u32[]{:S(2)}, u32[]{:S(2)}) collective-permute-start(bf16[8,40,256]{2,1,0:T(8,128)(2,1)S(1)} %all-to-all-done.refs_0_), channel_id=1, source_target_pairs={{0,16},{16,32},{32,48},{48,0},{1,17},{17,33},{33,49},{49,1},{2,18}... | collective-permute-start | bytes 491528 | tf_op jit(solution)/shard_map/ppermute | solution.py:228
  23.8 0.0 collective-permute-start
  23.8 0.5 shard_map.61
  24.3 3.5 %collective-permute-done.2.refs_2_.refs_3_ = bf16[8,40,256]{2,1,0:T(8,128)(2,1)S(1)} collective-permute-done((bf16[8,40,256]{2,1,0:T(8,128)(2,1)S(1)}, bf16[8,40,256]{2,1,0:T(8,128)(2,1)S(1)}, u32[]{:S(2)}, u32[]{:S(2)}) %collective-permute-start.2) | collective-permute-done | bytes 163872 | tf_op jit(solution)/shard_map/ppermute | solution.py:228
  27.8 0.0 collective-permute-done.1.refs_1_.refs_2_
  27.8 2.5 %collective-permute-done.refs_0_.refs_1_ = bf16[8,40,256]{2,1,0:T(8,128)(2,1)S(1)} collective-permute-done((bf16[8,40,256]{2,1,0:T(8,128)(2,1)S(1)}, bf16[8,40,256]{2,1,0:T(8,128)(2,1)S(1)}, u32[]{:S(2)}, u32[]{:S(2)}) %collective-permute-start) | collective-permute-done | bytes 163872 | tf_op jit(solution)/shard_map/ppermute | solution.py:228
  30.3 0.1 pad_maximum_fusion
  30.4 0.1 collective-permute-start.3
  30.5 1.1 %shard_map.62 = (f32[256,1024]{1,0:T(8,128)S(1)}, f32[256,1024]{1,0:T(8,128)S(1)}, f32[256,1024]{1,0:T(8,128)S(1)}, f32[64,1024]{1,0:T(8,128)S(1)}) custom-call(bf16[8,40,256]{2,1,0:T(8,128)(2,1)S(1)} %collective-permute-done.refs_0_.refs_1_, bf16[8,40,256]{2,1,0:T(8,128)(2,1)S(1)} %collective-permute-done.1.refs_1_.refs_2_, ...), custom_call_target="tpu_custom_call" | custom-call | tf_op jit(solution)/shard_map/pallas_call | solution.py:21
  31.7 0.9 %collective-permute-done.3.refs_0_.refs_4_ = bf16[32,40,256]{2,1,0:T(8,128)(2,1)S(1)} collective-permute-done((bf16[32,40,256]{2,1,0:T(8,128)(2,1)S(1)}, bf16[32,40,256]{2,1,0:T(8,128)(2,1)S(1)}, u32[]{:S(2)}, u32[]{:S(2)}) %collective-permute-start.3) | collective-permute-done | bytes 655392 | tf_op jit(solution)/shard_map/ppermute | solution.py:228
  32.6 1.6 %shard_map.63 = (f32[256,1024]{1,0:T(8,128)S(1)}, f32[256,1024]{1,0:T(8,128)S(1)}, f32[256,1024]{1,0:T(8,128)S(1)}, f32[256,1024]{1,0:T(8,128)S(1)}, f32[64,1024...) custom-call(bf16[32,40,256]{2,1,0:T(8,128)(2,1)S(1)} %collective-permute-done.3.refs_0_.refs_4_, ...), custom_call_target="tpu_custom_call" | custom-call | tf_op jit(solution)/shard_map/pallas_call | solution.py:21
  34.1 1.6 %collective-permute-start.4 = (bf16[64,1024]{1,0:T(8,128)(2,1)S(1)}, bf16[64,1024]{1,0:T(8,128)(2,1)S(1)}, u32[]{:S(2)}, u32[]{:S(2)}) collective-permute-start(bf16[64,1024]{1,0:T(8,128)(2,1)S(1)} %get-tuple-element.57), channel_id=1, source_target_pairs={{0,64},{1,193},{64,0},{65,129},{128,192},{129,65},{192,128},{193,1... | collective-permute-start | bytes 393224 | tf_op jit(solution)/shard_map/ppermute | solution.py:234
  35.7 3.5 %collective-permute-done.4.other = bf16[64,1024]{1,0:T(8,128)(2,1)S(1)} collective-permute-done((bf16[64,1024]{1,0:T(8,128)(2,1)S(1)}, bf16[64,1024]{1,0:T(8,128)(2,1)S(1)}, u32[]{:S(2)}, u32[]{:S(2)}) %collective-permute-start.4) | collective-permute-done | bytes 131104 | tf_op jit(solution)/shard_map/ppermute | solution.py:234
  39.2 2.9 %collective-permute-start.5 = (bf16[64,1024]{1,0:T(8,128)(2,1)S(1)}, bf16[64,1024]{1,0:T(8,128)(2,1)S(1)}, u32[]{:S(2)}, u32[]{:S(2)}) collective-permute-start(bf16[64,1024]{1,0:T(8,128)(2,1)S(1)} %get-tuple-element.59), channel_id=1, source_target_pairs={{0,192},{1,65},{64,128},{65,1},{128,64},{129,193},{192,0},{193,129... | collective-permute-start | bytes 393224 | tf_op jit(solution)/shard_map/ppermute | solution.py:234
  42.1 3.4 %collective-permute-done.5.other = bf16[64,1024]{1,0:T(8,128)(2,1)S(1)} collective-permute-done((bf16[64,1024]{1,0:T(8,128)(2,1)S(1)}, bf16[64,1024]{1,0:T(8,128)(2,1)S(1)}, u32[]{:S(2)}, u32[]{:S(2)}) %collective-permute-start.5) | collective-permute-done | bytes 131104 | tf_op jit(solution)/shard_map/ppermute | solution.py:234
  45.5 0.1 shard_map.65.refs_5_.refs_8_
  45.6 1.5 %shard_map.66 = (bf16[1024,1024]{1,0:T(8,128)(2,1)S(1)}, bf16[1024,256]{1,0:T(8,128)(2,1)S(1)}, f32[1,1024]{1,0:T(1,128)S(1)}) custom-call(bf16[32,40,256]{2,1,0:T(8,128)(2,1)S(1)} %collective-permute-done.3.refs_0_.refs_4_, f32[256,1024]{1,0:T(8,128)S(1)} %get-tuple-element.62.refs_1_, f32[256,1024]{1,0:T(8,128)S(1)} %get-tuple-element.63.refs_2_, ...), custom_call_target="tpu_custom_call" | custom-call | tf_op jit(solution)/shard_map/pallas_call | solution.py:21
  47.2 0.1 collective-permute-start.9
  47.3 1.5 %shard_map.67 = (bf16[1024,1024]{1,0:T(8,128)(2,1)S(1)}, f32[1024,256]{1,0:T(8,128)S(1)}, f32[1,1024]{1,0:T(1,128)S(1)}) custom-call(bf16[8,40,256]{2,1,0:T(8,128)(2,1)S(1)} %all-to-all-done.refs_0_, bf16[8,40,256]{2,1,0:T(8,128)(2,1)S(1)} %collective-permute-done.refs_0_.refs_1_, bf16[8,40,256]{2,1,0:T(8,128)(2,1)S(1)} %collective-permute-done.1.refs_1_.refs_2_, ...), custom_call_target="tpu_custom_call" | custom-call | tf_op jit(solution)/shard_map/pallas_call | solution.py:21
  48.8 0.4 collective-permute-done.9
  49.2 0.2 fusion
  49.4 0.6 collective-permute-start.12
  50.0 1.2 %collective-permute-start.10 = (bf16[8,32,256]{2,1,0:T(8,128)(2,1)S(1)}, bf16[8,32,256]{2,1,0:T(8,128)(2,1)S(1)}, u32[]{:S(2)}, u32[]{:S(2)}) collective-permute-start(bf16[8,32,256]{2,1,0:T(8,128)(2,1)S(1)} %bitcast.10), channel_id=1, source_target_pairs={{0,16},{16,32},{32,48},{48,0},{1,17},{17,33},{33,49},{49,1},{2,18}... | collective-permute-start | bytes 393224 | tf_op jit(solution)/shard_map/ppermute | solution.py:228
  51.2 0.8 %collective-permute-start.11 = (bf16[8,32,256]{2,1,0:T(8,128)(2,1)S(1)}, bf16[8,32,256]{2,1,0:T(8,128)(2,1)S(1)}, u32[]{:S(2)}, u32[]{:S(2)}) collective-permute-start(bf16[8,32,256]{2,1,0:T(8,128)(2,1)S(1)} %bitcast.9), channel_id=1, source_target_pairs={{0,48},{16,0},{32,16},{48,32},{1,49},{17,1},{33,17},{49,33},{2,50}... | collective-permute-start | bytes 393224 | tf_op jit(solution)/shard_map/ppermute | solution.py:228
  52.1 1.3 %shard_map.68 = (f32[256,256]{1,0:T(8,128)S(1)}, bf16[256,256]{1,0:T(8,128)(2,1)S(1)}, bf16[256,256]{1,0:T(8,128)(2,1)S(1)}, bf16[256,256]{1,0:T(8,128)(2,1)S(1)}) custom-call(bf16[8,40,256]{2,1,0:T(8,128)(2,1)S(1)} %all-to-all-done.refs_0_, bf16[8,40,256]{2,1,0:T(8,128)(2,1)S(1)} %collective-permute-done.refs_0_.refs_1_, ...), custom_call_target="tpu_custom_call" | custom-call | tf_op jit(solution)/shard_map/pallas_call | solution.py:21
  53.3 0.4 collective-permute-start.6
  53.7 2.6 %collective-permute-start.7 = (bf16[256,256]{1,0:T(8,128)(2,1)S(1)}, bf16[256,256]{1,0:T(8,128)(2,1)S(1)}, u32[]{:S(2)}, u32[]{:S(2)}) collective-permute-start(bf16[256,256]{1,0:T(8,128)(2,1)S(1)} %get-tuple-element.72), channel_id=1, source_target_pairs={{0,192},{1,65},{64,128},{65,1},{128,64},{129,193},{192,0},{193,129... | collective-permute-start | bytes 393224 | tf_op jit(solution)/shard_map/ppermute | solution.py:234
  56.3 1.0 %collective-permute-done.12 = bf16[8,32,256]{2,1,0:T(8,128)(2,1)S(1)} collective-permute-done((bf16[8,32,256]{2,1,0:T(8,128)(2,1)S(1)}, bf16[8,32,256]{2,1,0:T(8,128)(2,1)S(1)}, u32[]{:S(2)}, u32[]{:S(2)}) %collective-permute-start.12) | collective-permute-done | bytes 131104 | tf_op jit(solution)/shard_map/ppermute | solution.py:228
  57.3 1.8 %collective-permute-start.8 = (bf16[256,256]{1,0:T(8,128)(2,1)S(1)}, bf16[256,256]{1,0:T(8,128)(2,1)S(1)}, u32[]{:S(2)}, u32[]{:S(2)}) collective-permute-start(bf16[256,256]{1,0:T(8,128)(2,1)S(1)} %get-tuple-element.73), channel_id=1, source_target_pairs={{0,128},{64,192},{128,0},{192,64},{1,129},{65,193},{129,1},{193,65... | collective-permute-start | bytes 393224 | tf_op jit(solution)/shard_map/ppermute | solution.py:228
  59.1 0.0 collective-permute-done.10
  59.2 0.2 collective-permute-done.11
  59.3 0.7 add_convert_fusion
  60.1 3.4 %all-to-all-start.1 = ((bf16[8,32,256]{2,1,0:T(8,128)(2,1)}), bf16[8,32,256]{2,1,0:T(8,128)(2,1)S(1)}, u32[]{:S(2)}, u32[]{:S(2)}) async-start(bf16[8,32,256]{2,1,0:T(8,128)(2,1)} %add_convert_fusion), calls=%async_computation.1 | async-start | bytes 262144 | tf_op jit(solution)/shard_map/all_to_all | solution.py:249
  63.4 0.0 collective-permute-done.6
  63.5 0.0 collective-permute-done.7
  63.5 0.3 collective-permute-done.8
  63.8 0.1 add_bitcast_fusion
  63.9 0.8 %copy.6 = f32[256,256]{1,0:T(8,128)} copy(f32[256,256]{0,1:T(8,128)S(1)} %add_bitcast_fusion) | data formatting | bytes 524288
  64.7 8.1 %all-to-all-done.1 = bf16[8,32,256]{2,1,0:T(8,128)(2,1)S(1)} async-done(((bf16[8,32,256]{2,1,0:T(8,128)(2,1)}), bf16[8,32,256]{2,1,0:T(8,128)(2,1)S(1)}, u32[]{:S(2)}, u32[]{:S(2)}) %all-to-all-start.1) | async-done | bytes 131104 | tf_op jit(solution)/shard_map/all_to_all | solution.py:249
  72.8 0.6 convert_reduce_fusion
  (4 shorter events, 0.1 us)
Async XLA Ops:
  2.1 18.2 %all-to-all-start = ((bf16[8,40,256]{2,1,0:T(8,128)(2,1)}), bf16[8,40,256]{2,1,0:T(8,128)(2,1)S(1)}, u32[]{:S(2)}, u32[]{:S(2)}) async-start(bf16[8,40,256]{2,1,0:T(8,128)(2,1)} %shard_map.59), calls=%async_computation | async-start | bytes 327680 | tf_op jit(solution)/shard_map/all_to_all | solution.py:264
  10.6 1.2 %copy-start = (bf16[2048,256]{1,0:T(8,128)(2,1)S(1)}, bf16[2048,256]{1,0:T(8,128)(2,1)}, u32[]{:S(2)}) copy-start(bf16[2048,256]{1,0:T(8,128)(2,1)} %features.1) | copy-start | bytes 3145732
  11.8 0.9 %copy-start.1 = (bf16[2048,64]{0,1:T(8,128)(2,1)S(1)}, bf16[2048,64]{0,1:T(8,128)(2,1)}, u32[]{:S(2)}) copy-start(bf16[2048,64]{0,1:T(8,128)(2,1)} %param.7) | copy-start | bytes 786436
  20.4 7.4 %collective-permute-start.2 = (bf16[8,40,256]{2,1,0:T(8,128)(2,1)S(1)}, bf16[8,40,256]{2,1,0:T(8,128)(2,1)S(1)}, u32[]{:S(2)}, u32[]{:S(2)}) collective-permute-start(bf16[8,40,256]{2,1,0:T(8,128)(2,1)S(1)} %all-to-all-done.refs_0_), channel_id=1, source_target_pairs={{0,32},{16,48},{32,0},{48,16},{1,33},{17,49},{33,1},{49,17},{2,34}... | collective-permute-start | bytes 491528 | tf_op jit(solution)/shard_map/ppermute | solution.py:228
  21.6 6.2 %collective-permute-start.1 = (bf16[8,40,256]{2,1,0:T(8,128)(2,1)S(1)}, bf16[8,40,256]{2,1,0:T(8,128)(2,1)S(1)}, u32[]{:S(2)}, u32[]{:S(2)}) collective-permute-start(bf16[8,40,256]{2,1,0:T(8,128)(2,1)S(1)} %all-to-all-done.refs_0_), channel_id=1, source_target_pairs={{0,16},{16,32},{32,48},{48,0},{1,17},{17,33},{33,49},{49,1},{2,18}... | collective-permute-start | bytes 491528 | tf_op jit(solution)/shard_map/ppermute | solution.py:228
  23.8 6.5 %collective-permute-start = (bf16[8,40,256]{2,1,0:T(8,128)(2,1)S(1)}, bf16[8,40,256]{2,1,0:T(8,128)(2,1)S(1)}, u32[]{:S(2)}, u32[]{:S(2)}) collective-permute-start(bf16[8,40,256]{2,1,0:T(8,128)(2,1)S(1)} %all-to-all-done.refs_0_), channel_id=1, source_target_pairs={{0,48},{16,0},{32,16},{48,32},{1,49},{17,1},{33,17},{49,33},{2,50}... | collective-permute-start | bytes 491528 | tf_op jit(solution)/shard_map/ppermute | solution.py:228
  30.4 2.2 %collective-permute-start.3 = (bf16[32,40,256]{2,1,0:T(8,128)(2,1)S(1)}, bf16[32,40,256]{2,1,0:T(8,128)(2,1)S(1)}, u32[]{:S(2)}, u32[]{:S(2)}) collective-permute-start(bf16[32,40,256]{2,1,0:T(8,128)(2,1)S(1)} %pad_maximum_fusion), channel_id=1, source_target_pairs={{0,1},{1,0},{2,3},{3,2},{4,5},{5,4},{6,7},{7,6},{8,9},{9,8},{10,11... | collective-permute-start | bytes 1966088 | tf_op jit(solution)/shard_map/ppermute | solution.py:228
  34.1 5.1 %collective-permute-start.4 = (bf16[64,1024]{1,0:T(8,128)(2,1)S(1)}, bf16[64,1024]{1,0:T(8,128)(2,1)S(1)}, u32[]{:S(2)}, u32[]{:S(2)}) collective-permute-start(bf16[64,1024]{1,0:T(8,128)(2,1)S(1)} %get-tuple-element.57), channel_id=1, source_target_pairs={{0,64},{1,193},{64,0},{65,129},{128,192},{129,65},{192,128},{193,1... | collective-permute-start | bytes 393224 | tf_op jit(solution)/shard_map/ppermute | solution.py:234
  39.2 6.3 %collective-permute-start.5 = (bf16[64,1024]{1,0:T(8,128)(2,1)S(1)}, bf16[64,1024]{1,0:T(8,128)(2,1)S(1)}, u32[]{:S(2)}, u32[]{:S(2)}) collective-permute-start(bf16[64,1024]{1,0:T(8,128)(2,1)S(1)} %get-tuple-element.59), channel_id=1, source_target_pairs={{0,192},{1,65},{64,128},{65,1},{128,64},{129,193},{192,0},{193,129... | collective-permute-start | bytes 393224 | tf_op jit(solution)/shard_map/ppermute | solution.py:234
  47.2 2.0 %collective-permute-start.9 = (bf16[1024,256]{1,0:T(8,128)(2,1)S(1)}, bf16[1024,256]{1,0:T(8,128)(2,1)S(1)}, u32[]{:S(2)}, u32[]{:S(2)}) collective-permute-start(bf16[1024,256]{1,0:T(8,128)(2,1)S(1)} %get-tuple-element.75), channel_id=1, source_target_pairs={{0,1},{1,0},{2,3},{3,2},{4,5},{5,4},{6,7},{7,6},{8,9},{9,8},{10,11... | collective-permute-start | bytes 1572872 | tf_op jit(solution)/shard_map/ppermute | solution.py:228
  49.4 7.9 %collective-permute-start.12 = (bf16[8,32,256]{2,1,0:T(8,128)(2,1)S(1)}, bf16[8,32,256]{2,1,0:T(8,128)(2,1)S(1)}, u32[]{:S(2)}, u32[]{:S(2)}) collective-permute-start(bf16[8,32,256]{2,1,0:T(8,128)(2,1)S(1)} %bitcast.11), channel_id=1, source_target_pairs={{0,32},{16,48},{32,0},{48,16},{1,33},{17,49},{33,1},{49,17},{2,34}... | collective-permute-start | bytes 393224 | tf_op jit(solution)/shard_map/ppermute | solution.py:228
  50.0 9.1 %collective-permute-start.10 = (bf16[8,32,256]{2,1,0:T(8,128)(2,1)S(1)}, bf16[8,32,256]{2,1,0:T(8,128)(2,1)S(1)}, u32[]{:S(2)}, u32[]{:S(2)}) collective-permute-start(bf16[8,32,256]{2,1,0:T(8,128)(2,1)S(1)} %bitcast.10), channel_id=1, source_target_pairs={{0,16},{16,32},{32,48},{48,0},{1,17},{17,33},{33,49},{49,1},{2,18}... | collective-permute-start | bytes 393224 | tf_op jit(solution)/shard_map/ppermute | solution.py:228
  51.2 8.1 %collective-permute-start.11 = (bf16[8,32,256]{2,1,0:T(8,128)(2,1)S(1)}, bf16[8,32,256]{2,1,0:T(8,128)(2,1)S(1)}, u32[]{:S(2)}, u32[]{:S(2)}) collective-permute-start(bf16[8,32,256]{2,1,0:T(8,128)(2,1)S(1)} %bitcast.9), channel_id=1, source_target_pairs={{0,48},{16,0},{32,16},{48,32},{1,49},{17,1},{33,17},{49,33},{2,50}... | collective-permute-start | bytes 393224 | tf_op jit(solution)/shard_map/ppermute | solution.py:228
  53.3 10.1 %collective-permute-start.6 = (bf16[256,256]{1,0:T(8,128)(2,1)S(1)}, bf16[256,256]{1,0:T(8,128)(2,1)S(1)}, u32[]{:S(2)}, u32[]{:S(2)}) collective-permute-start(bf16[256,256]{1,0:T(8,128)(2,1)S(1)} %get-tuple-element.71), channel_id=1, source_target_pairs={{0,64},{1,193},{64,0},{65,129},{128,192},{129,65},{192,128},{193,1... | collective-permute-start | bytes 393224 | tf_op jit(solution)/shard_map/ppermute | solution.py:234
  53.7 9.8 %collective-permute-start.7 = (bf16[256,256]{1,0:T(8,128)(2,1)S(1)}, bf16[256,256]{1,0:T(8,128)(2,1)S(1)}, u32[]{:S(2)}, u32[]{:S(2)}) collective-permute-start(bf16[256,256]{1,0:T(8,128)(2,1)S(1)} %get-tuple-element.72), channel_id=1, source_target_pairs={{0,192},{1,65},{64,128},{65,1},{128,64},{129,193},{192,0},{193,129... | collective-permute-start | bytes 393224 | tf_op jit(solution)/shard_map/ppermute | solution.py:234
  57.3 6.5 %collective-permute-start.8 = (bf16[256,256]{1,0:T(8,128)(2,1)S(1)}, bf16[256,256]{1,0:T(8,128)(2,1)S(1)}, u32[]{:S(2)}, u32[]{:S(2)}) collective-permute-start(bf16[256,256]{1,0:T(8,128)(2,1)S(1)} %get-tuple-element.73), channel_id=1, source_target_pairs={{0,128},{64,192},{128,0},{192,64},{1,129},{65,193},{129,1},{193,65... | collective-permute-start | bytes 393224 | tf_op jit(solution)/shard_map/ppermute | solution.py:228
  60.1 12.8 %all-to-all-start.1 = ((bf16[8,32,256]{2,1,0:T(8,128)(2,1)}), bf16[8,32,256]{2,1,0:T(8,128)(2,1)S(1)}, u32[]{:S(2)}, u32[]{:S(2)}) async-start(bf16[8,32,256]{2,1,0:T(8,128)(2,1)} %add_convert_fusion), calls=%async_computation.1 | async-start | bytes 262144 | tf_op jit(solution)/shard_map/all_to_all | solution.py:249

commit v14 on v13

--- a/solution.py
+++ b/solution.py
@@ -9,7 +9,7 @@
 
 X = ("x",)
 Y = ("h", "l")
-SHIFTS = (3, 1, 2)
+SHIFTS = (3, 2, 1)
 F32 = jnp.float32
 BF16 = jnp.bfloat16
 LOG2E = 1.4426950408889634
@@ -240,8 +240,8 @@
 
 def collect(pieces, axes):
     total = pieces[0]
-    for i, s in enumerate(SHIFTS):
-        total = total + shift(pieces[i + 1].astype(BF16), axes, -s).astype(F32)
+    for s in (2, 1, 3):
+        total = total + shift(pieces[SHIFTS.index(s) + 1].astype(BF16), axes, -s).astype(F32)
     return total
 
 

time: 74 us -> 74.6 us (level); the launches traced: 73.5 us -> 73.1 us
  no operation moved by 1% of the time
where the time goes in v14:
time: 74.6 us; the launch traced here: 73.1 us
  waiting for transfers between devices  31.5 us (42%)
  starting transfers between devices  26.6 us (36%)
  Pallas kernels  9.4 us (13%)
  local copies, waits for them, and re-layouts  3.05 us (4%)
  other arithmetic  1.69 us (2%)
  between operations  0.78 us (1%)
    ppermute x9, waiting for transfers between devices, shift(): lax.ppermute(block, axes, [(i, (i + step) % size) for i in range(size)])  9.21 us
    all_to_all x1, starting transfers between devices, per_device(): lax.all_to_all(pack(landmarks, whitening, n_z), 'z', 0, 0, tiled=True)  8.48 us
    all_to_all x1, waiting for transfers between devices, collect_at_once(): lax.all_to_all(pieces.astype(BF16), axes, 0, 0, tiled=True).astype(F32)  8.06 us
    pallas_call x9, Pallas kernels, call(): pl.pallas_call(body, out_shape=out_shape, in_specs=[WHOLE] * len(operands...  7.92 us
    ppermute x9, starting transfers between devices, shift(): lax.ppermute(block, axes, [(i, (i + step) % size) for i in range(size)])  7.42 us
    ppermute x4, starting transfers between devices, partner(): return lax.ppermute(block, ring + ('c',), perm)  7.37 us
    all_to_all x1, waiting for transfers between devices, per_device(): lax.all_to_all(pack(landmarks, whitening, n_z), 'z', 0, 0, tiled=True)  7.35 us
    ppermute x4, waiting for transfers between devices, partner(): return lax.ppermute(block, ring + ('c',), perm)  6.89 us
  transfers between devices with their start and end apart: 15, of which 11 were waited for; matrix products, arithmetic and copies ran while one was open for 2% of the time, Pallas kernels for 6%

profile of v14, /device:TPU:24, one launch (start us, length us, event | category | flops | bytes accessed | tf_op | source)
XLA Modules:
  0.0 73.1 jit_solution(1305223529809540856)
XLA Ops:
  0.6 1.5 %shard_map.59 = bf16[8,40,256]{2,1,0:T(8,128)(2,1)} custom-call(bf16[32,256]{1,0:T(8,128)(2,1)} %landmarks.1, bf16[32,64]{1,0:T(8,128)(2,1)} %whitening.1), custom_call_target="tpu_custom_call" | custom-call | tf_op jit(solution)/shard_map/pallas_call | solution.py:52
  2.1 8.5 %all-to-all-start = ((bf16[8,40,256]{2,1,0:T(8,128)(2,1)}), bf16[8,40,256]{2,1,0:T(8,128)(2,1)S(1)}, u32[]{:S(2)}, u32[]{:S(2)}) async-start(bf16[8,40,256]{2,1,0:T(8,128)(2,1)} %shard_map.59), calls=%async_computation | async-start | bytes 327680 | tf_op jit(solution)/shard_map/all_to_all | solution.py:264
  10.6 0.0 copy-start
  10.6 1.2 %copy-done = bf16[2048,256]{1,0:T(8,128)(2,1)S(1)} copy-done((bf16[2048,256]{1,0:T(8,128)(2,1)S(1)}, bf16[2048,256]{1,0:T(8,128)(2,1)}, u32[]{:S(2)}) %copy-start) | copy-done | bytes 1048600
  11.8 0.9 %copy-done.1 = bf16[2048,64]{0,1:T(8,128)(2,1)S(1)} copy-done((bf16[2048,64]{0,1:T(8,128)(2,1)S(1)}, bf16[2048,64]{0,1:T(8,128)(2,1)}, u32[]{:S(2)}) %copy-start.1) | copy-done | bytes 262168
  12.8 0.2 shard_map.60
  13.0 7.3 %all-to-all-done.refs_0_ = bf16[8,40,256]{2,1,0:T(8,128)(2,1)S(1)} async-done(((bf16[8,40,256]{2,1,0:T(8,128)(2,1)}), bf16[8,40,256]{2,1,0:T(8,128)(2,1)S(1)}, u32[]{:S(2)}, u32[]{:S(2)}) %all-to-all-start) | async-done | bytes 163872 | tf_op jit(solution)/shard_map/all_to_all | solution.py:264
  20.4 0.2 collective-permute-start.2
  20.6 2.6 %collective-permute-start.1 = (bf16[8,40,256]{2,1,0:T(8,128)(2,1)S(1)}, bf16[8,40,256]{2,1,0:T(8,128)(2,1)S(1)}, u32[]{:S(2)}, u32[]{:S(2)}) collective-permute-start(bf16[8,40,256]{2,1,0:T(8,128)(2,1)S(1)} %all-to-all-done.refs_0_), channel_id=1, source_target_pairs={{0,32},{16,48},{32,0},{48,16},{1,33},{17,49},{33,1},{49,17},{2,34}... | collective-permute-start | bytes 491528 | tf_op jit(solution)/shard_map/ppermute | solution.py:228
  23.2 0.0 collective-permute-start
  23.2 0.5 shard_map.61
  23.7 2.5 %collective-permute-done.2.refs_2_.refs_3_ = bf16[8,40,256]{2,1,0:T(8,128)(2,1)S(1)} collective-permute-done((bf16[8,40,256]{2,1,0:T(8,128)(2,1)S(1)}, bf16[8,40,256]{2,1,0:T(8,128)(2,1)S(1)}, u32[]{:S(2)}, u32[]{:S(2)}) %collective-permute-start.2) | collective-permute-done | bytes 163872 | tf_op jit(solution)/shard_map/ppermute | solution.py:228
  26.2 1.8 %collective-permute-done.1.refs_1_.refs_2_ = bf16[8,40,256]{2,1,0:T(8,128)(2,1)S(1)} collective-permute-done((bf16[8,40,256]{2,1,0:T(8,128)(2,1)S(1)}, bf16[8,40,256]{2,1,0:T(8,128)(2,1)S(1)}, u32[]{:S(2)}, u32[]{:S(2)}) %collective-permute-start.1) | collective-permute-done | bytes 163872 | tf_op jit(solution)/shard_map/ppermute | solution.py:228
  28.0 1.8 %collective-permute-done.refs_0_.refs_1_ = bf16[8,40,256]{2,1,0:T(8,128)(2,1)S(1)} collective-permute-done((bf16[8,40,256]{2,1,0:T(8,128)(2,1)S(1)}, bf16[8,40,256]{2,1,0:T(8,128)(2,1)S(1)}, u32[]{:S(2)}, u32[]{:S(2)}) %collective-permute-start) | collective-permute-done | bytes 163872 | tf_op jit(solution)/shard_map/ppermute | solution.py:228
  29.7 0.1 pad_maximum_fusion
  29.8 0.1 collective-permute-start.3
  29.9 1.2 %shard_map.62 = (f32[256,1024]{1,0:T(8,128)S(1)}, f32[256,1024]{1,0:T(8,128)S(1)}, f32[256,1024]{1,0:T(8,128)S(1)}, f32[64,1024]{1,0:T(8,128)S(1)}) custom-call(bf16[8,40,256]{2,1,0:T(8,128)(2,1)S(1)} %collective-permute-done.refs_0_.refs_1_, bf16[8,40,256]{2,1,0:T(8,128)(2,1)S(1)} %collective-permute-done.1.refs_1_.refs_2_, ...), custom_call_target="tpu_custom_call" | custom-call | tf_op jit(solution)/shard_map/pallas_call | solution.py:21
  31.1 0.9 %collective-permute-done.3.refs_0_.refs_4_ = bf16[32,40,256]{2,1,0:T(8,128)(2,1)S(1)} collective-permute-done((bf16[32,40,256]{2,1,0:T(8,128)(2,1)S(1)}, bf16[32,40,256]{2,1,0:T(8,128)(2,1)S(1)}, u32[]{:S(2)}, u32[]{:S(2)}) %collective-permute-start.3) | collective-permute-done | bytes 655392 | tf_op jit(solution)/shard_map/ppermute | solution.py:228
  32.0 1.5 %shard_map.63 = (f32[256,1024]{1,0:T(8,128)S(1)}, f32[256,1024]{1,0:T(8,128)S(1)}, f32[256,1024]{1,0:T(8,128)S(1)}, f32[256,1024]{1,0:T(8,128)S(1)}, f32[64,1024...) custom-call(bf16[32,40,256]{2,1,0:T(8,128)(2,1)S(1)} %collective-permute-done.3.refs_0_.refs_4_, ...), custom_call_target="tpu_custom_call" | custom-call | tf_op jit(solution)/shard_map/pallas_call | solution.py:21
  33.5 1.6 %collective-permute-start.4 = (bf16[64,1024]{1,0:T(8,128)(2,1)S(1)}, bf16[64,1024]{1,0:T(8,128)(2,1)S(1)}, u32[]{:S(2)}, u32[]{:S(2)}) collective-permute-start(bf16[64,1024]{1,0:T(8,128)(2,1)S(1)} %get-tuple-element.57), channel_id=1, source_target_pairs={{0,64},{1,193},{64,0},{65,129},{128,192},{129,65},{192,128},{193,1... | collective-permute-start | bytes 393224 | tf_op jit(solution)/shard_map/ppermute | solution.py:234
  35.1 3.5 %collective-permute-done.4.other = bf16[64,1024]{1,0:T(8,128)(2,1)S(1)} collective-permute-done((bf16[64,1024]{1,0:T(8,128)(2,1)S(1)}, bf16[64,1024]{1,0:T(8,128)(2,1)S(1)}, u32[]{:S(2)}, u32[]{:S(2)}) %collective-permute-start.4) | collective-permute-done | bytes 131104 | tf_op jit(solution)/shard_map/ppermute | solution.py:234
  38.6 2.9 %collective-permute-start.5 = (bf16[64,1024]{1,0:T(8,128)(2,1)S(1)}, bf16[64,1024]{1,0:T(8,128)(2,1)S(1)}, u32[]{:S(2)}, u32[]{:S(2)}) collective-permute-start(bf16[64,1024]{1,0:T(8,128)(2,1)S(1)} %get-tuple-element.59), channel_id=1, source_target_pairs={{0,192},{1,65},{64,128},{65,1},{128,64},{129,193},{192,0},{193,129... | collective-permute-start | bytes 393224 | tf_op jit(solution)/shard_map/ppermute | solution.py:234
  41.5 3.4 %collective-permute-done.5.other = bf16[64,1024]{1,0:T(8,128)(2,1)S(1)} collective-permute-done((bf16[64,1024]{1,0:T(8,128)(2,1)S(1)}, bf16[64,1024]{1,0:T(8,128)(2,1)S(1)}, u32[]{:S(2)}, u32[]{:S(2)}) %collective-permute-start.5) | collective-permute-done | bytes 131104 | tf_op jit(solution)/shard_map/ppermute | solution.py:234
  44.9 0.1 shard_map.65.refs_5_.refs_8_
  45.1 1.5 %shard_map.66 = (bf16[1024,1024]{1,0:T(8,128)(2,1)S(1)}, bf16[1024,256]{1,0:T(8,128)(2,1)S(1)}, f32[1,1024]{1,0:T(1,128)S(1)}) custom-call(bf16[32,40,256]{2,1,0:T(8,128)(2,1)S(1)} %collective-permute-done.3.refs_0_.refs_4_, f32[256,1024]{1,0:T(8,128)S(1)} %get-tuple-element.62.refs_1_, f32[256,1024]{1,0:T(8,128)S(1)} %get-tuple-element.63.refs_2_, ...), custom_call_target="tpu_custom_call" | custom-call | tf_op jit(solution)/shard_map/pallas_call | solution.py:21
  46.6 0.1 collective-permute-start.9
  46.7 1.5 %shard_map.67 = (bf16[1024,1024]{1,0:T(8,128)(2,1)S(1)}, f32[1024,256]{1,0:T(8,128)S(1)}, f32[1,1024]{1,0:T(1,128)S(1)}) custom-call(bf16[8,40,256]{2,1,0:T(8,128)(2,1)S(1)} %all-to-all-done.refs_0_, bf16[8,40,256]{2,1,0:T(8,128)(2,1)S(1)} %collective-permute-done.refs_0_.refs_1_, bf16[8,40,256]{2,1,0:T(8,128)(2,1)S(1)} %collective-permute-done.1.refs_1_.refs_2_, ...), custom_call_target="tpu_custom_call" | custom-call | tf_op jit(solution)/shard_map/pallas_call | solution.py:21
  48.2 0.4 collective-permute-done.9
  48.6 0.2 fusion
  48.8 0.9 %collective-permute-start.12 = (bf16[8,32,256]{2,1,0:T(8,128)(2,1)S(1)}, bf16[8,32,256]{2,1,0:T(8,128)(2,1)S(1)}, u32[]{:S(2)}, u32[]{:S(2)}) collective-permute-start(bf16[8,32,256]{2,1,0:T(8,128)(2,1)S(1)} %bitcast.11), channel_id=1, source_target_pairs={{0,16},{16,32},{32,48},{48,0},{1,17},{17,33},{33,49},{49,1},{2,18}... | collective-permute-start | bytes 393224 | tf_op jit(solution)/shard_map/ppermute | solution.py:228
  49.8 2.0 %collective-permute-start.10 = (bf16[8,32,256]{2,1,0:T(8,128)(2,1)S(1)}, bf16[8,32,256]{2,1,0:T(8,128)(2,1)S(1)}, u32[]{:S(2)}, u32[]{:S(2)}) collective-permute-start(bf16[8,32,256]{2,1,0:T(8,128)(2,1)S(1)} %bitcast.10), channel_id=1, source_target_pairs={{0,32},{16,48},{32,0},{48,16},{1,33},{17,49},{33,1},{49,17},{2,34}... | collective-permute-start | bytes 393224 | tf_op jit(solution)/shard_map/ppermute | solution.py:228
  51.8 0.0 collective-permute-start.11
  51.8 1.3 %shard_map.68 = (f32[256,256]{1,0:T(8,128)S(1)}, bf16[256,256]{1,0:T(8,128)(2,1)S(1)}, bf16[256,256]{1,0:T(8,128)(2,1)S(1)}, bf16[256,256]{1,0:T(8,128)(2,1)S(1)}) custom-call(bf16[8,40,256]{2,1,0:T(8,128)(2,1)S(1)} %all-to-all-done.refs_0_, bf16[8,40,256]{2,1,0:T(8,128)(2,1)S(1)} %collective-permute-done.refs_0_.refs_1_, ...), custom_call_target="tpu_custom_call" | custom-call | tf_op jit(solution)/shard_map/pallas_call | solution.py:21
  53.1 0.4 collective-permute-start.6
  53.4 2.6 %collective-permute-start.7 = (bf16[256,256]{1,0:T(8,128)(2,1)S(1)}, bf16[256,256]{1,0:T(8,128)(2,1)S(1)}, u32[]{:S(2)}, u32[]{:S(2)}) collective-permute-start(bf16[256,256]{1,0:T(8,128)(2,1)S(1)} %get-tuple-element.72), channel_id=1, source_target_pairs={{0,192},{1,65},{64,128},{65,1},{128,64},{129,193},{192,0},{193,129... | collective-permute-start | bytes 393224 | tf_op jit(solution)/shard_map/ppermute | solution.py:234
  56.0 0.0 collective-permute-done.12
  56.0 1.5 %collective-permute-start.8 = (bf16[256,256]{1,0:T(8,128)(2,1)S(1)}, bf16[256,256]{1,0:T(8,128)(2,1)S(1)}, u32[]{:S(2)}, u32[]{:S(2)}) collective-permute-start(bf16[256,256]{1,0:T(8,128)(2,1)S(1)} %get-tuple-element.73), channel_id=1, source_target_pairs={{0,128},{64,192},{128,0},{192,64},{1,129},{65,193},{129,1},{193,65... | collective-permute-start | bytes 393224 | tf_op jit(solution)/shard_map/ppermute | solution.py:228
  57.5 0.2 collective-permute-done.10
  57.6 1.7 %collective-permute-done.11 = bf16[8,32,256]{2,1,0:T(8,128)(2,1)S(1)} collective-permute-done((bf16[8,32,256]{2,1,0:T(8,128)(2,1)S(1)}, bf16[8,32,256]{2,1,0:T(8,128)(2,1)S(1)}, u32[]{:S(2)}, u32[]{:S(2)}) %collective-permute-start.11) | collective-permute-done | bytes 131104 | tf_op jit(solution)/shard_map/ppermute | solution.py:228
  59.3 0.7 %add_convert_fusion = bf16[8,32,256]{2,1,0:T(8,128)(2,1)} fusion(bf16[8,32,256]{2,1,0:T(8,128)(2,1)S(1)} %collective-permute-done.12, bf16[8,32,256]{2,1,0:T(8,128)(2,1)S(1)} %collective-permute-done.11, f32[8,32,256]{2,1,0:T(8,128)S(1)} %bitcast.8, bf16[8,32,256]{2,1,0:T(8,128)(2,1)S(1)} %collective-permute-done.10), kind=kLoop, calls=%fused_computation.3 | loop fusion | flops 458752 | bytes 786432 | tf_op jit(solution)/shard_map/convert_element_type | solution.py:249
  60.1 3.4 %all-to-all-start.1 = ((bf16[8,32,256]{2,1,0:T(8,128)(2,1)}), bf16[8,32,256]{2,1,0:T(8,128)(2,1)S(1)}, u32[]{:S(2)}, u32[]{:S(2)}) async-start(bf16[8,32,256]{2,1,0:T(8,128)(2,1)} %add_convert_fusion), calls=%async_computation.1 | async-start | bytes 262144 | tf_op jit(solution)/shard_map/all_to_all | solution.py:249
  63.4 0.0 collective-permute-done.6
  63.4 0.0 collective-permute-done.7
  63.5 0.0 collective-permute-done.8
  63.5 0.1 add_bitcast_fusion
  63.5 0.8 %copy.6 = f32[256,256]{1,0:T(8,128)} copy(f32[256,256]{0,1:T(8,128)S(1)} %add_bitcast_fusion) | data formatting | bytes 524288
  64.4 8.1 %all-to-all-done.1 = bf16[8,32,256]{2,1,0:T(8,128)(2,1)S(1)} async-done(((bf16[8,32,256]{2,1,0:T(8,128)(2,1)}), bf16[8,32,256]{2,1,0:T(8,128)(2,1)S(1)}, u32[]{:S(2)}, u32[]{:S(2)}) %all-to-all-start.1) | async-done | bytes 131104 | tf_op jit(solution)/shard_map/all_to_all | solution.py:249
  72.4 0.6 convert_reduce_fusion
  (4 shorter events, 0.1 us)
Async XLA Ops:
  2.1 18.2 %all-to-all-start = ((bf16[8,40,256]{2,1,0:T(8,128)(2,1)}), bf16[8,40,256]{2,1,0:T(8,128)(2,1)S(1)}, u32[]{:S(2)}, u32[]{:S(2)}) async-start(bf16[8,40,256]{2,1,0:T(8,128)(2,1)} %shard_map.59), calls=%async_computation | async-start | bytes 327680 | tf_op jit(solution)/shard_map/all_to_all | solution.py:264
  10.6 1.2 %copy-start = (bf16[2048,256]{1,0:T(8,128)(2,1)S(1)}, bf16[2048,256]{1,0:T(8,128)(2,1)}, u32[]{:S(2)}) copy-start(bf16[2048,256]{1,0:T(8,128)(2,1)} %features.1) | copy-start | bytes 3145732
  11.8 0.9 %copy-start.1 = (bf16[2048,64]{0,1:T(8,128)(2,1)S(1)}, bf16[2048,64]{0,1:T(8,128)(2,1)}, u32[]{:S(2)}) copy-start(bf16[2048,64]{0,1:T(8,128)(2,1)} %param.7) | copy-start | bytes 786436
  20.4 5.8 %collective-permute-start.2 = (bf16[8,40,256]{2,1,0:T(8,128)(2,1)S(1)}, bf16[8,40,256]{2,1,0:T(8,128)(2,1)S(1)}, u32[]{:S(2)}, u32[]{:S(2)}) collective-permute-start(bf16[8,40,256]{2,1,0:T(8,128)(2,1)S(1)} %all-to-all-done.refs_0_), channel_id=1, source_target_pairs={{0,16},{16,32},{32,48},{48,0},{1,17},{17,33},{33,49},{49,1},{2,18}... | collective-permute-start | bytes 491528 | tf_op jit(solution)/shard_map/ppermute | solution.py:228
  20.6 7.4 %collective-permute-start.1 = (bf16[8,40,256]{2,1,0:T(8,128)(2,1)S(1)}, bf16[8,40,256]{2,1,0:T(8,128)(2,1)S(1)}, u32[]{:S(2)}, u32[]{:S(2)}) collective-permute-start(bf16[8,40,256]{2,1,0:T(8,128)(2,1)S(1)} %all-to-all-done.refs_0_), channel_id=1, source_target_pairs={{0,32},{16,48},{32,0},{48,16},{1,33},{17,49},{33,1},{49,17},{2,34}... | collective-permute-start | bytes 491528 | tf_op jit(solution)/shard_map/ppermute | solution.py:228
  23.2 6.6 %collective-permute-start = (bf16[8,40,256]{2,1,0:T(8,128)(2,1)S(1)}, bf16[8,40,256]{2,1,0:T(8,128)(2,1)S(1)}, u32[]{:S(2)}, u32[]{:S(2)}) collective-permute-start(bf16[8,40,256]{2,1,0:T(8,128)(2,1)S(1)} %all-to-all-done.refs_0_), channel_id=1, source_target_pairs={{0,48},{16,0},{32,16},{48,32},{1,49},{17,1},{33,17},{49,33},{2,50}... | collective-permute-start | bytes 491528 | tf_op jit(solution)/shard_map/ppermute | solution.py:228
  29.8 2.2 %collective-permute-start.3 = (bf16[32,40,256]{2,1,0:T(8,128)(2,1)S(1)}, bf16[32,40,256]{2,1,0:T(8,128)(2,1)S(1)}, u32[]{:S(2)}, u32[]{:S(2)}) collective-permute-start(bf16[32,40,256]{2,1,0:T(8,128)(2,1)S(1)} %pad_maximum_fusion), channel_id=1, source_target_pairs={{0,1},{1,0},{2,3},{3,2},{4,5},{5,4},{6,7},{7,6},{8,9},{9,8},{10,11... | collective-permute-start | bytes 1966088 | tf_op jit(solution)/shard_map/ppermute | solution.py:228
  33.5 5.1 %collective-permute-start.4 = (bf16[64,1024]{1,0:T(8,128)(2,1)S(1)}, bf16[64,1024]{1,0:T(8,128)(2,1)S(1)}, u32[]{:S(2)}, u32[]{:S(2)}) collective-permute-start(bf16[64,1024]{1,0:T(8,128)(2,1)S(1)} %get-tuple-element.57), channel_id=1, source_target_pairs={{0,64},{1,193},{64,0},{65,129},{128,192},{129,65},{192,128},{193,1... | collective-permute-start | bytes 393224 | tf_op jit(solution)/shard_map/ppermute | solution.py:234
  38.6 6.3 %collective-permute-start.5 = (bf16[64,1024]{1,0:T(8,128)(2,1)S(1)}, bf16[64,1024]{1,0:T(8,128)(2,1)S(1)}, u32[]{:S(2)}, u32[]{:S(2)}) collective-permute-start(bf16[64,1024]{1,0:T(8,128)(2,1)S(1)} %get-tuple-element.59), channel_id=1, source_target_pairs={{0,192},{1,65},{64,128},{65,1},{128,64},{129,193},{192,0},{193,129... | collective-permute-start | bytes 393224 | tf_op jit(solution)/shard_map/ppermute | solution.py:234
  46.6 2.0 %collective-permute-start.9 = (bf16[1024,256]{1,0:T(8,128)(2,1)S(1)}, bf16[1024,256]{1,0:T(8,128)(2,1)S(1)}, u32[]{:S(2)}, u32[]{:S(2)}) collective-permute-start(bf16[1024,256]{1,0:T(8,128)(2,1)S(1)} %get-tuple-element.75), channel_id=1, source_target_pairs={{0,1},{1,0},{2,3},{3,2},{4,5},{5,4},{6,7},{7,6},{8,9},{9,8},{10,11... | collective-permute-start | bytes 1572872 | tf_op jit(solution)/shard_map/ppermute | solution.py:228
  48.8 7.2 %collective-permute-start.12 = (bf16[8,32,256]{2,1,0:T(8,128)(2,1)S(1)}, bf16[8,32,256]{2,1,0:T(8,128)(2,1)S(1)}, u32[]{:S(2)}, u32[]{:S(2)}) collective-permute-start(bf16[8,32,256]{2,1,0:T(8,128)(2,1)S(1)} %bitcast.11), channel_id=1, source_target_pairs={{0,16},{16,32},{32,48},{48,0},{1,17},{17,33},{33,49},{49,1},{2,18}... | collective-permute-start | bytes 393224 | tf_op jit(solution)/shard_map/ppermute | solution.py:228
  49.8 7.9 %collective-permute-start.10 = (bf16[8,32,256]{2,1,0:T(8,128)(2,1)S(1)}, bf16[8,32,256]{2,1,0:T(8,128)(2,1)S(1)}, u32[]{:S(2)}, u32[]{:S(2)}) collective-permute-start(bf16[8,32,256]{2,1,0:T(8,128)(2,1)S(1)} %bitcast.10), channel_id=1, source_target_pairs={{0,32},{16,48},{32,0},{48,16},{1,33},{17,49},{33,1},{49,17},{2,34}... | collective-permute-start | bytes 393224 | tf_op jit(solution)/shard_map/ppermute | solution.py:228
  51.8 7.5 %collective-permute-start.11 = (bf16[8,32,256]{2,1,0:T(8,128)(2,1)S(1)}, bf16[8,32,256]{2,1,0:T(8,128)(2,1)S(1)}, u32[]{:S(2)}, u32[]{:S(2)}) collective-permute-start(bf16[8,32,256]{2,1,0:T(8,128)(2,1)S(1)} %bitcast.9), channel_id=1, source_target_pairs={{0,48},{16,0},{32,16},{48,32},{1,49},{17,1},{33,17},{49,33},{2,50}... | collective-permute-start | bytes 393224 | tf_op jit(solution)/shard_map/ppermute | solution.py:228
  53.1 10.4 %collective-permute-start.6 = (bf16[256,256]{1,0:T(8,128)(2,1)S(1)}, bf16[256,256]{1,0:T(8,128)(2,1)S(1)}, u32[]{:S(2)}, u32[]{:S(2)}) collective-permute-start(bf16[256,256]{1,0:T(8,128)(2,1)S(1)} %get-tuple-element.71), channel_id=1, source_target_pairs={{0,64},{1,193},{64,0},{65,129},{128,192},{129,65},{192,128},{193,1... | collective-permute-start | bytes 393224 | tf_op jit(solution)/shard_map/ppermute | solution.py:234
  53.4 10.0 %collective-permute-start.7 = (bf16[256,256]{1,0:T(8,128)(2,1)S(1)}, bf16[256,256]{1,0:T(8,128)(2,1)S(1)}, u32[]{:S(2)}, u32[]{:S(2)}) collective-permute-start(bf16[256,256]{1,0:T(8,128)(2,1)S(1)} %get-tuple-element.72), channel_id=1, source_target_pairs={{0,192},{1,65},{64,128},{65,1},{128,64},{129,193},{192,0},{193,129... | collective-permute-start | bytes 393224 | tf_op jit(solution)/shard_map/ppermute | solution.py:234
  56.0 7.4 %collective-permute-start.8 = (bf16[256,256]{1,0:T(8,128)(2,1)S(1)}, bf16[256,256]{1,0:T(8,128)(2,1)S(1)}, u32[]{:S(2)}, u32[]{:S(2)}) collective-permute-start(bf16[256,256]{1,0:T(8,128)(2,1)S(1)} %get-tuple-element.73), channel_id=1, source_target_pairs={{0,128},{64,192},{128,0},{192,64},{1,129},{65,193},{129,1},{193,65... | collective-permute-start | bytes 393224 | tf_op jit(solution)/shard_map/ppermute | solution.py:228
  60.1 12.4 %all-to-all-start.1 = ((bf16[8,32,256]{2,1,0:T(8,128)(2,1)}), bf16[8,32,256]{2,1,0:T(8,128)(2,1)S(1)}, u32[]{:S(2)}, u32[]{:S(2)}) async-start(bf16[8,32,256]{2,1,0:T(8,128)(2,1)} %add_convert_fusion), calls=%async_computation.1 | async-start | bytes 262144 | tf_op jit(solution)/shard_map/all_to_all | solution.py:249

commit v15 on v12

--- a/solution.py
+++ b/solution.py
@@ -9,6 +9,7 @@
 
 X = ("x",)
 Y = ("h", "l")
+SHIFTS = (3, 2, 1)
 F32 = jnp.float32
 BF16 = jnp.bfloat16
 LOG2E = 1.4426950408889634
@@ -246,13 +247,13 @@
 
 
 def spread(block, axes):
-    return [block] + [shift(block, axes, s) for s in range(1, lax.axis_size(axes))]
-
-
-def collect(pieces, axes, direction):
+    return [block] + [shift(block, axes, s) for s in SHIFTS]
+
+
+def collect(pieces, axes):
     total = pieces[0]
-    for s in range(1, lax.axis_size(axes)):
-        total = total + shift(pieces[s].astype(BF16), axes, direction * s).astype(F32)
+    for s in (2, 1, 3):
+        total = total + shift(pieces[SHIFTS.index(s) + 1].astype(BF16), axes, -s).astype(F32)
     return total
 
 
@@ -289,7 +290,7 @@
     coef_theirs, land_theirs, row_total, dembed = backward_first(theirs, n_z, kern_theirs, shares, cot, feat, -gamma, n_x)
     coef_mine, land_mine, row_total = backward(mine, n_z, kern_mine, dembed, feat, row_total)
     land_share = (land_mine + shift(land_theirs, "c", 1).astype(F32)).reshape(n_y, n_z, rows, width)
-    land_share = collect(land_share, Y, -1)
+    land_share = collect(land_share, Y)
 
     own, first, second, opposite = feature_share(mine + theirs, n_z, [coef_mine, coef_theirs], feat_t, row_total, n_x, rank)
     landmark_grad = collect_at_once(land_share, "z")

time: 75 us -> 74.3 us (level); the launches traced: 74.4 us -> 72.9 us
  starting transfers between devices: 29 us -> 26.6 us
  waiting for transfers between devices: 30.7 us -> 31.5 us
    ppermute x9, starting transfers between devices: 9.75 us -> 7.4 us  [shift(): lax.ppermute(block, axes, [(i, (i + step) % size) for i in range(size)])]
    ppermute x9, waiting for transfers between devices: 8.38 us -> 9.22 us  [shift(): lax.ppermute(block, axes, [(i, (i + step) % size) for i in range(size)])]
  transfers between devices with their start and end apart: 15 -> 15, of which waited for: 9 -> 11; matrix products, arithmetic and copies ran while one was open for 2% -> 2% of each run, Pallas kernels for 6% -> 6%
where the time goes in v15:
time: 74.3 us; the launch traced here: 72.9 us
  waiting for transfers between devices  31.5 us (42%)
  starting transfers between devices  26.6 us (36%)
  Pallas kernels  9.23 us (12%)
  local copies, waits for them, and re-layouts  3.05 us (4%)
  other arithmetic  1.65 us (2%)
  between operations  0.78 us (1%)
    ppermute x9, waiting for transfers between devices, shift(): lax.ppermute(block, axes, [(i, (i + step) % size) for i in range(size)])  9.22 us
    all_to_all x1, starting transfers between devices, per_device(): lax.all_to_all(pack(landmarks, whitening, n_z), 'z', 0, 0, tiled=True)  8.48 us
    all_to_all x1, waiting for transfers between devices, collect_at_once(): lax.all_to_all(pieces.astype(BF16), axes, 0, 0, tiled=True).astype(F32)  8.06 us
    pallas_call x8, Pallas kernels, call(): pl.pallas_call(body, out_shape=out_shape, in_specs=[WHOLE] * len(operands...  7.75 us
    ppermute x9, starting transfers between devices, shift(): lax.ppermute(block, axes, [(i, (i + step) % size) for i in range(size)])  7.4 us
    ppermute x4, starting transfers between devices, partner(): return lax.ppermute(block, ring + ('c',), perm)  7.37 us
    all_to_all x1, waiting for transfers between devices, per_device(): lax.all_to_all(pack(landmarks, whitening, n_z), 'z', 0, 0, tiled=True)  7.35 us
    ppermute x4, waiting for transfers between devices, partner(): return lax.ppermute(block, ring + ('c',), perm)  6.91 us
  transfers between devices with their start and end apart: 15, of which 11 were waited for; matrix products, arithmetic and copies ran while one was open for 2% of the time, Pallas kernels for 6%

profile of v15, /device:TPU:24, one launch (start us, length us, event | category | flops | bytes accessed | tf_op | source)
XLA Modules:
  0.0 72.9 jit_solution(9555452027571899738)
XLA Ops:
  0.6 1.5 %shard_map.59 = bf16[8,40,256]{2,1,0:T(8,128)(2,1)} custom-call(bf16[32,256]{1,0:T(8,128)(2,1)} %landmarks.1, bf16[32,64]{1,0:T(8,128)(2,1)} %whitening.1), custom_call_target="tpu_custom_call" | custom-call | tf_op jit(solution)/shard_map/pallas_call | solution.py:52
  2.1 8.5 %all-to-all-start = ((bf16[8,40,256]{2,1,0:T(8,128)(2,1)}), bf16[8,40,256]{2,1,0:T(8,128)(2,1)S(1)}, u32[]{:S(2)}, u32[]{:S(2)}) async-start(bf16[8,40,256]{2,1,0:T(8,128)(2,1)} %shard_map.59), calls=%async_computation | async-start | bytes 327680 | tf_op jit(solution)/shard_map/all_to_all | solution.py:276
  10.6 0.0 copy-start
  10.6 1.2 %copy-done = bf16[2048,256]{1,0:T(8,128)(2,1)S(1)} copy-done((bf16[2048,256]{1,0:T(8,128)(2,1)S(1)}, bf16[2048,256]{1,0:T(8,128)(2,1)}, u32[]{:S(2)}) %copy-start) | copy-done | bytes 1048600
  11.8 0.0 copy-start.1
  11.8 0.9 %copy-done.1 = bf16[2048,64]{0,1:T(8,128)(2,1)S(1)} copy-done((bf16[2048,64]{0,1:T(8,128)(2,1)S(1)}, bf16[2048,64]{0,1:T(8,128)(2,1)}, u32[]{:S(2)}) %copy-start.1) | copy-done | bytes 262168
  12.8 0.2 shard_map.60
  13.0 7.3 %all-to-all-done.refs_0_ = bf16[8,40,256]{2,1,0:T(8,128)(2,1)S(1)} async-done(((bf16[8,40,256]{2,1,0:T(8,128)(2,1)}), bf16[8,40,256]{2,1,0:T(8,128)(2,1)S(1)}, u32[]{:S(2)}, u32[]{:S(2)}) %all-to-all-start) | async-done | bytes 163872 | tf_op jit(solution)/shard_map/all_to_all | solution.py:276
  20.4 0.2 collective-permute-start.2
  20.6 2.6 %collective-permute-start.1 = (bf16[8,40,256]{2,1,0:T(8,128)(2,1)S(1)}, bf16[8,40,256]{2,1,0:T(8,128)(2,1)S(1)}, u32[]{:S(2)}, u32[]{:S(2)}) collective-permute-start(bf16[8,40,256]{2,1,0:T(8,128)(2,1)S(1)} %all-to-all-done.refs_0_), channel_id=1, source_target_pairs={{0,32},{16,48},{32,0},{48,16},{1,33},{17,49},{33,1},{49,17},{2,34}... | collective-permute-start | bytes 491528 | tf_op jit(solution)/shard_map/ppermute | solution.py:240
  23.2 0.0 collective-permute-start
  23.2 0.5 shard_map.61
  23.7 2.5 %collective-permute-done.2.refs_2_.refs_3_ = bf16[8,40,256]{2,1,0:T(8,128)(2,1)S(1)} collective-permute-done((bf16[8,40,256]{2,1,0:T(8,128)(2,1)S(1)}, bf16[8,40,256]{2,1,0:T(8,128)(2,1)S(1)}, u32[]{:S(2)}, u32[]{:S(2)}) %collective-permute-start.2) | collective-permute-done | bytes 163872 | tf_op jit(solution)/shard_map/ppermute | solution.py:240
  26.2 1.8 %collective-permute-done.1.refs_1_.refs_2_ = bf16[8,40,256]{2,1,0:T(8,128)(2,1)S(1)} collective-permute-done((bf16[8,40,256]{2,1,0:T(8,128)(2,1)S(1)}, bf16[8,40,256]{2,1,0:T(8,128)(2,1)S(1)}, u32[]{:S(2)}, u32[]{:S(2)}) %collective-permute-start.1) | collective-permute-done | bytes 163872 | tf_op jit(solution)/shard_map/ppermute | solution.py:240
  28.0 1.8 %collective-permute-done.refs_0_.refs_1_ = bf16[8,40,256]{2,1,0:T(8,128)(2,1)S(1)} collective-permute-done((bf16[8,40,256]{2,1,0:T(8,128)(2,1)S(1)}, bf16[8,40,256]{2,1,0:T(8,128)(2,1)S(1)}, u32[]{:S(2)}, u32[]{:S(2)}) %collective-permute-start) | collective-permute-done | bytes 163872 | tf_op jit(solution)/shard_map/ppermute | solution.py:240
  29.7 0.1 pad_maximum_fusion
  29.8 0.1 collective-permute-start.3
  29.9 1.2 %shard_map.62 = (f32[256,1024]{1,0:T(8,128)S(1)}, f32[256,1024]{1,0:T(8,128)S(1)}, f32[256,1024]{1,0:T(8,128)S(1)}, f32[64,1024]{1,0:T(8,128)S(1)}) custom-call(bf16[8,40,256]{2,1,0:T(8,128)(2,1)S(1)} %collective-permute-done.refs_0_.refs_1_, bf16[8,40,256]{2,1,0:T(8,128)(2,1)S(1)} %collective-permute-done.1.refs_1_.refs_2_, ...), custom_call_target="tpu_custom_call" | custom-call | tf_op jit(solution)/shard_map/pallas_call | solution.py:21
  31.1 0.9 %collective-permute-done.3.refs_0_.refs_4_ = bf16[32,40,256]{2,1,0:T(8,128)(2,1)S(1)} collective-permute-done((bf16[32,40,256]{2,1,0:T(8,128)(2,1)S(1)}, bf16[32,40,256]{2,1,0:T(8,128)(2,1)S(1)}, u32[]{:S(2)}, u32[]{:S(2)}) %collective-permute-start.3) | collective-permute-done | bytes 655392 | tf_op jit(solution)/shard_map/ppermute | solution.py:240
  32.0 1.5 %shard_map.63 = (f32[256,1024]{1,0:T(8,128)S(1)}, f32[256,1024]{1,0:T(8,128)S(1)}, f32[256,1024]{1,0:T(8,128)S(1)}, f32[256,1024]{1,0:T(8,128)S(1)}, f32[64,1024...) custom-call(bf16[32,40,256]{2,1,0:T(8,128)(2,1)S(1)} %collective-permute-done.3.refs_0_.refs_4_, ...), custom_call_target="tpu_custom_call" | custom-call | tf_op jit(solution)/shard_map/pallas_call | solution.py:21
  33.5 1.6 %collective-permute-start.4 = (bf16[64,1024]{1,0:T(8,128)(2,1)S(1)}, bf16[64,1024]{1,0:T(8,128)(2,1)S(1)}, u32[]{:S(2)}, u32[]{:S(2)}) collective-permute-start(bf16[64,1024]{1,0:T(8,128)(2,1)S(1)} %get-tuple-element.62), channel_id=1, source_target_pairs={{0,64},{1,193},{64,0},{65,129},{128,192},{129,65},{192,128},{193,1... | collective-permute-start | bytes 393224 | tf_op jit(solution)/shard_map/ppermute | solution.py:246
  35.1 3.5 %collective-permute-done.4.other = bf16[64,1024]{1,0:T(8,128)(2,1)S(1)} collective-permute-done((bf16[64,1024]{1,0:T(8,128)(2,1)S(1)}, bf16[64,1024]{1,0:T(8,128)(2,1)S(1)}, u32[]{:S(2)}, u32[]{:S(2)}) %collective-permute-start.4) | collective-permute-done | bytes 131104 | tf_op jit(solution)/shard_map/ppermute | solution.py:246
  38.7 2.8 %collective-permute-start.5 = (bf16[64,1024]{1,0:T(8,128)(2,1)S(1)}, bf16[64,1024]{1,0:T(8,128)(2,1)S(1)}, u32[]{:S(2)}, u32[]{:S(2)}) collective-permute-start(bf16[64,1024]{1,0:T(8,128)(2,1)S(1)} %get-tuple-element.64), channel_id=1, source_target_pairs={{0,192},{1,65},{64,128},{65,1},{128,64},{129,193},{192,0},{193,129... | collective-permute-start | bytes 393224 | tf_op jit(solution)/shard_map/ppermute | solution.py:246
  41.5 3.4 %collective-permute-done.5.refs_6_ = bf16[64,1024]{1,0:T(8,128)(2,1)S(1)} collective-permute-done((bf16[64,1024]{1,0:T(8,128)(2,1)S(1)}, bf16[64,1024]{1,0:T(8,128)(2,1)S(1)}, u32[]{:S(2)}, u32[]{:S(2)}) %collective-permute-start.5) | collective-permute-done | bytes 131104 | tf_op jit(solution)/shard_map/ppermute | solution.py:246
  44.9 1.5 %shard_map.65 = (bf16[1024,1024]{1,0:T(8,128)(2,1)S(1)}, bf16[1024,256]{1,0:T(8,128)(2,1)S(1)}, f32[1,1024]{1,0:T(1,128)S(1)}, bf16[64,1024]{1,0:T(8,128)(2,1)S(1)}) custom-call(bf16[32,40,256]{2,1,0:T(8,128)(2,1)S(1)} %collective-permute-done.3.refs_0_.refs_4_, f32[256,1024]{1,0:T(8,128)S(1)} %get-tuple-element.57.refs_1_, ...), custom_call_target="tpu_custom_call" | custom-call | tf_op jit(solution)/shard_map/pallas_call | solution.py:21
  46.4 0.1 collective-permute-start.9
  46.5 1.5 %shard_map.66 = (bf16[1024,1024]{1,0:T(8,128)(2,1)S(1)}, f32[1024,256]{1,0:T(8,128)S(1)}, f32[1,1024]{1,0:T(1,128)S(1)}) custom-call(bf16[8,40,256]{2,1,0:T(8,128)(2,1)S(1)} %all-to-all-done.refs_0_, bf16[8,40,256]{2,1,0:T(8,128)(2,1)S(1)} %collective-permute-done.refs_0_.refs_1_, bf16[8,40,256]{2,1,0:T(8,128)(2,1)S(1)} %collective-permute-done.1.refs_1_.refs_2_, ...), custom_call_target="tpu_custom_call" | custom-call | tf_op jit(solution)/shard_map/pallas_call | solution.py:21
  48.0 0.4 collective-permute-done.9
  48.4 0.1 fusion
  48.6 0.9 %collective-permute-start.12 = (bf16[8,32,256]{2,1,0:T(8,128)(2,1)S(1)}, bf16[8,32,256]{2,1,0:T(8,128)(2,1)S(1)}, u32[]{:S(2)}, u32[]{:S(2)}) collective-permute-start(bf16[8,32,256]{2,1,0:T(8,128)(2,1)S(1)} %bitcast.11), channel_id=1, source_target_pairs={{0,16},{16,32},{32,48},{48,0},{1,17},{17,33},{33,49},{49,1},{2,18}... | collective-permute-start | bytes 393224 | tf_op jit(solution)/shard_map/ppermute | solution.py:240
  49.5 2.0 %collective-permute-start.10 = (bf16[8,32,256]{2,1,0:T(8,128)(2,1)S(1)}, bf16[8,32,256]{2,1,0:T(8,128)(2,1)S(1)}, u32[]{:S(2)}, u32[]{:S(2)}) collective-permute-start(bf16[8,32,256]{2,1,0:T(8,128)(2,1)S(1)} %bitcast.10), channel_id=1, source_target_pairs={{0,32},{16,48},{32,0},{48,16},{1,33},{17,49},{33,1},{49,17},{2,34}... | collective-permute-start | bytes 393224 | tf_op jit(solution)/shard_map/ppermute | solution.py:240
  51.6 0.0 collective-permute-start.11
  51.6 1.3 %shard_map.67 = (f32[256,256]{1,0:T(8,128)S(1)}, bf16[256,256]{1,0:T(8,128)(2,1)S(1)}, bf16[256,256]{1,0:T(8,128)(2,1)S(1)}, bf16[256,256]{1,0:T(8,128)(2,1)S(1)}) custom-call(bf16[8,40,256]{2,1,0:T(8,128)(2,1)S(1)} %all-to-all-done.refs_0_, bf16[8,40,256]{2,1,0:T(8,128)(2,1)S(1)} %collective-permute-done.refs_0_.refs_1_, ...), custom_call_target="tpu_custom_call" | custom-call | tf_op jit(solution)/shard_map/pallas_call | solution.py:21
  52.8 0.4 collective-permute-start.6
  53.2 2.6 %collective-permute-start.7 = (bf16[256,256]{1,0:T(8,128)(2,1)S(1)}, bf16[256,256]{1,0:T(8,128)(2,1)S(1)}, u32[]{:S(2)}, u32[]{:S(2)}) collective-permute-start(bf16[256,256]{1,0:T(8,128)(2,1)S(1)} %get-tuple-element.74), channel_id=1, source_target_pairs={{0,192},{1,65},{64,128},{65,1},{128,64},{129,193},{192,0},{193,129... | collective-permute-start | bytes 393224 | tf_op jit(solution)/shard_map/ppermute | solution.py:246
  55.8 0.0 collective-permute-done.12
  55.8 1.5 %collective-permute-start.8 = (bf16[256,256]{1,0:T(8,128)(2,1)S(1)}, bf16[256,256]{1,0:T(8,128)(2,1)S(1)}, u32[]{:S(2)}, u32[]{:S(2)}) collective-permute-start(bf16[256,256]{1,0:T(8,128)(2,1)S(1)} %get-tuple-element.75), channel_id=1, source_target_pairs={{0,128},{64,192},{128,0},{192,64},{1,129},{65,193},{129,1},{193,65... | collective-permute-start | bytes 393224 | tf_op jit(solution)/shard_map/ppermute | solution.py:240
  57.3 0.2 collective-permute-done.10
  57.4 1.7 %collective-permute-done.11 = bf16[8,32,256]{2,1,0:T(8,128)(2,1)S(1)} collective-permute-done((bf16[8,32,256]{2,1,0:T(8,128)(2,1)S(1)}, bf16[8,32,256]{2,1,0:T(8,128)(2,1)S(1)}, u32[]{:S(2)}, u32[]{:S(2)}) %collective-permute-start.11) | collective-permute-done | bytes 131104 | tf_op jit(solution)/shard_map/ppermute | solution.py:240
  59.1 0.7 %add_convert_fusion = bf16[8,32,256]{2,1,0:T(8,128)(2,1)} fusion(bf16[8,32,256]{2,1,0:T(8,128)(2,1)S(1)} %collective-permute-done.12, bf16[8,32,256]{2,1,0:T(8,128)(2,1)S(1)} %collective-permute-done.11, f32[8,32,256]{2,1,0:T(8,128)S(1)} %bitcast.8, bf16[8,32,256]{2,1,0:T(8,128)(2,1)S(1)} %collective-permute-done.10), kind=kLoop, calls=%fused_computation.3 | loop fusion | flops 458752 | bytes 786432 | tf_op jit(solution)/shard_map/convert_element_type | solution.py:261
  59.9 3.4 %all-to-all-start.1 = ((bf16[8,32,256]{2,1,0:T(8,128)(2,1)}), bf16[8,32,256]{2,1,0:T(8,128)(2,1)S(1)}, u32[]{:S(2)}, u32[]{:S(2)}) async-start(bf16[8,32,256]{2,1,0:T(8,128)(2,1)} %add_convert_fusion), calls=%async_computation.1 | async-start | bytes 262144 | tf_op jit(solution)/shard_map/all_to_all | solution.py:261
  63.2 0.0 collective-permute-done.6
  63.2 0.0 collective-permute-done.7
  63.3 0.0 collective-permute-done.8
  63.3 0.1 add_bitcast_fusion
  63.3 0.8 %copy.6 = f32[256,256]{1,0:T(8,128)} copy(f32[256,256]{0,1:T(8,128)S(1)} %add_bitcast_fusion) | data formatting | bytes 524288
  64.2 8.1 %all-to-all-done.1 = bf16[8,32,256]{2,1,0:T(8,128)(2,1)S(1)} async-done(((bf16[8,32,256]{2,1,0:T(8,128)(2,1)}), bf16[8,32,256]{2,1,0:T(8,128)(2,1)S(1)}, u32[]{:S(2)}, u32[]{:S(2)}) %all-to-all-start.1) | async-done | bytes 131104 | tf_op jit(solution)/shard_map/all_to_all | solution.py:261
  72.2 0.6 convert_reduce_fusion
  (3 shorter events, 0.1 us)
Async XLA Ops:
  2.1 18.2 %all-to-all-start = ((bf16[8,40,256]{2,1,0:T(8,128)(2,1)}), bf16[8,40,256]{2,1,0:T(8,128)(2,1)S(1)}, u32[]{:S(2)}, u32[]{:S(2)}) async-start(bf16[8,40,256]{2,1,0:T(8,128)(2,1)} %shard_map.59), calls=%async_computation | async-start | bytes 327680 | tf_op jit(solution)/shard_map/all_to_all | solution.py:276
  10.6 1.2 %copy-start = (bf16[2048,256]{1,0:T(8,128)(2,1)S(1)}, bf16[2048,256]{1,0:T(8,128)(2,1)}, u32[]{:S(2)}) copy-start(bf16[2048,256]{1,0:T(8,128)(2,1)} %features.1) | copy-start | bytes 3145732
  11.8 0.9 %copy-start.1 = (bf16[2048,64]{0,1:T(8,128)(2,1)S(1)}, bf16[2048,64]{0,1:T(8,128)(2,1)}, u32[]{:S(2)}) copy-start(bf16[2048,64]{0,1:T(8,128)(2,1)} %param.7) | copy-start | bytes 786436
  20.4 5.8 %collective-permute-start.2 = (bf16[8,40,256]{2,1,0:T(8,128)(2,1)S(1)}, bf16[8,40,256]{2,1,0:T(8,128)(2,1)S(1)}, u32[]{:S(2)}, u32[]{:S(2)}) collective-permute-start(bf16[8,40,256]{2,1,0:T(8,128)(2,1)S(1)} %all-to-all-done.refs_0_), channel_id=1, source_target_pairs={{0,16},{16,32},{32,48},{48,0},{1,17},{17,33},{33,49},{49,1},{2,18}... | collective-permute-start | bytes 491528 | tf_op jit(solution)/shard_map/ppermute | solution.py:240
  20.6 7.4 %collective-permute-start.1 = (bf16[8,40,256]{2,1,0:T(8,128)(2,1)S(1)}, bf16[8,40,256]{2,1,0:T(8,128)(2,1)S(1)}, u32[]{:S(2)}, u32[]{:S(2)}) collective-permute-start(bf16[8,40,256]{2,1,0:T(8,128)(2,1)S(1)} %all-to-all-done.refs_0_), channel_id=1, source_target_pairs={{0,32},{16,48},{32,0},{48,16},{1,33},{17,49},{33,1},{49,17},{2,34}... | collective-permute-start | bytes 491528 | tf_op jit(solution)/shard_map/ppermute | solution.py:240
  23.2 6.6 %collective-permute-start = (bf16[8,40,256]{2,1,0:T(8,128)(2,1)S(1)}, bf16[8,40,256]{2,1,0:T(8,128)(2,1)S(1)}, u32[]{:S(2)}, u32[]{:S(2)}) collective-permute-start(bf16[8,40,256]{2,1,0:T(8,128)(2,1)S(1)} %all-to-all-done.refs_0_), channel_id=1, source_target_pairs={{0,48},{16,0},{32,16},{48,32},{1,49},{17,1},{33,17},{49,33},{2,50}... | collective-permute-start | bytes 491528 | tf_op jit(solution)/shard_map/ppermute | solution.py:240
  29.8 2.2 %collective-permute-start.3 = (bf16[32,40,256]{2,1,0:T(8,128)(2,1)S(1)}, bf16[32,40,256]{2,1,0:T(8,128)(2,1)S(1)}, u32[]{:S(2)}, u32[]{:S(2)}) collective-permute-start(bf16[32,40,256]{2,1,0:T(8,128)(2,1)S(1)} %pad_maximum_fusion), channel_id=1, source_target_pairs={{0,1},{1,0},{2,3},{3,2},{4,5},{5,4},{6,7},{7,6},{8,9},{9,8},{10,11... | collective-permute-start | bytes 1966088 | tf_op jit(solution)/shard_map/ppermute | solution.py:240
  33.5 5.1 %collective-permute-start.4 = (bf16[64,1024]{1,0:T(8,128)(2,1)S(1)}, bf16[64,1024]{1,0:T(8,128)(2,1)S(1)}, u32[]{:S(2)}, u32[]{:S(2)}) collective-permute-start(bf16[64,1024]{1,0:T(8,128)(2,1)S(1)} %get-tuple-element.62), channel_id=1, source_target_pairs={{0,64},{1,193},{64,0},{65,129},{128,192},{129,65},{192,128},{193,1... | collective-permute-start | bytes 393224 | tf_op jit(solution)/shard_map/ppermute | solution.py:246
  38.7 6.3 %collective-permute-start.5 = (bf16[64,1024]{1,0:T(8,128)(2,1)S(1)}, bf16[64,1024]{1,0:T(8,128)(2,1)S(1)}, u32[]{:S(2)}, u32[]{:S(2)}) collective-permute-start(bf16[64,1024]{1,0:T(8,128)(2,1)S(1)} %get-tuple-element.64), channel_id=1, source_target_pairs={{0,192},{1,65},{64,128},{65,1},{128,64},{129,193},{192,0},{193,129... | collective-permute-start | bytes 393224 | tf_op jit(solution)/shard_map/ppermute | solution.py:246
  46.4 2.0 %collective-permute-start.9 = (bf16[1024,256]{1,0:T(8,128)(2,1)S(1)}, bf16[1024,256]{1,0:T(8,128)(2,1)S(1)}, u32[]{:S(2)}, u32[]{:S(2)}) collective-permute-start(bf16[1024,256]{1,0:T(8,128)(2,1)S(1)} %get-tuple-element.77), channel_id=1, source_target_pairs={{0,1},{1,0},{2,3},{3,2},{4,5},{5,4},{6,7},{7,6},{8,9},{9,8},{10,11... | collective-permute-start | bytes 1572872 | tf_op jit(solution)/shard_map/ppermute | solution.py:240
  48.6 7.2 %collective-permute-start.12 = (bf16[8,32,256]{2,1,0:T(8,128)(2,1)S(1)}, bf16[8,32,256]{2,1,0:T(8,128)(2,1)S(1)}, u32[]{:S(2)}, u32[]{:S(2)}) collective-permute-start(bf16[8,32,256]{2,1,0:T(8,128)(2,1)S(1)} %bitcast.11), channel_id=1, source_target_pairs={{0,16},{16,32},{32,48},{48,0},{1,17},{17,33},{33,49},{49,1},{2,18}... | collective-permute-start | bytes 393224 | tf_op jit(solution)/shard_map/ppermute | solution.py:240
  49.5 7.9 %collective-permute-start.10 = (bf16[8,32,256]{2,1,0:T(8,128)(2,1)S(1)}, bf16[8,32,256]{2,1,0:T(8,128)(2,1)S(1)}, u32[]{:S(2)}, u32[]{:S(2)}) collective-permute-start(bf16[8,32,256]{2,1,0:T(8,128)(2,1)S(1)} %bitcast.10), channel_id=1, source_target_pairs={{0,32},{16,48},{32,0},{48,16},{1,33},{17,49},{33,1},{49,17},{2,34}... | collective-permute-start | bytes 393224 | tf_op jit(solution)/shard_map/ppermute | solution.py:240
  51.6 7.6 %collective-permute-start.11 = (bf16[8,32,256]{2,1,0:T(8,128)(2,1)S(1)}, bf16[8,32,256]{2,1,0:T(8,128)(2,1)S(1)}, u32[]{:S(2)}, u32[]{:S(2)}) collective-permute-start(bf16[8,32,256]{2,1,0:T(8,128)(2,1)S(1)} %bitcast.9), channel_id=1, source_target_pairs={{0,48},{16,0},{32,16},{48,32},{1,49},{17,1},{33,17},{49,33},{2,50}... | collective-permute-start | bytes 393224 | tf_op jit(solution)/shard_map/ppermute | solution.py:240
  52.8 10.4 %collective-permute-start.6 = (bf16[256,256]{1,0:T(8,128)(2,1)S(1)}, bf16[256,256]{1,0:T(8,128)(2,1)S(1)}, u32[]{:S(2)}, u32[]{:S(2)}) collective-permute-start(bf16[256,256]{1,0:T(8,128)(2,1)S(1)} %get-tuple-element.73), channel_id=1, source_target_pairs={{0,64},{1,193},{64,0},{65,129},{128,192},{129,65},{192,128},{193,1... | collective-permute-start | bytes 393224 | tf_op jit(solution)/shard_map/ppermute | solution.py:246
  53.2 10.0 %collective-permute-start.7 = (bf16[256,256]{1,0:T(8,128)(2,1)S(1)}, bf16[256,256]{1,0:T(8,128)(2,1)S(1)}, u32[]{:S(2)}, u32[]{:S(2)}) collective-permute-start(bf16[256,256]{1,0:T(8,128)(2,1)S(1)} %get-tuple-element.74), channel_id=1, source_target_pairs={{0,192},{1,65},{64,128},{65,1},{128,64},{129,193},{192,0},{193,129... | collective-permute-start | bytes 393224 | tf_op jit(solution)/shard_map/ppermute | solution.py:246
  55.8 7.4 %collective-permute-start.8 = (bf16[256,256]{1,0:T(8,128)(2,1)S(1)}, bf16[256,256]{1,0:T(8,128)(2,1)S(1)}, u32[]{:S(2)}, u32[]{:S(2)}) collective-permute-start(bf16[256,256]{1,0:T(8,128)(2,1)S(1)} %get-tuple-element.75), channel_id=1, source_target_pairs={{0,128},{64,192},{128,0},{192,64},{1,129},{65,193},{129,1},{193,65... | collective-permute-start | bytes 393224 | tf_op jit(solution)/shard_map/ppermute | solution.py:240
  59.9 12.4 %all-to-all-start.1 = ((bf16[8,32,256]{2,1,0:T(8,128)(2,1)}), bf16[8,32,256]{2,1,0:T(8,128)(2,1)S(1)}, u32[]{:S(2)}, u32[]{:S(2)}) async-start(bf16[8,32,256]{2,1,0:T(8,128)(2,1)} %add_convert_fusion), calls=%async_computation.1 | async-start | bytes 262144 | tf_op jit(solution)/shard_map/all_to_all | solution.py:261

commit v16 on v14

--- a/solution.py
+++ b/solution.py
@@ -9,7 +9,7 @@
 
 X = ("x",)
 Y = ("h", "l")
-SHIFTS = (3, 2, 1)
+SHIFTS = (3, 1, 2)
 F32 = jnp.float32
 BF16 = jnp.bfloat16
 LOG2E = 1.4426950408889634

time: 74.6 us -> 74.5 us (level)
  transfers between devices with their start and end apart: 15 -> 15, of which waited for: 11 -> 10; matrix products, arithmetic and copies ran while one was open for 2% -> 2% of each run, Pallas kernels for 6% -> 6%
where the time goes in v16:
time: 74.5 us; the launch traced here: 73.6 us
  waiting for transfers between devices  31.9 us (43%)
  starting transfers between devices  26.7 us (36%)
  Pallas kernels  9.41 us (13%)
  local copies, waits for them, and re-layouts  3.05 us (4%)
  other arithmetic  1.69 us (2%)
  between operations  0.77 us (1%)
    ppermute x9, waiting for transfers between devices, shift(): lax.ppermute(block, axes, [(i, (i + step) % size) for i in range(size)])  9.19 us
    all_to_all x1, waiting for transfers between devices, collect_at_once(): lax.all_to_all(pieces.astype(BF16), axes, 0, 0, tiled=True).astype(F32)  8.5 us
    all_to_all x1, starting transfers between devices, per_device(): lax.all_to_all(pack(landmarks, whitening, n_z), 'z', 0, 0, tiled=True)  8.48 us
    pallas_call x9, Pallas kernels, call(): pl.pallas_call(body, out_shape=out_shape, in_specs=[WHOLE] * len(operands...  7.93 us
    ppermute x9, starting transfers between devices, shift(): lax.ppermute(block, axes, [(i, (i + step) % size) for i in range(size)])  7.53 us
    ppermute x4, starting transfers between devices, partner(): return lax.ppermute(block, ring + ('c',), perm)  7.37 us
    all_to_all x1, waiting for transfers between devices, per_device(): lax.all_to_all(pack(landmarks, whitening, n_z), 'z', 0, 0, tiled=True)  7.35 us
    ppermute x4, waiting for transfers between devices, partner(): return lax.ppermute(block, ring + ('c',), perm)  6.9 us
  transfers between devices with their start and end apart: 15, of which 10 were waited for; matrix products, arithmetic and copies ran while one was open for 2% of the time, Pallas kernels for 6%

profile of v16, /device:TPU:24, one launch (start us, length us, event | category | flops | bytes accessed | tf_op | source)
XLA Modules:
  0.0 73.6 jit_solution(3379241505339574562)
XLA Ops:
  0.6 1.5 %shard_map.59 = bf16[8,40,256]{2,1,0:T(8,128)(2,1)} custom-call(bf16[32,256]{1,0:T(8,128)(2,1)} %landmarks.1, bf16[32,64]{1,0:T(8,128)(2,1)} %whitening.1), custom_call_target="tpu_custom_call" | custom-call | tf_op jit(solution)/shard_map/pallas_call | solution.py:52
  2.1 8.5 %all-to-all-start = ((bf16[8,40,256]{2,1,0:T(8,128)(2,1)}), bf16[8,40,256]{2,1,0:T(8,128)(2,1)S(1)}, u32[]{:S(2)}, u32[]{:S(2)}) async-start(bf16[8,40,256]{2,1,0:T(8,128)(2,1)} %shard_map.59), calls=%async_computation | async-start | bytes 327680 | tf_op jit(solution)/shard_map/all_to_all | solution.py:264
  10.6 0.0 copy-start
  10.6 1.2 %copy-done = bf16[2048,256]{1,0:T(8,128)(2,1)S(1)} copy-done((bf16[2048,256]{1,0:T(8,128)(2,1)S(1)}, bf16[2048,256]{1,0:T(8,128)(2,1)}, u32[]{:S(2)}) %copy-start) | copy-done | bytes 1048600
  11.8 0.9 %copy-done.1 = bf16[2048,64]{0,1:T(8,128)(2,1)S(1)} copy-done((bf16[2048,64]{0,1:T(8,128)(2,1)S(1)}, bf16[2048,64]{0,1:T(8,128)(2,1)}, u32[]{:S(2)}) %copy-start.1) | copy-done | bytes 262168
  12.8 0.2 shard_map.60
  13.0 7.3 %all-to-all-done.refs_0_ = bf16[8,40,256]{2,1,0:T(8,128)(2,1)S(1)} async-done(((bf16[8,40,256]{2,1,0:T(8,128)(2,1)}), bf16[8,40,256]{2,1,0:T(8,128)(2,1)S(1)}, u32[]{:S(2)}, u32[]{:S(2)}) %all-to-all-start) | async-done | bytes 163872 | tf_op jit(solution)/shard_map/all_to_all | solution.py:264
  20.4 1.2 %collective-permute-start.2 = (bf16[8,40,256]{2,1,0:T(8,128)(2,1)S(1)}, bf16[8,40,256]{2,1,0:T(8,128)(2,1)S(1)}, u32[]{:S(2)}, u32[]{:S(2)}) collective-permute-start(bf16[8,40,256]{2,1,0:T(8,128)(2,1)S(1)} %all-to-all-done.refs_0_), channel_id=1, source_target_pairs={{0,32},{16,48},{32,0},{48,16},{1,33},{17,49},{33,1},{49,17},{2,34}... | collective-permute-start | bytes 491528 | tf_op jit(solution)/shard_map/ppermute | solution.py:228
  21.6 2.2 %collective-permute-start.1 = (bf16[8,40,256]{2,1,0:T(8,128)(2,1)S(1)}, bf16[8,40,256]{2,1,0:T(8,128)(2,1)S(1)}, u32[]{:S(2)}, u32[]{:S(2)}) collective-permute-start(bf16[8,40,256]{2,1,0:T(8,128)(2,1)S(1)} %all-to-all-done.refs_0_), channel_id=1, source_target_pairs={{0,16},{16,32},{32,48},{48,0},{1,17},{17,33},{33,49},{49,1},{2,18}... | collective-permute-start | bytes 491528 | tf_op jit(solution)/shard_map/ppermute | solution.py:228
  23.8 0.0 collective-permute-start
  23.8 0.5 shard_map.61
  24.3 3.5 %collective-permute-done.2.refs_2_.refs_3_ = bf16[8,40,256]{2,1,0:T(8,128)(2,1)S(1)} collective-permute-done((bf16[8,40,256]{2,1,0:T(8,128)(2,1)S(1)}, bf16[8,40,256]{2,1,0:T(8,128)(2,1)S(1)}, u32[]{:S(2)}, u32[]{:S(2)}) %collective-permute-start.2) | collective-permute-done | bytes 163872 | tf_op jit(solution)/shard_map/ppermute | solution.py:228
  27.8 0.0 collective-permute-done.1.refs_1_.refs_2_
  27.8 2.5 %collective-permute-done.refs_0_.refs_1_ = bf16[8,40,256]{2,1,0:T(8,128)(2,1)S(1)} collective-permute-done((bf16[8,40,256]{2,1,0:T(8,128)(2,1)S(1)}, bf16[8,40,256]{2,1,0:T(8,128)(2,1)S(1)}, u32[]{:S(2)}, u32[]{:S(2)}) %collective-permute-start) | collective-permute-done | bytes 163872 | tf_op jit(solution)/shard_map/ppermute | solution.py:228
  30.3 0.1 pad_maximum_fusion
  30.4 0.1 collective-permute-start.3
  30.5 1.1 %shard_map.62 = (f32[256,1024]{1,0:T(8,128)S(1)}, f32[256,1024]{1,0:T(8,128)S(1)}, f32[256,1024]{1,0:T(8,128)S(1)}, f32[64,1024]{1,0:T(8,128)S(1)}) custom-call(bf16[8,40,256]{2,1,0:T(8,128)(2,1)S(1)} %collective-permute-done.refs_0_.refs_1_, bf16[8,40,256]{2,1,0:T(8,128)(2,1)S(1)} %collective-permute-done.1.refs_1_.refs_2_, ...), custom_call_target="tpu_custom_call" | custom-call | tf_op jit(solution)/shard_map/pallas_call | solution.py:21
  31.7 0.9 %collective-permute-done.3.refs_0_.refs_4_ = bf16[32,40,256]{2,1,0:T(8,128)(2,1)S(1)} collective-permute-done((bf16[32,40,256]{2,1,0:T(8,128)(2,1)S(1)}, bf16[32,40,256]{2,1,0:T(8,128)(2,1)S(1)}, u32[]{:S(2)}, u32[]{:S(2)}) %collective-permute-start.3) | collective-permute-done | bytes 655392 | tf_op jit(solution)/shard_map/ppermute | solution.py:228
  32.6 1.6 %shard_map.63 = (f32[256,1024]{1,0:T(8,128)S(1)}, f32[256,1024]{1,0:T(8,128)S(1)}, f32[256,1024]{1,0:T(8,128)S(1)}, f32[256,1024]{1,0:T(8,128)S(1)}, f32[64,1024...) custom-call(bf16[32,40,256]{2,1,0:T(8,128)(2,1)S(1)} %collective-permute-done.3.refs_0_.refs_4_, ...), custom_call_target="tpu_custom_call" | custom-call | tf_op jit(solution)/shard_map/pallas_call | solution.py:21
  34.1 1.6 %collective-permute-start.4 = (bf16[64,1024]{1,0:T(8,128)(2,1)S(1)}, bf16[64,1024]{1,0:T(8,128)(2,1)S(1)}, u32[]{:S(2)}, u32[]{:S(2)}) collective-permute-start(bf16[64,1024]{1,0:T(8,128)(2,1)S(1)} %get-tuple-element.57), channel_id=1, source_target_pairs={{0,64},{1,193},{64,0},{65,129},{128,192},{129,65},{192,128},{193,1... | collective-permute-start | bytes 393224 | tf_op jit(solution)/shard_map/ppermute | solution.py:234
  35.7 3.5 %collective-permute-done.4.other = bf16[64,1024]{1,0:T(8,128)(2,1)S(1)} collective-permute-done((bf16[64,1024]{1,0:T(8,128)(2,1)S(1)}, bf16[64,1024]{1,0:T(8,128)(2,1)S(1)}, u32[]{:S(2)}, u32[]{:S(2)}) %collective-permute-start.4) | collective-permute-done | bytes 131104 | tf_op jit(solution)/shard_map/ppermute | solution.py:234
  39.2 2.9 %collective-permute-start.5 = (bf16[64,1024]{1,0:T(8,128)(2,1)S(1)}, bf16[64,1024]{1,0:T(8,128)(2,1)S(1)}, u32[]{:S(2)}, u32[]{:S(2)}) collective-permute-start(bf16[64,1024]{1,0:T(8,128)(2,1)S(1)} %get-tuple-element.59), channel_id=1, source_target_pairs={{0,192},{1,65},{64,128},{65,1},{128,64},{129,193},{192,0},{193,129... | collective-permute-start | bytes 393224 | tf_op jit(solution)/shard_map/ppermute | solution.py:234
  42.1 3.4 %collective-permute-done.5.other = bf16[64,1024]{1,0:T(8,128)(2,1)S(1)} collective-permute-done((bf16[64,1024]{1,0:T(8,128)(2,1)S(1)}, bf16[64,1024]{1,0:T(8,128)(2,1)S(1)}, u32[]{:S(2)}, u32[]{:S(2)}) %collective-permute-start.5) | collective-permute-done | bytes 131104 | tf_op jit(solution)/shard_map/ppermute | solution.py:234
  45.5 0.1 shard_map.65.refs_5_.refs_8_
  45.6 1.5 %shard_map.66 = (bf16[1024,1024]{1,0:T(8,128)(2,1)S(1)}, bf16[1024,256]{1,0:T(8,128)(2,1)S(1)}, f32[1,1024]{1,0:T(1,128)S(1)}) custom-call(bf16[32,40,256]{2,1,0:T(8,128)(2,1)S(1)} %collective-permute-done.3.refs_0_.refs_4_, f32[256,1024]{1,0:T(8,128)S(1)} %get-tuple-element.62.refs_1_, f32[256,1024]{1,0:T(8,128)S(1)} %get-tuple-element.63.refs_2_, ...), custom_call_target="tpu_custom_call" | custom-call | tf_op jit(solution)/shard_map/pallas_call | solution.py:21
  47.2 0.1 collective-permute-start.9
  47.3 1.5 %shard_map.67 = (bf16[1024,1024]{1,0:T(8,128)(2,1)S(1)}, f32[1024,256]{1,0:T(8,128)S(1)}, f32[1,1024]{1,0:T(1,128)S(1)}) custom-call(bf16[8,40,256]{2,1,0:T(8,128)(2,1)S(1)} %all-to-all-done.refs_0_, bf16[8,40,256]{2,1,0:T(8,128)(2,1)S(1)} %collective-permute-done.refs_0_.refs_1_, bf16[8,40,256]{2,1,0:T(8,128)(2,1)S(1)} %collective-permute-done.1.refs_1_.refs_2_, ...), custom_call_target="tpu_custom_call" | custom-call | tf_op jit(solution)/shard_map/pallas_call | solution.py:21
  48.8 0.4 collective-permute-done.9
  49.2 0.2 fusion
  49.4 0.3 collective-permute-start.12
  49.7 0.9 %collective-permute-start.10 = (bf16[8,32,256]{2,1,0:T(8,128)(2,1)S(1)}, bf16[8,32,256]{2,1,0:T(8,128)(2,1)S(1)}, u32[]{:S(2)}, u32[]{:S(2)}) collective-permute-start(bf16[8,32,256]{2,1,0:T(8,128)(2,1)S(1)} %bitcast.10), channel_id=1, source_target_pairs={{0,32},{16,48},{32,0},{48,16},{1,33},{17,49},{33,1},{49,17},{2,34}... | collective-permute-start | bytes 393224 | tf_op jit(solution)/shard_map/ppermute | solution.py:228
  50.6 0.9 %collective-permute-start.11 = (bf16[8,32,256]{2,1,0:T(8,128)(2,1)S(1)}, bf16[8,32,256]{2,1,0:T(8,128)(2,1)S(1)}, u32[]{:S(2)}, u32[]{:S(2)}) collective-permute-start(bf16[8,32,256]{2,1,0:T(8,128)(2,1)S(1)} %bitcast.9), channel_id=1, source_target_pairs={{0,48},{16,0},{32,16},{48,32},{1,49},{17,1},{33,17},{49,33},{2,50}... | collective-permute-start | bytes 393224 | tf_op jit(solution)/shard_map/ppermute | solution.py:228
  51.5 1.3 %shard_map.68 = (f32[256,256]{1,0:T(8,128)S(1)}, bf16[256,256]{1,0:T(8,128)(2,1)S(1)}, bf16[256,256]{1,0:T(8,128)(2,1)S(1)}, bf16[256,256]{1,0:T(8,128)(2,1)S(1)}) custom-call(bf16[8,40,256]{2,1,0:T(8,128)(2,1)S(1)} %all-to-all-done.refs_0_, bf16[8,40,256]{2,1,0:T(8,128)(2,1)S(1)} %collective-permute-done.refs_0_.refs_1_, ...), custom_call_target="tpu_custom_call" | custom-call | tf_op jit(solution)/shard_map/pallas_call | solution.py:21
  52.8 0.4 collective-permute-start.6
  53.1 2.6 %collective-permute-start.7 = (bf16[256,256]{1,0:T(8,128)(2,1)S(1)}, bf16[256,256]{1,0:T(8,128)(2,1)S(1)}, u32[]{:S(2)}, u32[]{:S(2)}) collective-permute-start(bf16[256,256]{1,0:T(8,128)(2,1)S(1)} %get-tuple-element.72), channel_id=1, source_target_pairs={{0,192},{1,65},{64,128},{65,1},{128,64},{129,193},{192,0},{193,129... | collective-permute-start | bytes 393224 | tf_op jit(solution)/shard_map/ppermute | solution.py:234
  55.8 0.1 collective-permute-done.12
  55.8 1.8 %collective-permute-start.8 = (bf16[256,256]{1,0:T(8,128)(2,1)S(1)}, bf16[256,256]{1,0:T(8,128)(2,1)S(1)}, u32[]{:S(2)}, u32[]{:S(2)}) collective-permute-start(bf16[256,256]{1,0:T(8,128)(2,1)S(1)} %get-tuple-element.73), channel_id=1, source_target_pairs={{0,128},{64,192},{128,0},{192,64},{1,129},{65,193},{129,1},{193,65... | collective-permute-start | bytes 393224 | tf_op jit(solution)/shard_map/ppermute | solution.py:228
  57.6 0.0 collective-permute-done.10
  57.6 1.8 %collective-permute-done.11 = bf16[8,32,256]{2,1,0:T(8,128)(2,1)S(1)} collective-permute-done((bf16[8,32,256]{2,1,0:T(8,128)(2,1)S(1)}, bf16[8,32,256]{2,1,0:T(8,128)(2,1)S(1)}, u32[]{:S(2)}, u32[]{:S(2)}) %collective-permute-start.11) | collective-permute-done | bytes 131104 | tf_op jit(solution)/shard_map/ppermute | solution.py:228
  59.4 0.7 add_convert_fusion
  60.2 3.4 %all-to-all-start.1 = ((bf16[8,32,256]{2,1,0:T(8,128)(2,1)}), bf16[8,32,256]{2,1,0:T(8,128)(2,1)S(1)}, u32[]{:S(2)}, u32[]{:S(2)}) async-start(bf16[8,32,256]{2,1,0:T(8,128)(2,1)} %add_convert_fusion), calls=%async_computation.1 | async-start | bytes 262144 | tf_op jit(solution)/shard_map/all_to_all | solution.py:249
  63.5 0.0 collective-permute-done.6
  63.5 0.0 collective-permute-done.7
  63.6 0.0 collective-permute-done.8
  63.6 0.1 add_bitcast_fusion
  63.6 0.8 %copy.6 = f32[256,256]{1,0:T(8,128)} copy(f32[256,256]{0,1:T(8,128)S(1)} %add_bitcast_fusion) | data formatting | bytes 524288
  64.5 8.5 %all-to-all-done.1 = bf16[8,32,256]{2,1,0:T(8,128)(2,1)S(1)} async-done(((bf16[8,32,256]{2,1,0:T(8,128)(2,1)}), bf16[8,32,256]{2,1,0:T(8,128)(2,1)S(1)}, u32[]{:S(2)}, u32[]{:S(2)}) %all-to-all-start.1) | async-done | bytes 131104 | tf_op jit(solution)/shard_map/all_to_all | solution.py:249
  73.0 0.6 convert_reduce_fusion
  (4 shorter events, 0.1 us)
Async XLA Ops:
  2.1 18.2 %all-to-all-start = ((bf16[8,40,256]{2,1,0:T(8,128)(2,1)}), bf16[8,40,256]{2,1,0:T(8,128)(2,1)S(1)}, u32[]{:S(2)}, u32[]{:S(2)}) async-start(bf16[8,40,256]{2,1,0:T(8,128)(2,1)} %shard_map.59), calls=%async_computation | async-start | bytes 327680 | tf_op jit(solution)/shard_map/all_to_all | solution.py:264
  10.6 1.2 %copy-start = (bf16[2048,256]{1,0:T(8,128)(2,1)S(1)}, bf16[2048,256]{1,0:T(8,128)(2,1)}, u32[]{:S(2)}) copy-start(bf16[2048,256]{1,0:T(8,128)(2,1)} %features.1) | copy-start | bytes 3145732
  11.8 0.9 %copy-start.1 = (bf16[2048,64]{0,1:T(8,128)(2,1)S(1)}, bf16[2048,64]{0,1:T(8,128)(2,1)}, u32[]{:S(2)}) copy-start(bf16[2048,64]{0,1:T(8,128)(2,1)} %param.7) | copy-start | bytes 786436
  20.4 7.4 %collective-permute-start.2 = (bf16[8,40,256]{2,1,0:T(8,128)(2,1)S(1)}, bf16[8,40,256]{2,1,0:T(8,128)(2,1)S(1)}, u32[]{:S(2)}, u32[]{:S(2)}) collective-permute-start(bf16[8,40,256]{2,1,0:T(8,128)(2,1)S(1)} %all-to-all-done.refs_0_), channel_id=1, source_target_pairs={{0,32},{16,48},{32,0},{48,16},{1,33},{17,49},{33,1},{49,17},{2,34}... | collective-permute-start | bytes 491528 | tf_op jit(solution)/shard_map/ppermute | solution.py:228
  21.6 6.2 %collective-permute-start.1 = (bf16[8,40,256]{2,1,0:T(8,128)(2,1)S(1)}, bf16[8,40,256]{2,1,0:T(8,128)(2,1)S(1)}, u32[]{:S(2)}, u32[]{:S(2)}) collective-permute-start(bf16[8,40,256]{2,1,0:T(8,128)(2,1)S(1)} %all-to-all-done.refs_0_), channel_id=1, source_target_pairs={{0,16},{16,32},{32,48},{48,0},{1,17},{17,33},{33,49},{49,1},{2,18}... | collective-permute-start | bytes 491528 | tf_op jit(solution)/shard_map/ppermute | solution.py:228
  23.8 6.5 %collective-permute-start = (bf16[8,40,256]{2,1,0:T(8,128)(2,1)S(1)}, bf16[8,40,256]{2,1,0:T(8,128)(2,1)S(1)}, u32[]{:S(2)}, u32[]{:S(2)}) collective-permute-start(bf16[8,40,256]{2,1,0:T(8,128)(2,1)S(1)} %all-to-all-done.refs_0_), channel_id=1, source_target_pairs={{0,48},{16,0},{32,16},{48,32},{1,49},{17,1},{33,17},{49,33},{2,50}... | collective-permute-start | bytes 491528 | tf_op jit(solution)/shard_map/ppermute | solution.py:228
  30.4 2.2 %collective-permute-start.3 = (bf16[32,40,256]{2,1,0:T(8,128)(2,1)S(1)}, bf16[32,40,256]{2,1,0:T(8,128)(2,1)S(1)}, u32[]{:S(2)}, u32[]{:S(2)}) collective-permute-start(bf16[32,40,256]{2,1,0:T(8,128)(2,1)S(1)} %pad_maximum_fusion), channel_id=1, source_target_pairs={{0,1},{1,0},{2,3},{3,2},{4,5},{5,4},{6,7},{7,6},{8,9},{9,8},{10,11... | collective-permute-start | bytes 1966088 | tf_op jit(solution)/shard_map/ppermute | solution.py:228
  34.1 5.1 %collective-permute-start.4 = (bf16[64,1024]{1,0:T(8,128)(2,1)S(1)}, bf16[64,1024]{1,0:T(8,128)(2,1)S(1)}, u32[]{:S(2)}, u32[]{:S(2)}) collective-permute-start(bf16[64,1024]{1,0:T(8,128)(2,1)S(1)} %get-tuple-element.57), channel_id=1, source_target_pairs={{0,64},{1,193},{64,0},{65,129},{128,192},{129,65},{192,128},{193,1... | collective-permute-start | bytes 393224 | tf_op jit(solution)/shard_map/ppermute | solution.py:234
  39.2 6.3 %collective-permute-start.5 = (bf16[64,1024]{1,0:T(8,128)(2,1)S(1)}, bf16[64,1024]{1,0:T(8,128)(2,1)S(1)}, u32[]{:S(2)}, u32[]{:S(2)}) collective-permute-start(bf16[64,1024]{1,0:T(8,128)(2,1)S(1)} %get-tuple-element.59), channel_id=1, source_target_pairs={{0,192},{1,65},{64,128},{65,1},{128,64},{129,193},{192,0},{193,129... | collective-permute-start | bytes 393224 | tf_op jit(solution)/shard_map/ppermute | solution.py:234
  47.2 2.0 %collective-permute-start.9 = (bf16[1024,256]{1,0:T(8,128)(2,1)S(1)}, bf16[1024,256]{1,0:T(8,128)(2,1)S(1)}, u32[]{:S(2)}, u32[]{:S(2)}) collective-permute-start(bf16[1024,256]{1,0:T(8,128)(2,1)S(1)} %get-tuple-element.75), channel_id=1, source_target_pairs={{0,1},{1,0},{2,3},{3,2},{4,5},{5,4},{6,7},{7,6},{8,9},{9,8},{10,11... | collective-permute-start | bytes 1572872 | tf_op jit(solution)/shard_map/ppermute | solution.py:228
  49.4 6.4 %collective-permute-start.12 = (bf16[8,32,256]{2,1,0:T(8,128)(2,1)S(1)}, bf16[8,32,256]{2,1,0:T(8,128)(2,1)S(1)}, u32[]{:S(2)}, u32[]{:S(2)}) collective-permute-start(bf16[8,32,256]{2,1,0:T(8,128)(2,1)S(1)} %bitcast.11), channel_id=1, source_target_pairs={{0,16},{16,32},{32,48},{48,0},{1,17},{17,33},{33,49},{49,1},{2,18}... | collective-permute-start | bytes 393224 | tf_op jit(solution)/shard_map/ppermute | solution.py:228
  49.7 8.0 %collective-permute-start.10 = (bf16[8,32,256]{2,1,0:T(8,128)(2,1)S(1)}, bf16[8,32,256]{2,1,0:T(8,128)(2,1)S(1)}, u32[]{:S(2)}, u32[]{:S(2)}) collective-permute-start(bf16[8,32,256]{2,1,0:T(8,128)(2,1)S(1)} %bitcast.10), channel_id=1, source_target_pairs={{0,32},{16,48},{32,0},{48,16},{1,33},{17,49},{33,1},{49,17},{2,34}... | collective-permute-start | bytes 393224 | tf_op jit(solution)/shard_map/ppermute | solution.py:228
  50.6 8.8 %collective-permute-start.11 = (bf16[8,32,256]{2,1,0:T(8,128)(2,1)S(1)}, bf16[8,32,256]{2,1,0:T(8,128)(2,1)S(1)}, u32[]{:S(2)}, u32[]{:S(2)}) collective-permute-start(bf16[8,32,256]{2,1,0:T(8,128)(2,1)S(1)} %bitcast.9), channel_id=1, source_target_pairs={{0,48},{16,0},{32,16},{48,32},{1,49},{17,1},{33,17},{49,33},{2,50}... | collective-permute-start | bytes 393224 | tf_op jit(solution)/shard_map/ppermute | solution.py:228
  52.8 10.8 %collective-permute-start.6 = (bf16[256,256]{1,0:T(8,128)(2,1)S(1)}, bf16[256,256]{1,0:T(8,128)(2,1)S(1)}, u32[]{:S(2)}, u32[]{:S(2)}) collective-permute-start(bf16[256,256]{1,0:T(8,128)(2,1)S(1)} %get-tuple-element.71), channel_id=1, source_target_pairs={{0,64},{1,193},{64,0},{65,129},{128,192},{129,65},{192,128},{193,1... | collective-permute-start | bytes 393224 | tf_op jit(solution)/shard_map/ppermute | solution.py:234
  53.1 10.4 %collective-permute-start.7 = (bf16[256,256]{1,0:T(8,128)(2,1)S(1)}, bf16[256,256]{1,0:T(8,128)(2,1)S(1)}, u32[]{:S(2)}, u32[]{:S(2)}) collective-permute-start(bf16[256,256]{1,0:T(8,128)(2,1)S(1)} %get-tuple-element.72), channel_id=1, source_target_pairs={{0,192},{1,65},{64,128},{65,1},{128,64},{129,193},{192,0},{193,129... | collective-permute-start | bytes 393224 | tf_op jit(solution)/shard_map/ppermute | solution.py:234
  55.8 7.7 %collective-permute-start.8 = (bf16[256,256]{1,0:T(8,128)(2,1)S(1)}, bf16[256,256]{1,0:T(8,128)(2,1)S(1)}, u32[]{:S(2)}, u32[]{:S(2)}) collective-permute-start(bf16[256,256]{1,0:T(8,128)(2,1)S(1)} %get-tuple-element.73), channel_id=1, source_target_pairs={{0,128},{64,192},{128,0},{192,64},{1,129},{65,193},{129,1},{193,65... | collective-permute-start | bytes 393224 | tf_op jit(solution)/shard_map/ppermute | solution.py:228
  60.2 12.8 %all-to-all-start.1 = ((bf16[8,32,256]{2,1,0:T(8,128)(2,1)}), bf16[8,32,256]{2,1,0:T(8,128)(2,1)S(1)}, u32[]{:S(2)}, u32[]{:S(2)}) async-start(bf16[8,32,256]{2,1,0:T(8,128)(2,1)} %add_convert_fusion), calls=%async_computation.1 | async-start | bytes 262144 | tf_op jit(solution)/shard_map/all_to_all | solution.py:249
